TPU v7x, 32 devices: a whole 2x2x4 slice. The times are simulated.
32 devices in a mesh: edge: 8 (over y, x, core), feat: 4 (over z).
Axes of the slice: x: 2, y: 2, z: 4, core: 2. Of those that a mesh axis runs over, the one named last changes fastest.
Arguments:
- node_latents: bfloat16 [4, 4096, 256], P('feat', 'edge'), may hold values from -6 to 6
- edge_latents: bfloat16 [4, 32768, 256], P('feat', 'edge'), may hold values from -6 to 6
- senders: int32 [32768], P('edge'), may hold values from 0 to 4095, as said below
- receivers: int32 [32768], P('edge'), may hold values from 0 to 4095, as said below
- regions: int32 [32768], P('edge'), may hold values from 0 to 23
- forced: int32 [4096], P('edge'), may hold values 0 or 1
- params: float32 [1824, 256], P('feat'), may hold values from -1.5 to 1.5, as said below
- first_moment: float32 [1824, 256], P('feat'), may hold values from -0.34 to 0.34
- second_moment: float32 [1824, 256], P('feat'), may hold values from 0.004 to 0.22
- averaged: float32 [1824, 256], P('feat'), may hold values from -1.7 to 1.7
- step: int32 [1], replicated, may hold values from 1 to 20
- cotangent: float32 [4, 4096, 256], P('feat', 'edge'), may hold values from -6 to 6
Outputs:
- new_latents: float32 [4, 4096, 256], P('feat', 'edge')
- grad_latents: float32 [4, 4096, 256], P('feat', 'edge')
- grad_edges: bfloat16 [4, 32768, 256], P('feat', 'edge')
- new_first: float32 [1824, 256], P('feat')
- new_second: float32 [1824, 256], P('feat')
- new_params: float32 [1824, 256], P('feat')
- new_average: float32 [1824, 256], P('feat')
- grad_norm: float32 [1], replicated
- vector_grads: float32 [8, 256], replicated
Inputs may be any that keep to these rules, and one draw needn't show every extreme that they name: `senders`: nodes are numbered so that node block b is nodes b * 512 to (b + 1) * 512 - 1. Edge k lies in edge block e = k // 4096; its sender lies in node block e - 1, e or e + 1, taken cyclically over the 4096 nodes. `receivers`: the receiver of edge k lies in node block e - 1, e or e + 1 of its edge block e = k // 4096, taken cyclically. `params`: parameters scaled by fan-in; gains near one.
All inputs are finite; a program needn't handle non-finite values. No bound on the sum of `forced` on one device may be relied on, other than what follows from the above.
Results may differ from a plain program's by a relative error of at most 0.0039.
The roundings to bfloat16 on the way count: a program that leaves them out, or rounds other values in their place, can miss the bound.
Values may be sent and summed in bfloat16 or wider, within the bound.
No kernel may reach another device: no remote copies, remote signals or barrier semaphores. Data moves between devices by JAX's collectives and lax.ppermute only.
A program may use at most 128 MiB of HBM per device.

v0:
```python
import jax
import jax.numpy as jnp
from jax import lax
from jax.sharding import PartitionSpec as P

NORM_EPS = 1e-05
MAX_NORM = 512.0
RATE = 0.05
BETA_ONE = 0.9
BETA_TWO = 0.95
ADAM_EPS = 1e-08
WEIGHT_DECAY = 0.1
AVERAGE_DECAY = 0.999


def padded(cells, sides, width):
    for axis, dim in sides:
        count = lax.axis_size(axis)
        head = lax.slice_in_dim(cells, 0, width, axis=dim)
        tail = lax.slice_in_dim(cells, cells.shape[dim] - width, cells.shape[dim], axis=dim)
        cells = jnp.concatenate(
            [
                lax.ppermute(tail, axis, [(i, (i + 1) % count) for i in range(count)]),
                cells,
                lax.ppermute(head, axis, [((i + 1) % count, i) for i in range(count)]),
            ],
            axis=dim,
        )
    return cells


def passed_along(value, axis, steps):
    count = lax.axis_size(axis)
    pairs = [(source, (source + steps) % count) for source in range(count)]
    return lax.ppermute(value, axis, pairs)


def product(left, right):
    return jnp.dot(left, right, preferred_element_type=jnp.float32)


def outer_product(left, right):
    return lax.dot_general(
        left, right, (((0,), (0,)), ((), ())), preferred_element_type=jnp.float32
    )


def product_transposed(left, right):
    return lax.dot_general(
        left, right, (((1,), (1,)), ((), ())), preferred_element_type=jnp.float32
    )


def pick_rows(table, indices):
    return jnp.take(table, indices, axis=0)


def add_rows(values, indices, rows):
    return jax.ops.segment_sum(values, indices, num_segments=rows)


def normalized(values):
    center = values - jnp.mean(values, axis=-1, keepdims=True)
    spread = jnp.mean(center * center, axis=-1, keepdims=True)
    inverse = lax.rsqrt(spread + NORM_EPS)
    return (center * inverse, inverse)


def layer_norm(values, gain, shift):
    unit, inverse = normalized(values)
    return unit * gain + shift


def norm_backward(values, gain, upstream):
    unit, inverse = normalized(values)
    scaled = upstream * gain
    inner = (
        scaled
        - jnp.mean(scaled, axis=-1, keepdims=True)
        - unit * jnp.mean(scaled * unit, axis=-1, keepdims=True)
    )
    return (inverse * inner, jnp.sum(upstream * unit, axis=0), jnp.sum(upstream, axis=0))


def silu_slope(values):
    sigma = jax.nn.sigmoid(values)
    return sigma * (1.0 + values * (1.0 - sigma))


def neighbourhood(latents):
    return padded(latents, (("edge", 0),), latents.shape[0])


def on_device(
    node_latents,
    edge_latents,
    senders,
    receivers,
    regions,
    forced,
    params,
    first_moment,
    second_moment,
    averaged,
    step,
    cotangent,
):
    latents = node_latents[0]
    edges = edge_latents[0]
    upstream = cotangent[0]
    width = latents.shape[1]
    node_rows = latents.shape[0]
    total_nodes = node_rows * lax.axis_size("edge")
    lowest = (lax.axis_index("edge") - 1) * node_rows
    send_local = jnp.mod(senders - lowest, total_nodes)
    recv_local = jnp.mod(receivers - lowest, total_nodes)
    weights = lax.all_gather(params.astype(jnp.bfloat16), "feat", axis=0, tiled=True)
    first = weights[0 : 3 * width]
    second = weights[3 * width : 4 * width]
    node_first = weights[4 * width : 6 * width]
    node_second = weights[6 * width : 7 * width]
    vectors = weights[7 * width : 7 * width + 8].astype(jnp.float32)
    table = weights[7 * width + 8 :]
    region_onehot = jax.nn.one_hot(regions, table.shape[0], dtype=jnp.bfloat16)
    near_nodes = neighbourhood(latents)
    from_send = pick_rows(near_nodes, send_local)
    from_recv = pick_rows(near_nodes, recv_local)
    pre = product(from_send, first[0:width]) + product(from_recv, first[width : 2 * width])
    pre = (
        pre
        + product(edges, first[2 * width : 3 * width])
        + vectors[0]
        + product(region_onehot, table)
    )
    hidden = jax.nn.silu(pre).astype(jnp.bfloat16)
    inner = product(hidden, second) + vectors[1]
    from_send, from_recv, pre, hidden, inner = (from_send, from_recv, pre, hidden, inner)
    messages = layer_norm(inner, vectors[2], vectors[3])
    partial_value = add_rows(messages, recv_local, 3 * node_rows)
    from_below = passed_along(partial_value[2 * node_rows :], "edge", 1)
    from_above = passed_along(partial_value[0:node_rows], "edge", -1)
    aggregate = (partial_value[node_rows : 2 * node_rows] + from_below + from_above).astype(
        jnp.bfloat16
    )
    pre_node = (
        product(latents, node_first[0:width])
        + product(aggregate, node_first[width : 2 * width])
        + vectors[4]
    )
    hidden_node = jax.nn.silu(pre_node).astype(jnp.bfloat16)
    inner_node = product(hidden_node, node_second) + vectors[5]
    update = layer_norm(inner_node, vectors[6], vectors[7])
    keep = (1 - forced).astype(jnp.float32)[:, None]
    new_latents = latents.astype(jnp.float32) + keep * update
    d_update = upstream * keep
    d_inner_node, d_gain_node, d_shift_node = norm_backward(inner_node, vectors[6], d_update)
    d_inner_node = d_inner_node.astype(jnp.bfloat16)
    g_node_second = outer_product(hidden_node, d_inner_node)
    d_bias_node_second = jnp.sum(d_inner_node.astype(jnp.float32), axis=0)
    d_pre_node = (product_transposed(d_inner_node, node_second) * silu_slope(pre_node)).astype(
        jnp.bfloat16
    )
    g_node_first = jnp.concatenate(
        [outer_product(latents, d_pre_node), outer_product(aggregate, d_pre_node)], axis=0
    )
    d_bias_node_first = jnp.sum(d_pre_node.astype(jnp.float32), axis=0)
    d_from_nodes = product_transposed(d_pre_node, node_first[0:width])
    d_aggregate = product_transposed(d_pre_node, node_first[width : 2 * width]).astype(jnp.bfloat16)
    near_back = padded(d_aggregate, (("edge", 0),), node_rows)
    d_messages = pick_rows(near_back, recv_local).astype(jnp.float32)
    d_inner, d_gain_edge, d_shift_edge = norm_backward(inner, vectors[2], d_messages)
    d_inner = d_inner.astype(jnp.bfloat16)
    g_second = outer_product(hidden, d_inner)
    d_bias_second = jnp.sum(d_inner.astype(jnp.float32), axis=0)
    d_pre = (product_transposed(d_inner, second) * silu_slope(pre)).astype(jnp.bfloat16)
    g_first = jnp.concatenate(
        [
            outer_product(from_send, d_pre),
            outer_product(from_recv, d_pre),
            outer_product(edges, d_pre),
        ],
        axis=0,
    )
    d_bias_first = jnp.sum(d_pre.astype(jnp.float32), axis=0)
    g_table = outer_product(region_onehot, d_pre)
    d_send = product_transposed(d_pre, first[0:width])
    d_recv = product_transposed(d_pre, first[width : 2 * width])
    grad_edges = product_transposed(d_pre, first[2 * width : 3 * width]).astype(jnp.bfloat16)
    node_partial = add_rows(d_send, send_local, 3 * node_rows) + add_rows(
        d_recv, recv_local, 3 * node_rows
    )
    grads_below = passed_along(
        node_partial[2 * node_rows :].astype(jnp.bfloat16), "edge", 1
    ).astype(jnp.float32)
    grads_above = passed_along(node_partial[0:node_rows].astype(jnp.bfloat16), "edge", -1).astype(
        jnp.float32
    )
    d_nodes = node_partial[node_rows : 2 * node_rows] + grads_below + grads_above
    grad_latents = upstream + d_from_nodes + d_nodes
    vector_rows = jnp.stack(
        [
            d_bias_first,
            d_bias_second,
            d_gain_edge,
            d_shift_edge,
            d_bias_node_first,
            d_bias_node_second,
            d_gain_node,
            d_shift_node,
        ],
        axis=0,
    )
    local_grad = jnp.concatenate(
        [g_first, g_second, g_node_first, g_node_second, vector_rows, g_table], axis=0
    )
    share = params.shape[0]
    summed = lax.psum(local_grad, ("edge", "feat"))
    owned = lax.dynamic_slice_in_dim(summed, lax.axis_index("feat") * share, share, 0)
    rows_here = lax.axis_index("feat") * share + lax.broadcasted_iota(jnp.int32, (8, share), 1)
    wanted = 7 * width + lax.broadcasted_iota(jnp.int32, (8, share), 0)
    select = (rows_here == wanted).astype(jnp.float32)
    vector_piece = jnp.dot(
        select, owned, precision=lax.Precision.HIGHEST, preferred_element_type=jnp.float32
    )
    squares, vector_total = lax.psum((jnp.sum(owned * owned), vector_piece), "feat")
    grad_norm = jnp.sqrt(squares)
    factor = jnp.minimum(1.0, MAX_NORM / (grad_norm + 1e-06))
    clipped = owned * factor
    vector_grads = vector_total * factor
    new_first = BETA_ONE * first_moment + (1.0 - BETA_ONE) * clipped
    new_second = BETA_TWO * second_moment + (1.0 - BETA_TWO) * clipped * clipped
    count_steps = step[0].astype(jnp.float32)
    first_hat = new_first / (1.0 - jnp.power(BETA_ONE, count_steps))
    second_hat = new_second / (1.0 - jnp.power(BETA_TWO, count_steps))
    new_params = params - RATE * (
        first_hat / (jnp.sqrt(second_hat) + ADAM_EPS) + WEIGHT_DECAY * params
    )
    decay_now = jnp.minimum(AVERAGE_DECAY, (1.0 + count_steps) / (10.0 + count_steps))
    new_average = decay_now * averaged + (1.0 - decay_now) * new_params
    return (
        new_latents[None],
        grad_latents[None],
        grad_edges[None],
        new_first,
        new_second,
        new_params,
        new_average,
        grad_norm.reshape(1),
        vector_grads,
    )


def solution(mesh):
    placed = (
        P("feat", "edge", None),
        P("feat", "edge", None),
        P("edge"),
        P("edge"),
        P("edge"),
        P("edge"),
        P("feat", None),
        P("feat", None),
        P("feat", None),
        P("feat", None),
        P(),
        P("feat", "edge", None),
    )
    return jax.shard_map(
        on_device,
        mesh=mesh,
        in_specs=placed,
        out_specs=(
            P("feat", "edge", None),
            P("feat", "edge", None),
            P("feat", "edge", None),
            P("feat", None),
            P("feat", None),
            P("feat", None),
            P("feat", None),
            P(),
            P(),
        ),
        check_vma=False,
    )
```

profile of v0, /device:TPU:0, one launch (start us, length us, event | category | flops | bytes accessed | tf_op | source)
XLA Modules:
  0.0 374.1 jit_solution(12631992785596046417)
XLA Ops:
  7.2 1.2 copy.42
  9.0 2.9 collective-permute-start.1
  12.7 1.0 convert_element_type.71
  13.8 22.2 %all_gather.3 = bf16[1824,256]{1,0:T(8,128)(2,1)S(1)} all-gather(bf16[456,256]{1,0:T(8,128)(2,1)S(1)} %convert_element_type.71), channel_id=1, replica_groups=mesh['edge'=8,'feat'=4] {'feat'}, dimensions={0}, use_global_device_ids=true | all-gather | bytes 1167360 | tf_op jit(solution)/shard_map/all_gather | solution.py:117
  36.0 0.9 copy-done.10
  37.0 0.9 pad_maximum_fusion
  37.9 1.4 copy.43
  39.3 17.0 %gather_fusion = bf16[4096,256]{1,0:T(8,128)(2,1)} fusion(bf16[1536,256]{1,0:T(8,128)(2,1)S(1)} %copy.43, s32[4096]{0:T(1024)S(1)} %fusion.66), kind=kCustom, calls=%fused_computation.clone | custom fusion | bytes 4210688 | tf_op jit(solution)/shard_map/jit(_take)/gather | solution.py:55
  56.4 16.9 %gather_fusion.1 = bf16[4096,256]{1,0:T(8,128)(2,1)} fusion(bf16[1536,256]{1,0:T(8,128)(2,1)S(1)} %copy.43, s32[4096]{0:T(1024)S(1)} %fusion.67), kind=kCustom, calls=%fused_computation.1.clone | custom fusion | bytes 4210688 | tf_op jit(solution)/shard_map/jit(_take)/gather | solution.py:55
  73.3 4.0 %fusion.20 = f32[4096,256]{1,0:T(8,128)S(1)} fusion(bf16[4096,256]{1,0:T(8,128)(2,1)} %gather_fusion, pred[4096]{0:T(1024)(128)(4,1)S(1)} %get-tuple-element.86, bf16[1824,256]{1,0:T(8,128)(2,1)} %copy-done.10), kind=kOutput, calls=%fused_computation.49 | convolution fusion | flops 537919488 | bytes 6426624 | tf_op jit(solution)/shard_map/dot_general | solution.py:39
  77.3 1.7 convolution_add_fusion.3
  79.0 1.7 fusion.3
  80.7 4.0 %multiply_convert_fusion = (bf16[4096,256]{1,0:T(8,128)(2,1)S(1)}, f32[4096,256]{1,0:T(8,128)}) fusion(f32[4096,256]{1,0:T(8,128)S(1)} %fusion.3, bf16[1824,256]{1,0:T(8,128)(2,1)} %copy-done.10, s32[4096]{0:T(1024)S(1)} %copy-done.23), kind=kOutput, calls=%fused_computation.30 | convolution fusion | flops 56721408 | bytes 10514432 | tf_op jit(solution)/shard_map/dot_general | solution.py:39
  84.7 1.8 fusion.82
  87.0 1.5 copy-done.1
  88.5 2.7 multiply_add_fusion
  91.2 5.6 %copy.45 = f32[4096,256]{1,0:T(8,128)} copy(f32[4096,256]{0,1:T(8,128)} %multiply_add_fusion) | data formatting | bytes 8388608 | tf_op jit(solution)/shard_map/add | solution.py:71
  96.8 24.1 %scatter_custom_fusion = f32[1536,256]{1,0:T(8,128)} fusion(s32[4096]{0:T(1024)S(1)} %get-tuple-element.58, f32[4096,256]{1,0:T(8,128)} %copy.45, f32[]{:T(128)} %constant.42.clone.1), kind=kCustom, calls=%fused_computation.57 | custom fusion | flops 1048576 | bytes 1573376 | tf_op jit(solution)/shard_map/scatter-add | solution.py:59
  120.9 2.2 fusion.79
  123.2 2.6 collective-permute-start.3
  126.4 1.2 copy.46
  127.7 1.1 fusion.41
  128.8 8.7 %collective-permute-done.2 = f32[512,256]{1,0:T(8,128)S(1)} collective-permute-done((f32[512,256]{1,0:T(8,128)}, f32[512,256]{1,0:T(8,128)S(1)}, u32[]{:S(2)}, u32[]{:S(2)}) %collective-permute-start.2) | collective-permute-done | bytes 524320 | tf_op jit(solution)/shard_map/ppermute | solution.py:35
  137.5 0.8 copy-done.21
  138.3 1.4 fusion.32
  139.8 1.3 multiply_convert_fusion.2
  141.1 1.2 fusion.83
  142.7 1.1 convert_reduce_fusion.3
  143.8 1.0 fusion.86
  144.8 1.2 convert_reduce_fusion.4
  146.1 1.3 convolution_convert_fusion.1
  147.4 2.6 collective-permute-start.5
  150.0 1.0 fusion.85
  151.0 1.0 convolution_bitcast_fusion
  152.0 4.5 %collective-permute-done.4 = bf16[512,256]{1,0:T(8,128)(2,1)S(1)} collective-permute-done((bf16[512,256]{1,0:T(8,128)(2,1)S(1)}, bf16[512,256]{1,0:T(8,128)(2,1)S(1)}, u32[]{:S(2)}, u32[]{:S(2)}) %collective-permute-start.4) | collective-permute-done | bytes 262176 | tf_op jit(solution)/shard_map/ppermute | solution.py:23
  156.6 16.9 %gather_fusion.2 = bf16[4096,256]{1,0:T(8,128)(2,1)} fusion(bf16[1536,256]{1,0:T(8,128)(2,1)S(1)} %pad_maximum_fusion.1, s32[4096]{0:T(1024)S(1)} %fusion.67), kind=kCustom, calls=%fused_computation.2.clone | custom fusion | bytes 4210688 | tf_op jit(solution)/shard_map/jit(_take)/gather | solution.py:55
  173.5 4.1 %copy.48 = bf16[4096,256]{0,1:T(8,128)(2,1)} copy(bf16[4096,256]{1,0:T(8,128)(2,1)} %gather_fusion.2) | data formatting | bytes 4194304 | tf_op jit(solution)/shard_map/jit(_take)/gather | solution.py:55
  177.6 5.3 %fusion.10 = (f32[256]{0:T(256)S(1)}, f32[4096]{0:T(1024)S(1)}, f32[4096]{0:T(1024)S(1)}, f32[256]{0:T(256)S(1)}) fusion(f32[4096,256]{0,1:T(8,128)} %copy-done.1, f32[4096]{0:T(1024)S(1)} %add_rsqrt_fusion, f32[4096]{0:T(1024)S(1)} %broadcast_multiply_fusion.2, bf16[4096,256]{0,1:T(8,128)(2,1)} %copy.48, pred[4096]{0:T(1024)(128)(4,1)S(1)} %get-tuple-element.57, ...), kind=kLoop, calls=%fused_computation.25 | loop fusion | flops 11525632 | bytes 6364160 | tf_op jit(solution)/shard_map/reduce_sum | solution.py:82
  183.0 2.3 convert_reduce_fusion.1
  185.3 1.5 fusion.84
  186.8 0.8 copy-done.25
  187.6 3.0 convert_reduce_fusion.2
  190.6 2.1 fusion.19
  192.9 2.1 fusion.21
  195.1 1.7 fusion.16
  197.1 3.6 fusion.53
  200.8 3.8 %fusion.56 = f32[4096,256]{1,0:T(8,128)} fusion(bf16[4096,256]{1,0:T(8,128)(2,1)S(1)} %get-tuple-element.83, bf16[1824,256]{1,0:T(8,128)(2,1)} %copy-done.10), kind=kOutput, calls=%fused_computation.106 | convolution fusion | flops 536870912 | bytes 6422528 | tf_op jit(solution)/shard_map/dot_general | solution.py:49
  204.6 10.1 %concatenate.11 = f32[1824,256]{1,0:T(8,128)} concatenate(f32[256,256]{1,0:T(8,128)} %fusion.19, f32[256,256]{1,0:T(8,128)} %fusion.21, f32[256,256]{1,0:T(8,128)} %fusion.16, f32[256,256]{1,0:T(8,128)} %fusion.84, f32[256,256]{1,0:T(8,128)S(1)} %copy-done.20, f32[256,256]{1,0:T(8,128)S(1)} %copy-done.19, f32[256,256]{1,0:T(8,128)S(1)} %copy-done.18, f32[1,256]{1,0:T(1,128)S(1)} %bitcast.104, ...), dimensions={0} | concatenate | bytes 3735552 | tf_op jit(solution)/shard_map/concatenate | solution.py:213
  214.7 24.0 %scatter_custom_fusion.2 = f32[1536,256]{1,0:T(8,128)} fusion(s32[4096]{0:T(1024)S(1)} %get-tuple-element.58, f32[4096,256]{1,0:T(8,128)} %fusion.53, f32[]{:T(128)} %constant.42.clone.1), kind=kCustom, calls=%fused_computation.53 | custom fusion | flops 1048576 | bytes 1573376 | tf_op jit(solution)/shard_map/scatter-add | solution.py:59
  238.8 3.1 copy.50
  241.9 24.0 %scatter_custom_fusion.1 = f32[1536,256]{1,0:T(8,128)} fusion(s32[4096]{0:T(1024)S(1)} %get-tuple-element.87, f32[4096,256]{1,0:T(8,128)} %fusion.56, f32[]{:T(128)} %constant.42.clone.1), kind=kCustom, calls=%fused_computation.55 | custom fusion | flops 1048576 | bytes 1573376 | tf_op jit(solution)/shard_map/scatter-add | solution.py:59
  265.9 3.1 copy.49
  269.0 3.4 fusion.78
  272.4 0.8 fusion.80
  273.2 2.6 collective-permute-start.7
  277.1 1.0 copy.51
  278.1 3.7 fusion.5
  282.0 1.4 fusion.30
  283.5 61.5 %all-reduce.3.cloned.1.call-done = f32[1824,256]{1,0:T(8,128)} async-done(((f32[1824,256]{1,0:T(8,128)}), f32[1824,256]{1,0:T(8,128)}) %all-reduce.3.cloned.1.call-update) | async-done | bytes 1867792 | tf_op jit(solution)/shard_map/psum | solution.py:217
  344.9 1.7 multiply_reduce_fusion.4
  346.7 1.9 fusion.38
  348.6 1.0 copy.52
  349.6 12.4 %all-reduce = (f32[]{:T(128)}, f32[8,256]{1,0:T(8,128)S(1)}) all-reduce(f32[]{:T(128)} %multiply_reduce_fusion.4, f32[8,256]{1,0:T(8,128)} %fusion.38), channel_id=1, replica_groups=mesh['edge'=8,'feat'=4] {'feat'}, use_global_device_ids=true, to_apply=%region_21.23 | all-reduce | flops 2049 | bytes 16392 | tf_op jit(solution)/shard_map/psum | solution.py:225
  363.3 2.8 multiply_add_fusion.1
  (82 shorter events, 5.0 us)
Async XLA Ops:
  7.2 71.8 %copy-start = (bf16[1,4096,256]{2,1,0:T(8,128)(2,1)S(1)}, bf16[1,4096,256]{2,1,0:T(8,128)(2,1)}, u32[]{:S(2)}) copy-start(bf16[1,4096,256]{2,1,0:T(8,128)(2,1)} %param.15) | copy-start | bytes 6291460
  7.2 337.8 %all-reduce.3.cloned.1.call-start = ((), (), s32[]{:S(2)}) async-start(), calls=%async_computation | async-start | bytes 3735552 | tf_op jit(solution)/shard_map/psum | solution.py:217
  8.5 28.5 %copy-start.14 = (bf16[1,512,256]{1,2,0:T(8,128)(2,1)}, bf16[1,512,256]{1,2,0:T(8,128)(2,1)S(1)}, u32[]{:S(2)}) copy-start(bf16[1,512,256]{1,2,0:T(8,128)(2,1)S(1)} %copy.42) | copy-start | bytes 786436
  8.5 28.5 %collective-permute-start = (bf16[512,256]{0,1:T(8,128)(2,1)S(1)}, bf16[512,256]{0,1:T(8,128)(2,1)S(1)}, u32[]{:S(2)}, u32[]{:S(2)}) collective-permute-start(bf16[512,256]{0,1:T(8,128)(2,1)S(1)} %bitcast.84), channel_id=1, source_target_pairs={{0,4},{4,8},{8,12},{12,16},{16,20},{20,24},{24,28},{28,0},{1,5},{5... | collective-permute-start | bytes 786440 | tf_op jit(solution)/shard_map/ppermute | solution.py:23
  9.0 28.0 %collective-permute-start.1 = (bf16[512,256]{0,1:T(8,128)(2,1)S(1)}, bf16[512,256]{0,1:T(8,128)(2,1)S(1)}, u32[]{:S(2)}, u32[]{:S(2)}) collective-permute-start(bf16[512,256]{0,1:T(8,128)(2,1)S(1)} %bitcast.85), channel_id=1, source_target_pairs={{4,0},{8,4},{12,8},{16,12},{20,16},{24,20},{28,24},{0,28},{5,1},{9... | collective-permute-start | bytes 786440 | tf_op jit(solution)/shard_map/ppermute | solution.py:25
  36.0 0.9 copy-start.10
  73.3 4.0 %copy-start.8 = (bf16[4096,256]{1,0:T(8,128)(2,1)S(1)}, bf16[4096,256]{1,0:T(8,128)(2,1)}, u32[]{:S(2)}) copy-start(bf16[4096,256]{1,0:T(8,128)(2,1)} %gather_fusion.1) | copy-start | bytes 6291460
  79.0 1.7 copy-start.23
  84.7 1.8 copy-start.6
  86.5 2.0 copy-start.1
  96.8 30.8 %copy-start.24 = (s32[512]{0:T(512)S(1)}, s32[512]{0:T(512)}, u32[]{:S(2)}) copy-start(s32[512]{0:T(512)} %param.19) | copy-start | bytes 6148
  96.8 30.8 %copy-start.13 = (bf16[1,512,256]{2,1,0:T(8,128)(2,1)S(1)}, bf16[1,512,256]{2,1,0:T(8,128)(2,1)}, u32[]{:S(2)}) copy-start(bf16[1,512,256]{2,1,0:T(8,128)(2,1)} %param.14) | copy-start | bytes 786436
  123.2 14.4 %collective-permute-start.2 = (f32[512,256]{1,0:T(8,128)}, f32[512,256]{1,0:T(8,128)S(1)}, u32[]{:S(2)}, u32[]{:S(2)}) collective-permute-start(f32[512,256]{1,0:T(8,128)} %get-tuple-element.61), channel_id=1, source_target_pairs={{0,4},{4,8},{8,12},{12,16},{16,20},{20,24},{24,28},{28,0},{1,5},{5... | collective-permute-start | bytes 1572872 | tf_op jit(solution)/shard_map/ppermute | solution.py:35
  123.2 15.2 %collective-permute-start.3 = (f32[512,256]{1,0:T(8,128)}, f32[512,256]{1,0:T(8,128)}, u32[]{:S(2)}, u32[]{:S(2)}) collective-permute-start(f32[512,256]{1,0:T(8,128)} %get-tuple-element.62), channel_id=1, source_target_pairs={{0,28},{4,0},{8,4},{12,8},{16,12},{20,16},{24,20},{28,24},{1,29},{... | collective-permute-start | bytes 1572872 | tf_op jit(solution)/shard_map/ppermute | solution.py:35
  137.5 0.8 copy-start.21
  139.8 2.9 copy-start.15
  146.0 10.5 %copy-start.11 = (bf16[512,256]{1,0:T(8,128)(2,1)}, bf16[512,256]{1,0:T(8,128)(2,1)S(1)}, u32[]{:S(2)}) copy-start(bf16[512,256]{1,0:T(8,128)(2,1)S(1)} %get-tuple-element.85) | copy-start | bytes 786436
  147.3 9.2 %collective-permute-start.4 = (bf16[512,256]{1,0:T(8,128)(2,1)S(1)}, bf16[512,256]{1,0:T(8,128)(2,1)S(1)}, u32[]{:S(2)}, u32[]{:S(2)}) collective-permute-start(bf16[512,256]{1,0:T(8,128)(2,1)S(1)} %convolution_convert_fusion.1), channel_id=1, source_target_pairs={{0,4},{4,8},{8,12},{12,16},{16,20},{20,24},{24,28},{28,0},{1,5},{5... | collective-permute-start | bytes 786440 | tf_op jit(solution)/shard_map/ppermute | solution.py:23
  147.4 9.1 %collective-permute-start.5 = (bf16[512,256]{1,0:T(8,128)(2,1)S(1)}, bf16[512,256]{1,0:T(8,128)(2,1)S(1)}, u32[]{:S(2)}, u32[]{:S(2)}) collective-permute-start(bf16[512,256]{1,0:T(8,128)(2,1)S(1)} %convolution_convert_fusion.1), channel_id=1, source_target_pairs={{4,0},{8,4},{12,8},{16,12},{20,16},{24,20},{28,24},{0,28},{5,1},{9... | collective-permute-start | bytes 786440 | tf_op jit(solution)/shard_map/ppermute | solution.py:25
  177.6 5.4 %copy-start.2 = (f32[4096,256]{0,1:T(8,128)S(1)}, f32[4096,256]{0,1:T(8,128)}, u32[]{:S(2)}) copy-start(f32[4096,256]{0,1:T(8,128)} %copy-done.1) | copy-start | bytes 12582916
  177.6 5.4 %copy-start.4 = (bf16[4096,256]{0,1:T(8,128)(2,1)S(1)}, bf16[4096,256]{0,1:T(8,128)(2,1)}, u32[]{:S(2)}) copy-start(bf16[4096,256]{0,1:T(8,128)(2,1)} %copy.48) | copy-start | bytes 6291460
  183.0 2.3 copy-start.7
  185.3 2.3 copy-start.25
  187.6 3.0 copy-start.5
  190.6 10.2 %copy-start.3 = (bf16[4096,256]{1,0:T(8,128)(2,1)}, bf16[4096,256]{1,0:T(8,128)(2,1)S(1)}, u32[]{:S(2)}) copy-start(bf16[4096,256]{1,0:T(8,128)(2,1)S(1)} %get-tuple-element.83) | copy-start | bytes 6291460
  190.6 2.3 copy-start.9
  200.8 3.8 %copy-start.18 = (f32[256,256]{1,0:T(8,128)S(1)}, f32[256,256]{1,0:T(8,128)}, u32[]{:S(2)}) copy-start(f32[256,256]{1,0:T(8,128)} %fusion.86) | copy-start | bytes 786436
  200.8 3.8 %copy-start.19 = (f32[256,256]{1,0:T(8,128)S(1)}, f32[256,256]{1,0:T(8,128)}, u32[]{:S(2)}) copy-start(f32[256,256]{1,0:T(8,128)} %fusion.85) | copy-start | bytes 786436
  200.8 3.8 %copy-start.20 = (f32[256,256]{1,0:T(8,128)S(1)}, f32[256,256]{1,0:T(8,128)}, u32[]{:S(2)}) copy-start(f32[256,256]{1,0:T(8,128)} %convolution_bitcast_fusion) | copy-start | bytes 786436
  269.0 8.2 %copy-start.16 = (f32[1,512,256]{1,2,0:T(8,128)S(1)}, f32[1,512,256]{1,2,0:T(8,128)}, u32[]{:S(2)}) copy-start(f32[1,512,256]{1,2,0:T(8,128)} %get-tuple-element.65) | copy-start | bytes 1572868
  273.2 8.8 %collective-permute-start.6 = (bf16[512,256]{0,1:T(8,128)(2,1)}, bf16[512,256]{0,1:T(8,128)(2,1)S(1)}, u32[]{:S(2)}, u32[]{:S(2)}) collective-permute-start(bf16[512,256]{0,1:T(8,128)(2,1)} %get-tuple-element.63), channel_id=1, source_target_pairs={{0,4},{4,8},{8,12},{12,16},{16,20},{20,24},{24,28},{28,0},{1,5},{5... | collective-permute-start | bytes 786440 | tf_op jit(solution)/shard_map/ppermute | solution.py:35
  273.2 8.8 %collective-permute-start.7 = (bf16[512,256]{0,1:T(8,128)(2,1)}, bf16[512,256]{0,1:T(8,128)(2,1)}, u32[]{:S(2)}, u32[]{:S(2)}) collective-permute-start(bf16[512,256]{0,1:T(8,128)(2,1)} %get-tuple-element.64), channel_id=1, source_target_pairs={{0,28},{4,0},{8,4},{12,8},{16,12},{20,16},{24,20},{28,24},{1,29},{... | collective-permute-start | bytes 786440 | tf_op jit(solution)/shard_map/ppermute | solution.py:35
  278.1 3.9 %copy-start.12 = (bf16[512,256]{1,0:T(8,128)(2,1)S(1)}, bf16[512,256]{1,0:T(8,128)(2,1)}, u32[]{:S(2)}) copy-start(bf16[512,256]{1,0:T(8,128)(2,1)} %copy-done.11) | copy-start | bytes 786436
  283.5 79.8 %copy-start.17 = (f32[456,256]{1,0:T(8,128)S(1)}, f32[456,256]{1,0:T(8,128)}, u32[]{:S(2)}) copy-start(f32[456,256]{1,0:T(8,128)} %param.20) | copy-start | bytes 1400836
  283.5 79.8 %copy-start.22 = (f32[456,256]{1,0:T(8,128)S(1)}, f32[456,256]{1,0:T(8,128)}, u32[]{:S(2)}) copy-start(f32[456,256]{1,0:T(8,128)} %param.23) | copy-start | bytes 1400836
Sparse Core Ops, SparseCore 0:
  214.8 130.0 all-reduce.2
where the time goes:
time: 375 us; the launch traced here: 374 us
  other arithmetic  98.5 us (26%)
  local copies, waits for them, and re-layouts  90 us (24%)
  waiting for transfers between devices  74.9 us (20%)
  matrix products  47.4 us (13%)
  blocking collectives  34.6 us (9%)
  between operations  17.2 us (5%)
  starting transfers between devices  11.5 us (3%)
    scatter-add x3, other arithmetic, add_rows(): return jax.ops.segment_sum(values, indices, num_segments=rows)  72.2 us
    psum x1, waiting for transfers between devices, on_device(): summed = lax.psum(local_grad, ('edge', 'feat'))  61.5 us
    gather x4, local copies, waits for them, and re-layouts, pick_rows(): return jnp.take(table, indices, axis=0)  55 us
    all_gather x1, blocking collectives, on_device(): lax.all_gather(params.astype(jnp.bfloat16), 'feat', axis=0, tiled=True)  22.2 us
    dot_general x7, matrix products, product_transposed(): lax.dot_general(left, right, (((1,), (1,)), ((), ())), preferred_element_...  18 us
    dot_general x8, matrix products, product(): return jnp.dot(left, right, preferred_element_type=jnp.float32)  16.7 us
    psum x1, blocking collectives, on_device(): lax.psum((jnp.sum(owned * owned), vector_piece), 'feat')  12.4 us
    dot_general x8, matrix products, outer_product(): lax.dot_general(left, right, (((0,), (0,)), ((), ())), preferred_element_...  10.7 us
  transfers between devices with their start and end apart: 9, of which 4 were waited for; matrix products, arithmetic and copies ran while one was open for 19% of the time, Pallas kernels for 0%

commit v1 on v0

v1 whole, which is shorter than its diff:
```python
import functools

import jax
import jax.numpy as jnp
from jax import lax
from jax.experimental import pallas as pl
from jax.experimental.pallas import tpu as pltpu
from jax.sharding import PartitionSpec as P

NORM_EPS = 1e-05
MAX_NORM = 512.0
RATE = 0.05
BETA_ONE = 0.9
BETA_TWO = 0.95
ADAM_EPS = 1e-08
WEIGHT_DECAY = 0.1
AVERAGE_DECAY = 0.999

LANES = 128
TILE = 1024
B16 = jnp.bfloat16
F32 = jnp.float32
I32 = jnp.int32
PARAMS = pltpu.CompilerParams(vmem_limit_bytes=56 * 1024 * 1024)


def dot(left, right):
    return jnp.dot(left, right, preferred_element_type=F32)


def dot_rows(left, right):
    return lax.dot_general(left, right, (((0,), (0,)), ((), ())), preferred_element_type=F32)


def dot_back(left, right):
    return lax.dot_general(left, right, (((1,), (1,)), ((), ())), preferred_element_type=F32)


def split(values):
    high = values.astype(B16)
    return high, (values - high.astype(F32)).astype(B16)


def whole(shape):
    return pl.BlockSpec(shape, lambda i: (0,) * len(shape))


def tiled(rows, cols):
    return pl.BlockSpec((rows, cols), lambda i: (i, 0))


def column(row):
    return jnp.broadcast_to(row, (LANES, LANES)).T


def chosen_columns(index_ref, tile, rows, first, last):
    lane = lax.broadcasted_iota(I32, (LANES, LANES), 1)
    groups = []
    for g in range(rows // LANES):
        col = column(index_ref[pl.ds(tile * (rows // LANES) + g, 1), :])
        groups.append(
            jnp.concatenate(
                [jnp.where(col == lane + base, 1.0, 0.0).astype(B16) for base in range(first, last, LANES)],
                axis=1,
            )
        )
    return jnp.concatenate(groups, axis=0)


def chosen_rows(index_row, first, count):
    node = lax.broadcasted_iota(I32, (count, index_row.shape[1]), 0) + first
    return jnp.where(index_row == node, 1.0, 0.0).astype(B16)


def gather_kernel(send_ref, recv_ref, own_ref, pair_ref, off_ref, hs_ref, hr_ref):
    tile = pl.program_id(0)
    rows = hs_ref.shape[0]
    nodes = own_ref.shape[0]
    for index_ref, out_ref in ((send_ref, hs_ref), (recv_ref, hr_ref)):
        total = None
        for slot, table in enumerate((own_ref, pair_ref, off_ref)):
            part = dot(chosen_columns(index_ref, tile, rows, slot * nodes, (slot + 1) * nodes), table[...])
            total = part if total is None else total + part
        out_ref[...] = total.astype(B16)


def gather_latents(send, recv, own, pair, off):
    nodes, width = own.shape
    edges = send.size
    out = jax.ShapeDtypeStruct((edges, width), B16)
    index = whole((edges // LANES, LANES))
    return pl.pallas_call(
        gather_kernel,
        grid=(edges // TILE,),
        in_specs=[index, index] + [whole((nodes, width))] * 3,
        out_specs=[tiled(TILE, width)] * 2,
        out_shape=[out, out],
        compiler_params=PARAMS,
        name="gather_latents",
        cost_estimate=pl.CostEstimate(
            flops=2 * 2 * edges * 3 * nodes * width, transcendentals=0, bytes_accessed=edges * width * 4
        ),
    )(send.reshape(-1, LANES), recv.reshape(-1, LANES), own, pair, off)


def edge_forward_kernel(
    region_ref, recv_row_ref, hs_ref, hr_ref, x_ref, w_ref, table_ref, vec_ref,
    hidden_ref, slope_ref, unit_ref, inverse_ref, high_ref, low_ref, pair_ref, off_ref,
):
    step = pl.program_id(0)
    rows = x_ref.shape[0]
    width = x_ref.shape[1]
    nodes = pair_ref.shape[0]
    steps = pl.num_programs(0)

    @pl.when(step < steps - 1)
    def _():
        pre = dot(hs_ref[...], w_ref[0:width, :])
        pre = pre + dot(hr_ref[...], w_ref[width : 2 * width, :])
        pre = pre + dot(x_ref[...], w_ref[2 * width : 3 * width, :])
        pre = pre + dot(chosen_columns(region_ref, step, rows, 0, LANES), table_ref[...])
        pre = pre + vec_ref[0:1, :]
        sigma = 1.0 / (1.0 + jnp.exp(-pre))
        hidden = (pre * sigma).astype(B16)
        hidden_ref[...] = hidden
        slope_ref[...] = sigma * (1.0 + pre * (1.0 - sigma))
        inner = dot(hidden, w_ref[3 * width : 4 * width, :]) + vec_ref[1:2, :]
        center = inner - jnp.mean(inner, axis=-1, keepdims=True)
        inverse = lax.rsqrt(jnp.mean(center * center, axis=-1, keepdims=True) + NORM_EPS)
        unit = center * inverse
        unit_ref[...] = unit
        inverse_ref[...] = jnp.broadcast_to(inverse, (rows, LANES))
        high, low = split(unit * vec_ref[2:3, :] + vec_ref[3:4, :])
        base = pl.multiple_of(step * rows, rows)
        high_ref[pl.ds(base, rows), :] = high
        low_ref[pl.ds(base, rows), :] = low

    @pl.when(step == steps - 1)
    def _():
        for slot, out_ref in ((1, pair_ref), (2, off_ref)):
            onehot = chosen_rows(recv_row_ref[...], slot * nodes, nodes)
            total = dot(onehot, high_ref[...]) + dot(onehot, low_ref[...])
            out_ref[...] = total.astype(out_ref.dtype)


def edge_forward(regions, recv, hs, hr, edges, weights, table, vectors, nodes, wire):
    count, width = edges.shape
    steps = count // TILE
    last = steps - 1
    tile = pl.BlockSpec((TILE, width), lambda i: (jnp.minimum(i, last), 0))
    thin = pl.BlockSpec((TILE, LANES), lambda i: (jnp.minimum(i, last), 0))
    return pl.pallas_call(
        edge_forward_kernel,
        grid=(steps + 1,),
        in_specs=[
            whole((count // LANES, LANES)), whole((1, count)), tile, tile, tile,
            whole(weights.shape), whole(table.shape), whole(vectors.shape),
        ],
        out_specs=[tile, tile, tile, thin, whole((count, width)), whole((count, width)), whole((nodes, width)), whole((nodes, width))],
        out_shape=[
            jax.ShapeDtypeStruct((count, width), B16),
            jax.ShapeDtypeStruct((count, width), F32),
            jax.ShapeDtypeStruct((count, width), F32),
            jax.ShapeDtypeStruct((count, LANES), F32),
            jax.ShapeDtypeStruct((count, width), B16),
            jax.ShapeDtypeStruct((count, width), B16),
            jax.ShapeDtypeStruct((nodes, width), wire),
            jax.ShapeDtypeStruct((nodes, width), wire),
        ],
        compiler_params=PARAMS,
        name="edge_forward",
        cost_estimate=pl.CostEstimate(
            flops=2 * count * width * (5 * width + 4 * nodes), transcendentals=2 * count * width,
            bytes_accessed=count * width * 20,
        ),
    )(regions.reshape(-1, LANES), recv.reshape(1, -1), hs, hr, edges, weights, table, vectors)


def own_sum_kernel(recv_row_ref, high_ref, low_ref, out_ref):
    onehot = chosen_rows(recv_row_ref[...], 0, out_ref.shape[0])
    total = dot(onehot, high_ref[...]) + dot(onehot, low_ref[...])

    @pl.when(pl.program_id(0) == 0)
    def _():
        out_ref[...] = total

    @pl.when(pl.program_id(0) > 0)
    def _():
        out_ref[...] += total


def own_sum(recv, high, low, nodes):
    count, width = high.shape
    return pl.pallas_call(
        own_sum_kernel,
        grid=(count // TILE,),
        in_specs=[pl.BlockSpec((1, TILE), lambda i: (0, i)), tiled(TILE, width), tiled(TILE, width)],
        out_specs=whole((nodes, width)),
        out_shape=jax.ShapeDtypeStruct((nodes, width), F32),
        compiler_params=PARAMS,
        name="own_sum",
        cost_estimate=pl.CostEstimate(
            flops=4 * count * width * nodes, transcendentals=0, bytes_accessed=count * width * 4
        ),
    )(recv.reshape(1, -1), high, low)


def node_kernel(
    h_ref, own_ref, pair_ref, off_ref, w_ref, vec_ref, keep_ref, up_ref,
    new_ref, d_agg_ref, agg_ref, hidden_ref, d_inner_ref, d_pre_ref, sums_ref,
):
    width = h_ref.shape[1]
    agg = (own_ref[...] + pair_ref[...].astype(F32) + off_ref[...].astype(F32)).astype(B16)
    agg_ref[...] = agg
    h = h_ref[...]
    latent, aggregate = w_ref[4 * width : 5 * width, :], w_ref[5 * width : 6 * width, :]
    second = w_ref[6 * width : 7 * width, :]
    pre = dot(h, latent) + dot(agg, aggregate) + vec_ref[4:5, :]
    sigma = 1.0 / (1.0 + jnp.exp(-pre))
    hidden = (pre * sigma).astype(B16)
    hidden_ref[...] = hidden
    inner = dot(hidden, second) + vec_ref[5:6, :]
    center = inner - jnp.mean(inner, axis=-1, keepdims=True)
    inverse = lax.rsqrt(jnp.mean(center * center, axis=-1, keepdims=True) + NORM_EPS)
    unit = center * inverse
    keep = keep_ref[...].astype(F32)
    new_ref[...] = h.astype(F32) + keep * (unit * vec_ref[6:7, :] + vec_ref[7:8, :])
    d_update = keep * up_ref[...]
    scaled = d_update * vec_ref[6:7, :]
    d_inner = inverse * (
        scaled
        - jnp.mean(scaled, axis=-1, keepdims=True)
        - unit * jnp.mean(scaled * unit, axis=-1, keepdims=True)
    )
    d_inner = d_inner.astype(B16)
    d_inner_ref[...] = d_inner
    slope = sigma * (1.0 + pre * (1.0 - sigma))
    d_pre = (dot_back(d_inner, second) * slope).astype(B16)
    d_pre_ref[...] = d_pre
    d_agg_ref[...] = dot_back(d_pre, aggregate).astype(B16)
    sums_ref[...] = jnp.concatenate(
        [
            jnp.sum(d_pre.astype(F32), axis=0, keepdims=True),
            jnp.sum(d_inner.astype(F32), axis=0, keepdims=True),
            jnp.sum(d_update * unit, axis=0, keepdims=True),
            jnp.sum(d_update, axis=0, keepdims=True),
        ],
        axis=0,
    )


def node_update(h, own, pair, off, weights, vectors, keep, upstream):
    nodes, width = h.shape
    full = jax.ShapeDtypeStruct((nodes, width), F32)
    half = jax.ShapeDtypeStruct((nodes, width), B16)
    return pl.pallas_call(
        node_kernel,
        out_shape=[full, half, half, half, half, half, jax.ShapeDtypeStruct((4, width), F32)],
        compiler_params=PARAMS,
        name="node_update",
        cost_estimate=pl.CostEstimate(
            flops=2 * nodes * width * width * 5, transcendentals=2 * nodes * width, bytes_accessed=nodes * width * 20
        ),
    )(h, own, pair, off, weights, vectors, keep, upstream)


def node_grads_kernel(h_ref, agg_ref, hidden_ref, d_inner_ref, d_pre_ref, w_ref, up_ref, grad_ref, back_ref):
    width = h_ref.shape[1]
    d_pre = d_pre_ref[...]
    grad_ref[0:width, :] = dot_rows(h_ref[...], d_pre)
    grad_ref[width : 2 * width, :] = dot_rows(agg_ref[...], d_pre)
    grad_ref[2 * width : 3 * width, :] = dot_rows(hidden_ref[...], d_inner_ref[...])
    back_ref[...] = up_ref[...] + dot_back(d_pre, w_ref[4 * width : 5 * width, :])


def node_grads(h, agg, hidden, d_inner, d_pre, weights, upstream):
    nodes, width = h.shape
    return pl.pallas_call(
        node_grads_kernel,
        out_shape=[jax.ShapeDtypeStruct((3 * width, width), F32), jax.ShapeDtypeStruct((nodes, width), F32)],
        compiler_params=PARAMS,
        name="node_grads",
        cost_estimate=pl.CostEstimate(
            flops=2 * nodes * width * width * 4, transcendentals=0, bytes_accessed=nodes * width * 18
        ),
    )(h, agg, hidden, d_inner, d_pre, weights, upstream)


def edge_backward_kernel(
    core_ref, recv_ref, send_row_ref, recv_row_ref, region_row_ref, own_ref, pair_ref, off_ref,
    h_own_ref, h_pair_ref, h_off_ref, x_ref, hidden_ref, slope_ref, unit_ref, inverse_ref, w_ref, vec_ref,
    node_grad_ref, node_sum_ref,
    grad_x_ref, kept_ref, sent_ref, part_own_ref, part_pair_ref, part_off_ref,
    d_pre_ref, second_ref, third_ref, vec_acc_ref,
):
    step = pl.program_id(0)
    steps = pl.num_programs(0)
    rows, width = x_ref.shape
    nodes = own_ref.shape[0]
    regions = third_ref.shape[0] - width

    @pl.when(step == 0)
    def _():
        second_ref[...] = jnp.zeros_like(second_ref)
        third_ref[...] = jnp.zeros_like(third_ref)
        vec_acc_ref[...] = jnp.zeros_like(vec_acc_ref)

    @pl.when(step < steps - 1)
    def _():
        d_message = None
        for slot, table in enumerate((own_ref, pair_ref, off_ref)):
            part = dot(chosen_columns(recv_ref, step, rows, slot * nodes, (slot + 1) * nodes), table[...])
            d_message = part if d_message is None else d_message + part
        unit = unit_ref[...]
        gained = d_message * unit
        scaled = d_message * vec_ref[2:3, :]
        inverse = inverse_ref[:, 0:1]
        d_inner = inverse * (
            scaled
            - jnp.mean(scaled, axis=-1, keepdims=True)
            - unit * jnp.mean(scaled * unit, axis=-1, keepdims=True)
        )
        vec_acc_ref[0:8, :] += jnp.sum(gained.reshape(rows // 8, 8, width), axis=0)
        vec_acc_ref[8:16, :] += jnp.sum(d_message.reshape(rows // 8, 8, width), axis=0)
        d_inner = d_inner.astype(B16)
        second_ref[0:width, :] += dot_rows(hidden_ref[...], d_inner)
        second_ref[width : width + 16, :] += dot(jnp.ones((16, rows), B16), d_inner)
        d_pre = (dot_back(d_inner, w_ref[3 * width : 4 * width, :]) * slope_ref[...]).astype(B16)
        base = pl.multiple_of(step * rows, rows)
        d_pre_ref[pl.ds(base, rows), :] = d_pre
        third_ref[0:width, :] += dot_rows(x_ref[...], d_pre)
        region_row = region_row_ref[:, pl.ds(base, rows)]
        third_ref[width : width + regions, :] += dot(chosen_rows(region_row, 0, regions), d_pre)
        grad_x_ref[...] = dot_back(d_pre, w_ref[2 * width : 3 * width, :]).astype(B16)

    @pl.when(step == steps - 1)
    def _():
        table_rows = node_grad_ref.shape[0] + 4 * width
        sender, receiver = w_ref[0:width, :], w_ref[width : 2 * width, :]
        first_send = first_recv = None
        d_pre = d_pre_ref[...]
        for slot, (h_ref, out_ref) in enumerate(
            ((h_own_ref, part_own_ref), (h_pair_ref, part_pair_ref), (h_off_ref, part_off_ref))
        ):
            h = h_ref[...]
            s_high, s_low = split(dot(chosen_rows(send_row_ref[...], slot * nodes, nodes), d_pre))
            r_high, r_low = split(dot(chosen_rows(recv_row_ref[...], slot * nodes, nodes), d_pre))
            part = dot_back(s_high, sender) + dot_back(s_low, sender)
            part = part + dot_back(r_high, receiver) + dot_back(r_low, receiver)
            out_ref[...] = part.astype(out_ref.dtype)
            grad_send = dot_rows(h, s_high) + dot_rows(h, s_low)
            grad_recv = dot_rows(h, r_high) + dot_rows(h, r_low)
            first_send = grad_send if first_send is None else first_send + grad_send
            first_recv = grad_recv if first_recv is None else first_recv + grad_recv
        table_grad = third_ref[width : width + regions, :]
        vector_rows = jnp.concatenate(
            [
                jnp.sum(table_grad, axis=0, keepdims=True),
                second_ref[width : width + 1, :],
                jnp.sum(vec_acc_ref[0:8, :], axis=0, keepdims=True),
                jnp.sum(vec_acc_ref[8:16, :], axis=0, keepdims=True),
                node_sum_ref[...],
            ],
            axis=0,
        )
        pieces = (
            (0, first_send),
            (width, first_recv),
            (2 * width, third_ref[0:width, :]),
            (3 * width, second_ref[0:width, :]),
            (4 * width, node_grad_ref[...]),
            (table_rows, vector_rows),
            (table_rows + 8, table_grad),
        )
        odd = core_ref[0] == 1
        for start, piece in pieces:
            left, right = piece[:, 0:LANES], piece[:, LANES:]
            kept_ref[start : start + piece.shape[0], :] = jnp.where(odd, right, left)
            sent_ref[start : start + piece.shape[0], :] = jnp.where(odd, left, right)


def edge_backward(
    core, recv, send, regions, near_back, near, edges, hidden, slope, unit, inverse, weights, vectors,
    node_grad, node_sum, region_count,
):
    count, width = edges.shape
    nodes = near[0].shape[0]
    steps = count // TILE
    last = steps - 1
    tile = pl.BlockSpec((TILE, width), lambda i: (jnp.minimum(i, last), 0))
    thin = pl.BlockSpec((TILE, LANES), lambda i: (jnp.minimum(i, last), 0))
    node = whole((nodes, width))
    grad_rows = weights.shape[0]
    row = whole((1, count))
    half = whole((grad_rows, LANES))
    return pl.pallas_call(
        edge_backward_kernel,
        grid=(steps + 1,),
        in_specs=[
            pl.BlockSpec(memory_space=pltpu.SMEM), whole((count // LANES, LANES)), row, row, row,
            node, node, node, node, node, node, tile, tile, tile, tile, thin,
            whole(weights.shape), whole(vectors.shape), whole(node_grad.shape), whole(node_sum.shape),
        ],
        out_specs=[tile, half, half, node, node, node],
        out_shape=[
            jax.ShapeDtypeStruct((count, width), B16),
            jax.ShapeDtypeStruct((grad_rows, LANES), F32),
            jax.ShapeDtypeStruct((grad_rows, LANES), F32),
            jax.ShapeDtypeStruct((nodes, width), F32),
            jax.ShapeDtypeStruct((nodes, width), B16),
            jax.ShapeDtypeStruct((nodes, width), B16),
        ],
        scratch_shapes=[
            pltpu.VMEM((count, width), B16),
            pltpu.VMEM((width + 16, width), F32),
            pltpu.VMEM((width + region_count, width), F32),
            pltpu.VMEM((16, width), F32),
        ],
        compiler_params=PARAMS,
        name="edge_backward",
        cost_estimate=pl.CostEstimate(
            flops=2 * count * width * (5 * width + 9 * nodes), transcendentals=0, bytes_accessed=count * width * 16
        ),
    )(
        core, recv.reshape(-1, LANES), send.reshape(1, -1), recv.reshape(1, -1), regions.reshape(1, -1),
        *near_back, *near, edges, hidden, slope, unit, inverse, weights, vectors, node_grad, node_sum,
    )


def flipped(value, axis, bit):
    return lax.ppermute(value, axis, [(i, i ^ bit) for i in range(lax.axis_size(axis))])


def across(value, axis):
    count = lax.axis_size(axis)
    return lax.ppermute(value, axis, [(i, (i + 1 if i % 2 else i - 1) % count) for i in range(count)])


def neighbours(value):
    off = across(value, "edge")
    return flipped(value, "edge", 1), off


def on_device(
    node_latents, edge_latents, senders, receivers, regions, forced, params, first_moment, second_moment,
    averaged, step, cotangent,
):
    latents = node_latents[0]
    edges = edge_latents[0]
    upstream = cotangent[0]
    nodes, width = latents.shape
    share = params.shape[0]
    e, f = lax.axis_index("edge"), lax.axis_index("feat")
    blocks, feats = lax.axis_size("edge"), lax.axis_size("feat")
    core = e % 2
    total = share * feats
    vector_row = 7 * width
    region_count = total - vector_row - 8

    pair, off = neighbours(latents)

    mine = lax.dynamic_slice_in_dim(params, core * LANES, LANES, 1).astype(B16)
    shares = jnp.stack([mine] + [flipped(mine, "feat", k) for k in range(1, feats)])
    mine = jnp.concatenate([lax.dynamic_index_in_dim(shares, k ^ f, 0, keepdims=False) for k in range(feats)])
    other = flipped(mine, "edge", 1)
    odd = core == 1
    weights = jnp.concatenate([jnp.where(odd, other, mine), jnp.where(odd, mine, other)], axis=1)
    vectors = weights[vector_row : vector_row + 8].astype(F32)
    table = jnp.pad(weights[vector_row + 8 :], ((0, LANES - region_count), (0, 0)))

    def local(index):
        block = index // nodes
        slot = jnp.where(block == e, 0, jnp.where(block == e + 1 - 2 * core, 1, 2))
        return slot * nodes + index % nodes

    send, recv = local(senders), local(receivers)

    hs, hr = gather_latents(send, recv, latents, pair, off)
    hidden, slope, unit, inverse, high, low, to_pair, to_off = edge_forward(
        regions, recv, hs, hr, edges, weights, table, vectors, nodes, F32
    )
    from_off = across(to_off, "edge")
    from_pair = flipped(to_pair, "edge", 1)
    own = own_sum(recv, high, low, nodes)

    keep = (1 - forced)[:, None]
    new_latents, d_agg, agg, node_hidden, d_inner, d_pre, node_sum = node_update(
        latents, own, from_pair, from_off, weights, vectors, keep, upstream
    )
    back_pair, back_off = neighbours(d_agg)
    node_grad, back = node_grads(latents, agg, node_hidden, d_inner, d_pre, weights, upstream)

    grad_edges, kept, sent, part_own, part_pair, part_off = edge_backward(
        core.reshape(1), recv, send, regions, (d_agg, back_pair, back_off), (latents, pair, off),
        edges, hidden, slope, unit, inverse, weights, vectors, node_grad, node_sum, region_count,
    )

    grad = kept + flipped(sent, "edge", 1)
    low_rows = vector_row % share

    def packed(values):
        top, rest = split(values)
        return jnp.concatenate([top, rest[..., low_rows : low_rows + 8, :]], axis=-2)

    def unpacked(values):
        values = values.astype(F32)
        rest = jnp.pad(values[..., share:, :], ((0, 0),) * (values.ndim - 2) + ((low_rows, share - low_rows - 8), (0, 0)))
        return values[..., :share, :] + rest

    part = grad.reshape(feats, share, LANES)
    bit = 1
    while bit < feats:
        part = part.reshape(-1, 2, share, LANES)
        here = (f // bit) % 2
        keep_part = lax.dynamic_index_in_dim(part, here, 1, keepdims=False)
        send_part = lax.dynamic_index_in_dim(part, 1 - here, 1, keepdims=False)
        part = keep_part + unpacked(flipped(packed(send_part), "feat", bit))
        bit *= 2
    part = part.reshape(share, LANES)

    grads_off = across(part_off, "edge").astype(F32)
    grads_pair = flipped(part_pair, "edge", 1).astype(F32)
    grad_latents = back + part_own + grads_pair + grads_off

    bit = 2
    while bit < blocks:
        wire = packed(part)
        part = unpacked(wire) + unpacked(flipped(wire, "edge", bit))
        bit *= 2

    owner = vector_row // share
    rows = jnp.where(f == owner, part[low_rows : low_rows + 8], 0.0)
    squares = jnp.broadcast_to(jnp.sum(part * part), (8, LANES))
    stats = jnp.concatenate([rows, squares], axis=0)
    bit = 1
    while bit < feats:
        stats = stats + flipped(stats, "feat", bit)
        bit *= 2
    both = flipped(jnp.concatenate([part, stats], axis=0), "edge", 1)
    there, stats_there = both[:share], both[share:]
    grad_norm = jnp.sqrt(stats[8, 0] + stats_there[8, 0])

    def joined(here_half, there_half):
        return jnp.concatenate(
            [jnp.where(odd, there_half, here_half), jnp.where(odd, here_half, there_half)], axis=1
        )

    factor = jnp.minimum(1.0, MAX_NORM / (grad_norm + 1e-06))
    clipped = joined(part, there) * factor
    vector_grads = joined(stats[:8], stats_there[:8]) * factor
    new_first = BETA_ONE * first_moment + (1.0 - BETA_ONE) * clipped
    new_second = BETA_TWO * second_moment + (1.0 - BETA_TWO) * clipped * clipped
    count_steps = step[0].astype(F32)
    first_hat = new_first / (1.0 - jnp.power(BETA_ONE, count_steps))
    second_hat = new_second / (1.0 - jnp.power(BETA_TWO, count_steps))
    new_params = params - RATE * (first_hat / (jnp.sqrt(second_hat) + ADAM_EPS) + WEIGHT_DECAY * params)
    decay_now = jnp.minimum(AVERAGE_DECAY, (1.0 + count_steps) / (10.0 + count_steps))
    new_average = decay_now * averaged + (1.0 - decay_now) * new_params
    return (
        new_latents[None],
        grad_latents[None],
        grad_edges[None],
        new_first,
        new_second,
        new_params,
        new_average,
        grad_norm.reshape(1),
        vector_grads,
    )


def solution(mesh):
    nodes, rows = P("feat", "edge", None), P("feat", None)
    return jax.shard_map(
        on_device,
        mesh=mesh,
        in_specs=(nodes, nodes, P("edge"), P("edge"), P("edge"), P("edge"), rows, rows, rows, rows, P(), nodes),
        out_specs=(nodes, nodes, nodes, rows, rows, rows, rows, P(), P()),
        check_vma=False,
    )
```

time: 375 us -> 155 us (0.41)
  other arithmetic: 98.5 us -> 10.5 us
  local copies, waits for them, and re-layouts: 90 us -> 7.46 us
  Pallas kernels: 0 us -> 67.3 us
  matrix products: 47.4 us -> 0 us
  blocking collectives: 34.6 us -> 0 us
  waiting for transfers between devices: 74.9 us -> 40.9 us
  between operations: 17.2 us -> 4.35 us
  starting transfers between devices: 11.5 us -> 23.8 us
    scatter-add x3 -> x0, other arithmetic: 72.2 us -> none  [add_rows(): return jax.ops.segment_sum(values, indices, num_segments=rows)]
    pallas_call x0 -> x6, Pallas kernels: none -> 67.3 us  [the longest x1 28 us: edge_backward(): pl.pallas_call(edge_backward_kernel, grid=(steps + 1,), in_specs=[pl.Bloc...]
    psum x1 -> x0, waiting for transfers between devices: 61.5 us -> none  [on_device(): summed = lax.psum(local_grad, ('edge', 'feat'))]
    gather x4 -> x0, local copies, waits for them, and re-layouts: 55 us -> none  [pick_rows(): return jnp.take(table, indices, axis=0)]
    dot_general x24 -> x0, matrix products: 47.4 us -> none  [the longest x7 18 us: product_transposed(): lax.dot_general(left, right, (((1,), (1,)), ((), ())), preferred_element_...]
    ppermute x8 -> x20, waiting for transfers between devices: 13.5 us -> 40.9 us  [the longest x16 29.5 us: flipped(): lax.ppermute(value, axis, [(i, i ^ bit) for i in range(lax.axis_size(axis...]
    all_gather x1 -> x0, blocking collectives: 22.2 us -> none  [on_device(): lax.all_gather(params.astype(jnp.bfloat16), 'feat', axis=0, tiled=True)]
    ppermute x8 -> x20, starting transfers between devices: 11.4 us -> 23.8 us  [the longest x16 15.2 us: flipped(): lax.ppermute(value, axis, [(i, i ^ bit) for i in range(lax.axis_size(axis...]
  transfers between devices with their start and end apart: 9 -> 20, of which waited for: 4 -> 11; matrix products, arithmetic and copies ran while one was open for 19% -> 4% of each run, Pallas kernels for 0% -> 12%
where the time goes in v1:
time: 155 us; the launch traced here: 154 us
  Pallas kernels  67.3 us (43%)
  waiting for transfers between devices  40.9 us (26%)
  starting transfers between devices  23.8 us (15%)
  other arithmetic  10.5 us (7%)
  local copies, waits for them, and re-layouts  7.46 us (5%)
  between operations  4.35 us (3%)
    ppermute x16, waiting for transfers between devices, flipped(): lax.ppermute(value, axis, [(i, i ^ bit) for i in range(lax.axis_size(axis...  29.5 us
    pallas_call x1, Pallas kernels, edge_backward(): pl.pallas_call(edge_backward_kernel, grid=(steps + 1,), in_specs=[pl.Bloc...  28 us
    pallas_call x1, Pallas kernels, edge_forward(): pl.pallas_call(edge_forward_kernel, grid=(steps + 1,), in_specs=[whole((c...  16.9 us
    ppermute x16, starting transfers between devices, flipped(): lax.ppermute(value, axis, [(i, i ^ bit) for i in range(lax.axis_size(axis...  15.2 us
    ppermute x4, waiting for transfers between devices, across(): lax.ppermute(value, axis, [(i, (i + 1 if i % 2 else i - 1) % count) for i...  11.4 us
    pallas_call x1, Pallas kernels, gather_latents(): pl.pallas_call(gather_kernel, grid=(edges // TILE,), in_specs=[index, ind...  9.53 us
    ppermute x4, starting transfers between devices, across(): lax.ppermute(value, axis, [(i, (i + 1 if i % 2 else i - 1) % count) for i...  8.6 us
    pallas_call x1, Pallas kernels, own_sum(): pl.pallas_call(own_sum_kernel, grid=(count // TILE,), in_specs=[pl.BlockS...  5.56 us
  transfers between devices with their start and end apart: 20, of which 11 were waited for; matrix products, arithmetic and copies ran while one was open for 4% of the time, Pallas kernels for 12%

profile of v1, /device:TPU:0, one launch (start us, length us, event | category | flops | bytes accessed | tf_op | source)
XLA Modules:
  0.0 154.3 jit_solution(18098931913922649786)
XLA Ops:
  0.7 1.0 dynamic-slice_convert_fusion.1
  1.6 3.1 %collective-permute-start.2 = (bf16[456,128]{1,0:T(8,128)(2,1)S(1)}, bf16[456,128]{1,0:T(8,128)(2,1)S(1)}, u32[]{:S(2)}, u32[]{:S(2)}) collective-permute-start(bf16[456,128]{1,0:T(8,128)(2,1)S(1)} %dynamic-slice_convert_fusion.1), channel_id=1, source_target_pairs={{0,1},{1,0},{2,3},{3,2},{4,5},{5,4},{6,7},{7,6},{8,9},{9,8},{10,11... | collective-permute-start | bytes 350216 | tf_op jit(solution)/shard_map/ppermute | solution.py:431
  4.7 2.6 %collective-permute-start.3 = (bf16[456,128]{1,0:T(8,128)(2,1)S(1)}, bf16[456,128]{1,0:T(8,128)(2,1)S(1)}, u32[]{:S(2)}, u32[]{:S(2)}) collective-permute-start(bf16[456,128]{1,0:T(8,128)(2,1)S(1)} %dynamic-slice_convert_fusion.1), channel_id=1, source_target_pairs={{0,2},{1,3},{2,0},{3,1},{4,6},{5,7},{6,4},{7,5},{8,10},{9,11},{10,... | collective-permute-start | bytes 350216 | tf_op jit(solution)/shard_map/ppermute | solution.py:431
  7.3 2.8 %collective-permute-start.1 = (bf16[512,256]{1,0:T(8,128)(2,1)}, bf16[512,256]{1,0:T(8,128)(2,1)S(1)}, u32[]{:S(2)}, u32[]{:S(2)}) collective-permute-start(bf16[512,256]{1,0:T(8,128)(2,1)} %bitcast.47), channel_id=1, source_target_pairs={{0,28},{4,8},{8,4},{12,16},{16,12},{20,24},{24,20},{28,0},{1,29},{... | collective-permute-start | bytes 786440 | tf_op jit(solution)/shard_map/ppermute | solution.py:436
  10.1 1.4 fusion.6
  11.5 1.0 fusion.26
  12.4 4.1 %collective-permute-done.3 = bf16[456,128]{1,0:T(8,128)(2,1)S(1)} collective-permute-done((bf16[456,128]{1,0:T(8,128)(2,1)S(1)}, bf16[456,128]{1,0:T(8,128)(2,1)S(1)}, u32[]{:S(2)}, u32[]{:S(2)}) %collective-permute-start.3) | collective-permute-done | bytes 116768 | tf_op jit(solution)/shard_map/ppermute | solution.py:431
  16.6 0.1 pad_maximum_fusion.1
  16.7 0.1 collective-permute-start.5
  16.8 0.0 copy-start.9
  16.8 0.0 copy-start.10
  16.9 0.7 copy-done.9
  17.5 0.1 copy-done.10
  17.6 9.5 %gather_latents.1 = (bf16[4096,256]{1,0:T(8,128)(2,1)}, bf16[4096,256]{1,0:T(8,128)(2,1)}) custom-call(s32[32,128]{1,0:T(8,128)} %bitcast.60, s32[32,128]{1,0:T(8,128)} %bitcast.55, bf16[512,256]{1,0:T(8,128)(2,1)} %bitcast.48, bf16[512,256]{1,0:T(8,128)(2,1)} %copy-done.9, bf16[512,256]{1,0:T(8,128)(2,1)} %copy-done.10), custom_call_target="tpu_custom_call" | custom-call | flops 6442450944 | bytes 4194304 | tf_op jit(solution)/shard_map/gather_latents/pallas_call | solution.py:92
  27.1 0.2 broadcast_select_fusion.1
  27.3 0.6 fusion.13.vec_ref
  27.9 1.0 pad_maximum_fusion.w_ref
  29.0 0.6 pad.26.table_ref
  29.6 16.9 %edge_forward.1 = (bf16[4096,256]{1,0:T(8,128)(2,1)}, f32[4096,256]{1,0:T(8,128)}, f32[4096,256]{1,0:T(8,128)}, f32[4096,128]{1,0:T(8,128)}, bf16[4096,256]{1,0:...) custom-call(s32[32,128]{1,0:T(8,128)} %bitcast.66, s32[1,4096]{1,0:T(1,128)} %bitcast.56, ...), custom_call_target="tpu_custom_call" | custom-call | flops 6979321856 | bytes 20971520 | tf_op jit(solution)/shard_map/edge_forward/pallas_call | solution.py:152
  46.5 0.6 collective-permute-start.6
  47.1 2.1 %collective-permute-start.7 = (f32[512,256]{1,0:T(8,128)}, f32[512,256]{1,0:T(8,128)S(1)}, u32[]{:S(2)}, u32[]{:S(2)}) collective-permute-start(f32[512,256]{1,0:T(8,128)} %get-tuple-element.39), channel_id=1, source_target_pairs={{0,28},{4,8},{8,4},{12,16},{16,12},{20,24},{24,20},{28,0},{1,29},{... | collective-permute-start | bytes 1572872 | tf_op jit(solution)/shard_map/ppermute | solution.py:436
  49.2 0.9 copy.21.keep_ref
  50.1 5.6 %own_sum.1.own_ref = f32[512,256]{1,0:T(8,128)} custom-call(s32[1,4096]{1,0:T(1,128)} %bitcast.57, bf16[4096,256]{1,0:T(8,128)(2,1)} %get-tuple-element.36.high_ref, bf16[4096,256]{1,0:T(8,128)(2,1)} %get-tuple-element.37.low_ref), custom_call_target="tpu_custom_call" | custom-call | flops 2147483648 | bytes 4194304 | tf_op jit(solution)/shard_map/own_sum/pallas_call | solution.py:194
  55.6 6.5 %collective-permute-done.7.off_ref = f32[512,256]{1,0:T(8,128)S(1)} collective-permute-done((f32[512,256]{1,0:T(8,128)}, f32[512,256]{1,0:T(8,128)S(1)}, u32[]{:S(2)}, u32[]{:S(2)}) %collective-permute-start.7) | collective-permute-done | bytes 524320 | tf_op jit(solution)/shard_map/ppermute | solution.py:436
  62.1 0.8 copy-done.2
  62.9 4.1 %node_update.1 = (f32[512,256]{1,0:T(8,128)}, bf16[512,256]{1,0:T(8,128)(2,1)}, bf16[512,256]{1,0:T(8,128)(2,1)}, bf16[512,256]{1,0:T(8,128)(2,1)}, bf16[512,256...) custom-call(bf16[512,256]{1,0:T(8,128)(2,1)} %bitcast.49, f32[512,256]{1,0:T(8,128)} %own_sum.1.own_ref, ...), custom_call_target="tpu_custom_call" | custom-call | flops 335544320 | bytes 2621440 | tf_op jit(solution)/shard_map/node_update/pallas_call | solution.py:256
  67.0 1.8 %collective-permute-start.9 = (bf16[512,256]{1,0:T(8,128)(2,1)}, bf16[512,256]{1,0:T(8,128)(2,1)S(1)}, u32[]{:S(2)}, u32[]{:S(2)}) collective-permute-start(bf16[512,256]{1,0:T(8,128)(2,1)} %get-tuple-element.46.own_ref), channel_id=1, source_target_pairs={{0,28},{4,8},{8,4},{12,16},{16,12},{20,24},{24,20},{28,0},{1,29},{... | collective-permute-start | bytes 786440 | tf_op jit(solution)/shard_map/ppermute | solution.py:436
  68.8 3.3 %node_grads.1 = (f32[768,256]{1,0:T(8,128)}, f32[512,256]{1,0:T(8,128)}) custom-call(bf16[512,256]{1,0:T(8,128)(2,1)} %bitcast.50, bf16[512,256]{1,0:T(8,128)(2,1)} %get-tuple-element.41.agg_ref, bf16[512,256]{1,0:T(8,128)(2,1)} %get-tuple-element.42.hidden_ref, bf16[512,256]{1,0:T(8,128)(2,1)} %get-tuple-element.43.d_inner_ref, ...), custom_call_target="tpu_custom_call" | custom-call | flops 268435456 | bytes 2359296 | tf_op jit(solution)/shard_map/node_grads/pallas_call | solution.py:278
  72.0 4.4 %collective-permute-done.9.off_ref = bf16[512,256]{1,0:T(8,128)(2,1)S(1)} collective-permute-done((bf16[512,256]{1,0:T(8,128)(2,1)}, bf16[512,256]{1,0:T(8,128)(2,1)S(1)}, u32[]{:S(2)}, u32[]{:S(2)}) %collective-permute-start.9) | collective-permute-done | bytes 262176 | tf_op jit(solution)/shard_map/ppermute | solution.py:436
  76.5 0.7 copy-done.12
  77.2 28.0 %edge_backward.1 = (bf16[4096,256]{1,0:T(8,128)(2,1)}, f32[1824,128]{1,0:T(8,128)}, f32[1824,128]{1,0:T(8,128)}, f32[512,256]{1,0:T(8,128)}, bf16[512,256]{1,0:T(8,128)(2,1)}, /*index=5*/bf16[512,256]{1,0:T(8,128)(2,1)}) custom-call(s32[1]{0:T(128)} %bitcast.17.core_ref, s32[32,128]{1,0:T(8,128)} %bitcast.59, s32[1,4096]{1,0:T(1,128)} %bitcast.61, ...), custom_call_target="tpu_custom_call" | custom-call | flops 12348030976 | bytes 16777216 | tf_op jit(solution)/shard_map/edge_backward/pallas_call | solution.py:396
  105.2 0.2 collective-permute-start.12
  105.3 2.6 %collective-permute-done.12 = f32[1824,128]{1,0:T(8,128)S(1)} collective-permute-done((f32[1824,128]{1,0:T(8,128)}, f32[1824,128]{1,0:T(8,128)S(1)}, u32[]{:S(2)}, u32[]{:S(2)}) %collective-permute-start.12) | collective-permute-done | bytes 933920 | tf_op jit(solution)/shard_map/ppermute | solution.py:431
  107.9 1.3 add.174
  109.2 0.1 fusion.25
  109.3 1.9 %collective-permute-start.13 = (bf16[2,464,128]{2,1,0:T(8,128)(2,1)S(1)}, bf16[2,464,128]{2,1,0:T(8,128)(2,1)S(1)}, u32[]{:S(2)}, u32[]{:S(2)}) collective-permute-start(bf16[2,464,128]{2,1,0:T(8,128)(2,1)S(1)} %pad_maximum_fusion.4), channel_id=1, source_target_pairs={{0,1},{1,0},{2,3},{3,2},{4,5},{5,4},{6,7},{7,6},{8,9},{9,8},{10,11... | collective-permute-start | bytes 712712 | tf_op jit(solution)/shard_map/ppermute | solution.py:431
  111.2 6.1 %collective-permute-done.13 = bf16[2,464,128]{2,1,0:T(8,128)(2,1)S(1)} collective-permute-done((bf16[2,464,128]{2,1,0:T(8,128)(2,1)S(1)}, bf16[2,464,128]{2,1,0:T(8,128)(2,1)S(1)}, u32[]{:S(2)}, u32[]{:S(2)}) %collective-permute-start.13) | collective-permute-done | bytes 237600 | tf_op jit(solution)/shard_map/ppermute | solution.py:431
  117.3 0.1 fusion.1
  117.5 2.8 %collective-permute-start.14 = (bf16[1,464,128]{2,1,0:T(8,128)(2,1)S(1)}, bf16[1,464,128]{2,1,0:T(8,128)(2,1)S(1)}, u32[]{:S(2)}, u32[]{:S(2)}) collective-permute-start(bf16[1,464,128]{2,1,0:T(8,128)(2,1)S(1)} %pad_maximum_fusion.5), channel_id=1, source_target_pairs={{0,2},{1,3},{2,0},{3,1},{4,6},{5,7},{6,4},{7,5},{8,10},{9,11},{10,... | collective-permute-start | bytes 356360 | tf_op jit(solution)/shard_map/ppermute | solution.py:431
  120.3 5.3 %collective-permute-done.14 = bf16[1,464,128]{2,1,0:T(8,128)(2,1)S(1)} collective-permute-done((bf16[1,464,128]{2,1,0:T(8,128)(2,1)S(1)}, bf16[1,464,128]{2,1,0:T(8,128)(2,1)S(1)}, u32[]{:S(2)}, u32[]{:S(2)}) %collective-permute-start.14) | collective-permute-done | bytes 118816 | tf_op jit(solution)/shard_map/ppermute | solution.py:431
  125.6 0.0 copy-start.3
  125.7 1.1 collective-permute-start.15
  126.7 3.8 %collective-permute-done.15 = bf16[464,128]{1,0:T(8,128)(2,1)S(1)} collective-permute-done((bf16[464,128]{1,0:T(8,128)(2,1)S(1)}, bf16[464,128]{1,0:T(8,128)(2,1)S(1)}, u32[]{:S(2)}, u32[]{:S(2)}) %collective-permute-start.15) | collective-permute-done | bytes 118816 | tf_op jit(solution)/shard_map/ppermute | solution.py:431
  130.7 1.4 collective-permute-start.16
  132.2 3.5 %collective-permute-done.16 = bf16[464,128]{1,0:T(8,128)(2,1)S(1)} collective-permute-done((bf16[464,128]{1,0:T(8,128)(2,1)S(1)}, bf16[464,128]{1,0:T(8,128)(2,1)S(1)}, u32[]{:S(2)}, u32[]{:S(2)}) %collective-permute-start.16) | collective-permute-done | bytes 118816 | tf_op jit(solution)/shard_map/ppermute | solution.py:431
  135.6 0.0 copy-start
  135.7 0.0 copy-start.5
  135.7 0.0 copy-start.6
  135.7 0.7 multiply_reduce_fusion
  136.4 0.6 concatenate.36
  137.0 0.1 collective-permute-start.17
  137.1 0.1 collective-permute-start.10
  137.2 1.9 %collective-permute-start.11 = (bf16[512,256]{1,0:T(8,128)(2,1)}, bf16[512,256]{1,0:T(8,128)(2,1)}, u32[]{:S(2)}, u32[]{:S(2)}) collective-permute-start(bf16[512,256]{1,0:T(8,128)(2,1)} %get-tuple-element.55), channel_id=1, source_target_pairs={{0,28},{4,8},{8,4},{12,16},{16,12},{20,24},{24,20},{28,0},{1,29},{... | collective-permute-start | bytes 786440 | tf_op jit(solution)/shard_map/ppermute | solution.py:436
  139.1 1.6 %collective-permute-done.17 = f32[16,128]{1,0:T(8,128)S(1)} collective-permute-done((f32[16,128]{1,0:T(8,128)S(1)}, f32[16,128]{1,0:T(8,128)S(1)}, u32[]{:S(2)}, u32[]{:S(2)}) %collective-permute-start.17) | collective-permute-done | bytes 8224 | tf_op jit(solution)/shard_map/ppermute | solution.py:431
  140.7 0.6 pad_add_fusion
  141.4 1.4 collective-permute-start.18
  143.5 2.5 %collective-permute-done.18 = f32[16,128]{1,0:T(8,128)S(1)} collective-permute-done((f32[16,128]{1,0:T(8,128)S(1)}, f32[16,128]{1,0:T(8,128)S(1)}, u32[]{:S(2)}, u32[]{:S(2)}) %collective-permute-start.18) | collective-permute-done | bytes 8224 | tf_op jit(solution)/shard_map/ppermute | solution.py:431
  146.0 0.1 collective-permute-start.19
  146.1 0.5 collective-permute-done.11
  146.6 1.9 %add_bitcast_fusion = f32[1,512,256]{2,1,0:T(8,128)} fusion(bf16[512,256]{1,0:T(8,128)(2,1)} %collective-permute-done.11, bf16[512,256]{1,0:T(8,128)(2,1)} %collective-permute-done.10, f32[512,256]{1,0:T(8,128)S(1)} %copy-done.3, f32[512,256]{1,0:T(8,128)S(1)} %copy-done.4), kind=kLoop, calls=%fused_computation.6 | loop fusion | flops 655360 | bytes 2097152 | tf_op jit(solution)/shard_map/broadcast_in_dim | solution.py:561
  148.5 0.5 slice.124
  149.1 0.5 slice.125
  151.0 0.6 maximum_multiply_fusion.1
  151.6 1.5 multiply_add_fusion
  (58 shorter events, 0.5 us)
Async XLA Ops:
  1.6 10.8 %collective-permute-start.2 = (bf16[456,128]{1,0:T(8,128)(2,1)S(1)}, bf16[456,128]{1,0:T(8,128)(2,1)S(1)}, u32[]{:S(2)}, u32[]{:S(2)}) collective-permute-start(bf16[456,128]{1,0:T(8,128)(2,1)S(1)} %dynamic-slice_convert_fusion.1), channel_id=1, source_target_pairs={{0,1},{1,0},{2,3},{3,2},{4,5},{5,4},{6,7},{7,6},{8,9},{9,8},{10,11... | collective-permute-start | bytes 350216 | tf_op jit(solution)/shard_map/ppermute | solution.py:431
  4.7 11.9 %collective-permute-start.3 = (bf16[456,128]{1,0:T(8,128)(2,1)S(1)}, bf16[456,128]{1,0:T(8,128)(2,1)S(1)}, u32[]{:S(2)}, u32[]{:S(2)}) collective-permute-start(bf16[456,128]{1,0:T(8,128)(2,1)S(1)} %dynamic-slice_convert_fusion.1), channel_id=1, source_target_pairs={{0,2},{1,3},{2,0},{3,1},{4,6},{5,7},{6,4},{7,5},{8,10},{9,11},{10,... | collective-permute-start | bytes 350216 | tf_op jit(solution)/shard_map/ppermute | solution.py:431
  7.3 9.3 %collective-permute-start.4 = (bf16[456,128]{1,0:T(8,128)(2,1)S(1)}, bf16[456,128]{1,0:T(8,128)(2,1)S(1)}, u32[]{:S(2)}, u32[]{:S(2)}) collective-permute-start(bf16[456,128]{1,0:T(8,128)(2,1)S(1)} %dynamic-slice_convert_fusion.1), channel_id=1, source_target_pairs={{0,3},{1,2},{2,1},{3,0},{4,7},{5,6},{6,5},{7,4},{8,11},{9,10},{10,... | collective-permute-start | bytes 350216 | tf_op jit(solution)/shard_map/ppermute | solution.py:431
  7.3 9.5 %collective-permute-start = (bf16[512,256]{1,0:T(8,128)(2,1)}, bf16[512,256]{1,0:T(8,128)(2,1)S(1)}, u32[]{:S(2)}, u32[]{:S(2)}) collective-permute-start(bf16[512,256]{1,0:T(8,128)(2,1)} %bitcast.46), channel_id=1, source_target_pairs={{0,4},{4,0},{8,12},{12,8},{16,20},{20,16},{24,28},{28,24},{1,5},{5... | collective-permute-start | bytes 786440 | tf_op jit(solution)/shard_map/ppermute | solution.py:431
  7.3 9.5 %collective-permute-start.1 = (bf16[512,256]{1,0:T(8,128)(2,1)}, bf16[512,256]{1,0:T(8,128)(2,1)S(1)}, u32[]{:S(2)}, u32[]{:S(2)}) collective-permute-start(bf16[512,256]{1,0:T(8,128)(2,1)} %bitcast.47), channel_id=1, source_target_pairs={{0,28},{4,8},{8,4},{12,16},{16,12},{20,24},{24,20},{28,0},{1,29},{... | collective-permute-start | bytes 786440 | tf_op jit(solution)/shard_map/ppermute | solution.py:436
  16.7 10.4 %collective-permute-start.5 = (bf16[1824,128]{1,0:T(8,128)(2,1)S(1)}, bf16[1824,128]{1,0:T(8,128)(2,1)S(1)}, u32[]{:S(2)}, u32[]{:S(2)}) collective-permute-start(bf16[1824,128]{1,0:T(8,128)(2,1)S(1)} %pad_maximum_fusion.2), channel_id=1, source_target_pairs={{0,4},{4,0},{8,12},{12,8},{16,20},{20,16},{24,28},{28,24},{1,5},{5... | collective-permute-start | bytes 1400840 | tf_op jit(solution)/shard_map/ppermute | solution.py:431
  16.8 0.7 copy-start.9
  16.8 0.8 copy-start.10
  29.6 19.6 %copy-start.8 = (s32[512]{0:T(512)S(1)}, s32[512]{0:T(512)}, u32[]{:S(2)}) copy-start(s32[512]{0:T(512)} %param.17) | copy-start | bytes 6148
  46.5 9.1 %collective-permute-start.6 = (f32[512,256]{1,0:T(8,128)}, f32[512,256]{1,0:T(8,128)S(1)}, u32[]{:S(2)}, u32[]{:S(2)}) collective-permute-start(f32[512,256]{1,0:T(8,128)} %get-tuple-element.38), channel_id=1, source_target_pairs={{0,4},{4,0},{8,12},{12,8},{16,20},{20,16},{24,28},{28,24},{1,5},{5... | collective-permute-start | bytes 1572872 | tf_op jit(solution)/shard_map/ppermute | solution.py:431
  47.1 15.0 %collective-permute-start.7 = (f32[512,256]{1,0:T(8,128)}, f32[512,256]{1,0:T(8,128)S(1)}, u32[]{:S(2)}, u32[]{:S(2)}) collective-permute-start(f32[512,256]{1,0:T(8,128)} %get-tuple-element.39), channel_id=1, source_target_pairs={{0,28},{4,8},{8,4},{12,16},{16,12},{20,24},{24,20},{28,0},{1,29},{... | collective-permute-start | bytes 1572872 | tf_op jit(solution)/shard_map/ppermute | solution.py:436
  55.6 6.5 %copy-start.1 = (f32[512,256]{1,0:T(8,128)}, f32[512,256]{1,0:T(8,128)S(1)}, u32[]{:S(2)}) copy-start(f32[512,256]{1,0:T(8,128)S(1)} %collective-permute-done.6.pair_ref) | copy-start | bytes 1572868
  62.1 0.8 copy-start.2
  67.0 5.0 %collective-permute-start.8 = (bf16[512,256]{1,0:T(8,128)(2,1)}, bf16[512,256]{1,0:T(8,128)(2,1)S(1)}, u32[]{:S(2)}, u32[]{:S(2)}) collective-permute-start(bf16[512,256]{1,0:T(8,128)(2,1)} %get-tuple-element.46.own_ref), channel_id=1, source_target_pairs={{0,4},{4,0},{8,12},{12,8},{16,20},{20,16},{24,28},{28,24},{1,5},{5... | collective-permute-start | bytes 786440 | tf_op jit(solution)/shard_map/ppermute | solution.py:431
  67.0 9.5 %collective-permute-start.9 = (bf16[512,256]{1,0:T(8,128)(2,1)}, bf16[512,256]{1,0:T(8,128)(2,1)S(1)}, u32[]{:S(2)}, u32[]{:S(2)}) collective-permute-start(bf16[512,256]{1,0:T(8,128)(2,1)} %get-tuple-element.46.own_ref), channel_id=1, source_target_pairs={{0,28},{4,8},{8,4},{12,16},{16,12},{20,24},{24,20},{28,0},{1,29},{... | collective-permute-start | bytes 786440 | tf_op jit(solution)/shard_map/ppermute | solution.py:436
  72.0 4.5 %copy-start.11 = (bf16[512,256]{1,0:T(8,128)(2,1)}, bf16[512,256]{1,0:T(8,128)(2,1)S(1)}, u32[]{:S(2)}) copy-start(bf16[512,256]{1,0:T(8,128)(2,1)S(1)} %collective-permute-done.8.pair_ref) | copy-start | bytes 786436
  76.5 0.7 copy-start.12
  105.2 2.8 %collective-permute-start.12 = (f32[1824,128]{1,0:T(8,128)}, f32[1824,128]{1,0:T(8,128)S(1)}, u32[]{:S(2)}, u32[]{:S(2)}) collective-permute-start(f32[1824,128]{1,0:T(8,128)} %get-tuple-element.58), channel_id=1, source_target_pairs={{0,4},{4,0},{8,12},{12,8},{16,20},{20,16},{24,28},{28,24},{1,5},{5... | collective-permute-start | bytes 2801672 | tf_op jit(solution)/shard_map/ppermute | solution.py:431
  109.3 8.0 %collective-permute-start.13 = (bf16[2,464,128]{2,1,0:T(8,128)(2,1)S(1)}, bf16[2,464,128]{2,1,0:T(8,128)(2,1)S(1)}, u32[]{:S(2)}, u32[]{:S(2)}) collective-permute-start(bf16[2,464,128]{2,1,0:T(8,128)(2,1)S(1)} %pad_maximum_fusion.4), channel_id=1, source_target_pairs={{0,1},{1,0},{2,3},{3,2},{4,5},{5,4},{6,7},{7,6},{8,9},{9,8},{10,11... | collective-permute-start | bytes 712712 | tf_op jit(solution)/shard_map/ppermute | solution.py:431
  117.5 8.1 %collective-permute-start.14 = (bf16[1,464,128]{2,1,0:T(8,128)(2,1)S(1)}, bf16[1,464,128]{2,1,0:T(8,128)(2,1)S(1)}, u32[]{:S(2)}, u32[]{:S(2)}) collective-permute-start(bf16[1,464,128]{2,1,0:T(8,128)(2,1)S(1)} %pad_maximum_fusion.5), channel_id=1, source_target_pairs={{0,2},{1,3},{2,0},{3,1},{4,6},{5,7},{6,4},{7,5},{8,10},{9,11},{10,... | collective-permute-start | bytes 356360 | tf_op jit(solution)/shard_map/ppermute | solution.py:431
  125.6 21.0 %copy-start.3 = (f32[512,256]{1,0:T(8,128)S(1)}, f32[512,256]{1,0:T(8,128)}, u32[]{:S(2)}) copy-start(f32[512,256]{1,0:T(8,128)} %get-tuple-element.45) | copy-start | bytes 1572868
  125.6 21.0 %copy-start.4 = (f32[512,256]{1,0:T(8,128)S(1)}, f32[512,256]{1,0:T(8,128)}, u32[]{:S(2)}) copy-start(f32[512,256]{1,0:T(8,128)} %get-tuple-element.53) | copy-start | bytes 1572868
  125.7 4.9 %collective-permute-start.15 = (bf16[464,128]{1,0:T(8,128)(2,1)S(1)}, bf16[464,128]{1,0:T(8,128)(2,1)S(1)}, u32[]{:S(2)}, u32[]{:S(2)}) collective-permute-start(bf16[464,128]{1,0:T(8,128)(2,1)S(1)} %get-tuple-element.84), channel_id=1, source_target_pairs={{0,8},{4,12},{8,0},{12,4},{16,24},{20,28},{24,16},{28,20},{1,9},{5... | collective-permute-start | bytes 356360 | tf_op jit(solution)/shard_map/ppermute | solution.py:431
  130.7 4.9 %collective-permute-start.16 = (bf16[464,128]{1,0:T(8,128)(2,1)S(1)}, bf16[464,128]{1,0:T(8,128)(2,1)S(1)}, u32[]{:S(2)}, u32[]{:S(2)}) collective-permute-start(bf16[464,128]{1,0:T(8,128)(2,1)S(1)} %get-tuple-element.82), channel_id=1, source_target_pairs={{0,16},{4,20},{8,24},{12,28},{16,0},{20,4},{24,8},{28,12},{1,17},{... | collective-permute-start | bytes 356360 | tf_op jit(solution)/shard_map/ppermute | solution.py:431
  135.6 16.0 %copy-start = (f32[456,256]{1,0:T(8,128)S(1)}, f32[456,256]{1,0:T(8,128)}, u32[]{:S(2)}) copy-start(f32[456,256]{1,0:T(8,128)} %param.18) | copy-start | bytes 1400836
  135.7 16.0 %copy-start.5 = (f32[456,256]{1,0:T(8,128)S(1)}, f32[456,256]{1,0:T(8,128)}, u32[]{:S(2)}) copy-start(f32[456,256]{1,0:T(8,128)} %param.21) | copy-start | bytes 1400836
  135.7 16.0 %copy-start.6 = (f32[456,256]{1,0:T(8,128)S(1)}, f32[456,256]{1,0:T(8,128)}, u32[]{:S(2)}) copy-start(f32[456,256]{1,0:T(8,128)} %param.20) | copy-start | bytes 1400836
  135.7 16.0 %copy-start.7 = (f32[456,256]{1,0:T(8,128)S(1)}, f32[456,256]{1,0:T(8,128)}, u32[]{:S(2)}) copy-start(f32[456,256]{1,0:T(8,128)} %param.19) | copy-start | bytes 1400836
  137.0 3.7 %collective-permute-start.17 = (f32[16,128]{1,0:T(8,128)S(1)}, f32[16,128]{1,0:T(8,128)S(1)}, u32[]{:S(2)}, u32[]{:S(2)}) collective-permute-start(f32[16,128]{1,0:T(8,128)S(1)} %concatenate.36), channel_id=1, source_target_pairs={{0,1},{1,0},{2,3},{3,2},{4,5},{5,4},{6,7},{7,6},{8,9},{9,8},{10,11... | collective-permute-start | bytes 24584 | tf_op jit(solution)/shard_map/ppermute | solution.py:431
  137.1 9.0 %collective-permute-start.10 = (bf16[512,256]{1,0:T(8,128)(2,1)}, bf16[512,256]{1,0:T(8,128)(2,1)}, u32[]{:S(2)}, u32[]{:S(2)}) collective-permute-start(bf16[512,256]{1,0:T(8,128)(2,1)} %get-tuple-element.54), channel_id=1, source_target_pairs={{0,4},{4,0},{8,12},{12,8},{16,20},{20,16},{24,28},{28,24},{1,5},{5... | collective-permute-start | bytes 786440 | tf_op jit(solution)/shard_map/ppermute | solution.py:431
  137.2 9.4 %collective-permute-start.11 = (bf16[512,256]{1,0:T(8,128)(2,1)}, bf16[512,256]{1,0:T(8,128)(2,1)}, u32[]{:S(2)}, u32[]{:S(2)}) collective-permute-start(bf16[512,256]{1,0:T(8,128)(2,1)} %get-tuple-element.55), channel_id=1, source_target_pairs={{0,28},{4,8},{8,4},{12,16},{16,12},{20,24},{24,20},{28,0},{1,29},{... | collective-permute-start | bytes 786440 | tf_op jit(solution)/shard_map/ppermute | solution.py:436
  141.4 4.6 %collective-permute-start.18 = (f32[16,128]{1,0:T(8,128)S(1)}, f32[16,128]{1,0:T(8,128)S(1)}, u32[]{:S(2)}, u32[]{:S(2)}) collective-permute-start(f32[16,128]{1,0:T(8,128)S(1)} %pad_add_fusion), channel_id=1, source_target_pairs={{0,2},{1,3},{2,0},{3,1},{4,6},{5,7},{6,4},{7,5},{8,10},{9,11},{10,... | collective-permute-start | bytes 24584 | tf_op jit(solution)/shard_map/ppermute | solution.py:431
  146.0 3.0 %collective-permute-start.19 = (f32[472,128]{1,0:T(8,128)S(1)}, f32[472,128]{1,0:T(8,128)S(1)}, u32[]{:S(2)}, u32[]{:S(2)}) collective-permute-start(f32[472,128]{1,0:T(8,128)S(1)} %pad_maximum_fusion.3), channel_id=1, source_target_pairs={{0,4},{4,0},{8,12},{12,8},{16,20},{20,16},{24,28},{28,24},{1,5},{5... | collective-permute-start | bytes 725000 | tf_op jit(solution)/shard_map/ppermute | solution.py:431

commit v2 on v1

v2 whole, which is shorter than its diff:
```python
import functools

import jax
import jax.numpy as jnp
from jax import lax
from jax.experimental import pallas as pl
from jax.experimental.pallas import tpu as pltpu
from jax.sharding import PartitionSpec as P

NORM_EPS = 1e-05
MAX_NORM = 512.0
RATE = 0.05
BETA_ONE = 0.9
BETA_TWO = 0.95
ADAM_EPS = 1e-08
WEIGHT_DECAY = 0.1
AVERAGE_DECAY = 0.999

LANES = 128
TILE = 1024
B16 = jnp.bfloat16
F32 = jnp.float32
I32 = jnp.int32
PARAMS = pltpu.CompilerParams(vmem_limit_bytes=20 * 1024 * 1024)


def dot(left, right):
    return jnp.dot(left, right, preferred_element_type=F32)


def dot_rows(left, right):
    return lax.dot_general(left, right, (((0,), (0,)), ((), ())), preferred_element_type=F32)


def dot_back(left, right):
    return lax.dot_general(left, right, (((1,), (1,)), ((), ())), preferred_element_type=F32)


def split(values):
    high = values.astype(B16)
    return high, (values - high.astype(F32)).astype(B16)


def whole(shape):
    return pl.BlockSpec(shape, lambda i: (0,) * len(shape))


def tiled(rows, cols):
    return pl.BlockSpec((rows, cols), lambda i: (i, 0))


def column(row):
    return jnp.broadcast_to(row, (LANES, LANES)).T


def chosen_columns(index_ref, tile, rows, first, last):
    lane = lax.broadcasted_iota(I32, (LANES, LANES), 1)
    groups = []
    for g in range(rows // LANES):
        col = column(index_ref[pl.ds(tile * (rows // LANES) + g, 1), :])
        groups.append(
            jnp.concatenate(
                [jnp.where(col == lane + base, 1.0, 0.0).astype(B16) for base in range(first, last, LANES)],
                axis=1,
            )
        )
    return jnp.concatenate(groups, axis=0)


def chosen_rows(index_row, first, count):
    node = lax.broadcasted_iota(I32, (count, index_row.shape[1]), 0) + first
    return jnp.where(index_row == node, 1.0, 0.0).astype(B16)


def gather_near_kernel(index_ref, own_ref, pair_ref, out_ref):
    tile = pl.program_id(0)
    rows = out_ref.shape[0]
    nodes = own_ref.shape[0]
    total = dot(chosen_columns(index_ref, tile, rows, 0, nodes), own_ref[...])
    total = total + dot(chosen_columns(index_ref, tile, rows, nodes, 2 * nodes), pair_ref[...])
    out_ref[...] = total.astype(B16)


def gather_near(index, own, pair):
    nodes, width = own.shape
    edges = index.size
    return pl.pallas_call(
        gather_near_kernel,
        grid=(edges // TILE,),
        in_specs=[whole((edges // LANES, LANES))] + [whole((nodes, width))] * 2,
        out_specs=tiled(TILE, width),
        out_shape=jax.ShapeDtypeStruct((edges, width), B16),
        compiler_params=PARAMS,
        name="gather_near",
        cost_estimate=pl.CostEstimate(
            flops=2 * edges * 2 * nodes * width, transcendentals=0, bytes_accessed=edges * width * 2
        ),
    )(index.reshape(-1, LANES), own, pair)


def gather_off_kernel(index_ref, off_ref, near_ref, out_ref):
    tile = pl.program_id(0)
    rows = out_ref.shape[0]
    nodes = off_ref.shape[0]
    total = dot(chosen_columns(index_ref, tile, rows, 2 * nodes, 3 * nodes), off_ref[...])
    out_ref[...] = (total + near_ref[...].astype(F32)).astype(B16)


def gather_off(index, off, near):
    nodes, width = off.shape
    edges = index.size
    return pl.pallas_call(
        gather_off_kernel,
        grid=(edges // TILE,),
        in_specs=[whole((edges // LANES, LANES)), whole((nodes, width)), tiled(TILE, width)],
        out_specs=tiled(TILE, width),
        out_shape=jax.ShapeDtypeStruct((edges, width), B16),
        compiler_params=PARAMS,
        name="gather_off",
        cost_estimate=pl.CostEstimate(
            flops=2 * edges * nodes * width, transcendentals=0, bytes_accessed=edges * width * 4
        ),
    )(index.reshape(-1, LANES), off, near)


def edge_forward_kernel(
    place_ref, region_ref, recv_row_ref, hs_ref, hr_ref, x_ref, *refs,
):
    pieces, refs = refs[:-9], refs[-9:]
    w_ref, hidden_ref, slope_ref, unit_ref, inverse_ref, high_ref, low_ref, halo_ref, wide_ref = refs
    step = pl.program_id(0)
    rows = x_ref.shape[0]
    width = x_ref.shape[1]
    nodes = halo_ref.shape[0]
    steps = pl.num_programs(0)
    vector_row = 7 * width
    regions = w_ref.shape[0] - vector_row - 8

    @pl.when(step == 0)
    def _():
        odd = place_ref[0] == 1
        shares = len(pieces) // 2
        share = pieces[0].shape[0]
        for k in range(shares):
            mine, other = pieces[k][...].astype(F32), pieces[shares + k][...].astype(F32)
            base = pl.multiple_of(place_ref[2 + k] * share, 8)
            wide_ref[pl.ds(base, share), 0:LANES] = jnp.where(odd, other, mine)
            wide_ref[pl.ds(base, share), LANES : 2 * LANES] = jnp.where(odd, mine, other)
        w_ref[...] = wide_ref[...].astype(B16)

    @pl.when(step < steps - 1)
    def _():
        vec = wide_ref[vector_row : vector_row + 8, :]
        table = jnp.concatenate(
            [wide_ref[vector_row + 8 :, :], jnp.zeros((LANES - regions, width), F32)], axis=0
        ).astype(B16)
        pre = dot(hs_ref[...], w_ref[0:width, :])
        pre = pre + dot(hr_ref[...], w_ref[width : 2 * width, :])
        pre = pre + dot(x_ref[...], w_ref[2 * width : 3 * width, :])
        pre = pre + dot(chosen_columns(region_ref, step, rows, 0, LANES), table)
        pre = pre + vec[0:1, :]
        sigma = 1.0 / (1.0 + jnp.exp(-pre))
        hidden = (pre * sigma).astype(B16)
        hidden_ref[...] = hidden
        slope_ref[...] = sigma * (1.0 + pre * (1.0 - sigma))
        inner = dot(hidden, w_ref[3 * width : 4 * width, :]) + vec[1:2, :]
        center = inner - jnp.mean(inner, axis=-1, keepdims=True)
        inverse = lax.rsqrt(jnp.mean(center * center, axis=-1, keepdims=True) + NORM_EPS)
        unit = center * inverse
        unit_ref[...] = unit
        inverse_ref[...] = jnp.broadcast_to(inverse, (rows, LANES))
        high, low = split(unit * vec[2:3, :] + vec[3:4, :])
        base = pl.multiple_of(step * rows, rows)
        high_ref[pl.ds(base, rows), :] = high
        low_ref[pl.ds(base, rows), :] = low

    @pl.when(step == steps - 1)
    def _():
        onehot = chosen_rows(recv_row_ref[...], 2 * nodes, nodes)
        halo_ref[...] = dot(onehot, high_ref[...]) + dot(onehot, low_ref[...])


def edge_forward(place, regions, recv, hs, hr, edges, pieces, total, nodes):
    count, width = edges.shape
    steps = count // TILE
    last = steps - 1
    tile = pl.BlockSpec((TILE, width), lambda i: (jnp.minimum(i, last), 0))
    thin = pl.BlockSpec((TILE, LANES), lambda i: (jnp.minimum(i, last), 0))
    return pl.pallas_call(
        edge_forward_kernel,
        grid=(steps + 1,),
        in_specs=[
            pl.BlockSpec(memory_space=pltpu.SMEM), whole((count // LANES, LANES)), whole((1, count)), tile, tile, tile,
            *[whole(piece.shape) for piece in pieces],
        ],
        out_specs=[
            whole((total, width)), tile, tile, tile, thin, whole((count, width)), whole((count, width)),
            whole((nodes, width)),
        ],
        out_shape=[
            jax.ShapeDtypeStruct((total, width), B16),
            jax.ShapeDtypeStruct((count, width), B16),
            jax.ShapeDtypeStruct((count, width), F32),
            jax.ShapeDtypeStruct((count, width), F32),
            jax.ShapeDtypeStruct((count, LANES), F32),
            jax.ShapeDtypeStruct((count, width), B16),
            jax.ShapeDtypeStruct((count, width), B16),
            jax.ShapeDtypeStruct((nodes, width), F32),
        ],
        scratch_shapes=[pltpu.VMEM((total, width), F32)],
        compiler_params=PARAMS,
        name="edge_forward",
        cost_estimate=pl.CostEstimate(
            flops=2 * count * width * (5 * width + 2 * nodes), transcendentals=2 * count * width,
            bytes_accessed=count * width * 20,
        ),
    )(place, regions.reshape(-1, LANES), recv.reshape(1, -1), hs, hr, edges, *pieces)


def near_sum_kernel(recv_row_ref, high_ref, low_ref, pair_ref, own_ref):
    nodes = own_ref.shape[0]
    for first, out_ref in ((nodes, pair_ref), (0, own_ref)):
        onehot = chosen_rows(recv_row_ref[...], first, nodes)
        out_ref[...] = dot(onehot, high_ref[...]) + dot(onehot, low_ref[...])


def near_sum(recv, high, low, nodes):
    count, width = high.shape
    out = jax.ShapeDtypeStruct((nodes, width), F32)
    return pl.pallas_call(
        near_sum_kernel,
        out_shape=[out, out],
        compiler_params=PARAMS,
        name="near_sum",
        cost_estimate=pl.CostEstimate(
            flops=8 * count * width * nodes, transcendentals=0, bytes_accessed=count * width * 4
        ),
    )(recv.reshape(1, -1), high, low)


def vectors_of(w_ref, width):
    return w_ref[7 * width : 7 * width + 8, :].astype(F32)


def node_kernel(
    h_ref, agg_ref, w_ref, forced_ref, up_ref,
    new_ref, d_agg_ref, hidden_ref, d_inner_ref, d_pre_ref, sums_ref,
):
    width = h_ref.shape[1]
    vec = vectors_of(w_ref, width)
    agg = agg_ref[...]
    h = h_ref[...]
    latent, aggregate = w_ref[4 * width : 5 * width, :], w_ref[5 * width : 6 * width, :]
    second = w_ref[6 * width : 7 * width, :]
    pre = dot(h, latent) + dot(agg, aggregate) + vec[4:5, :]
    sigma = 1.0 / (1.0 + jnp.exp(-pre))
    hidden = (pre * sigma).astype(B16)
    hidden_ref[...] = hidden
    inner = dot(hidden, second) + vec[5:6, :]
    center = inner - jnp.mean(inner, axis=-1, keepdims=True)
    inverse = lax.rsqrt(jnp.mean(center * center, axis=-1, keepdims=True) + NORM_EPS)
    unit = center * inverse
    keep = [column(forced_ref[g : g + 1, :]) for g in range(forced_ref.shape[0])]
    keep = 1.0 - jnp.concatenate(keep, axis=0).astype(F32)
    keep = jnp.concatenate([keep] * (width // LANES), axis=1)
    new_ref[...] = h.astype(F32) + keep * (unit * vec[6:7, :] + vec[7:8, :])
    d_update = keep * up_ref[...]
    scaled = d_update * vec[6:7, :]
    d_inner = inverse * (
        scaled
        - jnp.mean(scaled, axis=-1, keepdims=True)
        - unit * jnp.mean(scaled * unit, axis=-1, keepdims=True)
    )
    d_inner = d_inner.astype(B16)
    d_inner_ref[...] = d_inner
    slope = sigma * (1.0 + pre * (1.0 - sigma))
    d_pre = (dot_back(d_inner, second) * slope).astype(B16)
    d_pre_ref[...] = d_pre
    d_agg_ref[...] = dot_back(d_pre, aggregate).astype(B16)
    sums_ref[...] = jnp.concatenate(
        [
            jnp.sum(d_pre.astype(F32), axis=0, keepdims=True),
            jnp.sum(d_inner.astype(F32), axis=0, keepdims=True),
            jnp.sum(d_update * unit, axis=0, keepdims=True),
            jnp.sum(d_update, axis=0, keepdims=True),
        ],
        axis=0,
    )


def node_update(h, agg, weights, forced, upstream):
    nodes, width = h.shape
    full = jax.ShapeDtypeStruct((nodes, width), F32)
    half = jax.ShapeDtypeStruct((nodes, width), B16)
    return pl.pallas_call(
        node_kernel,
        out_shape=[full, half, half, half, half, jax.ShapeDtypeStruct((4, width), F32)],
        compiler_params=PARAMS,
        name="node_update",
        cost_estimate=pl.CostEstimate(
            flops=2 * nodes * width * width * 5, transcendentals=2 * nodes * width, bytes_accessed=nodes * width * 20
        ),
    )(h, agg, weights, forced.reshape(-1, LANES), upstream)


def node_grads_kernel(h_ref, agg_ref, hidden_ref, d_inner_ref, d_pre_ref, w_ref, up_ref, grad_ref, back_ref):
    width = h_ref.shape[1]
    d_pre = d_pre_ref[...]
    grad_ref[0:width, :] = dot_rows(h_ref[...], d_pre)
    grad_ref[width : 2 * width, :] = dot_rows(agg_ref[...], d_pre)
    grad_ref[2 * width : 3 * width, :] = dot_rows(hidden_ref[...], d_inner_ref[...])
    back_ref[...] = up_ref[...] + dot_back(d_pre, w_ref[4 * width : 5 * width, :])


def node_grads(h, agg, hidden, d_inner, d_pre, weights, upstream):
    nodes, width = h.shape
    return pl.pallas_call(
        node_grads_kernel,
        out_shape=[jax.ShapeDtypeStruct((3 * width, width), F32), jax.ShapeDtypeStruct((nodes, width), F32)],
        compiler_params=PARAMS,
        name="node_grads",
        cost_estimate=pl.CostEstimate(
            flops=2 * nodes * width * width * 4, transcendentals=0, bytes_accessed=nodes * width * 18
        ),
    )(h, agg, hidden, d_inner, d_pre, weights, upstream)


def edge_backward_kernel(
    place_ref, recv_ref, region_row_ref, off_ref, near_ref, hs_ref, hr_ref, x_ref, hidden_ref, slope_ref, unit_ref,
    inverse_ref, w_ref, node_grad_ref, node_sum_ref,
    d_pre_ref, kept_ref, sent_ref,
    first_ref, second_ref, table_ref, vec_acc_ref,
):
    step = pl.program_id(0)
    steps = pl.num_programs(0)
    rows, width = x_ref.shape
    nodes = off_ref.shape[0]
    regions = table_ref.shape[0]
    vec = vectors_of(w_ref, width)

    @pl.when(step == 0)
    def _():
        first_ref[...] = jnp.zeros_like(first_ref)
        second_ref[...] = jnp.zeros_like(second_ref)
        table_ref[...] = jnp.zeros_like(table_ref)
        vec_acc_ref[...] = jnp.zeros_like(vec_acc_ref)

    d_message = dot(chosen_columns(recv_ref, step, rows, 2 * nodes, 3 * nodes), off_ref[...])
    d_message = d_message + near_ref[...].astype(F32)
    unit = unit_ref[...]
    scaled = d_message * vec[2:3, :]
    inverse = inverse_ref[:, 0:1]
    d_inner = inverse * (
        scaled
        - jnp.mean(scaled, axis=-1, keepdims=True)
        - unit * jnp.mean(scaled * unit, axis=-1, keepdims=True)
    )
    vec_acc_ref[0:8, :] += jnp.sum((d_message * unit).reshape(rows // 8, 8, width), axis=0)
    vec_acc_ref[8:16, :] += jnp.sum(d_message.reshape(rows // 8, 8, width), axis=0)
    d_inner = d_inner.astype(B16)
    second_ref[0:width, :] += dot_rows(hidden_ref[...], d_inner)
    second_ref[width : width + 16, :] += dot(jnp.ones((16, rows), B16), d_inner)
    d_pre = (dot_back(d_inner, w_ref[3 * width : 4 * width, :]) * slope_ref[...]).astype(B16)
    d_pre_ref[...] = d_pre
    first_ref[0:width, :] += dot_rows(hs_ref[...], d_pre)
    first_ref[width : 2 * width, :] += dot_rows(hr_ref[...], d_pre)
    first_ref[2 * width : 3 * width, :] += dot_rows(x_ref[...], d_pre)
    base = pl.multiple_of(step * rows, rows)
    region_row = region_row_ref[:, pl.ds(base, rows)]
    table_ref[...] += dot(chosen_rows(region_row, 0, regions), d_pre)

    @pl.when(step == steps - 1)
    def _():
        table_rows = node_grad_ref.shape[0] + 4 * width
        table_grad = table_ref[...]
        vector_rows = jnp.concatenate(
            [
                jnp.sum(table_grad, axis=0, keepdims=True),
                second_ref[width : width + 1, :],
                jnp.sum(vec_acc_ref[0:8, :], axis=0, keepdims=True),
                jnp.sum(vec_acc_ref[8:16, :], axis=0, keepdims=True),
                node_sum_ref[...],
            ],
            axis=0,
        )
        pieces = (
            (0, first_ref[...]),
            (3 * width, second_ref[0:width, :]),
            (4 * width, node_grad_ref[...]),
            (table_rows, vector_rows),
            (table_rows + 8, table_grad),
        )
        odd = place_ref[0] == 1
        for start, piece in pieces:
            left, right = piece[:, 0:LANES], piece[:, LANES:]
            kept_ref[start : start + piece.shape[0], :] = jnp.where(odd, right, left)
            sent_ref[start : start + piece.shape[0], :] = jnp.where(odd, left, right)


def edge_backward(
    place, recv, regions, off, near, hs, hr, edges, hidden, slope, unit, inverse, weights, node_grad, node_sum,
    region_count,
):
    count, width = edges.shape
    tile = tiled(TILE, width)
    grad_rows = weights.shape[0]
    half = whole((grad_rows, LANES))
    return pl.pallas_call(
        edge_backward_kernel,
        grid=(count // TILE,),
        in_specs=[
            pl.BlockSpec(memory_space=pltpu.SMEM), whole((count // LANES, LANES)), whole((1, count)),
            whole(off.shape), tile, tile, tile, tile, tile, tile, tile, tiled(TILE, LANES),
            whole(weights.shape), whole(node_grad.shape), whole(node_sum.shape),
        ],
        out_specs=[tile, half, half],
        out_shape=[
            jax.ShapeDtypeStruct((count, width), B16),
            jax.ShapeDtypeStruct((grad_rows, LANES), F32),
            jax.ShapeDtypeStruct((grad_rows, LANES), F32),
        ],
        scratch_shapes=[
            pltpu.VMEM((3 * width, width), F32),
            pltpu.VMEM((width + 16, width), F32),
            pltpu.VMEM((region_count, width), F32),
            pltpu.VMEM((16, width), F32),
        ],
        compiler_params=PARAMS,
        name="edge_backward",
        cost_estimate=pl.CostEstimate(
            flops=2 * count * width * (6 * width + off.shape[0]), transcendentals=0, bytes_accessed=count * width * 20
        ),
    )(
        place, recv.reshape(-1, LANES), regions.reshape(1, -1), off, near, hs, hr, edges, hidden, slope, unit, inverse,
        weights, node_grad, node_sum,
    )


def node_part_kernel(index_row_ref, d_pre_ref, w_ref, out_ref, *, first):
    width = d_pre_ref.shape[1]
    weight = w_ref[first : first + width, :]
    count = out_ref.shape[0]
    base = pl.program_id(0) * count
    high, low = split(dot(chosen_rows(index_row_ref[...], base, count), d_pre_ref[...]))
    out_ref[...] = dot_back(high, weight) + dot_back(low, weight)


def node_part(index, d_pre, weights, first, nodes):
    count, width = d_pre.shape
    return pl.pallas_call(
        functools.partial(node_part_kernel, first=first),
        grid=(3,),
        in_specs=[whole((1, count)), whole((count, width)), whole(weights.shape)],
        out_specs=tiled(nodes, width),
        out_shape=jax.ShapeDtypeStruct((3 * nodes, width), F32),
        compiler_params=PARAMS,
        name="node_part",
        cost_estimate=pl.CostEstimate(
            flops=6 * count * width * nodes, transcendentals=0, bytes_accessed=count * width * 2
        ),
    )(index.reshape(1, -1), d_pre, weights)


def edge_grads_kernel(d_pre_ref, w_ref, out_ref):
    width = d_pre_ref.shape[1]
    out_ref[...] = dot_back(d_pre_ref[...], w_ref[2 * width : 3 * width, :]).astype(B16)


def edge_grads(d_pre, weights):
    count, width = d_pre.shape
    return pl.pallas_call(
        edge_grads_kernel,
        grid=(count // TILE,),
        in_specs=[tiled(TILE, width), whole(weights.shape)],
        out_specs=tiled(TILE, width),
        out_shape=jax.ShapeDtypeStruct((count, width), B16),
        compiler_params=PARAMS,
        name="edge_grads",
        cost_estimate=pl.CostEstimate(
            flops=2 * count * width * width, transcendentals=0, bytes_accessed=count * width * 4
        ),
    )(d_pre, weights)


def finish_kernel(place_ref, mine_ref, other_ref, out_ref, *, first):
    share = out_ref.shape[0] - 16
    rest = slice(share, share + 8)
    rows = slice(first, first + 8)
    part = mine_ref[0:share, :].astype(F32) + other_ref[0:share, :].astype(F32)
    exact = part[rows, :] + (mine_ref[rest, :].astype(F32) + other_ref[rest, :].astype(F32))
    out_ref[0:share, :] = part
    out_ref[rows, :] = exact
    part = out_ref[0:share, :]
    out_ref[share : share + 8, :] = jnp.where(place_ref[1] == 1, exact, 0.0)
    squares = jnp.sum(jnp.sum(part * part, axis=0, keepdims=True), axis=1, keepdims=True)
    out_ref[share + 8 : share + 16, :] = jnp.broadcast_to(squares, (8, LANES))


def finish(place, mine, other, share, first):
    return pl.pallas_call(
        functools.partial(finish_kernel, first=first),
        in_specs=[pl.BlockSpec(memory_space=pltpu.SMEM)] + [pl.BlockSpec(memory_space=pltpu.VMEM)] * 2,
        out_shape=jax.ShapeDtypeStruct((share + 16, LANES), F32),
        compiler_params=PARAMS,
        name="finish",
    )(place, mine, other)


def adam_kernel(
    place_ref, step_ref, stats_ref, more_ref, mine_ref, other_ref, params_ref, first_ref, second_ref, averaged_ref,
    new_first_ref, new_second_ref, new_params_ref, new_average_ref, norm_ref, vector_ref,
):
    share = params_ref.shape[0]
    odd = place_ref[0] == 1
    stats = stats_ref[...] + more_ref[...]
    norm = jnp.sqrt(stats[8:9, 0:1] + stats[24:25, 0:1])
    norm_ref[...] = norm
    factor = jnp.minimum(1.0, MAX_NORM / (norm + 1e-06))
    count = jnp.full((1, 1), step_ref[0], F32)
    first_scale = 1.0 - jnp.exp(count * jnp.log(jnp.full((1, 1), BETA_ONE, F32)))
    second_scale = 1.0 - jnp.exp(count * jnp.log(jnp.full((1, 1), BETA_TWO, F32)))
    decay = jnp.minimum(AVERAGE_DECAY, (1.0 + count) / (10.0 + count))
    for half in range(2):
        swap = odd if half == 0 else jnp.logical_not(odd)
        lanes = slice(half * LANES, (half + 1) * LANES)
        vector_ref[:, lanes] = jnp.where(swap, stats[16:24, :], stats[0:8, :]) * factor
        clipped = jnp.where(swap, other_ref[0:share, :], mine_ref[0:share, :]) * factor
        params = params_ref[:, lanes]
        new_first = BETA_ONE * first_ref[:, lanes] + (1.0 - BETA_ONE) * clipped
        new_second = BETA_TWO * second_ref[:, lanes] + (1.0 - BETA_TWO) * clipped * clipped
        new_first_ref[:, lanes] = new_first
        new_second_ref[:, lanes] = new_second
        first_hat = new_first / first_scale
        second_hat = new_second / second_scale
        new_params = params - RATE * (first_hat / (jnp.sqrt(second_hat) + ADAM_EPS) + WEIGHT_DECAY * params)
        new_params_ref[:, lanes] = new_params
        new_average_ref[:, lanes] = decay * averaged_ref[:, lanes] + (1.0 - decay) * new_params


def adam(place, step, stats, more, mine, other, params, first_moment, second_moment, averaged):
    rows = jax.ShapeDtypeStruct(params.shape, F32)
    smem, vmem = pl.BlockSpec(memory_space=pltpu.SMEM), pl.BlockSpec(memory_space=pltpu.VMEM)
    return pl.pallas_call(
        adam_kernel,
        in_specs=[smem, smem] + [vmem] * 8,
        out_shape=[rows, rows, rows, rows, jax.ShapeDtypeStruct((1, 1), F32), jax.ShapeDtypeStruct((8, params.shape[1]), F32)],
        compiler_params=PARAMS,
        name="adam",
        cost_estimate=pl.CostEstimate(
            flops=20 * params.size, transcendentals=2 * params.size, bytes_accessed=params.size * 32
        ),
    )(place, step, stats, more, mine, other, params, first_moment, second_moment, averaged)


def flipped(value, axis, bit):
    return lax.ppermute(value, axis, [(i, i ^ bit) for i in range(lax.axis_size(axis))])


def across(value, axis):
    count = lax.axis_size(axis)
    return lax.ppermute(value, axis, [(i, (i + 1 if i % 2 else i - 1) % count) for i in range(count)])


def neighbours(value):
    off = across(value, "edge")
    return flipped(value, "edge", 1), off


def on_device(
    node_latents, edge_latents, senders, receivers, regions, forced, params, first_moment, second_moment,
    averaged, step, cotangent,
):
    latents = node_latents[0]
    edges = edge_latents[0]
    upstream = cotangent[0]
    nodes, width = latents.shape
    share = params.shape[0]
    e, f = lax.axis_index("edge"), lax.axis_index("feat")
    blocks, feats = lax.axis_size("edge"), lax.axis_size("feat")
    core = e % 2
    total = share * feats
    vector_row = 7 * width
    region_count = total - vector_row - 8

    pair, off = neighbours(latents)

    mine = lax.dynamic_slice_in_dim(params, core * LANES, LANES, 1).astype(B16)
    fetched = [mine] + [flipped(mine, "feat", k) for k in range(1, feats)]
    owner = (f == vector_row // share).astype(I32)
    place = jnp.stack([core, owner] + [f ^ k for k in range(feats)])

    def local(index):
        block = index // nodes
        slot = jnp.where(block == e, 0, jnp.where(block == e + 1 - 2 * core, 1, 2))
        return slot * nodes + index % nodes

    send, recv = local(senders), local(receivers)

    near_send = gather_near(send, latents, pair)
    near_recv = gather_near(recv, latents, pair)
    fetched = lax.optimization_barrier((near_recv, *fetched))[1:]
    pieces = [*fetched, *(flipped(piece, "edge", 1) for piece in fetched)]
    hs = gather_off(send, off, near_send)
    hr = gather_off(recv, off, near_recv)
    weights, hidden, slope, unit, inverse, high, low, to_off = edge_forward(
        place, regions, recv, hs, hr, edges, pieces, total, nodes
    )
    from_off = across(to_off, "edge")
    to_pair, own = near_sum(recv, high, low, nodes)
    from_pair = flipped(to_pair, "edge", 1)
    agg = (own + from_pair + from_off).astype(B16)

    new_latents, d_agg, node_hidden, d_inner, d_pre, node_sum = node_update(
        latents, agg, weights, forced, upstream
    )
    back_pair, back_off = neighbours(d_agg)
    node_grad, back = node_grads(latents, agg, node_hidden, d_inner, d_pre, weights, upstream)
    near = gather_near(recv, d_agg, back_pair)

    d_pre, kept, sent = edge_backward(
        place, recv, regions, back_off, near, hs, hr, edges, hidden, slope, unit, inverse, weights, node_grad, node_sum,
        region_count,
    )
    grad_edges = edge_grads(d_pre, weights)
    node_grads_send = node_part(send, d_pre, weights, 0, nodes)
    node_grads_recv = node_part(recv, d_pre, weights, width, nodes)
    part_own = node_grads_send[:nodes] + node_grads_recv[:nodes]
    part_halo = (node_grads_send[nodes:] + node_grads_recv[nodes:]).astype(B16)

    grad = kept + flipped(sent, "edge", 1)
    low_rows = vector_row % share

    def packed(values):
        top, rest = split(values)
        return jnp.concatenate([top, rest[..., low_rows : low_rows + 8, :]], axis=-2)

    def unpacked(values):
        values = values.astype(F32)
        rest = jnp.pad(values[..., share:, :], ((0, 0),) * (values.ndim - 2) + ((low_rows, share - low_rows - 8), (0, 0)))
        return values[..., :share, :] + rest

    part = grad.reshape(feats, share, LANES)
    bit = 1
    while bit < feats:
        part = part.reshape(-1, 2, share, LANES)
        here = (f // bit) % 2
        keep_part = lax.dynamic_index_in_dim(part, here, 1, keepdims=False)
        send_part = lax.dynamic_index_in_dim(part, 1 - here, 1, keepdims=False)
        part = keep_part + unpacked(flipped(packed(send_part), "feat", bit))
        bit *= 2
    part = part.reshape(share, LANES)

    grads_off = across(part_halo[nodes:], "edge").astype(F32)
    grads_pair = flipped(part_halo[:nodes], "edge", 1).astype(F32)
    grad_latents = back + part_own + grads_pair + grads_off

    wire = packed(part)
    bit = 2
    while 2 * bit < blocks:
        wire = packed(unpacked(wire) + unpacked(flipped(wire, "edge", bit)))
        bit *= 2
    mine = finish(place, wire, flipped(wire, "edge", bit), share, low_rows)
    other = flipped(mine, "edge", 1)
    stats = jnp.concatenate([mine[share:], other[share:]], axis=0)
    bit = 1
    while 2 * bit < feats:
        stats = stats + flipped(stats, "feat", bit)
        bit *= 2
    more = flipped(stats, "feat", bit)
    new_first, new_second, new_params, new_average, grad_norm, vector_grads = adam(
        place, step, stats, more, mine, other, params, first_moment, second_moment, averaged
    )
    return (
        new_latents[None],
        grad_latents[None],
        grad_edges[None],
        new_first,
        new_second,
        new_params,
        new_average,
        grad_norm.reshape(1),
        vector_grads,
    )


def solution(mesh):
    nodes, rows = P("feat", "edge", None), P("feat", None)
    return jax.shard_map(
        on_device,
        mesh=mesh,
        in_specs=(nodes, nodes, P("edge"), P("edge"), P("edge"), P("edge"), rows, rows, rows, rows, P(), nodes),
        out_specs=(nodes, nodes, nodes, rows, rows, rows, rows, P(), P()),
        check_vma=False,
    )
```

time: 155 us -> 126 us (0.81)
  Pallas kernels: 67.3 us -> 55.6 us
  waiting for transfers between devices: 40.9 us -> 31.9 us
  between operations: 4.35 us -> 1.76 us
  local copies, waits for them, and re-layouts: 7.46 us -> 5.41 us
  starting transfers between devices: 23.8 us -> 21.8 us
  other arithmetic: 10.5 us -> 8.83 us
    ppermute x16 -> x19, waiting for transfers between devices: 29.5 us -> 17.1 us  [flipped(): lax.ppermute(value, axis, [(i, i ^ bit) for i in range(lax.axis_size(axis...]
    pallas_call x5 -> x14, Pallas kernels: 64.1 us -> 55.1 us  [the longest x1 11 us: edge_backward(): pl.pallas_call(edge_backward_kernel, grid=(count // TILE,), in_specs=[pl....]
    ppermute x4, waiting for transfers between devices: 11.4 us -> 14.7 us  [across(): lax.ppermute(value, axis, [(i, (i + 1 if i % 2 else i - 1) % count) for i...]
    pallas_call x1, Pallas kernels: 3.27 us -> 0.47 us  [node_grads(): pl.pallas_call(node_grads_kernel, out_shape=[jax.ShapeDtypeStruct((3 * wi...]
    unnamed x26 -> x38, local copies, waits for them, and re-layouts: 2.3 us -> 3.63 us
    ppermute x16 -> x19, starting transfers between devices: 15.2 us -> 13.9 us  [flipped(): lax.ppermute(value, axis, [(i, i ^ bit) for i in range(lax.axis_size(axis...]
  transfers between devices with their start and end apart: 20 -> 23, of which waited for: 11 -> 11; matrix products, arithmetic and copies ran while one was open for 4% -> 4% of each run, Pallas kernels for 12% -> 25%
where the time goes in v2:
time: 126 us; the launch traced here: 125 us
  Pallas kernels  55.6 us (44%)
  waiting for transfers between devices  31.9 us (25%)
  starting transfers between devices  21.8 us (17%)
  other arithmetic  8.83 us (7%)
  local copies, waits for them, and re-layouts  5.41 us (4%)
  between operations  1.76 us (1%)
    ppermute x19, waiting for transfers between devices, flipped(): lax.ppermute(value, axis, [(i, i ^ bit) for i in range(lax.axis_size(axis...  17.1 us
    ppermute x4, waiting for transfers between devices, across(): lax.ppermute(value, axis, [(i, (i + 1 if i % 2 else i - 1) % count) for i...  14.7 us
    ppermute x19, starting transfers between devices, flipped(): lax.ppermute(value, axis, [(i, i ^ bit) for i in range(lax.axis_size(axis...  13.9 us
    pallas_call x1, Pallas kernels, edge_backward(): pl.pallas_call(edge_backward_kernel, grid=(count // TILE,), in_specs=[pl....  11 us
    pallas_call x2, Pallas kernels, node_part(): pl.pallas_call(functools.partial(node_part_kernel, first=first), grid=(3,...  9.92 us
    pallas_call x1, Pallas kernels, edge_forward(): pl.pallas_call(edge_forward_kernel, grid=(steps + 1,), in_specs=[pl.Block...  9.31 us
    pallas_call x3, Pallas kernels, gather_near(): pl.pallas_call(gather_near_kernel, grid=(edges // TILE,), in_specs=[whole...  9.27 us
    ppermute x4, starting transfers between devices, across(): lax.ppermute(value, axis, [(i, (i + 1 if i % 2 else i - 1) % count) for i...  7.86 us
  transfers between devices with their start and end apart: 23, of which 11 were waited for; matrix products, arithmetic and copies ran while one was open for 4% of the time, Pallas kernels for 25%

profile of v2, /device:TPU:0, one launch (start us, length us, event | category | flops | bytes accessed | tf_op | source)
XLA Modules:
  0.0 125.2 jit_solution(18049785071726985218)
XLA Ops:
  0.6 3.4 %collective-permute-start = (bf16[512,256]{1,0:T(8,128)(2,1)}, bf16[512,256]{1,0:T(8,128)(2,1)S(1)}, u32[]{:S(2)}, u32[]{:S(2)}) collective-permute-start(bf16[512,256]{1,0:T(8,128)(2,1)} %bitcast.40), channel_id=1, source_target_pairs={{0,28},{4,8},{8,4},{12,16},{16,12},{20,24},{24,20},{28,0},{1,29},{... | collective-permute-start | bytes 786440 | tf_op jit(solution)/shard_map/ppermute | solution.py:561
  4.0 1.0 dynamic-slice_convert_fusion.1.refs_0_
  5.0 1.6 %collective-permute-start.2 = (bf16[456,128]{1,0:T(8,128)(2,1)S(1)}, bf16[456,128]{1,0:T(8,128)(2,1)S(1)}, u32[]{:S(2)}, u32[]{:S(2)}) collective-permute-start(bf16[456,128]{1,0:T(8,128)(2,1)S(1)} %dynamic-slice_convert_fusion.1.refs_0_), channel_id=1, source_target_pairs={{0,1},{1,0},{2,3},{3,2},{4,5},{5,4},{6,7},{7,6},{8,9},{9,8},{10,11... | collective-permute-start | bytes 350216 | tf_op jit(solution)/shard_map/ppermute | solution.py:556
  6.6 2.6 %collective-permute-start.3 = (bf16[456,128]{1,0:T(8,128)(2,1)S(1)}, bf16[456,128]{1,0:T(8,128)(2,1)S(1)}, u32[]{:S(2)}, u32[]{:S(2)}) collective-permute-start(bf16[456,128]{1,0:T(8,128)(2,1)S(1)} %dynamic-slice_convert_fusion.1.refs_0_), channel_id=1, source_target_pairs={{0,2},{1,3},{2,0},{3,1},{4,6},{5,7},{6,4},{7,5},{8,10},{9,11},{10,... | collective-permute-start | bytes 350216 | tf_op jit(solution)/shard_map/ppermute | solution.py:556
  9.2 0.2 collective-permute-start.4
  9.5 0.7 fusion.9
  10.2 0.0 copy-start.12
  10.2 0.7 fusion.25.index_ref.recv_ref
  11.0 0.1 stack.31.place_ref
  11.1 0.7 fusion.26.index_ref
  11.8 0.9 copy-done.2
  12.8 3.1 %gather_near.4.near_ref = bf16[4096,256]{1,0:T(8,128)(2,1)S(1)} custom-call(s32[32,128]{1,0:T(8,128)S(1)} %fusion.25.index_ref.recv_ref, bf16[512,256]{1,0:T(8,128)(2,1)S(1)} %bitcast.42, bf16[512,256]{1,0:T(8,128)(2,1)S(1)} %collective-permute-done.1.pair_ref), custom_call_target="tpu_custom_call" | custom-call | flops 2147483648 | bytes 2097152 | tf_op jit(solution)/shard_map/gather_near/pallas_call | solution.py:87
  15.9 2.7 %collective-permute-done.3.refs_2_ = bf16[456,128]{1,0:T(8,128)(2,1)S(1)} collective-permute-done((bf16[456,128]{1,0:T(8,128)(2,1)S(1)}, bf16[456,128]{1,0:T(8,128)(2,1)S(1)}, u32[]{:S(2)}, u32[]{:S(2)}) %collective-permute-start.3) | collective-permute-done | bytes 116768 | tf_op jit(solution)/shard_map/ppermute | solution.py:556
  18.6 0.5 collective-permute-start.6
  19.1 0.5 collective-permute-start.8
  19.6 3.1 %gather_near.3.near_ref = bf16[4096,256]{1,0:T(8,128)(2,1)S(1)} custom-call(s32[32,128]{1,0:T(8,128)S(1)} %fusion.26.index_ref, bf16[512,256]{1,0:T(8,128)(2,1)S(1)} %bitcast.43, bf16[512,256]{1,0:T(8,128)(2,1)S(1)} %collective-permute-done.1.pair_ref), custom_call_target="tpu_custom_call" | custom-call | flops 2147483648 | bytes 2097152 | tf_op jit(solution)/shard_map/gather_near/pallas_call | solution.py:87
  22.8 2.0 %gather_off.3.hr_ref = bf16[4096,256]{1,0:T(8,128)(2,1)S(1)} custom-call(s32[32,128]{1,0:T(8,128)S(1)} %fusion.25.index_ref.recv_ref, bf16[512,256]{1,0:T(8,128)(2,1)S(1)} %collective-permute-done.off_ref, bf16[4096,256]{1,0:T(8,128)(2,1)S(1)} %gather_near.4.near_ref), custom_call_target="tpu_custom_call" | custom-call | flops 1073741824 | bytes 4194304 | tf_op jit(solution)/shard_map/gather_off/pallas_call | solution.py:112
  24.7 0.0 copy-start
  24.7 0.0 copy-start.11
  24.8 2.0 %gather_off.2.hs_ref = bf16[4096,256]{1,0:T(8,128)(2,1)S(1)} custom-call(s32[32,128]{1,0:T(8,128)S(1)} %fusion.26.index_ref, bf16[512,256]{1,0:T(8,128)(2,1)S(1)} %collective-permute-done.off_ref, bf16[4096,256]{1,0:T(8,128)(2,1)S(1)} %gather_near.3.near_ref), custom_call_target="tpu_custom_call" | custom-call | flops 1073741824 | bytes 4194304 | tf_op jit(solution)/shard_map/gather_off/pallas_call | solution.py:112
  26.8 9.3 %edge_forward.1 = (bf16[1824,256]{1,0:T(8,128)(2,1)S(1)}, bf16[4096,256]{1,0:T(8,128)(2,1)S(1)}, f32[4096,256]{1,0:T(8,128)S(1)}, f32[4096,256]{1,0:T(8,128)S(1)...) custom-call(s32[6]{0:T(128)S(1)} %stack.31.place_ref, ...), custom_call_target="tpu_custom_call" | custom-call | flops 4831838208 | bytes 20971520 | tf_op jit(solution)/shard_map/edge_forward/pallas_call | solution.py:189
  36.1 0.9 collective-permute-start.10
  37.0 4.5 %near_sum.1 = (f32[512,256]{1,0:T(8,128)S(1)}, f32[512,256]{1,0:T(8,128)S(1)}) custom-call(s32[1,4096]{1,0:T(1,128)S(1)} %bitcast.49, bf16[4096,256]{1,0:T(8,128)(2,1)S(1)} %get-tuple-element.44.high_ref, bf16[4096,256]{1,0:T(8,128)(2,1)S(1)} %get-tuple-element.45.low_ref), custom_call_target="tpu_custom_call" | custom-call | flops 4294967296 | bytes 4194304 | tf_op jit(solution)/shard_map/near_sum/pallas_call | solution.py:230
  41.5 0.6 collective-permute-start.9
  42.2 9.1 %collective-permute-done.10 = f32[512,256]{1,0:T(8,128)S(1)} collective-permute-done((f32[512,256]{1,0:T(8,128)S(1)}, f32[512,256]{1,0:T(8,128)S(1)}, u32[]{:S(2)}, u32[]{:S(2)}) %collective-permute-start.10) | collective-permute-done | bytes 524320 | tf_op jit(solution)/shard_map/ppermute | solution.py:561
  51.3 0.1 add_convert_fusion.agg_ref
  51.4 1.7 %node_update.1 = (f32[512,256]{1,0:T(8,128)}, bf16[512,256]{1,0:T(8,128)(2,1)S(1)}, bf16[512,256]{1,0:T(8,128)(2,1)S(1)}, bf16[512,256]{1,0:T(8,128)(2,1)S(1)}, ...) custom-call(bf16[512,256]{1,0:T(8,128)(2,1)S(1)} %bitcast.44, bf16[512,256]{1,0:T(8,128)(2,1)S(1)} %add_convert_fusion.agg_ref, ...), custom_call_target="tpu_custom_call" | custom-call | flops 335544320 | bytes 2621440 | tf_op jit(solution)/shard_map/node_update/pallas_call | solution.py:295
  53.1 0.7 collective-permute-start.11
  53.8 0.5 node_grads.1
  54.3 0.4 collective-permute-done.12.pair_ref
  54.7 3.1 %gather_near.5.near_ref = bf16[4096,256]{1,0:T(8,128)(2,1)S(1)} custom-call(s32[32,128]{1,0:T(8,128)S(1)} %fusion.25.index_ref.recv_ref, bf16[512,256]{1,0:T(8,128)(2,1)S(1)} %get-tuple-element.55.own_ref, bf16[512,256]{1,0:T(8,128)(2,1)S(1)} %collective-permute-done.12.pair_ref), custom_call_target="tpu_custom_call" | custom-call | flops 2147483648 | bytes 2097152 | tf_op jit(solution)/shard_map/gather_near/pallas_call | solution.py:87
  57.8 4.9 %collective-permute-done.11.off_ref = bf16[512,256]{1,0:T(8,128)(2,1)S(1)} collective-permute-done((bf16[512,256]{1,0:T(8,128)(2,1)S(1)}, bf16[512,256]{1,0:T(8,128)(2,1)S(1)}, u32[]{:S(2)}, u32[]{:S(2)}) %collective-permute-start.11) | collective-permute-done | bytes 262176 | tf_op jit(solution)/shard_map/ppermute | solution.py:561
  62.6 0.7 copy-done.10
  63.3 11.0 %edge_backward.1 = (bf16[4096,256]{1,0:T(8,128)(2,1)S(1)}, f32[1824,128]{1,0:T(8,128)S(1)}, f32[1824,128]{1,0:T(8,128)}) custom-call(s32[6]{0:T(128)S(1)} %copy-done.15, s32[32,128]{1,0:T(8,128)S(1)} %copy-done.10, s32[1,4096]{1,0:T(1,128)S(1)} %bitcast.47, bf16[512,256]{1,0:T(8,128)(2,1)S(1)} %collective-permute-done.11.off_ref, ...), custom_call_target="tpu_custom_call" | custom-call | flops 4294967296 | bytes 20971520 | tf_op jit(solution)/shard_map/edge_backward/pallas_call | solution.py:408
  74.3 1.0 copy-done.4
  75.3 2.8 %collective-permute-done.15 = f32[1824,128]{1,0:T(8,128)} collective-permute-done((f32[1824,128]{1,0:T(8,128)}, f32[1824,128]{1,0:T(8,128)}, u32[]{:S(2)}, u32[]{:S(2)}) %collective-permute-start.15) | collective-permute-done | bytes 933920 | tf_op jit(solution)/shard_map/ppermute | solution.py:556
  78.1 1.6 %add.123 = f32[1824,128]{1,0:T(8,128)S(1)} add(f32[1824,128]{1,0:T(8,128)} %copy-done.4, f32[1824,128]{1,0:T(8,128)} %collective-permute-done.15) | non-fusion elementwise | flops 233472 | bytes 2801664 | tf_op jit(solution)/shard_map/add | solution.py:630
  79.7 0.9 copy-done.18
  80.6 0.1 fusion.23
  80.7 0.7 pad_maximum_fusion
  81.4 1.4 %collective-permute-start.16 = (bf16[2,464,128]{2,1,0:T(8,128)(2,1)}, bf16[2,464,128]{2,1,0:T(8,128)(2,1)}, u32[]{:S(2)}, u32[]{:S(2)}) collective-permute-start(bf16[2,464,128]{2,1,0:T(8,128)(2,1)} %pad_maximum_fusion), channel_id=1, source_target_pairs={{0,1},{1,0},{2,3},{3,2},{4,5},{5,4},{6,7},{7,6},{8,9},{9,8},{10,11... | collective-permute-start | bytes 712712 | tf_op jit(solution)/shard_map/ppermute | solution.py:556
  83.5 0.7 fusion.10
  84.2 5.3 %collective-permute-done.16 = bf16[2,464,128]{2,1,0:T(8,128)(2,1)} collective-permute-done((bf16[2,464,128]{2,1,0:T(8,128)(2,1)}, bf16[2,464,128]{2,1,0:T(8,128)(2,1)}, u32[]{:S(2)}, u32[]{:S(2)}) %collective-permute-start.16) | collective-permute-done | bytes 237600 | tf_op jit(solution)/shard_map/ppermute | solution.py:556
  89.5 1.0 convert_element_type.79
  90.5 0.7 slice.89
  91.2 1.1 fusion.5
  92.4 2.5 %collective-permute-start.17 = (bf16[1,464,128]{2,1,0:T(8,128)(2,1)S(1)}, bf16[1,464,128]{2,1,0:T(8,128)(2,1)S(1)}, u32[]{:S(2)}, u32[]{:S(2)}) collective-permute-start(bf16[1,464,128]{2,1,0:T(8,128)(2,1)S(1)} %pad_maximum_fusion.1), channel_id=1, source_target_pairs={{0,2},{1,3},{2,0},{3,1},{4,6},{5,7},{6,4},{7,5},{8,10},{9,11},{10,... | collective-permute-start | bytes 356360 | tf_op jit(solution)/shard_map/ppermute | solution.py:556
  94.9 5.0 %node_part.3 = f32[1536,256]{1,0:T(8,128)S(1)} custom-call(s32[1,4096]{1,0:T(1,128)S(1)} %bitcast.50, bf16[4096,256]{1,0:T(8,128)(2,1)S(1)} %get-tuple-element.62.d_pre_ref, bf16[1824,256]{1,0:T(8,128)(2,1)S(1)} %get-tuple-element.49.w_ref), custom_call_target="tpu_custom_call" | custom-call | flops 3221225472 | bytes 2097152 | tf_op jit(solution)/shard_map/node_part/pallas_call | solution.py:450
  99.8 0.5 collective-permute-done.17
  100.4 0.4 collective-permute-start.18
  100.9 5.0 %node_part.2 = f32[1536,256]{1,0:T(8,128)S(1)} custom-call(s32[1,4096]{1,0:T(1,128)S(1)} %bitcast.51, bf16[4096,256]{1,0:T(8,128)(2,1)S(1)} %get-tuple-element.62.d_pre_ref, bf16[1824,256]{1,0:T(8,128)(2,1)S(1)} %get-tuple-element.49.w_ref), custom_call_target="tpu_custom_call" | custom-call | flops 3221225472 | bytes 2097152 | tf_op jit(solution)/shard_map/node_part/pallas_call | solution.py:450
  106.0 1.4 %collective-permute-start.19 = (bf16[464,128]{1,0:T(8,128)(2,1)S(1)}, bf16[464,128]{1,0:T(8,128)(2,1)S(1)}, u32[]{:S(2)}, u32[]{:S(2)}) collective-permute-start(bf16[464,128]{1,0:T(8,128)(2,1)S(1)} %pad_maximum_fusion.3.mine_ref), channel_id=1, source_target_pairs={{0,16},{4,20},{8,24},{12,28},{16,0},{20,4},{24,8},{28,12},{1,17},{... | collective-permute-start | bytes 356360 | tf_op jit(solution)/shard_map/ppermute | solution.py:556
  107.4 0.2 fusion
  107.5 3.3 %collective-permute-done.19.other_ref = bf16[464,128]{1,0:T(8,128)(2,1)S(1)} collective-permute-done((bf16[464,128]{1,0:T(8,128)(2,1)S(1)}, bf16[464,128]{1,0:T(8,128)(2,1)S(1)}, u32[]{:S(2)}, u32[]{:S(2)}) %collective-permute-start.19) | collective-permute-done | bytes 118816 | tf_op jit(solution)/shard_map/ppermute | solution.py:556
  110.9 0.7 finish.1.mine_ref
  111.6 2.9 %collective-permute-start.14 = (bf16[512,256]{1,0:T(8,128)(2,1)S(1)}, bf16[512,256]{1,0:T(8,128)(2,1)S(1)}, u32[]{:S(2)}, u32[]{:S(2)}) collective-permute-start(bf16[512,256]{1,0:T(8,128)(2,1)S(1)} %get-tuple-element.78), channel_id=1, source_target_pairs={{0,28},{4,8},{8,4},{12,16},{16,12},{20,24},{24,20},{28,0},{1,29},{... | collective-permute-start | bytes 786440 | tf_op jit(solution)/shard_map/ppermute | solution.py:561
  114.6 0.1 collective-permute-start.21
  114.7 2.6 %edge_grads.1 = bf16[4096,256]{1,0:T(8,128)(2,1)} custom-call(bf16[4096,256]{1,0:T(8,128)(2,1)S(1)} %get-tuple-element.62.d_pre_ref, bf16[1824,256]{1,0:T(8,128)(2,1)S(1)} %get-tuple-element.49.w_ref), custom_call_target="tpu_custom_call" | custom-call | flops 536870912 | bytes 4194304 | tf_op jit(solution)/shard_map/edge_grads/pallas_call | solution.py:471
  117.3 1.1 collective-permute-done.21
  118.4 2.0 %collective-permute-start.22 = (f32[32,128]{1,0:T(8,128)S(1)}, f32[32,128]{1,0:T(8,128)S(1)}, u32[]{:S(2)}, u32[]{:S(2)}) collective-permute-start(f32[32,128]{1,0:T(8,128)S(1)} %fusion.17.stats_ref), channel_id=1, source_target_pairs={{0,2},{1,3},{2,0},{3,1},{4,6},{5,7},{6,4},{7,5},{8,10},{9,11},{10,... | collective-permute-start | bytes 49160 | tf_op jit(solution)/shard_map/ppermute | solution.py:556
  120.4 0.7 collective-permute-done.14
  121.1 1.0 fusion.4
  122.1 1.0 collective-permute-done.22.more_ref
  123.1 2.2 %adam.1 = (f32[456,256]{1,0:T(8,128)}, f32[456,256]{1,0:T(8,128)}, f32[456,256]{1,0:T(8,128)}, f32[456,256]{1,0:T(8,128)}, f32[1,1]{1,0:T(1,128)}, /*index=5*/f32[8,256]{1,0:T(8,128)}) custom-call(s32[6]{0:T(128)S(1)} %copy-done.16, s32[1]{0:T(128)S(6)} %copy.25.step_ref, f32[32,128]{1,0:T(8,128)S(1)} %fusion.17.stats_ref, ...), custom_call_target="tpu_custom_call" | custom-call | flops 2334720 | bytes 3735552 | tf_op jit(solution)/shard_map/adam/pallas_call | solution.py:543
  (70 shorter events, 0.4 us)
Async XLA Ops:
  0.6 22.1 %collective-permute-start = (bf16[512,256]{1,0:T(8,128)(2,1)}, bf16[512,256]{1,0:T(8,128)(2,1)S(1)}, u32[]{:S(2)}, u32[]{:S(2)}) collective-permute-start(bf16[512,256]{1,0:T(8,128)(2,1)} %bitcast.40), channel_id=1, source_target_pairs={{0,28},{4,8},{8,4},{12,16},{16,12},{20,24},{24,20},{28,0},{1,29},{... | collective-permute-start | bytes 786440 | tf_op jit(solution)/shard_map/ppermute | solution.py:561
  4.0 7.8 %collective-permute-start.1 = (bf16[512,256]{1,0:T(8,128)(2,1)}, bf16[512,256]{1,0:T(8,128)(2,1)S(1)}, u32[]{:S(2)}, u32[]{:S(2)}) collective-permute-start(bf16[512,256]{1,0:T(8,128)(2,1)} %bitcast.41), channel_id=1, source_target_pairs={{0,4},{4,0},{8,12},{12,8},{16,20},{20,16},{24,28},{28,24},{1,5},{5... | collective-permute-start | bytes 786440 | tf_op jit(solution)/shard_map/ppermute | solution.py:556
  5.0 10.9 %collective-permute-start.2 = (bf16[456,128]{1,0:T(8,128)(2,1)S(1)}, bf16[456,128]{1,0:T(8,128)(2,1)S(1)}, u32[]{:S(2)}, u32[]{:S(2)}) collective-permute-start(bf16[456,128]{1,0:T(8,128)(2,1)S(1)} %dynamic-slice_convert_fusion.1.refs_0_), channel_id=1, source_target_pairs={{0,1},{1,0},{2,3},{3,2},{4,5},{5,4},{6,7},{7,6},{8,9},{9,8},{10,11... | collective-permute-start | bytes 350216 | tf_op jit(solution)/shard_map/ppermute | solution.py:556
  6.6 12.0 %collective-permute-start.3 = (bf16[456,128]{1,0:T(8,128)(2,1)S(1)}, bf16[456,128]{1,0:T(8,128)(2,1)S(1)}, u32[]{:S(2)}, u32[]{:S(2)}) collective-permute-start(bf16[456,128]{1,0:T(8,128)(2,1)S(1)} %dynamic-slice_convert_fusion.1.refs_0_), channel_id=1, source_target_pairs={{0,2},{1,3},{2,0},{3,1},{4,6},{5,7},{6,4},{7,5},{8,10},{9,11},{10,... | collective-permute-start | bytes 350216 | tf_op jit(solution)/shard_map/ppermute | solution.py:556
  9.2 9.4 %collective-permute-start.4 = (bf16[456,128]{1,0:T(8,128)(2,1)S(1)}, bf16[456,128]{1,0:T(8,128)(2,1)S(1)}, u32[]{:S(2)}, u32[]{:S(2)}) collective-permute-start(bf16[456,128]{1,0:T(8,128)(2,1)S(1)} %dynamic-slice_convert_fusion.1.refs_0_), channel_id=1, source_target_pairs={{0,3},{1,2},{2,1},{3,0},{4,7},{5,6},{6,5},{7,4},{8,11},{9,10},{10,... | collective-permute-start | bytes 350216 | tf_op jit(solution)/shard_map/ppermute | solution.py:556
  10.2 26.8 %copy-start.12 = (s32[4096]{0:T(1024)}, s32[4096]{0:T(1024)S(1)}, u32[]{:S(2)}) copy-start(s32[4096]{0:T(1024)S(1)} %fusion.9) | copy-start | bytes 49156
  11.0 43.7 %copy-start.9 = (s32[32,128]{1,0:T(8,128)}, s32[32,128]{1,0:T(8,128)S(1)}, u32[]{:S(2)}) copy-start(s32[32,128]{1,0:T(8,128)S(1)} %fusion.25.index_ref.recv_ref) | copy-start | bytes 49156
  11.1 15.7 %copy-start.14 = (s32[6]{0:T(128)}, s32[6]{0:T(128)S(1)}, u32[]{:S(2)}) copy-start(s32[6]{0:T(128)S(1)} %stack.31.place_ref) | copy-start | bytes 76
  11.8 1.0 copy-start.2
  12.8 6.9 %copy-start.3 = (bf16[1,512,256]{2,1,0:T(8,128)(2,1)S(1)}, bf16[1,512,256]{2,1,0:T(8,128)(2,1)}, u32[]{:S(2)}) copy-start(bf16[1,512,256]{2,1,0:T(8,128)(2,1)} %param.12) | copy-start | bytes 786436
  18.6 8.1 %collective-permute-start.5 = (bf16[456,128]{1,0:T(8,128)(2,1)S(1)}, bf16[456,128]{1,0:T(8,128)(2,1)S(1)}, u32[]{:S(2)}, u32[]{:S(2)}) collective-permute-start(bf16[456,128]{1,0:T(8,128)(2,1)S(1)} %dynamic-slice_convert_fusion.1.refs_0_), channel_id=1, source_target_pairs={{0,4},{4,0},{8,12},{12,8},{16,20},{20,16},{24,28},{28,24},{1,5},{5... | collective-permute-start | bytes 350216 | tf_op jit(solution)/shard_map/ppermute | solution.py:556
  18.6 8.1 %collective-permute-start.6 = (bf16[456,128]{1,0:T(8,128)(2,1)S(1)}, bf16[456,128]{1,0:T(8,128)(2,1)S(1)}, u32[]{:S(2)}, u32[]{:S(2)}) collective-permute-start(bf16[456,128]{1,0:T(8,128)(2,1)S(1)} %collective-permute-done.2.refs_1_), channel_id=1, source_target_pairs={{0,4},{4,0},{8,12},{12,8},{16,20},{20,16},{24,28},{28,24},{1,5},{5... | collective-permute-start | bytes 350216 | tf_op jit(solution)/shard_map/ppermute | solution.py:556
  19.1 7.6 %collective-permute-start.7 = (bf16[456,128]{1,0:T(8,128)(2,1)S(1)}, bf16[456,128]{1,0:T(8,128)(2,1)S(1)}, u32[]{:S(2)}, u32[]{:S(2)}) collective-permute-start(bf16[456,128]{1,0:T(8,128)(2,1)S(1)} %collective-permute-done.3.refs_2_), channel_id=1, source_target_pairs={{0,4},{4,0},{8,12},{12,8},{16,20},{20,16},{24,28},{28,24},{1,5},{5... | collective-permute-start | bytes 350216 | tf_op jit(solution)/shard_map/ppermute | solution.py:556
  19.1 7.6 %collective-permute-start.8 = (bf16[456,128]{1,0:T(8,128)(2,1)S(1)}, bf16[456,128]{1,0:T(8,128)(2,1)S(1)}, u32[]{:S(2)}, u32[]{:S(2)}) collective-permute-start(bf16[456,128]{1,0:T(8,128)(2,1)S(1)} %collective-permute-done.4.refs_3_), channel_id=1, source_target_pairs={{0,4},{4,0},{8,12},{12,8},{16,20},{20,16},{24,28},{28,24},{1,5},{5... | collective-permute-start | bytes 350216 | tf_op jit(solution)/shard_map/ppermute | solution.py:556
  24.7 2.1 %copy-start = (bf16[1,4096,256]{2,1,0:T(8,128)(2,1)S(1)}, bf16[1,4096,256]{2,1,0:T(8,128)(2,1)}, u32[]{:S(2)}) copy-start(bf16[1,4096,256]{2,1,0:T(8,128)(2,1)} %param.13) | copy-start | bytes 6291460
  24.7 2.1 %copy-start.11 = (s32[4096]{0:T(1024)S(1)}, s32[4096]{0:T(1024)}, u32[]{:S(2)}) copy-start(s32[4096]{0:T(1024)} %param.16) | copy-start | bytes 49156
  36.1 15.2 %collective-permute-start.10 = (f32[512,256]{1,0:T(8,128)S(1)}, f32[512,256]{1,0:T(8,128)S(1)}, u32[]{:S(2)}, u32[]{:S(2)}) collective-permute-start(f32[512,256]{1,0:T(8,128)S(1)} %get-tuple-element.48), channel_id=1, source_target_pairs={{0,28},{4,8},{8,4},{12,16},{16,12},{20,24},{24,20},{28,0},{1,29},{... | collective-permute-start | bytes 1572872 | tf_op jit(solution)/shard_map/ppermute | solution.py:561
  37.0 14.4 %copy-start.17 = (s32[512]{0:T(512)S(1)}, s32[512]{0:T(512)}, u32[]{:S(2)}) copy-start(s32[512]{0:T(512)} %param.17) | copy-start | bytes 6148
  41.5 9.9 %copy-start.1 = (f32[1,512,256]{2,1,0:T(8,128)S(1)}, f32[1,512,256]{2,1,0:T(8,128)}, u32[]{:S(2)}) copy-start(f32[1,512,256]{2,1,0:T(8,128)} %param.23) | copy-start | bytes 1572868
  41.5 9.8 %collective-permute-start.9 = (f32[512,256]{1,0:T(8,128)S(1)}, f32[512,256]{1,0:T(8,128)S(1)}, u32[]{:S(2)}, u32[]{:S(2)}) collective-permute-start(f32[512,256]{1,0:T(8,128)S(1)} %get-tuple-element.47), channel_id=1, source_target_pairs={{0,4},{4,0},{8,12},{12,8},{16,20},{20,16},{24,28},{28,24},{1,5},{5... | collective-permute-start | bytes 1572872 | tf_op jit(solution)/shard_map/ppermute | solution.py:556
  53.1 1.5 %collective-permute-start.12 = (bf16[512,256]{1,0:T(8,128)(2,1)S(1)}, bf16[512,256]{1,0:T(8,128)(2,1)S(1)}, u32[]{:S(2)}, u32[]{:S(2)}) collective-permute-start(bf16[512,256]{1,0:T(8,128)(2,1)S(1)} %get-tuple-element.55.own_ref), channel_id=1, source_target_pairs={{0,4},{4,0},{8,12},{12,8},{16,20},{20,16},{24,28},{28,24},{1,5},{5... | collective-permute-start | bytes 786440 | tf_op jit(solution)/shard_map/ppermute | solution.py:556
  53.1 9.5 %collective-permute-start.11 = (bf16[512,256]{1,0:T(8,128)(2,1)S(1)}, bf16[512,256]{1,0:T(8,128)(2,1)S(1)}, u32[]{:S(2)}, u32[]{:S(2)}) collective-permute-start(bf16[512,256]{1,0:T(8,128)(2,1)S(1)} %get-tuple-element.55.own_ref), channel_id=1, source_target_pairs={{0,28},{4,8},{8,4},{12,16},{16,12},{20,24},{24,20},{28,0},{1,29},{... | collective-permute-start | bytes 786440 | tf_op jit(solution)/shard_map/ppermute | solution.py:561
  54.3 8.4 %copy-start.15 = (s32[6]{0:T(128)S(1)}, s32[6]{0:T(128)}, u32[]{:S(2)}) copy-start(s32[6]{0:T(128)} %copy-done.14) | copy-start | bytes 76
  62.6 0.7 copy-start.10
  74.3 1.0 copy-start.4
  75.3 2.8 %collective-permute-start.15 = (f32[1824,128]{1,0:T(8,128)}, f32[1824,128]{1,0:T(8,128)}, u32[]{:S(2)}, u32[]{:S(2)}) collective-permute-start(f32[1824,128]{1,0:T(8,128)} %get-tuple-element.64), channel_id=1, source_target_pairs={{0,4},{4,0},{8,12},{12,8},{16,20},{20,16},{24,28},{28,24},{1,5},{5... | collective-permute-start | bytes 2801672 | tf_op jit(solution)/shard_map/ppermute | solution.py:556
  79.7 0.9 copy-start.18
  81.4 8.1 %collective-permute-start.16 = (bf16[2,464,128]{2,1,0:T(8,128)(2,1)}, bf16[2,464,128]{2,1,0:T(8,128)(2,1)}, u32[]{:S(2)}, u32[]{:S(2)}) collective-permute-start(bf16[2,464,128]{2,1,0:T(8,128)(2,1)} %pad_maximum_fusion), channel_id=1, source_target_pairs={{0,1},{1,0},{2,3},{3,2},{4,5},{5,4},{6,7},{7,6},{8,9},{9,8},{10,11... | collective-permute-start | bytes 712712 | tf_op jit(solution)/shard_map/ppermute | solution.py:556
  83.5 11.4 %copy-start.13 = (s32[4096]{0:T(1024)S(1)}, s32[4096]{0:T(1024)}, u32[]{:S(2)}) copy-start(s32[4096]{0:T(1024)} %copy-done.12) | copy-start | bytes 49156
  92.4 8.0 %collective-permute-start.17 = (bf16[1,464,128]{2,1,0:T(8,128)(2,1)S(1)}, bf16[1,464,128]{2,1,0:T(8,128)(2,1)S(1)}, u32[]{:S(2)}, u32[]{:S(2)}) collective-permute-start(bf16[1,464,128]{2,1,0:T(8,128)(2,1)S(1)} %pad_maximum_fusion.1), channel_id=1, source_target_pairs={{0,2},{1,3},{2,0},{3,1},{4,6},{5,7},{6,4},{7,5},{8,10},{9,11},{10,... | collective-permute-start | bytes 356360 | tf_op jit(solution)/shard_map/ppermute | solution.py:556
  100.4 5.4 %collective-permute-start.18 = (bf16[464,128]{1,0:T(8,128)(2,1)S(1)}, bf16[464,128]{1,0:T(8,128)(2,1)S(1)}, u32[]{:S(2)}, u32[]{:S(2)}) collective-permute-start(bf16[464,128]{1,0:T(8,128)(2,1)S(1)} %get-tuple-element.80), channel_id=1, source_target_pairs={{0,8},{4,12},{8,0},{12,4},{16,24},{20,28},{24,16},{28,20},{1,9},{5... | collective-permute-start | bytes 356360 | tf_op jit(solution)/shard_map/ppermute | solution.py:556
  105.8 5.0 %copy-start.16 = (s32[6]{0:T(128)S(1)}, s32[6]{0:T(128)}, u32[]{:S(2)}) copy-start(s32[6]{0:T(128)} %copy-done.14) | copy-start | bytes 76
  106.0 4.9 %collective-permute-start.19 = (bf16[464,128]{1,0:T(8,128)(2,1)S(1)}, bf16[464,128]{1,0:T(8,128)(2,1)S(1)}, u32[]{:S(2)}, u32[]{:S(2)}) collective-permute-start(bf16[464,128]{1,0:T(8,128)(2,1)S(1)} %pad_maximum_fusion.3.mine_ref), channel_id=1, source_target_pairs={{0,16},{4,20},{8,24},{12,28},{16,0},{20,4},{24,8},{28,12},{1,17},{... | collective-permute-start | bytes 356360 | tf_op jit(solution)/shard_map/ppermute | solution.py:556
  111.6 3.0 %collective-permute-start.20 = (f32[472,128]{1,0:T(8,128)S(1)}, f32[472,128]{1,0:T(8,128)S(1)}, u32[]{:S(2)}, u32[]{:S(2)}) collective-permute-start(f32[472,128]{1,0:T(8,128)S(1)} %finish.1.mine_ref), channel_id=1, source_target_pairs={{0,4},{4,0},{8,12},{12,8},{16,20},{20,16},{24,28},{28,24},{1,5},{5... | collective-permute-start | bytes 725000 | tf_op jit(solution)/shard_map/ppermute | solution.py:556
  111.6 9.5 %collective-permute-start.14 = (bf16[512,256]{1,0:T(8,128)(2,1)S(1)}, bf16[512,256]{1,0:T(8,128)(2,1)S(1)}, u32[]{:S(2)}, u32[]{:S(2)}) collective-permute-start(bf16[512,256]{1,0:T(8,128)(2,1)S(1)} %get-tuple-element.78), channel_id=1, source_target_pairs={{0,28},{4,8},{8,4},{12,16},{16,12},{20,24},{24,20},{28,0},{1,29},{... | collective-permute-start | bytes 786440 | tf_op jit(solution)/shard_map/ppermute | solution.py:561
  114.6 6.6 %collective-permute-start.13 = (bf16[512,256]{1,0:T(8,128)(2,1)S(1)}, bf16[512,256]{1,0:T(8,128)(2,1)S(1)}, u32[]{:S(2)}, u32[]{:S(2)}) collective-permute-start(bf16[512,256]{1,0:T(8,128)(2,1)S(1)} %get-tuple-element.77), channel_id=1, source_target_pairs={{0,4},{4,0},{8,12},{12,8},{16,20},{20,16},{24,28},{28,24},{1,5},{5... | collective-permute-start | bytes 786440 | tf_op jit(solution)/shard_map/ppermute | solution.py:556
  114.6 3.8 %collective-permute-start.21 = (f32[32,128]{1,0:T(8,128)S(1)}, f32[32,128]{1,0:T(8,128)S(1)}, u32[]{:S(2)}, u32[]{:S(2)}) collective-permute-start(f32[32,128]{1,0:T(8,128)S(1)} %pad_maximum_fusion.4), channel_id=1, source_target_pairs={{0,1},{1,0},{2,3},{3,2},{4,5},{5,4},{6,7},{7,6},{8,9},{9,8},{10,11... | collective-permute-start | bytes 49160 | tf_op jit(solution)/shard_map/ppermute | solution.py:556
  117.3 5.8 %copy-start.5 = (f32[456,256]{1,0:T(8,128)S(1)}, f32[456,256]{1,0:T(8,128)}, u32[]{:S(2)}) copy-start(f32[456,256]{1,0:T(8,128)} %params_ref.1) | copy-start | bytes 1400836
  117.3 5.8 %copy-start.6 = (f32[456,256]{1,0:T(8,128)S(1)}, f32[456,256]{1,0:T(8,128)}, u32[]{:S(2)}) copy-start(f32[456,256]{1,0:T(8,128)} %first_ref.1) | copy-start | bytes 1400836
  117.3 5.8 %copy-start.7 = (f32[456,256]{1,0:T(8,128)S(1)}, f32[456,256]{1,0:T(8,128)}, u32[]{:S(2)}) copy-start(f32[456,256]{1,0:T(8,128)} %second_ref.1) | copy-start | bytes 1400836
  117.3 5.8 %copy-start.8 = (f32[456,256]{1,0:T(8,128)S(1)}, f32[456,256]{1,0:T(8,128)}, u32[]{:S(2)}) copy-start(f32[456,256]{1,0:T(8,128)} %averaged_ref.1) | copy-start | bytes 1400836
  118.4 4.6 %collective-permute-start.22 = (f32[32,128]{1,0:T(8,128)S(1)}, f32[32,128]{1,0:T(8,128)S(1)}, u32[]{:S(2)}, u32[]{:S(2)}) collective-permute-start(f32[32,128]{1,0:T(8,128)S(1)} %fusion.17.stats_ref), channel_id=1, source_target_pairs={{0,2},{1,3},{2,0},{3,1},{4,6},{5,7},{6,4},{7,5},{8,10},{9,11},{10,... | collective-permute-start | bytes 49160 | tf_op jit(solution)/shard_map/ppermute | solution.py:556

commit v3 on v2

v3 whole, which is shorter than its diff:
```python
import functools

import jax
import jax.numpy as jnp
from jax import lax
from jax.experimental import pallas as pl
from jax.experimental.pallas import tpu as pltpu
from jax.sharding import PartitionSpec as P

NORM_EPS = 1e-05
MAX_NORM = 512.0
RATE = 0.05
BETA_ONE = 0.9
BETA_TWO = 0.95
ADAM_EPS = 1e-08
WEIGHT_DECAY = 0.1
AVERAGE_DECAY = 0.999

LANES = 128
TINY = 1e-20
STEPS = 22
LOG_TWO = 0.6931471805599453
TILE = 2048
B16 = jnp.bfloat16
F32 = jnp.float32
I32 = jnp.int32
I16 = jnp.int16
PARAMS = pltpu.CompilerParams(vmem_limit_bytes=20 * 1024 * 1024)


def dot(left, right):
    return jnp.dot(left, right, preferred_element_type=F32)


def dot_rows(left, right):
    return lax.dot_general(left, right, (((0,), (0,)), ((), ())), preferred_element_type=F32)


def dot_back(left, right):
    return lax.dot_general(left, right, (((1,), (1,)), ((), ())), preferred_element_type=F32)


def vectors_of(w_ref, width):
    return w_ref[7 * width : 7 * width + 8, :].astype(F32)


def split(values):
    high = values.astype(B16)
    return high, (values - high.astype(F32)).astype(B16)


def whole(shape):
    return pl.BlockSpec(shape, lambda i: (0,) * len(shape))


def tiled(rows, cols):
    return pl.BlockSpec((rows, cols), lambda i: (i, 0))


def column(row):
    return jnp.broadcast_to(row, (LANES, LANES)).T


def chosen_columns(index_ref, tile, rows, first, last):
    lane = lax.broadcasted_iota(I32, (LANES, LANES), 1)
    groups = []
    for g in range(rows // LANES):
        col = column(index_ref[pl.ds(tile * (rows // LANES) + g, 1), :])
        groups.append(
            jnp.concatenate(
                [jnp.where(col == lane + base, 1.0, 0.0).astype(B16) for base in range(first, last, LANES)],
                axis=1,
            )
        )
    return jnp.concatenate(groups, axis=0)


def chosen_rows(index_row, first, count):
    node = lax.broadcasted_iota(I32, (count, index_row.shape[1]), 0) + first
    return jnp.where(index_row == node, 1.0, 0.0).astype(B16)


def prologue_kernel(
    params_hbm, send_hbm, recv_hbm, latents_hbm, half_ref, place_ref, send_ref, recv_ref, latents_ref,
    wide_ref, in_ref, sem, *, nodes, shares, owner,
):
    e, f = lax.axis_index("edge"), lax.axis_index("feat")
    core = e % 2
    lanes = pl.ds(pl.multiple_of(core * LANES, LANES), LANES)
    copies = [
        pltpu.make_async_copy(params_hbm.at[:, lanes], wide_ref, sem.at[0]),
        pltpu.make_async_copy(send_hbm, in_ref.at[0], sem.at[1]),
        pltpu.make_async_copy(recv_hbm, in_ref.at[1], sem.at[2]),
        pltpu.make_async_copy(latents_hbm, latents_ref, sem.at[3]),
    ]
    for copy in copies:
        copy.start()
    place_ref[0] = core
    place_ref[1] = e
    place_ref[2] = f
    place_ref[3] = jnp.where(f == owner, 1, 0)
    for k in range(shares):
        place_ref[4 + k] = jnp.bitwise_xor(f, k)
    for i, out_ref in ((0, send_ref), (1, recv_ref)):
        copies[1 + i].wait()
        index = in_ref[i]
        block = lax.div(index, nodes)
        slot = jnp.where(block == e, 0, jnp.where(block == e + 1 - 2 * core, 1, 2))
        out_ref[...] = (slot - block) * nodes + index
    copies[0].wait()
    half_ref[...] = wide_ref[...].astype(B16)
    copies[3].wait()


def prologue(params, senders, receivers, latents, shares, owner):
    shape = (senders.size // LANES, LANES)
    out = jax.ShapeDtypeStruct(shape, I32)
    vmem, hbm = pl.BlockSpec(memory_space=pltpu.VMEM), pl.BlockSpec(memory_space=pltpu.HBM)
    half, place, send, recv, own = pl.pallas_call(
        functools.partial(prologue_kernel, nodes=latents.shape[0], shares=shares, owner=owner),
        in_specs=[hbm] * 4,
        out_specs=[vmem, pl.BlockSpec(memory_space=pltpu.SMEM), vmem, vmem, vmem],
        out_shape=[
            jax.ShapeDtypeStruct((params.shape[0], LANES), B16), jax.ShapeDtypeStruct((4 + shares,), I32), out, out,
            jax.ShapeDtypeStruct(latents.shape, latents.dtype),
        ],
        scratch_shapes=[
            pltpu.VMEM((params.shape[0], LANES), F32), pltpu.VMEM((2, *shape), I32), pltpu.SemaphoreType.DMA((4,)),
        ],
        compiler_params=PARAMS,
        name="prologue",
    )(params, senders.reshape(shape), receivers.reshape(shape), latents)
    return half, place, send.reshape(-1), recv.reshape(-1), own


def gather_near_kernel(index_ref, own_ref, pair_ref, out_ref):
    tile = pl.program_id(0)
    rows = out_ref.shape[0]
    nodes = own_ref.shape[0]
    total = dot(chosen_columns(index_ref, tile, rows, 0, nodes), own_ref[...])
    total = total + dot(chosen_columns(index_ref, tile, rows, nodes, 2 * nodes), pair_ref[...])
    out_ref[...] = total.astype(B16)


def gather_near(index, own, pair):
    nodes, width = own.shape
    edges = index.size
    return pl.pallas_call(
        gather_near_kernel,
        grid=(1,),
        in_specs=[whole((edges // LANES, LANES))] + [whole((nodes, width))] * 2,
        out_specs=tiled(edges, width),
        out_shape=jax.ShapeDtypeStruct((edges, width), B16),
        compiler_params=PARAMS,
        name="gather_near",
        cost_estimate=pl.CostEstimate(
            flops=2 * edges * 2 * nodes * width, transcendentals=0, bytes_accessed=edges * width * 2
        ),
    )(index.reshape(-1, LANES), own, pair)


def gather_off_kernel(index_ref, off_ref, near_ref, out_ref):
    tile = pl.program_id(0)
    rows = out_ref.shape[0]
    nodes = off_ref.shape[0]
    total = dot(chosen_columns(index_ref, tile, rows, 2 * nodes, 3 * nodes), off_ref[...])
    out_ref[...] = (total + near_ref[...].astype(F32)).astype(B16)


def gather_off(index, off, near):
    nodes, width = off.shape
    edges = index.size
    return pl.pallas_call(
        gather_off_kernel,
        grid=(1,),
        in_specs=[whole((edges // LANES, LANES)), whole((nodes, width)), tiled(edges, width)],
        out_specs=tiled(edges, width),
        out_shape=jax.ShapeDtypeStruct((edges, width), B16),
        compiler_params=PARAMS,
        name="gather_off",
        cost_estimate=pl.CostEstimate(
            flops=2 * edges * nodes * width, transcendentals=0, bytes_accessed=edges * width * 4
        ),
    )(index.reshape(-1, LANES), off, near)


def before_silu(region_ref, tile, hs_ref, hr_ref, x_ref, w_ref):
    rows, width = x_ref.shape
    vector_row = 7 * width
    regions = w_ref.shape[0] - vector_row - 8
    table = jnp.concatenate(
        [w_ref[vector_row + 8 :, :].astype(F32), jnp.zeros((LANES - regions, width), F32)], axis=0
    ).astype(B16)
    pre = dot(hs_ref[...], w_ref[0:width, :])
    pre = pre + dot(hr_ref[...], w_ref[width : 2 * width, :])
    pre = pre + dot(x_ref[...], w_ref[2 * width : 3 * width, :])
    pre = pre + dot(chosen_columns(region_ref, tile, rows, 0, LANES), table)
    return pre + vectors_of(w_ref, width)[0:1, :]


def normalized(hidden, w_ref, vec):
    width = hidden.shape[1]
    inner = dot(hidden, w_ref[3 * width : 4 * width, :]) + vec[1:2, :]
    center = inner - jnp.mean(inner, axis=-1, keepdims=True)
    inverse = lax.rsqrt(jnp.mean(center * center, axis=-1, keepdims=True) + NORM_EPS)
    return center * inverse, inverse


def power_of_two(exponents):
    return jnp.exp(exponents * LOG_TWO)


def encoded(values):
    rows, width = values.shape
    half = width // 2
    largest = jnp.maximum(jnp.max(jnp.abs(values), axis=-1, keepdims=True), TINY)
    exponents = jnp.ceil(jnp.log(largest) * (1.0 / LOG_TWO))
    codes = jnp.round(values * power_of_two(STEPS - exponents)).astype(I32)
    upper = lax.shift_right_arithmetic(codes, 8)
    lower = jnp.bitwise_and(codes, 255)
    words = lax.shift_left(lower[:, :half], 8) + lower[:, half:] - 32768
    marks = [
        jnp.broadcast_to(exponents[g * LANES : (g + 1) * LANES, :], (LANES, LANES)).T[0:1, :]
        for g in range(rows // LANES)
    ]
    marks = jnp.concatenate([*marks, jnp.zeros((16 - len(marks), LANES), F32)], axis=0).astype(I32)
    marks = jnp.concatenate([marks, jnp.zeros((16, width + half - LANES), I32)], axis=1)
    return jnp.concatenate([jnp.concatenate([upper, words], axis=1), marks], axis=0).astype(I16)


def decoded(wire):
    rows, width = wire.shape[0] - 16, wire.shape[1] * 2 // 3
    half = width // 2
    wire = wire.astype(I32)
    words = wire[:rows, width:] + 32768
    lower = jnp.concatenate([lax.shift_right_arithmetic(words, 8), jnp.bitwise_and(words, 255)], axis=1)
    codes = (wire[:rows, :width] * 256 + lower).astype(F32)
    exponents = wire[rows:, :LANES].astype(F32)
    scale = [power_of_two(column(exponents[g : g + 1, :]) - STEPS) for g in range(rows // LANES)]
    return codes * jnp.concatenate([jnp.concatenate(scale, axis=0)] * (width // LANES), axis=1)


def edge_forward_kernel(
    place_ref, region_ref, recv_row_ref, hs_ref, hr_ref, x_ref, *refs,
):
    pieces, refs = refs[:-5], refs[-5:]
    w_ref, high_ref, low_ref, halo_ref, wide_ref = refs
    step = pl.program_id(0)
    rows = x_ref.shape[0]
    width = x_ref.shape[1]
    nodes = halo_ref.shape[0] - 16
    steps = pl.num_programs(0)

    @pl.when(step == 0)
    def _():
        odd = place_ref[0] == 1
        shares = len(pieces) // 2
        share = pieces[0].shape[0]
        for k in range(shares):
            mine, other = pieces[k][...].astype(F32), pieces[shares + k][...].astype(F32)
            base = pl.multiple_of(place_ref[4 + k] * share, 8)
            wide_ref[pl.ds(base, share), 0:LANES] = jnp.where(odd, other, mine)
            wide_ref[pl.ds(base, share), LANES : 2 * LANES] = jnp.where(odd, mine, other)
        w_ref[...] = wide_ref[...].astype(B16)

    vec = vectors_of(w_ref, width)
    pre = before_silu(region_ref, step, hs_ref, hr_ref, x_ref, w_ref)
    hidden = (pre / (1.0 + jnp.exp(-pre))).astype(B16)
    unit, _ = normalized(hidden, w_ref, vec)
    high, low = split(unit * vec[2:3, :] + vec[3:4, :])
    base = pl.multiple_of(step * rows, rows)
    high_ref[pl.ds(base, rows), :] = high
    low_ref[pl.ds(base, rows), :] = low

    @pl.when(step == steps - 1)
    def _():
        onehot = chosen_rows(recv_row_ref[...], 2 * nodes, nodes)
        halo_ref[...] = encoded(dot(onehot, high_ref[...]) + dot(onehot, low_ref[...]))


def edge_forward(place, regions, recv, hs, hr, edges, pieces, total, nodes):
    count, width = edges.shape
    tile = tiled(TILE, width)
    return pl.pallas_call(
        edge_forward_kernel,
        grid=(count // TILE,),
        in_specs=[
            pl.BlockSpec(memory_space=pltpu.SMEM), whole((count // LANES, LANES)), whole((1, count)), tile, tile, tile,
            *[whole(piece.shape) for piece in pieces],
        ],
        out_specs=[
            whole((total, width)), whole((count, width)), whole((count, width)),
            whole((nodes + 16, width + width // 2)),
        ],
        out_shape=[
            jax.ShapeDtypeStruct((total, width), B16),
            jax.ShapeDtypeStruct((count, width), B16),
            jax.ShapeDtypeStruct((count, width), B16),
            jax.ShapeDtypeStruct((nodes + 16, width + width // 2), I16),
        ],
        scratch_shapes=[pltpu.VMEM((total, width), F32)],
        compiler_params=PARAMS,
        name="edge_forward",
        cost_estimate=pl.CostEstimate(
            flops=2 * count * width * (5 * width + 2 * nodes), transcendentals=2 * count * width,
            bytes_accessed=count * width * 10,
        ),
    )(place, regions.reshape(-1, LANES), recv.reshape(1, -1), hs, hr, edges, *pieces)


def edge_slope_kernel(region_ref, hs_ref, hr_ref, x_ref, w_ref, hidden_ref, slope_ref):
    pre = before_silu(region_ref, pl.program_id(0), hs_ref, hr_ref, x_ref, w_ref)
    sigma = 1.0 / (1.0 + jnp.exp(-pre))
    hidden_ref[...] = (pre / (1.0 + jnp.exp(-pre))).astype(B16)
    slope_ref[...] = sigma * (1.0 + pre * (1.0 - sigma))


def edge_slope(regions, hs, hr, edges, weights):
    count, width = edges.shape
    tile = tiled(TILE, width)
    return pl.pallas_call(
        edge_slope_kernel,
        grid=(count // TILE,),
        in_specs=[whole((count // LANES, LANES)), tile, tile, tile, whole(weights.shape)],
        out_specs=[tile, tile],
        out_shape=[jax.ShapeDtypeStruct((count, width), B16), jax.ShapeDtypeStruct((count, width), F32)],
        compiler_params=PARAMS,
        name="edge_slope",
        cost_estimate=pl.CostEstimate(
            flops=2 * count * width * 4 * width, transcendentals=2 * count * width, bytes_accessed=count * width * 12
        ),
    )(regions.reshape(-1, LANES), hs, hr, edges, weights)


def edge_unit_kernel(hidden_ref, w_ref, unit_ref, inverse_ref):
    unit, inverse = normalized(hidden_ref[...], w_ref, vectors_of(w_ref, hidden_ref.shape[1]))
    unit_ref[...] = unit
    inverse_ref[...] = jnp.broadcast_to(inverse, inverse_ref.shape)


def edge_unit(hidden, weights):
    count, width = hidden.shape
    tile = tiled(TILE, width)
    return pl.pallas_call(
        edge_unit_kernel,
        grid=(count // TILE,),
        in_specs=[tile, whole(weights.shape)],
        out_specs=[tile, tiled(TILE, LANES)],
        out_shape=[jax.ShapeDtypeStruct((count, width), F32), jax.ShapeDtypeStruct((count, LANES), F32)],
        compiler_params=PARAMS,
        name="edge_unit",
        cost_estimate=pl.CostEstimate(
            flops=2 * count * width * width, transcendentals=count, bytes_accessed=count * width * 8
        ),
    )(hidden, weights)


def near_sum_kernel(recv_row_ref, high_ref, low_ref, pair_ref, more_ref, own_ref):
    nodes = own_ref.shape[0]
    half = nodes // 2
    for first, out_ref in ((nodes, pair_ref), (nodes + half, more_ref), (0, own_ref)):
        onehot = chosen_rows(recv_row_ref[...], first, out_ref.shape[0])
        out_ref[...] = dot(onehot, high_ref[...]) + dot(onehot, low_ref[...])


def near_sum(recv, high, low, nodes):
    count, width = high.shape
    half = jax.ShapeDtypeStruct((nodes // 2, width), F32)
    return pl.pallas_call(
        near_sum_kernel,
        out_shape=[half, half, jax.ShapeDtypeStruct((nodes, width), F32)],
        compiler_params=PARAMS,
        name="near_sum",
        cost_estimate=pl.CostEstimate(
            flops=8 * count * width * nodes, transcendentals=0, bytes_accessed=count * width * 4
        ),
    )(recv.reshape(1, -1), high, low)


def kept_nodes(forced_ref, width):
    keep = [column(forced_ref[g : g + 1, :]) for g in range(forced_ref.shape[0])]
    keep = 1.0 - jnp.concatenate(keep, axis=0).astype(F32)
    return jnp.concatenate([keep] * (width // LANES), axis=1)


def node_kernel(
    h_ref, own_ref, pair_ref, more_ref, off_ref, w_ref, forced_ref, up_ref,
    d_agg_ref, agg_ref, hidden_ref, d_inner_ref, d_pre_ref, unit_ref,
):
    width = h_ref.shape[1]
    pair = jnp.concatenate([pair_ref[...], more_ref[...]], axis=0)
    agg_ref[...] = (own_ref[...] + pair + decoded(off_ref[...])).astype(B16)
    vec = vectors_of(w_ref, width)
    latent, aggregate = w_ref[4 * width : 5 * width, :], w_ref[5 * width : 6 * width, :]
    second = w_ref[6 * width : 7 * width, :]
    pre = dot(h_ref[...], latent) + dot(agg_ref[...], aggregate) + vec[4:5, :]
    sigma = 1.0 / (1.0 + jnp.exp(-pre))
    hidden = (pre / (1.0 + jnp.exp(-pre))).astype(B16)
    hidden_ref[...] = hidden
    inner = dot(hidden, second) + vec[5:6, :]
    center = inner - jnp.mean(inner, axis=-1, keepdims=True)
    inverse = lax.rsqrt(jnp.mean(center * center, axis=-1, keepdims=True) + NORM_EPS)
    unit = center * inverse
    unit_ref[...] = unit
    scaled = kept_nodes(forced_ref, width) * up_ref[...] * vec[6:7, :]
    d_inner = inverse * (
        scaled
        - jnp.mean(scaled, axis=-1, keepdims=True)
        - unit * jnp.mean(scaled * unit, axis=-1, keepdims=True)
    )
    d_inner = d_inner.astype(B16)
    d_inner_ref[...] = d_inner
    slope = sigma * (1.0 + pre * (1.0 - sigma))
    d_pre = (dot_back(d_inner, second) * slope).astype(B16)
    d_pre_ref[...] = d_pre
    d_agg_ref[...] = dot_back(d_pre, aggregate).astype(B16)


def node_update(h, own, pair, more, off, weights, forced, upstream):
    nodes, width = h.shape
    half = jax.ShapeDtypeStruct((nodes, width), B16)
    return pl.pallas_call(
        node_kernel,
        out_shape=[half, half, half, half, half, jax.ShapeDtypeStruct((nodes, width), F32)],
        compiler_params=PARAMS,
        name="node_update",
        cost_estimate=pl.CostEstimate(
            flops=2 * nodes * width * width * 5, transcendentals=2 * nodes * width, bytes_accessed=nodes * width * 20
        ),
    )(h, own, pair, more, off, weights, forced.reshape(-1, LANES), upstream)


def node_grads_kernel(
    h_ref, agg_ref, hidden_ref, d_inner_ref, d_pre_ref, unit_ref, w_ref, forced_ref, up_ref,
    new_ref, grad_ref, sums_ref, back_ref,
):
    width = h_ref.shape[1]
    vec = vectors_of(w_ref, width)
    keep = kept_nodes(forced_ref, width)
    unit, upstream = unit_ref[...], up_ref[...]
    new_ref[...] = h_ref[...].astype(F32) + keep * (unit * vec[6:7, :] + vec[7:8, :])
    d_pre, d_inner, d_update = d_pre_ref[...], d_inner_ref[...], keep * upstream
    grad_ref[0:width, :] = dot_rows(h_ref[...], d_pre)
    grad_ref[width : 2 * width, :] = dot_rows(agg_ref[...], d_pre)
    grad_ref[2 * width : 3 * width, :] = dot_rows(hidden_ref[...], d_inner)
    back_ref[...] = upstream + dot_back(d_pre, w_ref[4 * width : 5 * width, :])
    sums_ref[...] = jnp.concatenate(
        [
            jnp.sum(d_pre.astype(F32), axis=0, keepdims=True),
            jnp.sum(d_inner.astype(F32), axis=0, keepdims=True),
            jnp.sum(d_update * unit, axis=0, keepdims=True),
            jnp.sum(d_update, axis=0, keepdims=True),
        ],
        axis=0,
    )


def node_grads(h, agg, hidden, d_inner, d_pre, unit, weights, forced, upstream):
    nodes, width = h.shape
    full = jax.ShapeDtypeStruct((nodes, width), F32)
    return pl.pallas_call(
        node_grads_kernel,
        out_shape=[full, jax.ShapeDtypeStruct((3 * width, width), F32), jax.ShapeDtypeStruct((4, width), F32), full],
        compiler_params=PARAMS,
        name="node_grads",
        cost_estimate=pl.CostEstimate(
            flops=2 * nodes * width * width * 4, transcendentals=0, bytes_accessed=nodes * width * 18
        ),
    )(h, agg, hidden, d_inner, d_pre, unit, weights, forced.reshape(-1, LANES), upstream)


def edge_backward_kernel(
    place_ref, recv_ref, region_row_ref, off_ref, near_ref, hs_ref, hr_ref, x_ref, hidden_ref, slope_ref, unit_ref,
    inverse_ref, w_ref, node_grad_ref, node_sum_ref,
    d_pre_ref, kept_ref, sent_ref,
    d_inner_ref, vec_acc_ref,
):
    step = pl.program_id(0)
    steps = pl.num_programs(0)
    rows = slope_ref.shape[0]
    width = x_ref.shape[1]
    nodes = off_ref.shape[0]
    regions = w_ref.shape[0] - 7 * width - 8
    vec = vectors_of(w_ref, width)

    @pl.when(step == 0)
    def _():
        vec_acc_ref[...] = jnp.zeros_like(vec_acc_ref)

    d_message = dot(chosen_columns(recv_ref, step, rows, 2 * nodes, 3 * nodes), off_ref[...])
    d_message = d_message + near_ref[...].astype(F32)
    unit = unit_ref[...]
    scaled = d_message * vec[2:3, :]
    inverse = inverse_ref[:, 0:1]
    d_inner = inverse * (
        scaled
        - jnp.mean(scaled, axis=-1, keepdims=True)
        - unit * jnp.mean(scaled * unit, axis=-1, keepdims=True)
    )
    vec_acc_ref[0:8, :] += jnp.sum((d_message * unit).reshape(rows // 8, 8, width), axis=0)
    vec_acc_ref[8:16, :] += jnp.sum(d_message.reshape(rows // 8, 8, width), axis=0)
    d_inner = d_inner.astype(B16)
    d_pre = (dot_back(d_inner, w_ref[3 * width : 4 * width, :]) * slope_ref[...]).astype(B16)
    base = pl.multiple_of(step * rows, rows)
    d_inner_ref[pl.ds(base, rows), :] = d_inner
    d_pre_ref[pl.ds(base, rows), :] = d_pre

    @pl.when(step == steps - 1)
    def _():
        odd = place_ref[0] == 1

        def put(start, piece):
            left, right = piece[:, 0:LANES], piece[:, LANES:]
            kept_ref[start : start + piece.shape[0], :] = jnp.where(odd, right, left)
            sent_ref[start : start + piece.shape[0], :] = jnp.where(odd, left, right)

        table_rows = node_grad_ref.shape[0] + 4 * width
        d_inner, d_pre = d_inner_ref[...], d_pre_ref[...]
        second_sum = dot(jnp.ones((16, d_inner.shape[0]), B16), d_inner)[0:1, :]
        table_grad = dot(chosen_rows(region_row_ref[...], 0, regions), d_pre)
        put(3 * width, dot_rows(hidden_ref[...], d_inner))
        put(0, dot_rows(hs_ref[...], d_pre))
        put(width, dot_rows(hr_ref[...], d_pre))
        put(2 * width, dot_rows(x_ref[...], d_pre))
        put(4 * width, node_grad_ref[...])
        vector_rows = jnp.concatenate(
            [
                jnp.sum(table_grad, axis=0, keepdims=True),
                second_sum,
                jnp.sum(vec_acc_ref[0:8, :], axis=0, keepdims=True),
                jnp.sum(vec_acc_ref[8:16, :], axis=0, keepdims=True),
                node_sum_ref[...],
            ],
            axis=0,
        )
        put(table_rows, vector_rows)
        put(table_rows + 8, table_grad)


def edge_backward(
    place, recv, regions, off, near, hs, hr, edges, hidden, slope, unit, inverse, weights, node_grad, node_sum,
):
    count, width = edges.shape
    tile, full = tiled(TILE, width), whole((count, width))
    grad_rows = weights.shape[0]
    half = whole((grad_rows, LANES))
    return pl.pallas_call(
        edge_backward_kernel,
        grid=(count // TILE,),
        in_specs=[
            pl.BlockSpec(memory_space=pltpu.SMEM), whole((count // LANES, LANES)), whole((1, count)),
            whole(off.shape), tile, full, full, full, full, tile, tile, tiled(TILE, LANES),
            whole(weights.shape), whole(node_grad.shape), whole(node_sum.shape),
        ],
        out_specs=[full, half, half],
        out_shape=[
            jax.ShapeDtypeStruct((count, width), B16),
            jax.ShapeDtypeStruct((grad_rows, LANES), F32),
            jax.ShapeDtypeStruct((grad_rows, LANES), F32),
        ],
        scratch_shapes=[pltpu.VMEM((count, width), B16), pltpu.VMEM((16, width), F32)],
        compiler_params=PARAMS,
        name="edge_backward",
        cost_estimate=pl.CostEstimate(
            flops=2 * count * width * (6 * width + off.shape[0]), transcendentals=0, bytes_accessed=count * width * 20
        ),
    )(
        place, recv.reshape(-1, LANES), regions.reshape(1, -1), off, near, hs, hr, edges, hidden, slope, unit, inverse,
        weights, node_grad, node_sum,
    )


def node_part_of(index_row_ref, d_pre_ref, weight, slot, nodes):
    high, low = split(dot(chosen_rows(index_row_ref[...], slot * nodes, nodes), d_pre_ref[...]))
    return dot_back(high, weight) + dot_back(low, weight)


def sender_part_kernel(index_row_ref, d_pre_ref, w_ref, out_ref):
    nodes, width = out_ref.shape
    out_ref[...] = node_part_of(index_row_ref, d_pre_ref, w_ref[0:width, :], pl.program_id(0), nodes)


def sender_part(index, d_pre, weights, nodes):
    count, width = d_pre.shape
    return pl.pallas_call(
        sender_part_kernel,
        grid=(3,),
        in_specs=[whole((1, count)), whole((count, width)), whole(weights.shape)],
        out_specs=tiled(nodes, width),
        out_shape=jax.ShapeDtypeStruct((3 * nodes, width), F32),
        compiler_params=PARAMS,
        name="sender_part",
        cost_estimate=pl.CostEstimate(
            flops=6 * count * width * nodes, transcendentals=0, bytes_accessed=count * width * 2
        ),
    )(index.reshape(1, -1), d_pre, weights)


def receiver_part_kernel(index_row_ref, d_pre_ref, w_ref, part_ref, back_ref, own_ref, pair_ref, off_ref):
    nodes, width = back_ref.shape
    slot = pl.program_id(0)
    part = node_part_of(index_row_ref, d_pre_ref, w_ref[width : 2 * width, :], slot, nodes) + part_ref[...]

    @pl.when(slot == 0)
    def _():
        own_ref[...] = part + back_ref[...]

    @pl.when(slot == 1)
    def _():
        pair_ref[...] = part.astype(B16)

    @pl.when(slot == 2)
    def _():
        off_ref[...] = part.astype(B16)


def receiver_part(index, d_pre, weights, part, back):
    count, width = d_pre.shape
    nodes = back.shape[0]
    half = jax.ShapeDtypeStruct(back.shape, B16)
    return pl.pallas_call(
        receiver_part_kernel,
        grid=(3,),
        in_specs=[
            whole((1, count)), whole((count, width)), whole(weights.shape), tiled(nodes, width), whole(back.shape),
        ],
        out_specs=[whole(back.shape)] * 3,
        out_shape=[jax.ShapeDtypeStruct(back.shape, F32), half, half],
        compiler_params=PARAMS,
        name="receiver_part",
        cost_estimate=pl.CostEstimate(
            flops=6 * count * width * nodes, transcendentals=0, bytes_accessed=count * width * 2
        ),
    )(index.reshape(1, -1), d_pre, weights, part, back)


def edge_grads_kernel(d_pre_ref, w_ref, out_ref):
    width = d_pre_ref.shape[1]
    out_ref[...] = dot_back(d_pre_ref[...], w_ref[2 * width : 3 * width, :]).astype(B16)


def edge_grads(d_pre, weights):
    count, width = d_pre.shape
    return pl.pallas_call(
        edge_grads_kernel,
        grid=(count // TILE,),
        in_specs=[tiled(TILE, width), whole(weights.shape)],
        out_specs=tiled(TILE, width),
        out_shape=jax.ShapeDtypeStruct((count, width), B16),
        compiler_params=PARAMS,
        name="edge_grads",
        cost_estimate=pl.CostEstimate(
            flops=2 * count * width * width, transcendentals=0, bytes_accessed=count * width * 4
        ),
    )(d_pre, weights)


def packed(values, first):
    rows = values[first : first + 8, :]
    return jnp.concatenate([values, rows - rows.astype(B16).astype(F32)], axis=0).astype(B16)


def unpacked(wire, first):
    values = wire.astype(F32)
    share = values.shape[0] - 8
    exact = values[first : first + 8, :] + values[share:, :]
    return jnp.concatenate([values[:first, :], exact, values[first + 8 : share, :]], axis=0)


def halve_kernel(place_ref, mine_ref, other_ref, kept_ref, sent_ref, *, share, first, bit, coded):
    here = (place_ref[2] // bit) % 2
    size = share + 8 if coded else share
    for j in range(kept_ref.shape[0] // share):
        for side, out_ref in ((here, kept_ref), (1 - here, sent_ref)):
            index = 2 * j + side
            other = other_ref[pl.ds(pl.multiple_of(index * size, 8), size), :]
            total = mine_ref[pl.ds(pl.multiple_of(index * share, 8), share), :] + (
                unpacked(other, first) if coded else other
            )
            if out_ref is kept_ref:
                out_ref[j * share : (j + 1) * share, :] = total
            else:
                out_ref[j * (share + 8) : (j + 1) * (share + 8), :] = packed(total, first)


def halve(place, mine, other, share, first, bit, coded):
    count = mine.shape[0] // share // 2
    vmem = pl.BlockSpec(memory_space=pltpu.VMEM)
    return pl.pallas_call(
        functools.partial(halve_kernel, share=share, first=first, bit=bit, coded=coded),
        in_specs=[pl.BlockSpec(memory_space=pltpu.SMEM), vmem, vmem],
        out_shape=[
            jax.ShapeDtypeStruct((count * share, LANES), F32),
            jax.ShapeDtypeStruct((count * (share + 8), LANES), B16),
        ],
        compiler_params=PARAMS,
        name="halve",
    )(place, mine, other)


def add_kernel(mine_ref, other_ref, out_ref, *, first):
    mine = mine_ref[...] if mine_ref.dtype == F32 else unpacked(mine_ref[...], first)
    out_ref[...] = packed(mine + unpacked(other_ref[...], first), first)


def add(mine, other, first):
    return pl.pallas_call(
        functools.partial(add_kernel, first=first),
        out_shape=jax.ShapeDtypeStruct(other.shape, B16),
        compiler_params=PARAMS,
        name="add",
    )(mine, other)


def finish_kernel(place_ref, mine_ref, other_ref, out_ref, *, first):
    share = out_ref.shape[0] - 16
    part = unpacked(mine_ref[...], first) + unpacked(other_ref[...], first)
    out_ref[0:share, :] = part
    out_ref[share : share + 8, :] = jnp.where(place_ref[3] == 1, part[first : first + 8, :], 0.0)
    squares = jnp.sum(jnp.sum(part * part, axis=0, keepdims=True), axis=1, keepdims=True)
    out_ref[share + 8 : share + 16, :] = jnp.broadcast_to(squares, (8, LANES))


def finish(place, mine, other, share, first):
    return pl.pallas_call(
        functools.partial(finish_kernel, first=first),
        in_specs=[pl.BlockSpec(memory_space=pltpu.SMEM)] + [pl.BlockSpec(memory_space=pltpu.VMEM)] * 2,
        out_shape=jax.ShapeDtypeStruct((share + 16, LANES), F32),
        compiler_params=PARAMS,
        name="finish",
    )(place, mine, other)


def adam_kernel(
    place_ref, step_ref, stats_ref, more_ref, mine_ref, other_ref, params_ref, first_ref, second_ref, averaged_ref,
    own_ref, pair_ref, off_ref,
    new_first_hbm, new_second_hbm, new_params_hbm, new_average_hbm, norm_ref, vector_ref, latents_hbm,
    new_first_ref, new_second_ref, new_params_ref, new_average_ref, latents_ref, sem,
):
    share = params_ref.shape[0]
    odd = place_ref[0] == 1
    latents_ref[...] = own_ref[...] + pair_ref[...].astype(F32) + off_ref[...].astype(F32)
    copies = [pltpu.make_async_copy(latents_ref, latents_hbm, sem.at[0])]
    copies[0].start()
    stats = stats_ref[...] + more_ref[...]
    norm = jnp.sqrt(stats[8:9, 0:1] + stats[24:25, 0:1])
    norm_ref[...] = norm
    factor = jnp.minimum(1.0, MAX_NORM / (norm + 1e-06))
    count = jnp.full((1, 1), step_ref[0], F32)
    first_scale = 1.0 - jnp.exp(count * jnp.log(jnp.full((1, 1), BETA_ONE, F32)))
    second_scale = 1.0 - jnp.exp(count * jnp.log(jnp.full((1, 1), BETA_TWO, F32)))
    decay = jnp.minimum(AVERAGE_DECAY, (1.0 + count) / (10.0 + count))
    vector_ref[:, 0:LANES] = jnp.where(odd, stats[16:24, :], stats[0:8, :]) * factor
    vector_ref[:, LANES : 2 * LANES] = jnp.where(odd, stats[0:8, :], stats[16:24, :]) * factor
    chunk = share // 3 if share % 24 == 0 else share
    for i in range(share // chunk):
        rows = slice(i * chunk, (i + 1) * chunk)
        mine, other = mine_ref[rows, :], other_ref[rows, :]
        both = jnp.concatenate([jnp.where(odd, other, mine), jnp.where(odd, mine, other)], axis=1)
        clipped = both * factor
        params = params_ref[rows, :]
        new_first = BETA_ONE * first_ref[rows, :] + (1.0 - BETA_ONE) * clipped
        new_second = BETA_TWO * second_ref[rows, :] + (1.0 - BETA_TWO) * clipped * clipped
        first_hat = new_first / first_scale
        second_hat = new_second / second_scale
        new_params = params - RATE * (first_hat / (jnp.sqrt(second_hat) + ADAM_EPS) + WEIGHT_DECAY * params)
        new_first_ref[rows, :] = new_first
        new_second_ref[rows, :] = new_second
        new_params_ref[rows, :] = new_params
        new_average_ref[rows, :] = decay * averaged_ref[rows, :] + (1.0 - decay) * new_params
        for k, (src, dst) in enumerate(
            (
                (new_first_ref, new_first_hbm), (new_second_ref, new_second_hbm), (new_params_ref, new_params_hbm),
                (new_average_ref, new_average_hbm),
            )
        ):
            copies.append(pltpu.make_async_copy(src.at[rows, :], dst.at[rows, :], sem.at[1 + 4 * i + k]))
            copies[-1].start()
    for copy in copies:
        copy.wait()


def adam(place, step, stats, more, mine, other, params, first_moment, second_moment, averaged, own, pair, off):
    rows = jax.ShapeDtypeStruct(params.shape, F32)
    smem, vmem, hbm = (pl.BlockSpec(memory_space=m) for m in (pltpu.SMEM, pltpu.VMEM, pltpu.HBM))
    return pl.pallas_call(
        adam_kernel,
        in_specs=[smem, smem] + [vmem] * 11,
        out_specs=[hbm] * 4 + [vmem] * 2 + [hbm],
        out_shape=[
            rows, rows, rows, rows, jax.ShapeDtypeStruct((1, 1), F32), jax.ShapeDtypeStruct((8, params.shape[1]), F32),
            jax.ShapeDtypeStruct(own.shape, F32),
        ],
        scratch_shapes=[pltpu.VMEM(params.shape, F32)] * 4
        + [pltpu.VMEM(own.shape, F32), pltpu.SemaphoreType.DMA((13,))],
        compiler_params=PARAMS,
        name="adam",
        cost_estimate=pl.CostEstimate(
            flops=20 * params.size, transcendentals=2 * params.size, bytes_accessed=params.size * 32
        ),
    )(place, step, stats, more, mine, other, params, first_moment, second_moment, averaged, own, pair, off)


def flipped(value, axis, bit):
    return lax.ppermute(value, axis, [(i, i ^ bit) for i in range(lax.axis_size(axis))])


def across(value, axis):
    count = lax.axis_size(axis)
    return lax.ppermute(value, axis, [(i, (i + 1 if i % 2 else i - 1) % count) for i in range(count)])


def neighbours(value):
    off = across(value, "edge")
    return flipped(value, "edge", 1), off


def on_device(
    node_latents, edge_latents, senders, receivers, regions, forced, params, first_moment, second_moment,
    averaged, step, cotangent,
):
    latents = node_latents[0]
    edges = edge_latents[0]
    upstream = cotangent[0]
    nodes, width = latents.shape
    share = params.shape[0]
    blocks, feats = lax.axis_size("edge"), lax.axis_size("feat")
    total = share * feats
    vector_row = 7 * width

    pair, off = neighbours(latents)

    mine, place, send, recv, latents = prologue(params, senders, receivers, latents, feats, vector_row // share)
    fetched = [mine] + [flipped(mine, "feat", k) for k in range(1, feats)]

    near_send = gather_near(send, latents, pair)
    near_recv = gather_near(recv, latents, pair)
    fetched = lax.optimization_barrier((near_send, near_recv, *fetched))[2:]
    pieces = [*fetched, *(flipped(piece, "edge", 1) for piece in fetched)]
    hs = gather_off(send, off, near_send)
    hr = gather_off(recv, off, near_recv)
    weights, high, low, to_off = edge_forward(place, regions, recv, hs, hr, edges, pieces, total, nodes)
    from_off = across(to_off, "edge")
    to_pair, more, own = near_sum(recv, high, low, nodes)
    from_pair, more = flipped(to_pair, "edge", 1), flipped(more, "edge", 1)
    hidden, slope = edge_slope(regions, hs, hr, edges, weights)
    own, hidden, slope = lax.optimization_barrier((own, hidden, slope))
    d_agg, agg, node_hidden, d_inner, d_pre, node_unit = node_update(
        latents, own, from_pair, more, from_off, weights, forced, upstream
    )
    back_pair, back_off = neighbours(d_agg)
    new_latents, node_grad, node_sum, back = node_grads(
        latents, agg, node_hidden, d_inner, d_pre, node_unit, weights, forced, upstream
    )
    near = gather_near(recv, d_agg, back_pair)
    unit, inverse = edge_unit(lax.optimization_barrier((hidden, d_agg))[0], weights)

    d_pre, kept, sent = edge_backward(
        place, recv, regions, back_off, near, hs, hr, edges, hidden, slope, unit, inverse, weights, node_grad, node_sum,
    )

    low_rows = vector_row % share
    part, other, coded, bit = kept, flipped(sent, "edge", 1), False, 1
    send_part = sender_part(send, d_pre, weights, nodes)
    while bit < feats:
        part, wire = halve(place, part, other, share, low_rows, bit, coded)
        if bit == 2:
            wire, send_part = lax.optimization_barrier((wire, send_part))
        other = flipped(wire, "feat", bit)
        coded, bit = True, 2 * bit
    wire = add(part, other, low_rows)
    part_own, part_pair, part_off = receiver_part(recv, d_pre, weights, send_part, back)
    wire, part_own, part_pair, part_off = lax.optimization_barrier((wire, part_own, part_pair, part_off))
    bit = 2
    while 2 * bit < blocks:
        wire = add(wire, flipped(wire, "edge", bit), low_rows)
        bit *= 2
    grad_edges = edge_grads(d_pre, weights)
    wire, part_pair, part_off, grad_edges = lax.optimization_barrier((wire, part_pair, part_off, grad_edges))
    mine = finish(place, wire, flipped(wire, "edge", bit), share, low_rows)
    grads_off = across(part_off, "edge")
    grads_pair = flipped(part_pair, "edge", 1)

    other = flipped(mine, "edge", 1)
    stats = jnp.concatenate([mine[share:], other[share:]], axis=0)
    bit = 1
    while 2 * bit < feats:
        stats = stats + flipped(stats, "feat", bit)
        bit *= 2
    more = flipped(stats, "feat", bit)
    new_first, new_second, new_params, new_average, grad_norm, vector_grads, grad_latents = adam(
        place, step, stats, more, mine, other, params, first_moment, second_moment, averaged,
        part_own, grads_pair, grads_off,
    )
    return (
        new_latents[None],
        grad_latents[None],
        grad_edges[None],
        new_first,
        new_second,
        new_params,
        new_average,
        grad_norm.reshape(1),
        vector_grads,
    )


def solution(mesh):
    nodes, rows = P("feat", "edge", None), P("feat", None)
    return jax.shard_map(
        on_device,
        mesh=mesh,
        in_specs=(nodes, nodes, P("edge"), P("edge"), P("edge"), P("edge"), rows, rows, rows, rows, P(), nodes),
        out_specs=(nodes, nodes, nodes, rows, rows, rows, rows, P(), P()),
        check_vma=False,
    )
```

time: 126 us -> 108 us (0.86)
  other arithmetic: 8.83 us -> 0.01 us
  waiting for transfers between devices: 31.9 us -> 23.4 us
  local copies, waits for them, and re-layouts: 5.41 us -> 2.72 us
  starting transfers between devices: 21.8 us -> 23.2 us
    ppermute x4, waiting for transfers between devices: 14.7 us -> 6.63 us  [across(): lax.ppermute(value, axis, [(i, (i + 1 if i % 2 else i - 1) % count) for i...]
    pallas_call x12 -> x19, Pallas kernels: 41.3 us -> 46 us  [the longest x1 8.38 us: edge_forward(): pl.pallas_call(edge_forward_kernel, grid=(count // TILE,), in_specs=[pl.B...]
    add x4 -> x0, other arithmetic: 4.14 us -> none  [the longest x1 1.56 us: on_device(): grad = kept + flipped(sent, 'edge', 1)]
    pallas_call x1, Pallas kernels: 11 us -> 7.57 us  [edge_backward(): pl.pallas_call(edge_backward_kernel, grid=(count // TILE,), in_specs=[pl....]
    ppermute x19 -> x20, starting transfers between devices: 13.9 us -> 16.2 us  [flipped(): lax.ppermute(value, axis, [(i, i ^ bit) for i in range(lax.axis_size(axis...]
    convert_element_type x13 -> x0, other arithmetic: 1.49 us -> none  [the longest x4 1.04 us: unpacked(): values = values.astype(F32)]
    reshape x2 -> x0, other arithmetic: 1.49 us -> none  [gather_off(): index.reshape(-1, LANES)]
    unnamed x38 -> x22, local copies, waits for them, and re-layouts: 3.63 us -> 2.72 us
  transfers between devices with their start and end apart: 23 -> 24, of which waited for: 11 -> 11; matrix products, arithmetic and copies ran while one was open for 4% -> 0% of each run, Pallas kernels for 25% -> 32%
where the time goes in v3:
time: 108 us; the launch traced here: 107 us
  Pallas kernels  56.2 us (52%)
  waiting for transfers between devices  23.4 us (22%)
  starting transfers between devices  23.2 us (21%)
  local copies, waits for them, and re-layouts  2.72 us (3%)
  between operations  1.77 us (2%)
    ppermute x20, waiting for transfers between devices, flipped(): lax.ppermute(value, axis, [(i, i ^ bit) for i in range(lax.axis_size(axis...  16.8 us
    ppermute x20, starting transfers between devices, flipped(): lax.ppermute(value, axis, [(i, i ^ bit) for i in range(lax.axis_size(axis...  16.2 us
    pallas_call x1, Pallas kernels, edge_forward(): pl.pallas_call(edge_forward_kernel, grid=(count // TILE,), in_specs=[pl.B...  8.38 us
    pallas_call x1, Pallas kernels, edge_backward(): pl.pallas_call(edge_backward_kernel, grid=(count // TILE,), in_specs=[pl....  7.57 us
    pallas_call x3, Pallas kernels, gather_near(): pl.pallas_call(gather_near_kernel, grid=(1,), in_specs=[whole((edges // L...  7.21 us
    ppermute x4, starting transfers between devices, across(): lax.ppermute(value, axis, [(i, (i + 1 if i % 2 else i - 1) % count) for i...  7.06 us
    ppermute x4, waiting for transfers between devices, across(): lax.ppermute(value, axis, [(i, (i + 1 if i % 2 else i - 1) % count) for i...  6.63 us
    pallas_call x1, Pallas kernels, receiver_part(): pl.pallas_call(receiver_part_kernel, grid=(3,), in_specs=[whole((1, count...  5.08 us
  transfers between devices with their start and end apart: 24, of which 11 were waited for; matrix products, arithmetic and copies ran while one was open for 0% of the time, Pallas kernels for 32%

profile of v3, /device:TPU:0, one launch (start us, length us, event | category | flops | bytes accessed | tf_op | source)
XLA Modules:
  0.0 107.3 jit_solution(5789631083421461555)
XLA Ops:
  0.6 0.5 collective-permute-start.1
  1.2 1.0 copy-done.2
  2.2 0.7 copy-done.8
  2.9 0.7 copy-done.9
  3.6 1.6 %prologue.1 = (bf16[456,128]{1,0:T(8,128)(2,1)S(1)}, s32[8]{0:T(128)S(1)}, s32[32,128]{1,0:T(8,128)S(1)}, s32[32,128]{1,0:T(8,128)S(1)}, bf16[512,256]{1,0:T(8,128)(2,1)S(1)}) custom-call(f32[456,256]{1,0:T(8,128)S(1)} %copy-done.2, s32[32,128]{1,0:T(8,128)S(1)} %bitcast.26, s32[32,128]{1,0:T(8,128)S(1)} %bitcast.27, bf16[512,256]{1,0:T(8,128)(2,1)} %bitcast.2.latents_hbm), custom_call_target="tpu_custom_call" | custom-call | tf_op jit(solution)/shard_map/prologue/pallas_call | solution.py:119
  5.3 2.7 %collective-permute-start.2 = (bf16[456,128]{1,0:T(8,128)(2,1)S(1)}, bf16[456,128]{1,0:T(8,128)(2,1)S(1)}, u32[]{:S(2)}, u32[]{:S(2)}) collective-permute-start(bf16[456,128]{1,0:T(8,128)(2,1)S(1)} %get-tuple-element.75.refs_0_), channel_id=1, source_target_pairs={{0,1},{1,0},{2,3},{3,2},{4,5},{5,4},{6,7},{7,6},{8,9},{9,8},{10,11... | collective-permute-start | bytes 350216 | tf_op jit(solution)/shard_map/ppermute | solution.py:805
  7.9 2.6 %collective-permute-start.3 = (bf16[456,128]{1,0:T(8,128)(2,1)S(1)}, bf16[456,128]{1,0:T(8,128)(2,1)S(1)}, u32[]{:S(2)}, u32[]{:S(2)}) collective-permute-start(bf16[456,128]{1,0:T(8,128)(2,1)S(1)} %get-tuple-element.75.refs_0_), channel_id=1, source_target_pairs={{0,2},{1,3},{2,0},{3,1},{4,6},{5,7},{6,4},{7,5},{8,10},{9,11},{10,... | collective-permute-start | bytes 350216 | tf_op jit(solution)/shard_map/ppermute | solution.py:805
  10.5 2.0 %collective-permute-start = (bf16[512,256]{1,0:T(8,128)(2,1)}, bf16[512,256]{1,0:T(8,128)(2,1)S(1)}, u32[]{:S(2)}, u32[]{:S(2)}) collective-permute-start(bf16[512,256]{1,0:T(8,128)(2,1)} %bitcast.2.latents_hbm), channel_id=1, source_target_pairs={{0,28},{4,8},{8,4},{12,16},{16,12},{20,24},{24,20},{28,0},{1,29},{... | collective-permute-start | bytes 786440 | tf_op jit(solution)/shard_map/ppermute | solution.py:810
  12.5 2.4 %gather_near.4.near_ref = bf16[4096,256]{1,0:T(8,128)(2,1)S(1)} custom-call(s32[32,128]{1,0:T(8,128)S(1)} %get-tuple-element.71.index_ref.recv_ref, bf16[512,256]{1,0:T(8,128)(2,1)S(1)} %get-tuple-element.70.own_ref.h_ref, bf16[512,256]{1,0:T(8,128)(2,1)S(1)} %collective-permute-done.1.pair_ref), custom_call_target="tpu_custom_call" | custom-call | flops 2147483648 | bytes 2097152 | tf_op jit(solution)/shard_map/gather_near/pallas_call | solution.py:148
  14.9 2.4 %gather_near.3.near_ref = bf16[4096,256]{1,0:T(8,128)(2,1)S(1)} custom-call(s32[32,128]{1,0:T(8,128)S(1)} %get-tuple-element.73.index_ref, bf16[512,256]{1,0:T(8,128)(2,1)S(1)} %get-tuple-element.70.own_ref.h_ref, bf16[512,256]{1,0:T(8,128)(2,1)S(1)} %collective-permute-done.1.pair_ref), custom_call_target="tpu_custom_call" | custom-call | flops 2147483648 | bytes 2097152 | tf_op jit(solution)/shard_map/gather_near/pallas_call | solution.py:148
  17.3 0.0 collective-permute-done.2.refs_1_
  17.3 2.6 %collective-permute-done.3.refs_2_ = bf16[456,128]{1,0:T(8,128)(2,1)S(1)} collective-permute-done((bf16[456,128]{1,0:T(8,128)(2,1)S(1)}, bf16[456,128]{1,0:T(8,128)(2,1)S(1)}, u32[]{:S(2)}, u32[]{:S(2)}) %collective-permute-start.3) | collective-permute-done | bytes 116768 | tf_op jit(solution)/shard_map/ppermute | solution.py:805
  19.9 0.5 collective-permute-start.6
  20.4 0.0 collective-permute-start.7
  20.4 0.5 collective-permute-start.8
  20.9 0.0 collective-permute-done.off_ref
  20.9 1.3 %gather_off.3.hr_ref = bf16[4096,256]{1,0:T(8,128)(2,1)S(1)} custom-call(s32[32,128]{1,0:T(8,128)S(1)} %get-tuple-element.71.index_ref.recv_ref, bf16[512,256]{1,0:T(8,128)(2,1)S(1)} %collective-permute-done.off_ref, bf16[4096,256]{1,0:T(8,128)(2,1)S(1)} %gather_near.4.near_ref), custom_call_target="tpu_custom_call" | custom-call | flops 1073741824 | bytes 4194304 | tf_op jit(solution)/shard_map/gather_off/pallas_call | solution.py:173
  22.2 0.0 copy-start
  22.2 0.0 copy-start.7
  22.2 1.3 %gather_off.2.hs_ref = bf16[4096,256]{1,0:T(8,128)(2,1)S(1)} custom-call(s32[32,128]{1,0:T(8,128)S(1)} %get-tuple-element.73.index_ref, bf16[512,256]{1,0:T(8,128)(2,1)S(1)} %collective-permute-done.off_ref, bf16[4096,256]{1,0:T(8,128)(2,1)S(1)} %gather_near.3.near_ref), custom_call_target="tpu_custom_call" | custom-call | flops 1073741824 | bytes 4194304 | tf_op jit(solution)/shard_map/gather_off/pallas_call | solution.py:173
  23.6 0.2 copy-done
  23.8 8.4 %edge_forward.1 = (bf16[1824,256]{1,0:T(8,128)(2,1)S(1)}, bf16[4096,256]{1,0:T(8,128)(2,1)S(1)}, bf16[4096,256]{1,0:T(8,128)(2,1)S(1)}, s16[528,384]{1,0:T(8,128)(2,1)S(1)}) custom-call(s32[8]{0:T(128)S(1)} %get-tuple-element.72.place_ref, s32[32,128]{1,0:T(8,128)S(1)} %bitcast.22, s32[1,4096]{1,0:T(1,128)S(1)} %bitcast.19, ...), custom_call_target="tpu_custom_call" | custom-call | flops 4831838208 | bytes 10485760 | tf_op jit(solution)/shard_map/edge_forward/pallas_call | solution.py:284
  32.2 2.1 %collective-permute-start.11 = (s16[528,384]{1,0:T(8,128)(2,1)S(1)}, s16[528,384]{1,0:T(8,128)(2,1)S(1)}, u32[]{:S(2)}, u32[]{:S(2)}) collective-permute-start(s16[528,384]{1,0:T(8,128)(2,1)S(1)} %get-tuple-element.88), channel_id=1, source_target_pairs={{0,28},{4,8},{8,4},{12,16},{16,12},{20,24},{24,20},{28,0},{1,29},{... | collective-permute-start | bytes 1216520 | tf_op jit(solution)/shard_map/ppermute | solution.py:810
  34.3 4.5 %near_sum.1 = (f32[256,256]{1,0:T(8,128)S(1)}, f32[256,256]{1,0:T(8,128)S(1)}, f32[512,256]{1,0:T(8,128)S(1)}) custom-call(s32[1,4096]{1,0:T(1,128)S(1)} %bitcast.20, bf16[4096,256]{1,0:T(8,128)(2,1)S(1)} %get-tuple-element.79.high_ref, bf16[4096,256]{1,0:T(8,128)(2,1)S(1)} %get-tuple-element.80.low_ref), custom_call_target="tpu_custom_call" | custom-call | flops 4294967296 | bytes 4194304 | tf_op jit(solution)/shard_map/near_sum/pallas_call | solution.py:369
  38.8 0.1 collective-permute-start.10
  38.9 0.5 collective-permute-start.9
  39.4 3.3 %edge_slope.1 = (bf16[4096,256]{1,0:T(8,128)(2,1)S(1)}, f32[4096,256]{1,0:T(8,128)S(1)}) custom-call(s32[32,128]{1,0:T(8,128)S(1)} %bitcast.23, bf16[4096,256]{1,0:T(8,128)(2,1)S(1)} %gather_off.2.hs_ref, bf16[4096,256]{1,0:T(8,128)(2,1)S(1)} %gather_off.3.hr_ref, bf16[4096,256]{1,0:T(8,128)(2,1)S(1)} %bitcast.15, bf16[1824,256]{1,0:T(8,128)(2,1)S(1)} %get-tuple-element.82.w_ref), custom_call_target="tpu_custom_call" | custom-call | flops 2147483648 | bytes 12582912 | tf_op jit(solution)/shard_map/edge_slope/pallas_call | solution.py:321
  42.8 1.8 %collective-permute-done.11.off_ref = s16[528,384]{1,0:T(8,128)(2,1)S(1)} collective-permute-done((s16[528,384]{1,0:T(8,128)(2,1)S(1)}, s16[528,384]{1,0:T(8,128)(2,1)S(1)}, u32[]{:S(2)}, u32[]{:S(2)}) %collective-permute-start.11) | collective-permute-done | bytes 405536 | tf_op jit(solution)/shard_map/ppermute | solution.py:810
  44.6 1.2 %node_update.1 = (bf16[512,256]{1,0:T(8,128)(2,1)S(1)}, bf16[512,256]{1,0:T(8,128)(2,1)S(1)}, bf16[512,256]{1,0:T(8,128)(2,1)S(1)}, bf16[512,256]{1,0:T(8,128)(2...) custom-call(bf16[512,256]{1,0:T(8,128)(2,1)S(1)} %get-tuple-element.70.own_ref.h_ref, ...), custom_call_target="tpu_custom_call" | custom-call | flops 335544320 | bytes 2621440 | tf_op jit(solution)/shard_map/node_update/pallas_call | solution.py:422
  45.8 0.1 collective-permute-start.13
  45.9 1.8 %collective-permute-start.12 = (bf16[512,256]{1,0:T(8,128)(2,1)S(1)}, bf16[512,256]{1,0:T(8,128)(2,1)S(1)}, u32[]{:S(2)}, u32[]{:S(2)}) collective-permute-start(bf16[512,256]{1,0:T(8,128)(2,1)S(1)} %get-tuple-element.95.own_ref), channel_id=1, source_target_pairs={{0,28},{4,8},{8,4},{12,16},{16,12},{20,24},{24,20},{28,0},{1,29},{... | collective-permute-start | bytes 786440 | tf_op jit(solution)/shard_map/ppermute | solution.py:810
  47.7 1.3 %node_grads.1 = (f32[512,256]{1,0:T(8,128)}, f32[768,256]{1,0:T(8,128)S(1)}, f32[4,256]{1,0:T(4,128)S(1)}, f32[512,256]{1,0:T(8,128)S(1)}) custom-call(bf16[512,256]{1,0:T(8,128)(2,1)S(1)} %get-tuple-element.70.own_ref.h_ref, bf16[512,256]{1,0:T(8,128)(2,1)S(1)} %get-tuple-element.89.agg_ref, bf16[512,256]{1,0:T(8,128)(2,1)S(1)} %get-tuple-element.90.hidden_ref, ...), custom_call_target="tpu_custom_call" | custom-call | flops 268435456 | bytes 2359296 | tf_op jit(solution)/shard_map/node_grads/pallas_call | solution.py:461
  49.0 1.7 %edge_unit.1 = (f32[4096,256]{1,0:T(8,128)S(1)}, f32[4096,128]{1,0:T(8,128)S(1)}) custom-call(bf16[4096,256]{1,0:T(8,128)(2,1)S(1)} %get-tuple-element.98.hidden_ref, bf16[1824,256]{1,0:T(8,128)(2,1)S(1)} %get-tuple-element.82.w_ref), custom_call_target="tpu_custom_call" | custom-call | flops 536870912 | bytes 8388608 | tf_op jit(solution)/shard_map/edge_unit/pallas_call | solution.py:344
  50.7 2.4 %gather_near.5.near_ref = bf16[4096,256]{1,0:T(8,128)(2,1)S(1)} custom-call(s32[32,128]{1,0:T(8,128)S(1)} %get-tuple-element.71.index_ref.recv_ref, bf16[512,256]{1,0:T(8,128)(2,1)S(1)} %get-tuple-element.95.own_ref, bf16[512,256]{1,0:T(8,128)(2,1)S(1)} %collective-permute-done.13.pair_ref), custom_call_target="tpu_custom_call" | custom-call | flops 2147483648 | bytes 2097152 | tf_op jit(solution)/shard_map/gather_near/pallas_call | solution.py:148
  53.1 2.3 %collective-permute-done.12.off_ref = bf16[512,256]{1,0:T(8,128)(2,1)S(1)} collective-permute-done((bf16[512,256]{1,0:T(8,128)(2,1)S(1)}, bf16[512,256]{1,0:T(8,128)(2,1)S(1)}, u32[]{:S(2)}, u32[]{:S(2)}) %collective-permute-start.12) | collective-permute-done | bytes 262176 | tf_op jit(solution)/shard_map/ppermute | solution.py:810
  55.3 7.6 %edge_backward.1 = (bf16[4096,256]{1,0:T(8,128)(2,1)S(1)}, f32[1824,128]{1,0:T(8,128)S(1)}, f32[1824,128]{1,0:T(8,128)S(1)}) custom-call(s32[8]{0:T(128)S(1)} %get-tuple-element.72.place_ref, s32[32,128]{1,0:T(8,128)S(1)} %get-tuple-element.71.index_ref.recv_ref, s32[1,4096]{1,0:T(1,128)S(1)} %bitcast.24, ...), custom_call_target="tpu_custom_call" | custom-call | flops 4294967296 | bytes 20971520 | tf_op jit(solution)/shard_map/edge_backward/pallas_call | solution.py:547
  62.9 0.1 collective-permute-start.14
  63.0 2.5 %collective-permute-done.14.other_ref = f32[1824,128]{1,0:T(8,128)S(1)} collective-permute-done((f32[1824,128]{1,0:T(8,128)S(1)}, f32[1824,128]{1,0:T(8,128)S(1)}, u32[]{:S(2)}, u32[]{:S(2)}) %collective-permute-start.14) | collective-permute-done | bytes 933920 | tf_op jit(solution)/shard_map/ppermute | solution.py:805
  65.5 0.6 halve.2
  66.1 2.4 %collective-permute-start.15 = (bf16[928,128]{1,0:T(8,128)(2,1)S(1)}, bf16[928,128]{1,0:T(8,128)(2,1)S(1)}, u32[]{:S(2)}, u32[]{:S(2)}) collective-permute-start(bf16[928,128]{1,0:T(8,128)(2,1)S(1)} %get-tuple-element.106), channel_id=1, source_target_pairs={{0,1},{1,0},{2,3},{3,2},{4,5},{5,4},{6,7},{7,6},{8,9},{9,8},{10,11... | collective-permute-start | bytes 712712 | tf_op jit(solution)/shard_map/ppermute | solution.py:805
  68.5 5.0 %sender_part.1.part_ref = f32[1536,256]{1,0:T(8,128)S(1)} custom-call(s32[1,4096]{1,0:T(1,128)S(1)} %bitcast.25, bf16[4096,256]{1,0:T(8,128)(2,1)S(1)} %get-tuple-element.109.d_pre_ref, bf16[1824,256]{1,0:T(8,128)(2,1)S(1)} %get-tuple-element.82.w_ref), custom_call_target="tpu_custom_call" | custom-call | flops 3221225472 | bytes 2097152 | tf_op jit(solution)/shard_map/sender_part/pallas_call | solution.py:585
  73.5 1.1 %collective-permute-done.15.other_ref = bf16[928,128]{1,0:T(8,128)(2,1)S(1)} collective-permute-done((bf16[928,128]{1,0:T(8,128)(2,1)S(1)}, bf16[928,128]{1,0:T(8,128)(2,1)S(1)}, u32[]{:S(2)}, u32[]{:S(2)}) %collective-permute-start.15) | collective-permute-done | bytes 237600 | tf_op jit(solution)/shard_map/ppermute | solution.py:805
  74.6 0.6 halve.3
  75.2 2.8 %collective-permute-start.16 = (bf16[464,128]{1,0:T(8,128)(2,1)S(1)}, bf16[464,128]{1,0:T(8,128)(2,1)S(1)}, u32[]{:S(2)}, u32[]{:S(2)}) collective-permute-start(bf16[464,128]{1,0:T(8,128)(2,1)S(1)} %get-tuple-element.110), channel_id=1, source_target_pairs={{0,2},{1,3},{2,0},{3,1},{4,6},{5,7},{6,4},{7,5},{8,10},{9,11},{10,... | collective-permute-start | bytes 356360 | tf_op jit(solution)/shard_map/ppermute | solution.py:805
  78.0 5.1 %receiver_part.1 = (f32[512,256]{1,0:T(8,128)S(1)}, bf16[512,256]{1,0:T(8,128)(2,1)S(1)}, bf16[512,256]{1,0:T(8,128)(2,1)S(1)}) custom-call(s32[1,4096]{1,0:T(1,128)S(1)} %bitcast.21, bf16[4096,256]{1,0:T(8,128)(2,1)S(1)} %get-tuple-element.109.d_pre_ref, bf16[1824,256]{1,0:T(8,128)(2,1)S(1)} %get-tuple-element.82.w_ref, ...), custom_call_target="tpu_custom_call" | custom-call | flops 3221225472 | bytes 2097152 | tf_op jit(solution)/shard_map/receiver_part/pallas_call | solution.py:621
  83.1 0.4 collective-permute-done.16.other_ref
  83.5 0.0 copy-start.3
  83.5 0.0 copy-start.4
  83.6 0.0 copy-start.5
  83.6 0.0 copy-start.6
  83.6 0.8 collective-permute-start.17
  84.4 1.9 %edge_grads.1 = bf16[4096,256]{1,0:T(8,128)(2,1)} custom-call(bf16[4096,256]{1,0:T(8,128)(2,1)S(1)} %get-tuple-element.109.d_pre_ref, bf16[1824,256]{1,0:T(8,128)(2,1)S(1)} %get-tuple-element.82.w_ref), custom_call_target="tpu_custom_call" | custom-call | flops 536870912 | bytes 4194304 | tf_op jit(solution)/shard_map/edge_grads/pallas_call | solution.py:644
  86.3 2.2 %collective-permute-done.17.other_ref = bf16[464,128]{1,0:T(8,128)(2,1)S(1)} collective-permute-done((bf16[464,128]{1,0:T(8,128)(2,1)S(1)}, bf16[464,128]{1,0:T(8,128)(2,1)S(1)}, u32[]{:S(2)}, u32[]{:S(2)}) %collective-permute-start.17) | collective-permute-done | bytes 118816 | tf_op jit(solution)/shard_map/ppermute | solution.py:805
  88.5 1.0 collective-permute-start.18
  89.5 3.9 %collective-permute-done.18.other_ref = bf16[464,128]{1,0:T(8,128)(2,1)S(1)} collective-permute-done((bf16[464,128]{1,0:T(8,128)(2,1)S(1)}, bf16[464,128]{1,0:T(8,128)(2,1)S(1)}, u32[]{:S(2)}, u32[]{:S(2)}) %collective-permute-start.18) | collective-permute-done | bytes 118816 | tf_op jit(solution)/shard_map/ppermute | solution.py:805
  93.4 0.7 finish.1.mine_ref
  94.1 0.5 collective-permute-start.22
  94.7 1.2 %collective-permute-start.23 = (bf16[512,256]{1,0:T(8,128)(2,1)S(1)}, bf16[512,256]{1,0:T(8,128)(2,1)S(1)}, u32[]{:S(2)}, u32[]{:S(2)}) collective-permute-start(bf16[512,256]{1,0:T(8,128)(2,1)S(1)} %get-tuple-element.122), channel_id=1, source_target_pairs={{0,28},{4,8},{8,4},{12,16},{16,12},{20,24},{24,20},{28,0},{1,29},{... | collective-permute-start | bytes 786440 | tf_op jit(solution)/shard_map/ppermute | solution.py:810
  95.9 0.1 collective-permute-start.20
  95.9 3.7 %collective-permute-done.20 = f32[32,128]{1,0:T(8,128)S(1)} collective-permute-done((f32[32,128]{1,0:T(8,128)S(1)}, f32[32,128]{1,0:T(8,128)S(1)}, u32[]{:S(2)}, u32[]{:S(2)}) %collective-permute-start.20) | collective-permute-done | bytes 16416 | tf_op jit(solution)/shard_map/ppermute | solution.py:805
  99.7 1.0 collective-permute-start.21
  101.4 2.5 %collective-permute-done.23.off_ref = bf16[512,256]{1,0:T(8,128)(2,1)S(1)} collective-permute-done((bf16[512,256]{1,0:T(8,128)(2,1)S(1)}, bf16[512,256]{1,0:T(8,128)(2,1)S(1)}, u32[]{:S(2)}, u32[]{:S(2)}) %collective-permute-start.23) | collective-permute-done | bytes 262176 | tf_op jit(solution)/shard_map/ppermute | solution.py:810
  103.9 0.4 collective-permute-done.21.more_ref
  104.3 2.8 %adam.1 = (f32[456,256]{1,0:T(8,128)}, f32[456,256]{1,0:T(8,128)}, f32[456,256]{1,0:T(8,128)}, f32[456,256]{1,0:T(8,128)}, f32[1,1]{1,0:T(1,128)}, /*index=5*/f32[8,256]{1,0:T(8,128)}, f32[512,256]{1,0:T(8,128)}) custom-call(s32[8]{0:T(128)S(1)} %get-tuple-element.72.place_ref, s32[1]{0:T(128)S(6)} %copy.21.step_ref, f32[32,128]{1,0:T(8,128)S(1)} %fusion.stats_ref, ...), custom_call_target="tpu_custom_call" | custom-call | flops 2334720 | bytes 3735552 | tf_op jit(solution)/shard_map/adam/pallas_call | solution.py:786
  (32 shorter events, 0.1 us)
Async XLA Ops:
  0.6 11.8 %collective-permute-start.1 = (bf16[512,256]{1,0:T(8,128)(2,1)}, bf16[512,256]{1,0:T(8,128)(2,1)S(1)}, u32[]{:S(2)}, u32[]{:S(2)}) collective-permute-start(bf16[512,256]{1,0:T(8,128)(2,1)} %bitcast.2.latents_hbm), channel_id=1, source_target_pairs={{0,4},{4,0},{8,12},{12,8},{16,20},{20,16},{24,28},{28,24},{1,5},{5... | collective-permute-start | bytes 786440 | tf_op jit(solution)/shard_map/ppermute | solution.py:805
  1.2 1.0 copy-start.2
  2.2 0.7 copy-start.8
  2.9 0.7 copy-start.9
  5.3 12.1 %collective-permute-start.2 = (bf16[456,128]{1,0:T(8,128)(2,1)S(1)}, bf16[456,128]{1,0:T(8,128)(2,1)S(1)}, u32[]{:S(2)}, u32[]{:S(2)}) collective-permute-start(bf16[456,128]{1,0:T(8,128)(2,1)S(1)} %get-tuple-element.75.refs_0_), channel_id=1, source_target_pairs={{0,1},{1,0},{2,3},{3,2},{4,5},{5,4},{6,7},{7,6},{8,9},{9,8},{10,11... | collective-permute-start | bytes 350216 | tf_op jit(solution)/shard_map/ppermute | solution.py:805
  7.9 12.0 %collective-permute-start.3 = (bf16[456,128]{1,0:T(8,128)(2,1)S(1)}, bf16[456,128]{1,0:T(8,128)(2,1)S(1)}, u32[]{:S(2)}, u32[]{:S(2)}) collective-permute-start(bf16[456,128]{1,0:T(8,128)(2,1)S(1)} %get-tuple-element.75.refs_0_), channel_id=1, source_target_pairs={{0,2},{1,3},{2,0},{3,1},{4,6},{5,7},{6,4},{7,5},{8,10},{9,11},{10,... | collective-permute-start | bytes 350216 | tf_op jit(solution)/shard_map/ppermute | solution.py:805
  10.5 9.4 %collective-permute-start.4 = (bf16[456,128]{1,0:T(8,128)(2,1)S(1)}, bf16[456,128]{1,0:T(8,128)(2,1)S(1)}, u32[]{:S(2)}, u32[]{:S(2)}) collective-permute-start(bf16[456,128]{1,0:T(8,128)(2,1)S(1)} %get-tuple-element.75.refs_0_), channel_id=1, source_target_pairs={{0,3},{1,2},{2,1},{3,0},{4,7},{5,6},{6,5},{7,4},{8,11},{9,10},{10,... | collective-permute-start | bytes 350216 | tf_op jit(solution)/shard_map/ppermute | solution.py:805
  10.5 10.4 %collective-permute-start = (bf16[512,256]{1,0:T(8,128)(2,1)}, bf16[512,256]{1,0:T(8,128)(2,1)S(1)}, u32[]{:S(2)}, u32[]{:S(2)}) collective-permute-start(bf16[512,256]{1,0:T(8,128)(2,1)} %bitcast.2.latents_hbm), channel_id=1, source_target_pairs={{0,28},{4,8},{8,4},{12,16},{16,12},{20,24},{24,20},{28,0},{1,29},{... | collective-permute-start | bytes 786440 | tf_op jit(solution)/shard_map/ppermute | solution.py:810
  19.9 3.7 %collective-permute-start.5 = (bf16[456,128]{1,0:T(8,128)(2,1)S(1)}, bf16[456,128]{1,0:T(8,128)(2,1)S(1)}, u32[]{:S(2)}, u32[]{:S(2)}) collective-permute-start(bf16[456,128]{1,0:T(8,128)(2,1)S(1)} %get-tuple-element.75.refs_0_), channel_id=1, source_target_pairs={{0,4},{4,0},{8,12},{12,8},{16,20},{20,16},{24,28},{28,24},{1,5},{5... | collective-permute-start | bytes 350216 | tf_op jit(solution)/shard_map/ppermute | solution.py:805
  19.9 3.7 %collective-permute-start.6 = (bf16[456,128]{1,0:T(8,128)(2,1)S(1)}, bf16[456,128]{1,0:T(8,128)(2,1)S(1)}, u32[]{:S(2)}, u32[]{:S(2)}) collective-permute-start(bf16[456,128]{1,0:T(8,128)(2,1)S(1)} %collective-permute-done.2.refs_1_), channel_id=1, source_target_pairs={{0,4},{4,0},{8,12},{12,8},{16,20},{20,16},{24,28},{28,24},{1,5},{5... | collective-permute-start | bytes 350216 | tf_op jit(solution)/shard_map/ppermute | solution.py:805
  20.4 3.2 %collective-permute-start.7 = (bf16[456,128]{1,0:T(8,128)(2,1)S(1)}, bf16[456,128]{1,0:T(8,128)(2,1)S(1)}, u32[]{:S(2)}, u32[]{:S(2)}) collective-permute-start(bf16[456,128]{1,0:T(8,128)(2,1)S(1)} %collective-permute-done.3.refs_2_), channel_id=1, source_target_pairs={{0,4},{4,0},{8,12},{12,8},{16,20},{20,16},{24,28},{28,24},{1,5},{5... | collective-permute-start | bytes 350216 | tf_op jit(solution)/shard_map/ppermute | solution.py:805
  20.4 3.2 %collective-permute-start.8 = (bf16[456,128]{1,0:T(8,128)(2,1)S(1)}, bf16[456,128]{1,0:T(8,128)(2,1)S(1)}, u32[]{:S(2)}, u32[]{:S(2)}) collective-permute-start(bf16[456,128]{1,0:T(8,128)(2,1)S(1)} %collective-permute-done.4.refs_3_), channel_id=1, source_target_pairs={{0,4},{4,0},{8,12},{12,8},{16,20},{20,16},{24,28},{28,24},{1,5},{5... | collective-permute-start | bytes 350216 | tf_op jit(solution)/shard_map/ppermute | solution.py:805
  22.2 1.6 %copy-start = (bf16[1,4096,256]{2,1,0:T(8,128)(2,1)S(1)}, bf16[1,4096,256]{2,1,0:T(8,128)(2,1)}, u32[]{:S(2)}) copy-start(bf16[1,4096,256]{2,1,0:T(8,128)(2,1)} %param.13) | copy-start | bytes 6291460
  22.2 1.6 %copy-start.7 = (s32[4096]{0:T(1024)S(1)}, s32[4096]{0:T(1024)}, u32[]{:S(2)}) copy-start(s32[4096]{0:T(1024)} %param.16) | copy-start | bytes 49156
  32.2 12.4 %collective-permute-start.11 = (s16[528,384]{1,0:T(8,128)(2,1)S(1)}, s16[528,384]{1,0:T(8,128)(2,1)S(1)}, u32[]{:S(2)}, u32[]{:S(2)}) collective-permute-start(s16[528,384]{1,0:T(8,128)(2,1)S(1)} %get-tuple-element.88), channel_id=1, source_target_pairs={{0,28},{4,8},{8,4},{12,16},{16,12},{20,24},{24,20},{28,0},{1,29},{... | collective-permute-start | bytes 1216520 | tf_op jit(solution)/shard_map/ppermute | solution.py:810
  38.8 3.9 %collective-permute-start.10 = (f32[256,256]{1,0:T(8,128)S(1)}, f32[256,256]{1,0:T(8,128)S(1)}, u32[]{:S(2)}, u32[]{:S(2)}) collective-permute-start(f32[256,256]{1,0:T(8,128)S(1)} %get-tuple-element.87), channel_id=1, source_target_pairs={{0,4},{4,0},{8,12},{12,8},{16,20},{20,16},{24,28},{28,24},{1,5},{5... | collective-permute-start | bytes 786440 | tf_op jit(solution)/shard_map/ppermute | solution.py:805
  38.9 3.9 %collective-permute-start.9 = (f32[256,256]{1,0:T(8,128)S(1)}, f32[256,256]{1,0:T(8,128)S(1)}, u32[]{:S(2)}, u32[]{:S(2)}) collective-permute-start(f32[256,256]{1,0:T(8,128)S(1)} %get-tuple-element.86), channel_id=1, source_target_pairs={{0,4},{4,0},{8,12},{12,8},{16,20},{20,16},{24,28},{28,24},{1,5},{5... | collective-permute-start | bytes 786440 | tf_op jit(solution)/shard_map/ppermute | solution.py:805
  39.4 5.2 %copy-start.1 = (f32[1,512,256]{2,1,0:T(8,128)S(1)}, f32[1,512,256]{2,1,0:T(8,128)}, u32[]{:S(2)}) copy-start(f32[1,512,256]{2,1,0:T(8,128)} %param.23) | copy-start | bytes 1572868
  39.4 5.2 %copy-start.10 = (s32[512]{0:T(512)S(1)}, s32[512]{0:T(512)}, u32[]{:S(2)}) copy-start(s32[512]{0:T(512)} %param.17) | copy-start | bytes 6148
  45.8 4.8 %collective-permute-start.13 = (bf16[512,256]{1,0:T(8,128)(2,1)S(1)}, bf16[512,256]{1,0:T(8,128)(2,1)S(1)}, u32[]{:S(2)}, u32[]{:S(2)}) collective-permute-start(bf16[512,256]{1,0:T(8,128)(2,1)S(1)} %get-tuple-element.95.own_ref), channel_id=1, source_target_pairs={{0,4},{4,0},{8,12},{12,8},{16,20},{20,16},{24,28},{28,24},{1,5},{5... | collective-permute-start | bytes 786440 | tf_op jit(solution)/shard_map/ppermute | solution.py:805
  45.9 9.4 %collective-permute-start.12 = (bf16[512,256]{1,0:T(8,128)(2,1)S(1)}, bf16[512,256]{1,0:T(8,128)(2,1)S(1)}, u32[]{:S(2)}, u32[]{:S(2)}) collective-permute-start(bf16[512,256]{1,0:T(8,128)(2,1)S(1)} %get-tuple-element.95.own_ref), channel_id=1, source_target_pairs={{0,28},{4,8},{8,4},{12,16},{16,12},{20,24},{24,20},{28,0},{1,29},{... | collective-permute-start | bytes 786440 | tf_op jit(solution)/shard_map/ppermute | solution.py:810
  62.9 2.6 %collective-permute-start.14 = (f32[1824,128]{1,0:T(8,128)S(1)}, f32[1824,128]{1,0:T(8,128)S(1)}, u32[]{:S(2)}, u32[]{:S(2)}) collective-permute-start(f32[1824,128]{1,0:T(8,128)S(1)} %get-tuple-element.104), channel_id=1, source_target_pairs={{0,4},{4,0},{8,12},{12,8},{16,20},{20,16},{24,28},{28,24},{1,5},{5... | collective-permute-start | bytes 2801672 | tf_op jit(solution)/shard_map/ppermute | solution.py:805
  66.1 8.5 %collective-permute-start.15 = (bf16[928,128]{1,0:T(8,128)(2,1)S(1)}, bf16[928,128]{1,0:T(8,128)(2,1)S(1)}, u32[]{:S(2)}, u32[]{:S(2)}) collective-permute-start(bf16[928,128]{1,0:T(8,128)(2,1)S(1)} %get-tuple-element.106), channel_id=1, source_target_pairs={{0,1},{1,0},{2,3},{3,2},{4,5},{5,4},{6,7},{7,6},{8,9},{9,8},{10,11... | collective-permute-start | bytes 712712 | tf_op jit(solution)/shard_map/ppermute | solution.py:805
  75.2 8.3 %collective-permute-start.16 = (bf16[464,128]{1,0:T(8,128)(2,1)S(1)}, bf16[464,128]{1,0:T(8,128)(2,1)S(1)}, u32[]{:S(2)}, u32[]{:S(2)}) collective-permute-start(bf16[464,128]{1,0:T(8,128)(2,1)S(1)} %get-tuple-element.110), channel_id=1, source_target_pairs={{0,2},{1,3},{2,0},{3,1},{4,6},{5,7},{6,4},{7,5},{8,10},{9,11},{10,... | collective-permute-start | bytes 356360 | tf_op jit(solution)/shard_map/ppermute | solution.py:805
  83.5 20.8 %copy-start.3 = (f32[456,256]{1,0:T(8,128)S(1)}, f32[456,256]{1,0:T(8,128)}, u32[]{:S(2)}) copy-start(f32[456,256]{1,0:T(8,128)} %params_ref.1) | copy-start | bytes 1400836
  83.5 20.8 %copy-start.4 = (f32[456,256]{1,0:T(8,128)S(1)}, f32[456,256]{1,0:T(8,128)}, u32[]{:S(2)}) copy-start(f32[456,256]{1,0:T(8,128)} %first_ref.1) | copy-start | bytes 1400836
  83.6 20.8 %copy-start.5 = (f32[456,256]{1,0:T(8,128)S(1)}, f32[456,256]{1,0:T(8,128)}, u32[]{:S(2)}) copy-start(f32[456,256]{1,0:T(8,128)} %second_ref.1) | copy-start | bytes 1400836
  83.6 20.7 %copy-start.6 = (f32[456,256]{1,0:T(8,128)S(1)}, f32[456,256]{1,0:T(8,128)}, u32[]{:S(2)}) copy-start(f32[456,256]{1,0:T(8,128)} %averaged_ref.1) | copy-start | bytes 1400836
  83.6 4.9 %collective-permute-start.17 = (bf16[464,128]{1,0:T(8,128)(2,1)S(1)}, bf16[464,128]{1,0:T(8,128)(2,1)S(1)}, u32[]{:S(2)}, u32[]{:S(2)}) collective-permute-start(bf16[464,128]{1,0:T(8,128)(2,1)S(1)} %add.7.mine_ref), channel_id=1, source_target_pairs={{0,8},{4,12},{8,0},{12,4},{16,24},{20,28},{24,16},{28,20},{1,9},{5... | collective-permute-start | bytes 356360 | tf_op jit(solution)/shard_map/ppermute | solution.py:805
  88.5 4.9 %collective-permute-start.18 = (bf16[464,128]{1,0:T(8,128)(2,1)S(1)}, bf16[464,128]{1,0:T(8,128)(2,1)S(1)}, u32[]{:S(2)}, u32[]{:S(2)}) collective-permute-start(bf16[464,128]{1,0:T(8,128)(2,1)S(1)} %add.8.mine_ref), channel_id=1, source_target_pairs={{0,16},{4,20},{8,24},{12,28},{16,0},{20,4},{24,8},{28,12},{1,17},{... | collective-permute-start | bytes 356360 | tf_op jit(solution)/shard_map/ppermute | solution.py:805
  94.1 1.7 %collective-permute-start.19 = (f32[472,128]{1,0:T(8,128)S(1)}, f32[472,128]{1,0:T(8,128)S(1)}, u32[]{:S(2)}, u32[]{:S(2)}) collective-permute-start(f32[472,128]{1,0:T(8,128)S(1)} %finish.1.mine_ref), channel_id=1, source_target_pairs={{0,4},{4,0},{8,12},{12,8},{16,20},{20,16},{24,28},{28,24},{1,5},{5... | collective-permute-start | bytes 725000 | tf_op jit(solution)/shard_map/ppermute | solution.py:805
  94.1 7.2 %collective-permute-start.22 = (bf16[512,256]{1,0:T(8,128)(2,1)S(1)}, bf16[512,256]{1,0:T(8,128)(2,1)S(1)}, u32[]{:S(2)}, u32[]{:S(2)}) collective-permute-start(bf16[512,256]{1,0:T(8,128)(2,1)S(1)} %get-tuple-element.121), channel_id=1, source_target_pairs={{0,4},{4,0},{8,12},{12,8},{16,20},{20,16},{24,28},{28,24},{1,5},{5... | collective-permute-start | bytes 786440 | tf_op jit(solution)/shard_map/ppermute | solution.py:805
  94.7 9.2 %collective-permute-start.23 = (bf16[512,256]{1,0:T(8,128)(2,1)S(1)}, bf16[512,256]{1,0:T(8,128)(2,1)S(1)}, u32[]{:S(2)}, u32[]{:S(2)}) collective-permute-start(bf16[512,256]{1,0:T(8,128)(2,1)S(1)} %get-tuple-element.122), channel_id=1, source_target_pairs={{0,28},{4,8},{8,4},{12,16},{16,12},{20,24},{24,20},{28,0},{1,29},{... | collective-permute-start | bytes 786440 | tf_op jit(solution)/shard_map/ppermute | solution.py:810
  95.9 3.8 %collective-permute-start.20 = (f32[32,128]{1,0:T(8,128)S(1)}, f32[32,128]{1,0:T(8,128)S(1)}, u32[]{:S(2)}, u32[]{:S(2)}) collective-permute-start(f32[32,128]{1,0:T(8,128)S(1)} %pad_maximum_fusion), channel_id=1, source_target_pairs={{0,1},{1,0},{2,3},{3,2},{4,5},{5,4},{6,7},{7,6},{8,9},{9,8},{10,11... | collective-permute-start | bytes 49160 | tf_op jit(solution)/shard_map/ppermute | solution.py:805
  99.7 4.6 %collective-permute-start.21 = (f32[32,128]{1,0:T(8,128)S(1)}, f32[32,128]{1,0:T(8,128)S(1)}, u32[]{:S(2)}, u32[]{:S(2)}) collective-permute-start(f32[32,128]{1,0:T(8,128)S(1)} %fusion.stats_ref), channel_id=1, source_target_pairs={{0,2},{1,3},{2,0},{3,1},{4,6},{5,7},{6,4},{7,5},{8,10},{9,11},{10,... | collective-permute-start | bytes 49160 | tf_op jit(solution)/shard_map/ppermute | solution.py:805

commit v4 on v3

--- a/solution.py
+++ b/solution.py
@@ -129,7 +129,7 @@
         ],
         compiler_params=PARAMS,
         name="prologue",
-    )(params, senders.reshape(shape), receivers.reshape(shape), latents)
+    )(*(pltpu.with_memory_space_constraint(a, pltpu.HBM) for a in (params, senders.reshape(shape), receivers.reshape(shape), latents)))
     return half, place, send.reshape(-1), recv.reshape(-1), own
 
 
@@ -254,10 +254,11 @@
     @pl.when(step == 0)
     def _():
         odd = place_ref[0] == 1
-        shares = len(pieces) // 2
         share = pieces[0].shape[0]
-        for k in range(shares):
-            mine, other = pieces[k][...].astype(F32), pieces[shares + k][...].astype(F32)
+        for k in range(w_ref.shape[0] // share):
+            rows = slice((k - 1) * share, k * share)
+            mine, other = (pieces[i][...] if k == 0 else pieces[i + 1][rows, :] for i in (0, 2))
+            mine, other = mine.astype(F32), other.astype(F32)
             base = pl.multiple_of(place_ref[4 + k] * share, 8)
             wide_ref[pl.ds(base, share), 0:LANES] = jnp.where(odd, other, mine)
             wide_ref[pl.ds(base, share), LANES : 2 * LANES] = jnp.where(odd, mine, other)
@@ -667,40 +668,43 @@
     return jnp.concatenate([values[:first, :], exact, values[first + 8 : share, :]], axis=0)
 
 
-def halve_kernel(place_ref, mine_ref, other_ref, kept_ref, sent_ref, *, share, first, bit, coded):
-    here = (place_ref[2] // bit) % 2
-    size = share + 8 if coded else share
-    for j in range(kept_ref.shape[0] // share):
-        for side, out_ref in ((here, kept_ref), (1 - here, sent_ref)):
-            index = 2 * j + side
-            other = other_ref[pl.ds(pl.multiple_of(index * size, 8), size), :]
-            total = mine_ref[pl.ds(pl.multiple_of(index * share, 8), share), :] + (
-                unpacked(other, first) if coded else other
-            )
-            if out_ref is kept_ref:
-                out_ref[j * share : (j + 1) * share, :] = total
-            else:
-                out_ref[j * (share + 8) : (j + 1) * (share + 8), :] = packed(total, first)
-
-
-def halve(place, mine, other, share, first, bit, coded):
-    count = mine.shape[0] // share // 2
+def parted_kernel(place_ref, mine_ref, other_ref, kept_ref, *sent_refs, share, first):
+    for k, out_ref in enumerate((kept_ref, *sent_refs)):
+        rows = pl.ds(pl.multiple_of(place_ref[4 + k] * share, 8), share)
+        total = mine_ref[rows, :] + other_ref[rows, :]
+        out_ref[...] = packed(total, first) if k else total
+
+
+def parted(place, mine, other, share, first):
     vmem = pl.BlockSpec(memory_space=pltpu.VMEM)
-    return pl.pallas_call(
-        functools.partial(halve_kernel, share=share, first=first, bit=bit, coded=coded),
+    sent = jax.ShapeDtypeStruct((share + 8, LANES), B16)
+    return pl.pallas_call(
+        functools.partial(parted_kernel, share=share, first=first),
         in_specs=[pl.BlockSpec(memory_space=pltpu.SMEM), vmem, vmem],
-        out_shape=[
-            jax.ShapeDtypeStruct((count * share, LANES), F32),
-            jax.ShapeDtypeStruct((count * (share + 8), LANES), B16),
-        ],
-        compiler_params=PARAMS,
-        name="halve",
+        out_shape=[jax.ShapeDtypeStruct((share, LANES), F32)] + [sent] * (mine.shape[0] // share - 1),
+        compiler_params=PARAMS,
+        name="parted",
     )(place, mine, other)
 
 
+def gathered_kernel(mine_ref, *refs, first):
+    total = mine_ref[...]
+    for ref in refs[:-1]:
+        total = total + unpacked(ref[...], first)
+    refs[-1][...] = packed(total, first)
+
+
+def gathered(mine, others, first):
+    return pl.pallas_call(
+        functools.partial(gathered_kernel, first=first),
+        out_shape=jax.ShapeDtypeStruct(others[0].shape, B16),
+        compiler_params=PARAMS,
+        name="gathered",
+    )(mine, *others)
+
+
 def add_kernel(mine_ref, other_ref, out_ref, *, first):
-    mine = mine_ref[...] if mine_ref.dtype == F32 else unpacked(mine_ref[...], first)
-    out_ref[...] = packed(mine + unpacked(other_ref[...], first), first)
+    out_ref[...] = packed(unpacked(mine_ref[...], first) + unpacked(other_ref[...], first), first)
 
 
 def add(mine, other, first):
@@ -835,8 +839,8 @@
 
     near_send = gather_near(send, latents, pair)
     near_recv = gather_near(recv, latents, pair)
-    fetched = lax.optimization_barrier((near_send, near_recv, *fetched))[2:]
-    pieces = [*fetched, *(flipped(piece, "edge", 1) for piece in fetched)]
+    others = jnp.concatenate(lax.optimization_barrier((near_send, near_recv, *fetched[1:]))[2:])
+    pieces = [fetched[0], others, flipped(fetched[0], "edge", 1), flipped(others, "edge", 1)]
     hs = gather_off(send, off, near_send)
     hr = gather_off(recv, off, near_recv)
     weights, high, low, to_off = edge_forward(place, regions, recv, hs, hr, edges, pieces, total, nodes)
@@ -860,17 +864,13 @@
     )
 
     low_rows = vector_row % share
-    part, other, coded, bit = kept, flipped(sent, "edge", 1), False, 1
+    part, *sent = parted(place, kept, flipped(sent, "edge", 1), share, low_rows)
+    came = [flipped(wire, "feat", k + 1) for k, wire in enumerate(sent)]
+    d_pre, part = lax.optimization_barrier((d_pre, part))
     send_part = sender_part(send, d_pre, weights, nodes)
-    while bit < feats:
-        part, wire = halve(place, part, other, share, low_rows, bit, coded)
-        if bit == 2:
-            wire, send_part = lax.optimization_barrier((wire, send_part))
-        other = flipped(wire, "feat", bit)
-        coded, bit = True, 2 * bit
-    wire = add(part, other, low_rows)
     part_own, part_pair, part_off = receiver_part(recv, d_pre, weights, send_part, back)
-    wire, part_own, part_pair, part_off = lax.optimization_barrier((wire, part_own, part_pair, part_off))
+    part, part_own, part_pair, part_off = lax.optimization_barrier((part, part_own, part_pair, part_off))
+    wire = gathered(part, came, low_rows)
     bit = 2
     while 2 * bit < blocks:
         wire = add(wire, flipped(wire, "edge", bit), low_rows)

time: 108 us -> 103 us (0.954)
  waiting for transfers between devices: 23.4 us -> 18 us
  starting transfers between devices: 23.2 us -> 25.9 us
  local copies, waits for them, and re-layouts: 2.72 us -> 0.33 us
    ppermute x20 -> x19, waiting for transfers between devices: 16.8 us -> 13.2 us  [flipped(): lax.ppermute(value, axis, [(i, i ^ bit) for i in range(lax.axis_size(axis...]
    ppermute x20 -> x19, starting transfers between devices: 16.2 us -> 18.8 us  [flipped(): lax.ppermute(value, axis, [(i, i ^ bit) for i in range(lax.axis_size(axis...]
    unnamed x22 -> x18, local copies, waits for them, and re-layouts: 2.72 us -> 0.31 us
    ppermute x4, waiting for transfers between devices: 6.63 us -> 4.82 us  [across(): lax.ppermute(value, axis, [(i, (i + 1 if i % 2 else i - 1) % count) for i...]
  transfers between devices with their start and end apart: 24 -> 23, of which waited for: 11 -> 9; matrix products, arithmetic and copies ran while one was open for 0% -> 0% of each run, Pallas kernels for 32% -> 34%
where the time goes in v4:
time: 103 us; the launch traced here: 102 us
  Pallas kernels  56.4 us (55%)
  starting transfers between devices  25.9 us (25%)
  waiting for transfers between devices  18 us (17%)
  between operations  1.78 us (2%)
    ppermute x19, starting transfers between devices, flipped(): lax.ppermute(value, axis, [(i, i ^ bit) for i in range(lax.axis_size(axis...  18.8 us
    ppermute x19, waiting for transfers between devices, flipped(): lax.ppermute(value, axis, [(i, i ^ bit) for i in range(lax.axis_size(axis...  13.2 us
    pallas_call x1, Pallas kernels, edge_forward(): pl.pallas_call(edge_forward_kernel, grid=(count // TILE,), in_specs=[pl.B...  8.44 us
    pallas_call x1, Pallas kernels, edge_backward(): pl.pallas_call(edge_backward_kernel, grid=(count // TILE,), in_specs=[pl....  8.07 us
    pallas_call x3, Pallas kernels, gather_near(): pl.pallas_call(gather_near_kernel, grid=(1,), in_specs=[whole((edges // L...  7.24 us
    ppermute x4, starting transfers between devices, across(): lax.ppermute(value, axis, [(i, (i + 1 if i % 2 else i - 1) % count) for i...  7.04 us
    pallas_call x1, Pallas kernels, receiver_part(): pl.pallas_call(receiver_part_kernel, grid=(3,), in_specs=[whole((1, count...  5.11 us
    pallas_call x1, Pallas kernels, sender_part(): pl.pallas_call(sender_part_kernel, grid=(3,), in_specs=[whole((1, count))...  4.97 us
  transfers between devices with their start and end apart: 23, of which 9 were waited for; matrix products, arithmetic and copies ran while one was open for 0% of the time, Pallas kernels for 34%

profile of v4, /device:TPU:0, one launch (start us, length us, event | category | flops | bytes accessed | tf_op | source)
XLA Modules:
  0.0 102.5 jit_solution(6692730652642329992)
XLA Ops:
  0.6 0.5 collective-permute-start.1
  1.2 1.7 %prologue.1 = (bf16[456,128]{1,0:T(8,128)(2,1)S(1)}, s32[8]{0:T(128)S(1)}, s32[32,128]{1,0:T(8,128)S(1)}, s32[32,128]{1,0:T(8,128)S(1)}, bf16[512,256]{1,0:T(8,128)(2,1)S(1)}) custom-call(f32[456,256]{1,0:T(8,128)} %params_ref.1, s32[32,128]{1,0:T(8,128)} %bitcast.32, s32[32,128]{1,0:T(8,128)} %bitcast.33, bf16[512,256]{1,0:T(8,128)(2,1)} %bitcast.30), custom_call_target="tpu_custom_call" | custom-call | tf_op jit(solution)/shard_map/prologue/pallas_call | solution.py:119
  2.9 2.7 %collective-permute-start.2 = (bf16[456,128]{1,0:T(8,128)(2,1)S(1)}, bf16[456,128]{1,0:T(8,128)(2,1)S(1)}, u32[]{:S(2)}, u32[]{:S(2)}) collective-permute-start(bf16[456,128]{1,0:T(8,128)(2,1)S(1)} %get-tuple-element.73.refs_0_), channel_id=1, source_target_pairs={{0,1},{1,0},{2,3},{3,2},{4,5},{5,4},{6,7},{7,6},{8,9},{9,8},{10,11... | collective-permute-start | bytes 350216 | tf_op jit(solution)/shard_map/ppermute | solution.py:809
  5.6 2.6 %collective-permute-start.3 = (bf16[456,128]{1,0:T(8,128)(2,1)S(1)}, bf16[456,128]{1,0:T(8,128)(2,1)S(1)}, u32[]{:S(2)}, u32[]{:S(2)}) collective-permute-start(bf16[456,128]{1,0:T(8,128)(2,1)S(1)} %get-tuple-element.73.refs_0_), channel_id=1, source_target_pairs={{0,2},{1,3},{2,0},{3,1},{4,6},{5,7},{6,4},{7,5},{8,10},{9,11},{10,... | collective-permute-start | bytes 350216 | tf_op jit(solution)/shard_map/ppermute | solution.py:809
  8.2 0.0 collective-permute-start.4
  8.2 2.0 %collective-permute-start = (bf16[512,256]{1,0:T(8,128)(2,1)}, bf16[512,256]{1,0:T(8,128)(2,1)S(1)}, u32[]{:S(2)}, u32[]{:S(2)}) collective-permute-start(bf16[512,256]{1,0:T(8,128)(2,1)} %bitcast.31), channel_id=1, source_target_pairs={{0,28},{4,8},{8,4},{12,16},{16,12},{20,24},{24,20},{28,0},{1,29},{... | collective-permute-start | bytes 786440 | tf_op jit(solution)/shard_map/ppermute | solution.py:814
  10.1 0.0 collective-permute-done.1.pair_ref
  10.1 2.4 %gather_near.4.near_ref = bf16[4096,256]{1,0:T(8,128)(2,1)S(1)} custom-call(s32[32,128]{1,0:T(8,128)S(1)} %get-tuple-element.70.index_ref.recv_ref, bf16[512,256]{1,0:T(8,128)(2,1)S(1)} %get-tuple-element.69.own_ref.h_ref, bf16[512,256]{1,0:T(8,128)(2,1)S(1)} %collective-permute-done.1.pair_ref), custom_call_target="tpu_custom_call" | custom-call | flops 2147483648 | bytes 2097152 | tf_op jit(solution)/shard_map/gather_near/pallas_call | solution.py:148
  12.6 2.4 %gather_near.3.near_ref = bf16[4096,256]{1,0:T(8,128)(2,1)S(1)} custom-call(s32[32,128]{1,0:T(8,128)S(1)} %get-tuple-element.72.index_ref, bf16[512,256]{1,0:T(8,128)(2,1)S(1)} %get-tuple-element.69.own_ref.h_ref, bf16[512,256]{1,0:T(8,128)(2,1)S(1)} %collective-permute-done.1.pair_ref), custom_call_target="tpu_custom_call" | custom-call | flops 2147483648 | bytes 2097152 | tf_op jit(solution)/shard_map/gather_near/pallas_call | solution.py:148
  15.0 0.0 collective-permute-done.2
  15.0 2.6 %collective-permute-done.3 = bf16[456,128]{1,0:T(8,128)(2,1)S(1)} collective-permute-done((bf16[456,128]{1,0:T(8,128)(2,1)S(1)}, bf16[456,128]{1,0:T(8,128)(2,1)S(1)}, u32[]{:S(2)}, u32[]{:S(2)}) %collective-permute-start.3) | collective-permute-done | bytes 116768 | tf_op jit(solution)/shard_map/ppermute | solution.py:809
  17.6 0.1 collective-permute-start.6
  17.7 0.5 collective-permute-start.5
  18.2 1.3 %gather_off.3.hr_ref = bf16[4096,256]{1,0:T(8,128)(2,1)S(1)} custom-call(s32[32,128]{1,0:T(8,128)S(1)} %get-tuple-element.70.index_ref.recv_ref, bf16[512,256]{1,0:T(8,128)(2,1)S(1)} %collective-permute-done.off_ref, bf16[4096,256]{1,0:T(8,128)(2,1)S(1)} %gather_near.4.near_ref), custom_call_target="tpu_custom_call" | custom-call | flops 1073741824 | bytes 4194304 | tf_op jit(solution)/shard_map/gather_off/pallas_call | solution.py:173
  19.5 0.0 copy-start
  19.5 0.0 copy-start.6
  19.5 1.3 %gather_off.2.hs_ref = bf16[4096,256]{1,0:T(8,128)(2,1)S(1)} custom-call(s32[32,128]{1,0:T(8,128)S(1)} %get-tuple-element.72.index_ref, bf16[512,256]{1,0:T(8,128)(2,1)S(1)} %collective-permute-done.off_ref, bf16[4096,256]{1,0:T(8,128)(2,1)S(1)} %gather_near.3.near_ref), custom_call_target="tpu_custom_call" | custom-call | flops 1073741824 | bytes 4194304 | tf_op jit(solution)/shard_map/gather_off/pallas_call | solution.py:173
  20.8 0.0 collective-permute-done.5.refs_2_
  20.8 0.0 collective-permute-done.6.refs_3_
  20.9 0.2 copy-done
  21.1 8.4 %edge_forward.1 = (bf16[1824,256]{1,0:T(8,128)(2,1)S(1)}, bf16[4096,256]{1,0:T(8,128)(2,1)S(1)}, bf16[4096,256]{1,0:T(8,128)(2,1)S(1)}, s16[528,384]{1,0:T(8,128)(2,1)S(1)}) custom-call(s32[8]{0:T(128)S(1)} %get-tuple-element.71.place_ref, s32[32,128]{1,0:T(8,128)S(1)} %bitcast.22, s32[1,4096]{1,0:T(1,128)S(1)} %bitcast.19, ...), custom_call_target="tpu_custom_call" | custom-call | flops 4831838208 | bytes 10485760 | tf_op jit(solution)/shard_map/edge_forward/pallas_call | solution.py:285
  29.5 2.2 %collective-permute-start.9 = (s16[528,384]{1,0:T(8,128)(2,1)S(1)}, s16[528,384]{1,0:T(8,128)(2,1)S(1)}, u32[]{:S(2)}, u32[]{:S(2)}) collective-permute-start(s16[528,384]{1,0:T(8,128)(2,1)S(1)} %get-tuple-element.86), channel_id=1, source_target_pairs={{0,28},{4,8},{8,4},{12,16},{16,12},{20,24},{24,20},{28,0},{1,29},{... | collective-permute-start | bytes 1216520 | tf_op jit(solution)/shard_map/ppermute | solution.py:814
  31.7 4.5 %near_sum.1 = (f32[256,256]{1,0:T(8,128)S(1)}, f32[256,256]{1,0:T(8,128)S(1)}, f32[512,256]{1,0:T(8,128)S(1)}) custom-call(s32[1,4096]{1,0:T(1,128)S(1)} %bitcast.20, bf16[4096,256]{1,0:T(8,128)(2,1)S(1)} %get-tuple-element.77.high_ref, bf16[4096,256]{1,0:T(8,128)(2,1)S(1)} %get-tuple-element.78.low_ref), custom_call_target="tpu_custom_call" | custom-call | flops 4294967296 | bytes 4194304 | tf_op jit(solution)/shard_map/near_sum/pallas_call | solution.py:370
  36.2 0.1 collective-permute-start.7
  36.3 0.5 collective-permute-start.8
  36.8 3.4 %edge_slope.1 = (bf16[4096,256]{1,0:T(8,128)(2,1)S(1)}, f32[4096,256]{1,0:T(8,128)S(1)}) custom-call(s32[32,128]{1,0:T(8,128)S(1)} %bitcast.23, bf16[4096,256]{1,0:T(8,128)(2,1)S(1)} %gather_off.2.hs_ref, bf16[4096,256]{1,0:T(8,128)(2,1)S(1)} %gather_off.3.hr_ref, bf16[4096,256]{1,0:T(8,128)(2,1)S(1)} %bitcast.15, bf16[1824,256]{1,0:T(8,128)(2,1)S(1)} %get-tuple-element.80.w_ref), custom_call_target="tpu_custom_call" | custom-call | flops 2147483648 | bytes 12582912 | tf_op jit(solution)/shard_map/edge_slope/pallas_call | solution.py:322
  40.2 1.6 %collective-permute-done.9.off_ref = s16[528,384]{1,0:T(8,128)(2,1)S(1)} collective-permute-done((s16[528,384]{1,0:T(8,128)(2,1)S(1)}, s16[528,384]{1,0:T(8,128)(2,1)S(1)}, u32[]{:S(2)}, u32[]{:S(2)}) %collective-permute-start.9) | collective-permute-done | bytes 405536 | tf_op jit(solution)/shard_map/ppermute | solution.py:814
  41.9 1.2 %node_update.1 = (bf16[512,256]{1,0:T(8,128)(2,1)S(1)}, bf16[512,256]{1,0:T(8,128)(2,1)S(1)}, bf16[512,256]{1,0:T(8,128)(2,1)S(1)}, bf16[512,256]{1,0:T(8,128)(2...) custom-call(bf16[512,256]{1,0:T(8,128)(2,1)S(1)} %get-tuple-element.69.own_ref.h_ref, ...), custom_call_target="tpu_custom_call" | custom-call | flops 335544320 | bytes 2621440 | tf_op jit(solution)/shard_map/node_update/pallas_call | solution.py:423
  43.1 0.1 collective-permute-start.11
  43.2 1.8 %collective-permute-start.10 = (bf16[512,256]{1,0:T(8,128)(2,1)S(1)}, bf16[512,256]{1,0:T(8,128)(2,1)S(1)}, u32[]{:S(2)}, u32[]{:S(2)}) collective-permute-start(bf16[512,256]{1,0:T(8,128)(2,1)S(1)} %get-tuple-element.93.own_ref), channel_id=1, source_target_pairs={{0,28},{4,8},{8,4},{12,16},{16,12},{20,24},{24,20},{28,0},{1,29},{... | collective-permute-start | bytes 786440 | tf_op jit(solution)/shard_map/ppermute | solution.py:814
  44.9 1.3 %node_grads.1 = (f32[512,256]{1,0:T(8,128)}, f32[768,256]{1,0:T(8,128)S(1)}, f32[4,256]{1,0:T(4,128)S(1)}, f32[512,256]{1,0:T(8,128)S(1)}) custom-call(bf16[512,256]{1,0:T(8,128)(2,1)S(1)} %get-tuple-element.69.own_ref.h_ref, bf16[512,256]{1,0:T(8,128)(2,1)S(1)} %get-tuple-element.87.agg_ref, bf16[512,256]{1,0:T(8,128)(2,1)S(1)} %get-tuple-element.88.hidden_ref, ...), custom_call_target="tpu_custom_call" | custom-call | flops 268435456 | bytes 2359296 | tf_op jit(solution)/shard_map/node_grads/pallas_call | solution.py:462
  46.2 1.7 %edge_unit.1 = (f32[4096,256]{1,0:T(8,128)S(1)}, f32[4096,128]{1,0:T(8,128)S(1)}) custom-call(bf16[4096,256]{1,0:T(8,128)(2,1)S(1)} %get-tuple-element.96.hidden_ref, bf16[1824,256]{1,0:T(8,128)(2,1)S(1)} %get-tuple-element.80.w_ref), custom_call_target="tpu_custom_call" | custom-call | flops 536870912 | bytes 8388608 | tf_op jit(solution)/shard_map/edge_unit/pallas_call | solution.py:345
  47.9 0.0 collective-permute-done.11.pair_ref
  48.0 2.4 %gather_near.5.near_ref = bf16[4096,256]{1,0:T(8,128)(2,1)S(1)} custom-call(s32[32,128]{1,0:T(8,128)S(1)} %get-tuple-element.70.index_ref.recv_ref, bf16[512,256]{1,0:T(8,128)(2,1)S(1)} %get-tuple-element.93.own_ref, bf16[512,256]{1,0:T(8,128)(2,1)S(1)} %collective-permute-done.11.pair_ref), custom_call_target="tpu_custom_call" | custom-call | flops 2147483648 | bytes 2097152 | tf_op jit(solution)/shard_map/gather_near/pallas_call | solution.py:148
  50.4 2.1 %collective-permute-done.10.off_ref = bf16[512,256]{1,0:T(8,128)(2,1)S(1)} collective-permute-done((bf16[512,256]{1,0:T(8,128)(2,1)S(1)}, bf16[512,256]{1,0:T(8,128)(2,1)S(1)}, u32[]{:S(2)}, u32[]{:S(2)}) %collective-permute-start.10) | collective-permute-done | bytes 262176 | tf_op jit(solution)/shard_map/ppermute | solution.py:814
  52.5 8.1 %edge_backward.1 = (bf16[4096,256]{1,0:T(8,128)(2,1)S(1)}, f32[1824,128]{1,0:T(8,128)S(1)}, f32[1824,128]{1,0:T(8,128)S(1)}) custom-call(s32[8]{0:T(128)S(1)} %get-tuple-element.71.place_ref, s32[32,128]{1,0:T(8,128)S(1)} %get-tuple-element.70.index_ref.recv_ref, s32[1,4096]{1,0:T(1,128)S(1)} %bitcast.24, ...), custom_call_target="tpu_custom_call" | custom-call | flops 4294967296 | bytes 20971520 | tf_op jit(solution)/shard_map/edge_backward/pallas_call | solution.py:548
  60.5 0.1 collective-permute-start.12
  60.7 2.4 %collective-permute-done.12.other_ref = f32[1824,128]{1,0:T(8,128)S(1)} collective-permute-done((f32[1824,128]{1,0:T(8,128)S(1)}, f32[1824,128]{1,0:T(8,128)S(1)}, u32[]{:S(2)}, u32[]{:S(2)}) %collective-permute-start.12) | collective-permute-done | bytes 933920 | tf_op jit(solution)/shard_map/ppermute | solution.py:809
  63.1 0.6 parted.1
  63.7 2.4 %collective-permute-start.13 = (bf16[464,128]{1,0:T(8,128)(2,1)S(1)}, bf16[464,128]{1,0:T(8,128)(2,1)S(1)}, u32[]{:S(2)}, u32[]{:S(2)}) collective-permute-start(bf16[464,128]{1,0:T(8,128)(2,1)S(1)} %get-tuple-element.112), channel_id=1, source_target_pairs={{0,1},{1,0},{2,3},{3,2},{4,5},{5,4},{6,7},{7,6},{8,9},{9,8},{10,11... | collective-permute-start | bytes 356360 | tf_op jit(solution)/shard_map/ppermute | solution.py:809
  66.1 1.3 %collective-permute-start.14 = (bf16[464,128]{1,0:T(8,128)(2,1)S(1)}, bf16[464,128]{1,0:T(8,128)(2,1)S(1)}, u32[]{:S(2)}, u32[]{:S(2)}) collective-permute-start(bf16[464,128]{1,0:T(8,128)(2,1)S(1)} %get-tuple-element.113), channel_id=1, source_target_pairs={{0,2},{1,3},{2,0},{3,1},{4,6},{5,7},{6,4},{7,5},{8,10},{9,11},{10,... | collective-permute-start | bytes 356360 | tf_op jit(solution)/shard_map/ppermute | solution.py:809
  67.4 1.2 %collective-permute-start.15 = (bf16[464,128]{1,0:T(8,128)(2,1)S(1)}, bf16[464,128]{1,0:T(8,128)(2,1)S(1)}, u32[]{:S(2)}, u32[]{:S(2)}) collective-permute-start(bf16[464,128]{1,0:T(8,128)(2,1)S(1)} %get-tuple-element.114), channel_id=1, source_target_pairs={{0,3},{1,2},{2,1},{3,0},{4,7},{5,6},{6,5},{7,4},{8,11},{9,10},{10,... | collective-permute-start | bytes 356360 | tf_op jit(solution)/shard_map/ppermute | solution.py:809
  68.6 5.0 %sender_part.1.part_ref = f32[1536,256]{1,0:T(8,128)S(1)} custom-call(s32[1,4096]{1,0:T(1,128)S(1)} %bitcast.25, bf16[4096,256]{1,0:T(8,128)(2,1)S(1)} %get-tuple-element.106.d_pre_ref, bf16[1824,256]{1,0:T(8,128)(2,1)S(1)} %get-tuple-element.80.w_ref), custom_call_target="tpu_custom_call" | custom-call | flops 3221225472 | bytes 2097152 | tf_op jit(solution)/shard_map/sender_part/pallas_call | solution.py:586
  73.6 5.1 %receiver_part.1 = (f32[512,256]{1,0:T(8,128)S(1)}, bf16[512,256]{1,0:T(8,128)(2,1)S(1)}, bf16[512,256]{1,0:T(8,128)(2,1)S(1)}) custom-call(s32[1,4096]{1,0:T(1,128)S(1)} %bitcast.21, bf16[4096,256]{1,0:T(8,128)(2,1)S(1)} %get-tuple-element.106.d_pre_ref, bf16[1824,256]{1,0:T(8,128)(2,1)S(1)} %get-tuple-element.80.w_ref, ...), custom_call_target="tpu_custom_call" | custom-call | flops 3221225472 | bytes 2097152 | tf_op jit(solution)/shard_map/receiver_part/pallas_call | solution.py:622
  78.7 0.0 collective-permute-done.14.refs_1_
  78.7 0.1 gathered.1.mine_ref
  78.8 0.0 copy-start.2
  78.8 0.0 copy-start.3
  78.8 0.0 copy-start.4
  78.8 0.0 copy-start.5
  78.8 0.6 collective-permute-start.16
  79.4 1.9 %edge_grads.1 = bf16[4096,256]{1,0:T(8,128)(2,1)} custom-call(bf16[4096,256]{1,0:T(8,128)(2,1)S(1)} %get-tuple-element.106.d_pre_ref, bf16[1824,256]{1,0:T(8,128)(2,1)S(1)} %get-tuple-element.80.w_ref), custom_call_target="tpu_custom_call" | custom-call | flops 536870912 | bytes 4194304 | tf_op jit(solution)/shard_map/edge_grads/pallas_call | solution.py:645
  81.3 2.4 %collective-permute-done.16.other_ref = bf16[464,128]{1,0:T(8,128)(2,1)S(1)} collective-permute-done((bf16[464,128]{1,0:T(8,128)(2,1)S(1)}, bf16[464,128]{1,0:T(8,128)(2,1)S(1)}, u32[]{:S(2)}, u32[]{:S(2)}) %collective-permute-start.16) | collective-permute-done | bytes 118816 | tf_op jit(solution)/shard_map/ppermute | solution.py:809
  83.8 1.4 %collective-permute-start.17 = (bf16[464,128]{1,0:T(8,128)(2,1)S(1)}, bf16[464,128]{1,0:T(8,128)(2,1)S(1)}, u32[]{:S(2)}, u32[]{:S(2)}) collective-permute-start(bf16[464,128]{1,0:T(8,128)(2,1)S(1)} %add.6.mine_ref), channel_id=1, source_target_pairs={{0,16},{4,20},{8,24},{12,28},{16,0},{20,4},{24,8},{28,12},{1,17},{... | collective-permute-start | bytes 356360 | tf_op jit(solution)/shard_map/ppermute | solution.py:809
  85.2 3.5 %collective-permute-done.17.other_ref = bf16[464,128]{1,0:T(8,128)(2,1)S(1)} collective-permute-done((bf16[464,128]{1,0:T(8,128)(2,1)S(1)}, bf16[464,128]{1,0:T(8,128)(2,1)S(1)}, u32[]{:S(2)}, u32[]{:S(2)}) %collective-permute-start.17) | collective-permute-done | bytes 118816 | tf_op jit(solution)/shard_map/ppermute | solution.py:809
  88.7 0.7 finish.1.mine_ref
  89.4 0.5 collective-permute-start.21
  89.9 1.1 %collective-permute-start.22 = (bf16[512,256]{1,0:T(8,128)(2,1)S(1)}, bf16[512,256]{1,0:T(8,128)(2,1)S(1)}, u32[]{:S(2)}, u32[]{:S(2)}) collective-permute-start(bf16[512,256]{1,0:T(8,128)(2,1)S(1)} %get-tuple-element.120), channel_id=1, source_target_pairs={{0,28},{4,8},{8,4},{12,16},{16,12},{20,24},{24,20},{28,0},{1,29},{... | collective-permute-start | bytes 786440 | tf_op jit(solution)/shard_map/ppermute | solution.py:814
  91.0 1.7 %collective-permute-start.19 = (f32[32,128]{1,0:T(8,128)S(1)}, f32[32,128]{1,0:T(8,128)S(1)}, u32[]{:S(2)}, u32[]{:S(2)}) collective-permute-start(f32[32,128]{1,0:T(8,128)S(1)} %pad_maximum_fusion), channel_id=1, source_target_pairs={{0,1},{1,0},{2,3},{3,2},{4,5},{5,4},{6,7},{7,6},{8,9},{9,8},{10,11... | collective-permute-start | bytes 49160 | tf_op jit(solution)/shard_map/ppermute | solution.py:809
  92.8 2.1 %collective-permute-done.19 = f32[32,128]{1,0:T(8,128)S(1)} collective-permute-done((f32[32,128]{1,0:T(8,128)S(1)}, f32[32,128]{1,0:T(8,128)S(1)}, u32[]{:S(2)}, u32[]{:S(2)}) %collective-permute-start.19) | collective-permute-done | bytes 16416 | tf_op jit(solution)/shard_map/ppermute | solution.py:809
  94.9 2.6 %collective-permute-start.20 = (f32[32,128]{1,0:T(8,128)S(1)}, f32[32,128]{1,0:T(8,128)S(1)}, u32[]{:S(2)}, u32[]{:S(2)}) collective-permute-start(f32[32,128]{1,0:T(8,128)S(1)} %fusion.stats_ref), channel_id=1, source_target_pairs={{0,2},{1,3},{2,0},{3,1},{4,6},{5,7},{6,4},{7,5},{8,10},{9,11},{10,... | collective-permute-start | bytes 49160 | tf_op jit(solution)/shard_map/ppermute | solution.py:809
  98.1 1.1 %collective-permute-done.22.off_ref = bf16[512,256]{1,0:T(8,128)(2,1)S(1)} collective-permute-done((bf16[512,256]{1,0:T(8,128)(2,1)S(1)}, bf16[512,256]{1,0:T(8,128)(2,1)S(1)}, u32[]{:S(2)}, u32[]{:S(2)}) %collective-permute-start.22) | collective-permute-done | bytes 262176 | tf_op jit(solution)/shard_map/ppermute | solution.py:814
  99.3 0.2 collective-permute-done.20.more_ref
  99.5 2.8 %adam.1 = (f32[456,256]{1,0:T(8,128)}, f32[456,256]{1,0:T(8,128)}, f32[456,256]{1,0:T(8,128)}, f32[456,256]{1,0:T(8,128)}, f32[1,1]{1,0:T(1,128)}, /*index=5*/f32[8,256]{1,0:T(8,128)}, f32[512,256]{1,0:T(8,128)}) custom-call(s32[8]{0:T(128)S(1)} %get-tuple-element.71.place_ref, s32[1]{0:T(128)S(6)} %copy.23.step_ref, f32[32,128]{1,0:T(8,128)S(1)} %fusion.stats_ref, ...), custom_call_target="tpu_custom_call" | custom-call | flops 2334720 | bytes 3735552 | tf_op jit(solution)/shard_map/adam/pallas_call | solution.py:790
  (26 shorter events, 0.1 us)
Async XLA Ops:
  0.6 9.5 %collective-permute-start.1 = (bf16[512,256]{1,0:T(8,128)(2,1)}, bf16[512,256]{1,0:T(8,128)(2,1)S(1)}, u32[]{:S(2)}, u32[]{:S(2)}) collective-permute-start(bf16[512,256]{1,0:T(8,128)(2,1)} %bitcast.29), channel_id=1, source_target_pairs={{0,4},{4,0},{8,12},{12,8},{16,20},{20,16},{24,28},{28,24},{1,5},{5... | collective-permute-start | bytes 786440 | tf_op jit(solution)/shard_map/ppermute | solution.py:809
  2.9 12.1 %collective-permute-start.2 = (bf16[456,128]{1,0:T(8,128)(2,1)S(1)}, bf16[456,128]{1,0:T(8,128)(2,1)S(1)}, u32[]{:S(2)}, u32[]{:S(2)}) collective-permute-start(bf16[456,128]{1,0:T(8,128)(2,1)S(1)} %get-tuple-element.73.refs_0_), channel_id=1, source_target_pairs={{0,1},{1,0},{2,3},{3,2},{4,5},{5,4},{6,7},{7,6},{8,9},{9,8},{10,11... | collective-permute-start | bytes 350216 | tf_op jit(solution)/shard_map/ppermute | solution.py:809
  5.6 12.0 %collective-permute-start.3 = (bf16[456,128]{1,0:T(8,128)(2,1)S(1)}, bf16[456,128]{1,0:T(8,128)(2,1)S(1)}, u32[]{:S(2)}, u32[]{:S(2)}) collective-permute-start(bf16[456,128]{1,0:T(8,128)(2,1)S(1)} %get-tuple-element.73.refs_0_), channel_id=1, source_target_pairs={{0,2},{1,3},{2,0},{3,1},{4,6},{5,7},{6,4},{7,5},{8,10},{9,11},{10,... | collective-permute-start | bytes 350216 | tf_op jit(solution)/shard_map/ppermute | solution.py:809
  8.2 9.4 %collective-permute-start.4 = (bf16[456,128]{1,0:T(8,128)(2,1)S(1)}, bf16[456,128]{1,0:T(8,128)(2,1)S(1)}, u32[]{:S(2)}, u32[]{:S(2)}) collective-permute-start(bf16[456,128]{1,0:T(8,128)(2,1)S(1)} %get-tuple-element.73.refs_0_), channel_id=1, source_target_pairs={{0,3},{1,2},{2,1},{3,0},{4,7},{5,6},{6,5},{7,4},{8,11},{9,10},{10,... | collective-permute-start | bytes 350216 | tf_op jit(solution)/shard_map/ppermute | solution.py:809
  8.2 10.0 %collective-permute-start = (bf16[512,256]{1,0:T(8,128)(2,1)}, bf16[512,256]{1,0:T(8,128)(2,1)S(1)}, u32[]{:S(2)}, u32[]{:S(2)}) collective-permute-start(bf16[512,256]{1,0:T(8,128)(2,1)} %bitcast.31), channel_id=1, source_target_pairs={{0,28},{4,8},{8,4},{12,16},{16,12},{20,24},{24,20},{28,0},{1,29},{... | collective-permute-start | bytes 786440 | tf_op jit(solution)/shard_map/ppermute | solution.py:814
  17.6 3.2 %collective-permute-start.6 = (bf16[1368,128]{1,0:T(8,128)(2,1)S(1)}, bf16[1368,128]{1,0:T(8,128)(2,1)S(1)}, u32[]{:S(2)}, u32[]{:S(2)}) collective-permute-start(bf16[1368,128]{1,0:T(8,128)(2,1)S(1)} %constant_dynamic-update-slice_fusion.refs_1_), channel_id=1, source_target_pairs={{0,4},{4,0},{8,12},{12,8},{16,20},{20,16},{24,28},{28,24},{1,5},{5... | collective-permute-start | bytes 1050632 | tf_op jit(solution)/shard_map/ppermute | solution.py:809
  17.7 3.1 %collective-permute-start.5 = (bf16[456,128]{1,0:T(8,128)(2,1)S(1)}, bf16[456,128]{1,0:T(8,128)(2,1)S(1)}, u32[]{:S(2)}, u32[]{:S(2)}) collective-permute-start(bf16[456,128]{1,0:T(8,128)(2,1)S(1)} %get-tuple-element.73.refs_0_), channel_id=1, source_target_pairs={{0,4},{4,0},{8,12},{12,8},{16,20},{20,16},{24,28},{28,24},{1,5},{5... | collective-permute-start | bytes 350216 | tf_op jit(solution)/shard_map/ppermute | solution.py:809
  19.5 1.6 %copy-start = (bf16[1,4096,256]{2,1,0:T(8,128)(2,1)S(1)}, bf16[1,4096,256]{2,1,0:T(8,128)(2,1)}, u32[]{:S(2)}) copy-start(bf16[1,4096,256]{2,1,0:T(8,128)(2,1)} %param.13) | copy-start | bytes 6291460
  19.5 1.6 %copy-start.6 = (s32[4096]{0:T(1024)S(1)}, s32[4096]{0:T(1024)}, u32[]{:S(2)}) copy-start(s32[4096]{0:T(1024)} %param.16) | copy-start | bytes 49156
  29.5 12.3 %collective-permute-start.9 = (s16[528,384]{1,0:T(8,128)(2,1)S(1)}, s16[528,384]{1,0:T(8,128)(2,1)S(1)}, u32[]{:S(2)}, u32[]{:S(2)}) collective-permute-start(s16[528,384]{1,0:T(8,128)(2,1)S(1)} %get-tuple-element.86), channel_id=1, source_target_pairs={{0,28},{4,8},{8,4},{12,16},{16,12},{20,24},{24,20},{28,0},{1,29},{... | collective-permute-start | bytes 1216520 | tf_op jit(solution)/shard_map/ppermute | solution.py:814
  36.2 4.0 %collective-permute-start.7 = (f32[256,256]{1,0:T(8,128)S(1)}, f32[256,256]{1,0:T(8,128)S(1)}, u32[]{:S(2)}, u32[]{:S(2)}) collective-permute-start(f32[256,256]{1,0:T(8,128)S(1)} %get-tuple-element.84), channel_id=1, source_target_pairs={{0,4},{4,0},{8,12},{12,8},{16,20},{20,16},{24,28},{28,24},{1,5},{5... | collective-permute-start | bytes 786440 | tf_op jit(solution)/shard_map/ppermute | solution.py:809
  36.3 3.9 %collective-permute-start.8 = (f32[256,256]{1,0:T(8,128)S(1)}, f32[256,256]{1,0:T(8,128)S(1)}, u32[]{:S(2)}, u32[]{:S(2)}) collective-permute-start(f32[256,256]{1,0:T(8,128)S(1)} %get-tuple-element.85), channel_id=1, source_target_pairs={{0,4},{4,0},{8,12},{12,8},{16,20},{20,16},{24,28},{28,24},{1,5},{5... | collective-permute-start | bytes 786440 | tf_op jit(solution)/shard_map/ppermute | solution.py:809
  36.8 5.0 %copy-start.1 = (f32[1,512,256]{2,1,0:T(8,128)S(1)}, f32[1,512,256]{2,1,0:T(8,128)}, u32[]{:S(2)}) copy-start(f32[1,512,256]{2,1,0:T(8,128)} %param.23) | copy-start | bytes 1572868
  36.8 5.0 %copy-start.7 = (s32[512]{0:T(512)S(1)}, s32[512]{0:T(512)}, u32[]{:S(2)}) copy-start(s32[512]{0:T(512)} %param.17) | copy-start | bytes 6148
  43.1 4.9 %collective-permute-start.11 = (bf16[512,256]{1,0:T(8,128)(2,1)S(1)}, bf16[512,256]{1,0:T(8,128)(2,1)S(1)}, u32[]{:S(2)}, u32[]{:S(2)}) collective-permute-start(bf16[512,256]{1,0:T(8,128)(2,1)S(1)} %get-tuple-element.93.own_ref), channel_id=1, source_target_pairs={{0,4},{4,0},{8,12},{12,8},{16,20},{20,16},{24,28},{28,24},{1,5},{5... | collective-permute-start | bytes 786440 | tf_op jit(solution)/shard_map/ppermute | solution.py:809
  43.2 9.3 %collective-permute-start.10 = (bf16[512,256]{1,0:T(8,128)(2,1)S(1)}, bf16[512,256]{1,0:T(8,128)(2,1)S(1)}, u32[]{:S(2)}, u32[]{:S(2)}) collective-permute-start(bf16[512,256]{1,0:T(8,128)(2,1)S(1)} %get-tuple-element.93.own_ref), channel_id=1, source_target_pairs={{0,28},{4,8},{8,4},{12,16},{16,12},{20,24},{24,20},{28,0},{1,29},{... | collective-permute-start | bytes 786440 | tf_op jit(solution)/shard_map/ppermute | solution.py:814
  60.5 2.6 %collective-permute-start.12 = (f32[1824,128]{1,0:T(8,128)S(1)}, f32[1824,128]{1,0:T(8,128)S(1)}, u32[]{:S(2)}, u32[]{:S(2)}) collective-permute-start(f32[1824,128]{1,0:T(8,128)S(1)} %get-tuple-element.103), channel_id=1, source_target_pairs={{0,4},{4,0},{8,12},{12,8},{16,20},{20,16},{24,28},{28,24},{1,5},{5... | collective-permute-start | bytes 2801672 | tf_op jit(solution)/shard_map/ppermute | solution.py:809
  63.7 15.0 %collective-permute-start.13 = (bf16[464,128]{1,0:T(8,128)(2,1)S(1)}, bf16[464,128]{1,0:T(8,128)(2,1)S(1)}, u32[]{:S(2)}, u32[]{:S(2)}) collective-permute-start(bf16[464,128]{1,0:T(8,128)(2,1)S(1)} %get-tuple-element.112), channel_id=1, source_target_pairs={{0,1},{1,0},{2,3},{3,2},{4,5},{5,4},{6,7},{7,6},{8,9},{9,8},{10,11... | collective-permute-start | bytes 356360 | tf_op jit(solution)/shard_map/ppermute | solution.py:809
  66.1 12.6 %collective-permute-start.14 = (bf16[464,128]{1,0:T(8,128)(2,1)S(1)}, bf16[464,128]{1,0:T(8,128)(2,1)S(1)}, u32[]{:S(2)}, u32[]{:S(2)}) collective-permute-start(bf16[464,128]{1,0:T(8,128)(2,1)S(1)} %get-tuple-element.113), channel_id=1, source_target_pairs={{0,2},{1,3},{2,0},{3,1},{4,6},{5,7},{6,4},{7,5},{8,10},{9,11},{10,... | collective-permute-start | bytes 356360 | tf_op jit(solution)/shard_map/ppermute | solution.py:809
  67.4 11.3 %collective-permute-start.15 = (bf16[464,128]{1,0:T(8,128)(2,1)S(1)}, bf16[464,128]{1,0:T(8,128)(2,1)S(1)}, u32[]{:S(2)}, u32[]{:S(2)}) collective-permute-start(bf16[464,128]{1,0:T(8,128)(2,1)S(1)} %get-tuple-element.114), channel_id=1, source_target_pairs={{0,3},{1,2},{2,1},{3,0},{4,7},{5,6},{6,5},{7,4},{8,11},{9,10},{10,... | collective-permute-start | bytes 356360 | tf_op jit(solution)/shard_map/ppermute | solution.py:809
  78.8 20.7 %copy-start.2 = (f32[456,256]{1,0:T(8,128)S(1)}, f32[456,256]{1,0:T(8,128)}, u32[]{:S(2)}) copy-start(f32[456,256]{1,0:T(8,128)} %params_ref.1) | copy-start | bytes 1400836
  78.8 20.7 %copy-start.3 = (f32[456,256]{1,0:T(8,128)S(1)}, f32[456,256]{1,0:T(8,128)}, u32[]{:S(2)}) copy-start(f32[456,256]{1,0:T(8,128)} %first_ref.1) | copy-start | bytes 1400836
  78.8 20.7 %copy-start.4 = (f32[456,256]{1,0:T(8,128)S(1)}, f32[456,256]{1,0:T(8,128)}, u32[]{:S(2)}) copy-start(f32[456,256]{1,0:T(8,128)} %second_ref.1) | copy-start | bytes 1400836
  78.8 20.7 %copy-start.5 = (f32[456,256]{1,0:T(8,128)S(1)}, f32[456,256]{1,0:T(8,128)}, u32[]{:S(2)}) copy-start(f32[456,256]{1,0:T(8,128)} %averaged_ref.1) | copy-start | bytes 1400836
  78.8 4.9 %collective-permute-start.16 = (bf16[464,128]{1,0:T(8,128)(2,1)S(1)}, bf16[464,128]{1,0:T(8,128)(2,1)S(1)}, u32[]{:S(2)}, u32[]{:S(2)}) collective-permute-start(bf16[464,128]{1,0:T(8,128)(2,1)S(1)} %gathered.1.mine_ref), channel_id=1, source_target_pairs={{0,8},{4,12},{8,0},{12,4},{16,24},{20,28},{24,16},{28,20},{1,9},{5... | collective-permute-start | bytes 356360 | tf_op jit(solution)/shard_map/ppermute | solution.py:809
  83.8 4.9 %collective-permute-start.17 = (bf16[464,128]{1,0:T(8,128)(2,1)S(1)}, bf16[464,128]{1,0:T(8,128)(2,1)S(1)}, u32[]{:S(2)}, u32[]{:S(2)}) collective-permute-start(bf16[464,128]{1,0:T(8,128)(2,1)S(1)} %add.6.mine_ref), channel_id=1, source_target_pairs={{0,16},{4,20},{8,24},{12,28},{16,0},{20,4},{24,8},{28,12},{1,17},{... | collective-permute-start | bytes 356360 | tf_op jit(solution)/shard_map/ppermute | solution.py:809
  89.4 1.6 %collective-permute-start.18 = (f32[472,128]{1,0:T(8,128)S(1)}, f32[472,128]{1,0:T(8,128)S(1)}, u32[]{:S(2)}, u32[]{:S(2)}) collective-permute-start(f32[472,128]{1,0:T(8,128)S(1)} %finish.1.mine_ref), channel_id=1, source_target_pairs={{0,4},{4,0},{8,12},{12,8},{16,20},{20,16},{24,28},{28,24},{1,5},{5... | collective-permute-start | bytes 725000 | tf_op jit(solution)/shard_map/ppermute | solution.py:809
  89.4 8.7 %collective-permute-start.21 = (bf16[512,256]{1,0:T(8,128)(2,1)S(1)}, bf16[512,256]{1,0:T(8,128)(2,1)S(1)}, u32[]{:S(2)}, u32[]{:S(2)}) collective-permute-start(bf16[512,256]{1,0:T(8,128)(2,1)S(1)} %get-tuple-element.119), channel_id=1, source_target_pairs={{0,4},{4,0},{8,12},{12,8},{16,20},{20,16},{24,28},{28,24},{1,5},{5... | collective-permute-start | bytes 786440 | tf_op jit(solution)/shard_map/ppermute | solution.py:809
  89.9 9.3 %collective-permute-start.22 = (bf16[512,256]{1,0:T(8,128)(2,1)S(1)}, bf16[512,256]{1,0:T(8,128)(2,1)S(1)}, u32[]{:S(2)}, u32[]{:S(2)}) collective-permute-start(bf16[512,256]{1,0:T(8,128)(2,1)S(1)} %get-tuple-element.120), channel_id=1, source_target_pairs={{0,28},{4,8},{8,4},{12,16},{16,12},{20,24},{24,20},{28,0},{1,29},{... | collective-permute-start | bytes 786440 | tf_op jit(solution)/shard_map/ppermute | solution.py:814
  91.0 3.8 %collective-permute-start.19 = (f32[32,128]{1,0:T(8,128)S(1)}, f32[32,128]{1,0:T(8,128)S(1)}, u32[]{:S(2)}, u32[]{:S(2)}) collective-permute-start(f32[32,128]{1,0:T(8,128)S(1)} %pad_maximum_fusion), channel_id=1, source_target_pairs={{0,1},{1,0},{2,3},{3,2},{4,5},{5,4},{6,7},{7,6},{8,9},{9,8},{10,11... | collective-permute-start | bytes 49160 | tf_op jit(solution)/shard_map/ppermute | solution.py:809
  94.9 4.6 %collective-permute-start.20 = (f32[32,128]{1,0:T(8,128)S(1)}, f32[32,128]{1,0:T(8,128)S(1)}, u32[]{:S(2)}, u32[]{:S(2)}) collective-permute-start(f32[32,128]{1,0:T(8,128)S(1)} %fusion.stats_ref), channel_id=1, source_target_pairs={{0,2},{1,3},{2,0},{3,1},{4,6},{5,7},{6,4},{7,5},{8,10},{9,11},{10,... | collective-permute-start | bytes 49160 | tf_op jit(solution)/shard_map/ppermute | solution.py:809

commit v5 on v4

--- a/solution.py
+++ b/solution.py
@@ -18,7 +18,7 @@
 
 LANES = 128
 TINY = 1e-20
-STEPS = 22
+STEPS = 18
 LOG_TWO = 0.6931471805599453
 TILE = 2048
 B16 = jnp.bfloat16
@@ -80,27 +80,28 @@
     return jnp.where(index_row == node, 1.0, 0.0).astype(B16)
 
 
+def core_of(e):
+    return e % 2
+
+
+def odd_core():
+    return core_of(lax.axis_index("edge")) == 1
+
+
 def prologue_kernel(
-    params_hbm, send_hbm, recv_hbm, latents_hbm, half_ref, place_ref, send_ref, recv_ref, latents_ref,
-    wide_ref, in_ref, sem, *, nodes, shares, owner,
+    params_hbm, send_hbm, recv_hbm, latents_hbm, half_ref, send_ref, recv_ref, latents_ref, wide_ref, in_ref, sem,
+    *, nodes,
 ):
-    e, f = lax.axis_index("edge"), lax.axis_index("feat")
-    core = e % 2
-    lanes = pl.ds(pl.multiple_of(core * LANES, LANES), LANES)
     copies = [
-        pltpu.make_async_copy(params_hbm.at[:, lanes], wide_ref, sem.at[0]),
+        pltpu.make_async_copy(params_hbm, wide_ref, sem.at[0]),
         pltpu.make_async_copy(send_hbm, in_ref.at[0], sem.at[1]),
         pltpu.make_async_copy(recv_hbm, in_ref.at[1], sem.at[2]),
         pltpu.make_async_copy(latents_hbm, latents_ref, sem.at[3]),
     ]
     for copy in copies:
         copy.start()
-    place_ref[0] = core
-    place_ref[1] = e
-    place_ref[2] = f
-    place_ref[3] = jnp.where(f == owner, 1, 0)
-    for k in range(shares):
-        place_ref[4 + k] = jnp.bitwise_xor(f, k)
+    e = lax.axis_index("edge")
+    core = core_of(e)
     for i, out_ref in ((0, send_ref), (1, recv_ref)):
         copies[1 + i].wait()
         index = in_ref[i]
@@ -108,29 +109,30 @@
         slot = jnp.where(block == e, 0, jnp.where(block == e + 1 - 2 * core, 1, 2))
         out_ref[...] = (slot - block) * nodes + index
     copies[0].wait()
-    half_ref[...] = wide_ref[...].astype(B16)
+    half_ref[...] = jnp.where(core == 1, wide_ref[:, LANES : 2 * LANES], wide_ref[:, 0:LANES]).astype(B16)
     copies[3].wait()
 
 
-def prologue(params, senders, receivers, latents, shares, owner):
+def prologue(params, senders, receivers, latents):
     shape = (senders.size // LANES, LANES)
     out = jax.ShapeDtypeStruct(shape, I32)
     vmem, hbm = pl.BlockSpec(memory_space=pltpu.VMEM), pl.BlockSpec(memory_space=pltpu.HBM)
-    half, place, send, recv, own = pl.pallas_call(
-        functools.partial(prologue_kernel, nodes=latents.shape[0], shares=shares, owner=owner),
+    operands = (params, senders.reshape(shape), receivers.reshape(shape), latents)
+    half, send, recv, own = pl.pallas_call(
+        functools.partial(prologue_kernel, nodes=latents.shape[0]),
         in_specs=[hbm] * 4,
-        out_specs=[vmem, pl.BlockSpec(memory_space=pltpu.SMEM), vmem, vmem, vmem],
+        out_specs=[vmem] * 4,
         out_shape=[
-            jax.ShapeDtypeStruct((params.shape[0], LANES), B16), jax.ShapeDtypeStruct((4 + shares,), I32), out, out,
+            jax.ShapeDtypeStruct((params.shape[0], LANES), B16), out, out,
             jax.ShapeDtypeStruct(latents.shape, latents.dtype),
         ],
         scratch_shapes=[
-            pltpu.VMEM((params.shape[0], LANES), F32), pltpu.VMEM((2, *shape), I32), pltpu.SemaphoreType.DMA((4,)),
+            pltpu.VMEM(params.shape, F32), pltpu.VMEM((2, *shape), I32), pltpu.SemaphoreType.DMA((4,)),
         ],
         compiler_params=PARAMS,
         name="prologue",
-    )(*(pltpu.with_memory_space_constraint(a, pltpu.HBM) for a in (params, senders.reshape(shape), receivers.reshape(shape), latents)))
-    return half, place, send.reshape(-1), recv.reshape(-1), own
+    )(*(pltpu.with_memory_space_constraint(a, pltpu.HBM) for a in operands))
+    return half, send.reshape(-1), recv.reshape(-1), own
 
 
 def gather_near_kernel(index_ref, own_ref, pair_ref, out_ref):
@@ -212,54 +214,56 @@
 
 def encoded(values):
     rows, width = values.shape
-    half = width // 2
+    quarter = rows // 4
     largest = jnp.maximum(jnp.max(jnp.abs(values), axis=-1, keepdims=True), TINY)
     exponents = jnp.ceil(jnp.log(largest) * (1.0 / LOG_TWO))
     codes = jnp.round(values * power_of_two(STEPS - exponents)).astype(I32)
-    upper = lax.shift_right_arithmetic(codes, 8)
-    lower = jnp.bitwise_and(codes, 255)
-    words = lax.shift_left(lower[:, :half], 8) + lower[:, half:] - 32768
+    upper = lax.shift_right_arithmetic(codes, 4)
+    words = jnp.full((quarter, width), -32768, I32)
+    for i in range(4):
+        words = words + lax.shift_left(jnp.bitwise_and(codes[i * quarter : (i + 1) * quarter, :], 15), 4 * i)
     marks = [
         jnp.broadcast_to(exponents[g * LANES : (g + 1) * LANES, :], (LANES, LANES)).T[0:1, :]
         for g in range(rows // LANES)
     ]
     marks = jnp.concatenate([*marks, jnp.zeros((16 - len(marks), LANES), F32)], axis=0).astype(I32)
-    marks = jnp.concatenate([marks, jnp.zeros((16, width + half - LANES), I32)], axis=1)
-    return jnp.concatenate([jnp.concatenate([upper, words], axis=1), marks], axis=0).astype(I16)
+    marks = jnp.concatenate([marks, jnp.zeros((16, width - LANES), I32)], axis=1)
+    return jnp.concatenate([upper, words, marks], axis=0).astype(I16)
 
 
 def decoded(wire):
-    rows, width = wire.shape[0] - 16, wire.shape[1] * 2 // 3
-    half = width // 2
+    width = wire.shape[1]
+    quarter = (wire.shape[0] - 16) // 5
+    rows = 4 * quarter
     wire = wire.astype(I32)
-    words = wire[:rows, width:] + 32768
-    lower = jnp.concatenate([lax.shift_right_arithmetic(words, 8), jnp.bitwise_and(words, 255)], axis=1)
-    codes = (wire[:rows, :width] * 256 + lower).astype(F32)
-    exponents = wire[rows:, :LANES].astype(F32)
+    words = wire[rows : rows + quarter, :] + 32768
+    lower = jnp.concatenate([jnp.bitwise_and(lax.shift_right_arithmetic(words, 4 * i), 15) for i in range(4)], axis=0)
+    codes = (wire[:rows, :] * 16 + lower).astype(F32)
+    exponents = wire[rows + quarter :, :LANES].astype(F32)
     scale = [power_of_two(column(exponents[g : g + 1, :]) - STEPS) for g in range(rows // LANES)]
     return codes * jnp.concatenate([jnp.concatenate(scale, axis=0)] * (width // LANES), axis=1)
 
 
 def edge_forward_kernel(
-    place_ref, region_ref, recv_row_ref, hs_ref, hr_ref, x_ref, *refs,
+    region_ref, recv_row_ref, hs_ref, hr_ref, x_ref, *refs,
 ):
     pieces, refs = refs[:-5], refs[-5:]
     w_ref, high_ref, low_ref, halo_ref, wide_ref = refs
     step = pl.program_id(0)
     rows = x_ref.shape[0]
     width = x_ref.shape[1]
-    nodes = halo_ref.shape[0] - 16
+    nodes = (halo_ref.shape[0] - 16) // 5 * 4
     steps = pl.num_programs(0)
 
     @pl.when(step == 0)
     def _():
-        odd = place_ref[0] == 1
+        odd, f = odd_core(), lax.axis_index("feat")
         share = pieces[0].shape[0]
         for k in range(w_ref.shape[0] // share):
             rows = slice((k - 1) * share, k * share)
             mine, other = (pieces[i][...] if k == 0 else pieces[i + 1][rows, :] for i in (0, 2))
             mine, other = mine.astype(F32), other.astype(F32)
-            base = pl.multiple_of(place_ref[4 + k] * share, 8)
+            base = pl.multiple_of(jnp.bitwise_xor(f, k) * share, 8)
             wide_ref[pl.ds(base, share), 0:LANES] = jnp.where(odd, other, mine)
             wide_ref[pl.ds(base, share), LANES : 2 * LANES] = jnp.where(odd, mine, other)
         w_ref[...] = wide_ref[...].astype(B16)
@@ -279,25 +283,25 @@
         halo_ref[...] = encoded(dot(onehot, high_ref[...]) + dot(onehot, low_ref[...]))
 
 
-def edge_forward(place, regions, recv, hs, hr, edges, pieces, total, nodes):
+def edge_forward(regions, recv, hs, hr, edges, pieces, total, nodes):
     count, width = edges.shape
     tile = tiled(TILE, width)
     return pl.pallas_call(
         edge_forward_kernel,
         grid=(count // TILE,),
         in_specs=[
-            pl.BlockSpec(memory_space=pltpu.SMEM), whole((count // LANES, LANES)), whole((1, count)), tile, tile, tile,
+            whole((count // LANES, LANES)), whole((1, count)), tile, tile, tile,
             *[whole(piece.shape) for piece in pieces],
         ],
         out_specs=[
             whole((total, width)), whole((count, width)), whole((count, width)),
-            whole((nodes + 16, width + width // 2)),
+            whole((nodes + nodes // 4 + 16, width)),
         ],
         out_shape=[
             jax.ShapeDtypeStruct((total, width), B16),
             jax.ShapeDtypeStruct((count, width), B16),
             jax.ShapeDtypeStruct((count, width), B16),
-            jax.ShapeDtypeStruct((nodes + 16, width + width // 2), I16),
+            jax.ShapeDtypeStruct((nodes + nodes // 4 + 16, width), I16),
         ],
         scratch_shapes=[pltpu.VMEM((total, width), F32)],
         compiler_params=PARAMS,
@@ -306,7 +310,7 @@
             flops=2 * count * width * (5 * width + 2 * nodes), transcendentals=2 * count * width,
             bytes_accessed=count * width * 10,
         ),
-    )(place, regions.reshape(-1, LANES), recv.reshape(1, -1), hs, hr, edges, *pieces)
+    )(regions.reshape(-1, LANES), recv.reshape(1, -1), hs, hr, edges, *pieces)
 
 
 def edge_slope_kernel(region_ref, hs_ref, hr_ref, x_ref, w_ref, hidden_ref, slope_ref):
@@ -471,7 +475,7 @@
 
 
 def edge_backward_kernel(
-    place_ref, recv_ref, region_row_ref, off_ref, near_ref, hs_ref, hr_ref, x_ref, hidden_ref, slope_ref, unit_ref,
+    recv_ref, region_row_ref, off_ref, near_ref, hs_ref, hr_ref, x_ref, hidden_ref, slope_ref, unit_ref,
     inverse_ref, w_ref, node_grad_ref, node_sum_ref,
     d_pre_ref, kept_ref, sent_ref,
     d_inner_ref, vec_acc_ref,
@@ -508,7 +512,7 @@
 
     @pl.when(step == steps - 1)
     def _():
-        odd = place_ref[0] == 1
+        odd = odd_core()
 
         def put(start, piece):
             left, right = piece[:, 0:LANES], piece[:, LANES:]
@@ -539,7 +543,7 @@
 
 
 def edge_backward(
-    place, recv, regions, off, near, hs, hr, edges, hidden, slope, unit, inverse, weights, node_grad, node_sum,
+    recv, regions, off, near, hs, hr, edges, hidden, slope, unit, inverse, weights, node_grad, node_sum,
 ):
     count, width = edges.shape
     tile, full = tiled(TILE, width), whole((count, width))
@@ -549,7 +553,7 @@
         edge_backward_kernel,
         grid=(count // TILE,),
         in_specs=[
-            pl.BlockSpec(memory_space=pltpu.SMEM), whole((count // LANES, LANES)), whole((1, count)),
+            whole((count // LANES, LANES)), whole((1, count)),
             whole(off.shape), tile, full, full, full, full, tile, tile, tiled(TILE, LANES),
             whole(weights.shape), whole(node_grad.shape), whole(node_sum.shape),
         ],
@@ -566,7 +570,7 @@
             flops=2 * count * width * (6 * width + off.shape[0]), transcendentals=0, bytes_accessed=count * width * 20
         ),
     )(
-        place, recv.reshape(-1, LANES), regions.reshape(1, -1), off, near, hs, hr, edges, hidden, slope, unit, inverse,
+        recv.reshape(-1, LANES), regions.reshape(1, -1), off, near, hs, hr, edges, hidden, slope, unit, inverse,
         weights, node_grad, node_sum,
     )
 
@@ -668,23 +672,21 @@
     return jnp.concatenate([values[:first, :], exact, values[first + 8 : share, :]], axis=0)
 
 
-def parted_kernel(place_ref, mine_ref, other_ref, kept_ref, *sent_refs, share, first):
+def parted_kernel(mine_ref, other_ref, kept_ref, *sent_refs, share, first):
     for k, out_ref in enumerate((kept_ref, *sent_refs)):
-        rows = pl.ds(pl.multiple_of(place_ref[4 + k] * share, 8), share)
+        rows = pl.ds(pl.multiple_of(jnp.bitwise_xor(lax.axis_index("feat"), k) * share, 8), share)
         total = mine_ref[rows, :] + other_ref[rows, :]
         out_ref[...] = packed(total, first) if k else total
 
 
-def parted(place, mine, other, share, first):
-    vmem = pl.BlockSpec(memory_space=pltpu.VMEM)
+def parted(mine, other, share, first):
     sent = jax.ShapeDtypeStruct((share + 8, LANES), B16)
     return pl.pallas_call(
         functools.partial(parted_kernel, share=share, first=first),
-        in_specs=[pl.BlockSpec(memory_space=pltpu.SMEM), vmem, vmem],
         out_shape=[jax.ShapeDtypeStruct((share, LANES), F32)] + [sent] * (mine.shape[0] // share - 1),
         compiler_params=PARAMS,
         name="parted",
-    )(place, mine, other)
+    )(mine, other)
 
 
 def gathered_kernel(mine_ref, *refs, first):
@@ -716,33 +718,32 @@
     )(mine, other)
 
 
-def finish_kernel(place_ref, mine_ref, other_ref, out_ref, *, first):
+def finish_kernel(mine_ref, other_ref, out_ref, *, first, owner):
     share = out_ref.shape[0] - 16
     part = unpacked(mine_ref[...], first) + unpacked(other_ref[...], first)
     out_ref[0:share, :] = part
-    out_ref[share : share + 8, :] = jnp.where(place_ref[3] == 1, part[first : first + 8, :], 0.0)
+    out_ref[share : share + 8, :] = jnp.where(lax.axis_index("feat") == owner, part[first : first + 8, :], 0.0)
     squares = jnp.sum(jnp.sum(part * part, axis=0, keepdims=True), axis=1, keepdims=True)
     out_ref[share + 8 : share + 16, :] = jnp.broadcast_to(squares, (8, LANES))
 
 
-def finish(place, mine, other, share, first):
-    return pl.pallas_call(
-        functools.partial(finish_kernel, first=first),
-        in_specs=[pl.BlockSpec(memory_space=pltpu.SMEM)] + [pl.BlockSpec(memory_space=pltpu.VMEM)] * 2,
+def finish(mine, other, share, first, owner):
+    return pl.pallas_call(
+        functools.partial(finish_kernel, first=first, owner=owner),
         out_shape=jax.ShapeDtypeStruct((share + 16, LANES), F32),
         compiler_params=PARAMS,
         name="finish",
-    )(place, mine, other)
+    )(mine, other)
 
 
 def adam_kernel(
-    place_ref, step_ref, stats_ref, more_ref, mine_ref, other_ref, params_ref, first_ref, second_ref, averaged_ref,
+    step_ref, stats_ref, more_ref, mine_ref, other_ref, params_ref, first_ref, second_ref, averaged_ref,
     own_ref, pair_ref, off_ref,
     new_first_hbm, new_second_hbm, new_params_hbm, new_average_hbm, norm_ref, vector_ref, latents_hbm,
     new_first_ref, new_second_ref, new_params_ref, new_average_ref, latents_ref, sem,
 ):
     share = params_ref.shape[0]
-    odd = place_ref[0] == 1
+    odd = odd_core()
     latents_ref[...] = own_ref[...] + pair_ref[...].astype(F32) + off_ref[...].astype(F32)
     copies = [pltpu.make_async_copy(latents_ref, latents_hbm, sem.at[0])]
     copies[0].start()
@@ -750,7 +751,7 @@
     norm = jnp.sqrt(stats[8:9, 0:1] + stats[24:25, 0:1])
     norm_ref[...] = norm
     factor = jnp.minimum(1.0, MAX_NORM / (norm + 1e-06))
-    count = jnp.full((1, 1), step_ref[0], F32)
+    count = step_ref[0:1, 0:1]
     first_scale = 1.0 - jnp.exp(count * jnp.log(jnp.full((1, 1), BETA_ONE, F32)))
     second_scale = 1.0 - jnp.exp(count * jnp.log(jnp.full((1, 1), BETA_TWO, F32)))
     decay = jnp.minimum(AVERAGE_DECAY, (1.0 + count) / (10.0 + count))
@@ -784,12 +785,12 @@
         copy.wait()
 
 
-def adam(place, step, stats, more, mine, other, params, first_moment, second_moment, averaged, own, pair, off):
+def adam(step, stats, more, mine, other, params, first_moment, second_moment, averaged, own, pair, off):
     rows = jax.ShapeDtypeStruct(params.shape, F32)
-    smem, vmem, hbm = (pl.BlockSpec(memory_space=m) for m in (pltpu.SMEM, pltpu.VMEM, pltpu.HBM))
+    vmem, hbm = (pl.BlockSpec(memory_space=m) for m in (pltpu.VMEM, pltpu.HBM))
     return pl.pallas_call(
         adam_kernel,
-        in_specs=[smem, smem] + [vmem] * 11,
+        in_specs=[vmem] * 12,
         out_specs=[hbm] * 4 + [vmem] * 2 + [hbm],
         out_shape=[
             rows, rows, rows, rows, jax.ShapeDtypeStruct((1, 1), F32), jax.ShapeDtypeStruct((8, params.shape[1]), F32),
@@ -802,7 +803,7 @@
         cost_estimate=pl.CostEstimate(
             flops=20 * params.size, transcendentals=2 * params.size, bytes_accessed=params.size * 32
         ),
-    )(place, step, stats, more, mine, other, params, first_moment, second_moment, averaged, own, pair, off)
+    )(jnp.broadcast_to(step.astype(F32), (8, LANES)), stats, more, mine, other, params, first_moment, second_moment, averaged, own, pair, off)
 
 
 def flipped(value, axis, bit):
@@ -834,7 +835,7 @@
 
     pair, off = neighbours(latents)
 
-    mine, place, send, recv, latents = prologue(params, senders, receivers, latents, feats, vector_row // share)
+    mine, send, recv, latents = prologue(params, senders, receivers, latents)
     fetched = [mine] + [flipped(mine, "feat", k) for k in range(1, feats)]
 
     near_send = gather_near(send, latents, pair)
@@ -843,7 +844,7 @@
     pieces = [fetched[0], others, flipped(fetched[0], "edge", 1), flipped(others, "edge", 1)]
     hs = gather_off(send, off, near_send)
     hr = gather_off(recv, off, near_recv)
-    weights, high, low, to_off = edge_forward(place, regions, recv, hs, hr, edges, pieces, total, nodes)
+    weights, high, low, to_off = edge_forward(regions, recv, hs, hr, edges, pieces, total, nodes)
     from_off = across(to_off, "edge")
     to_pair, more, own = near_sum(recv, high, low, nodes)
     from_pair, more = flipped(to_pair, "edge", 1), flipped(more, "edge", 1)
@@ -860,11 +861,11 @@
     unit, inverse = edge_unit(lax.optimization_barrier((hidden, d_agg))[0], weights)
 
     d_pre, kept, sent = edge_backward(
-        place, recv, regions, back_off, near, hs, hr, edges, hidden, slope, unit, inverse, weights, node_grad, node_sum,
+        recv, regions, back_off, near, hs, hr, edges, hidden, slope, unit, inverse, weights, node_grad, node_sum,
     )
 
     low_rows = vector_row % share
-    part, *sent = parted(place, kept, flipped(sent, "edge", 1), share, low_rows)
+    part, *sent = parted(kept, flipped(sent, "edge", 1), share, low_rows)
     came = [flipped(wire, "feat", k + 1) for k, wire in enumerate(sent)]
     d_pre, part = lax.optimization_barrier((d_pre, part))
     send_part = sender_part(send, d_pre, weights, nodes)
@@ -877,7 +878,7 @@
         bit *= 2
     grad_edges = edge_grads(d_pre, weights)
     wire, part_pair, part_off, grad_edges = lax.optimization_barrier((wire, part_pair, part_off, grad_edges))
-    mine = finish(place, wire, flipped(wire, "edge", bit), share, low_rows)
+    mine = finish(wire, flipped(wire, "edge", bit), share, low_rows, vector_row // share)
     grads_off = across(part_off, "edge")
     grads_pair = flipped(part_pair, "edge", 1)
 
@@ -889,7 +890,7 @@
         bit *= 2
     more = flipped(stats, "feat", bit)
     new_first, new_second, new_params, new_average, grad_norm, vector_grads, grad_latents = adam(
-        place, step, stats, more, mine, other, params, first_moment, second_moment, averaged,
+        step, stats, more, mine, other, params, first_moment, second_moment, averaged,
         part_own, grads_pair, grads_off,
     )
     return (

time: 103 us -> 97.8 us (0.950)
  Pallas kernels: 56.4 us -> 53 us
  waiting for transfers between devices: 18 us -> 16.5 us
    pallas_call x5, Pallas kernels: 21.7 us -> 19 us  [the longest x1 7.85 us: edge_forward(): pl.pallas_call(edge_forward_kernel, grid=(count // TILE,), in_specs=[whol...]
    ppermute x4, waiting for transfers between devices: 4.82 us -> 3.31 us  [across(): lax.ppermute(value, axis, [(i, (i + 1 if i % 2 else i - 1) % count) for i...]
  transfers between devices with their start and end apart: 23 -> 23, of which waited for: 9 -> 9; matrix products, arithmetic and copies ran while one was open for 0% -> 0% of each run, Pallas kernels for 34% -> 35%
where the time goes in v5:
time: 97.8 us; the launch traced here: 97.7 us
  Pallas kernels  53 us (54%)
  starting transfers between devices  26 us (27%)
  waiting for transfers between devices  16.5 us (17%)
  between operations  1.78 us (2%)
    ppermute x19, starting transfers between devices, flipped(): lax.ppermute(value, axis, [(i, i ^ bit) for i in range(lax.axis_size(axis...  19 us
    ppermute x19, waiting for transfers between devices, flipped(): lax.ppermute(value, axis, [(i, i ^ bit) for i in range(lax.axis_size(axis...  13.2 us
    pallas_call x1, Pallas kernels, edge_forward(): pl.pallas_call(edge_forward_kernel, grid=(count // TILE,), in_specs=[whol...  7.85 us
    pallas_call x1, Pallas kernels, edge_backward(): pl.pallas_call(edge_backward_kernel, grid=(count // TILE,), in_specs=[who...  7.49 us
    pallas_call x3, Pallas kernels, gather_near(): pl.pallas_call(gather_near_kernel, grid=(1,), in_specs=[whole((edges // L...  7.24 us
    ppermute x4, starting transfers between devices, across(): lax.ppermute(value, axis, [(i, (i + 1 if i % 2 else i - 1) % count) for i...  7.06 us
    pallas_call x1, Pallas kernels, receiver_part(): pl.pallas_call(receiver_part_kernel, grid=(3,), in_specs=[whole((1, count...  5.1 us
    pallas_call x1, Pallas kernels, sender_part(): pl.pallas_call(sender_part_kernel, grid=(3,), in_specs=[whole((1, count))...  4.96 us
  transfers between devices with their start and end apart: 23, of which 9 were waited for; matrix products, arithmetic and copies ran while one was open for 0% of the time, Pallas kernels for 35%

profile of v5, /device:TPU:0, one launch (start us, length us, event | category | flops | bytes accessed | tf_op | source)
XLA Modules:
  0.0 97.7 jit_solution(16963107867071946481)
XLA Ops:
  0.6 0.5 collective-permute-start.1
  1.2 1.2 %prologue.1 = (bf16[456,128]{1,0:T(8,128)(2,1)S(1)}, s32[32,128]{1,0:T(8,128)S(1)}, s32[32,128]{1,0:T(8,128)S(1)}, bf16[512,256]{1,0:T(8,128)(2,1)S(1)}) custom-call(f32[456,256]{1,0:T(8,128)} %params_ref.1, s32[32,128]{1,0:T(8,128)} %bitcast.33, s32[32,128]{1,0:T(8,128)} %bitcast.34, bf16[512,256]{1,0:T(8,128)(2,1)} %bitcast.31), custom_call_target="tpu_custom_call" | custom-call | tf_op jit(solution)/shard_map/prologue/pallas_call | solution.py:121
  2.3 2.7 %collective-permute-start.2 = (bf16[456,128]{1,0:T(8,128)(2,1)S(1)}, bf16[456,128]{1,0:T(8,128)(2,1)S(1)}, u32[]{:S(2)}, u32[]{:S(2)}) collective-permute-start(bf16[456,128]{1,0:T(8,128)(2,1)S(1)} %get-tuple-element.71.refs_0_), channel_id=1, source_target_pairs={{0,1},{1,0},{2,3},{3,2},{4,5},{5,4},{6,7},{7,6},{8,9},{9,8},{10,11... | collective-permute-start | bytes 350216 | tf_op jit(solution)/shard_map/ppermute | solution.py:810
  5.0 2.6 %collective-permute-start.3 = (bf16[456,128]{1,0:T(8,128)(2,1)S(1)}, bf16[456,128]{1,0:T(8,128)(2,1)S(1)}, u32[]{:S(2)}, u32[]{:S(2)}) collective-permute-start(bf16[456,128]{1,0:T(8,128)(2,1)S(1)} %get-tuple-element.71.refs_0_), channel_id=1, source_target_pairs={{0,2},{1,3},{2,0},{3,1},{4,6},{5,7},{6,4},{7,5},{8,10},{9,11},{10,... | collective-permute-start | bytes 350216 | tf_op jit(solution)/shard_map/ppermute | solution.py:810
  7.6 2.0 %collective-permute-start = (bf16[512,256]{1,0:T(8,128)(2,1)}, bf16[512,256]{1,0:T(8,128)(2,1)S(1)}, u32[]{:S(2)}, u32[]{:S(2)}) collective-permute-start(bf16[512,256]{1,0:T(8,128)(2,1)} %bitcast.32), channel_id=1, source_target_pairs={{0,28},{4,8},{8,4},{12,16},{16,12},{20,24},{24,20},{28,0},{1,29},{... | collective-permute-start | bytes 786440 | tf_op jit(solution)/shard_map/ppermute | solution.py:815
  9.6 0.0 collective-permute-done.1.pair_ref
  9.6 2.4 %gather_near.4.near_ref = bf16[4096,256]{1,0:T(8,128)(2,1)S(1)} custom-call(s32[32,128]{1,0:T(8,128)S(1)} %get-tuple-element.69.index_ref.recv_ref, bf16[512,256]{1,0:T(8,128)(2,1)S(1)} %get-tuple-element.68.own_ref.h_ref, bf16[512,256]{1,0:T(8,128)(2,1)S(1)} %collective-permute-done.1.pair_ref), custom_call_target="tpu_custom_call" | custom-call | flops 2147483648 | bytes 2097152 | tf_op jit(solution)/shard_map/gather_near/pallas_call | solution.py:150
  12.0 2.4 %gather_near.3.near_ref = bf16[4096,256]{1,0:T(8,128)(2,1)S(1)} custom-call(s32[32,128]{1,0:T(8,128)S(1)} %get-tuple-element.70.index_ref, bf16[512,256]{1,0:T(8,128)(2,1)S(1)} %get-tuple-element.68.own_ref.h_ref, bf16[512,256]{1,0:T(8,128)(2,1)S(1)} %collective-permute-done.1.pair_ref), custom_call_target="tpu_custom_call" | custom-call | flops 2147483648 | bytes 2097152 | tf_op jit(solution)/shard_map/gather_near/pallas_call | solution.py:150
  14.4 0.0 collective-permute-done.2
  14.4 2.6 %collective-permute-done.3 = bf16[456,128]{1,0:T(8,128)(2,1)S(1)} collective-permute-done((bf16[456,128]{1,0:T(8,128)(2,1)S(1)}, bf16[456,128]{1,0:T(8,128)(2,1)S(1)}, u32[]{:S(2)}, u32[]{:S(2)}) %collective-permute-start.3) | collective-permute-done | bytes 116768 | tf_op jit(solution)/shard_map/ppermute | solution.py:810
  17.0 0.0 collective-permute-done.4
  17.0 0.1 collective-permute-start.6
  17.1 0.5 collective-permute-start.5
  17.6 1.3 %gather_off.3.hr_ref = bf16[4096,256]{1,0:T(8,128)(2,1)S(1)} custom-call(s32[32,128]{1,0:T(8,128)S(1)} %get-tuple-element.69.index_ref.recv_ref, bf16[512,256]{1,0:T(8,128)(2,1)S(1)} %collective-permute-done.off_ref, bf16[4096,256]{1,0:T(8,128)(2,1)S(1)} %gather_near.4.near_ref), custom_call_target="tpu_custom_call" | custom-call | flops 1073741824 | bytes 4194304 | tf_op jit(solution)/shard_map/gather_off/pallas_call | solution.py:175
  18.9 0.0 copy-start.1
  18.9 0.0 copy-start.6
  18.9 1.3 %gather_off.2.hs_ref = bf16[4096,256]{1,0:T(8,128)(2,1)S(1)} custom-call(s32[32,128]{1,0:T(8,128)S(1)} %get-tuple-element.70.index_ref, bf16[512,256]{1,0:T(8,128)(2,1)S(1)} %collective-permute-done.off_ref, bf16[4096,256]{1,0:T(8,128)(2,1)S(1)} %gather_near.3.near_ref), custom_call_target="tpu_custom_call" | custom-call | flops 1073741824 | bytes 4194304 | tf_op jit(solution)/shard_map/gather_off/pallas_call | solution.py:175
  20.3 0.0 collective-permute-done.6.refs_3_
  20.3 0.2 copy-done.1
  20.5 7.8 %edge_forward.1 = (bf16[1824,256]{1,0:T(8,128)(2,1)S(1)}, bf16[4096,256]{1,0:T(8,128)(2,1)S(1)}, bf16[4096,256]{1,0:T(8,128)(2,1)S(1)}, s16[656,256]{1,0:T(8,128)(2,1)S(1)}) custom-call(s32[32,128]{1,0:T(8,128)S(1)} %bitcast.24, s32[1,4096]{1,0:T(1,128)S(1)} %bitcast.20, bf16[4096,256]{1,0:T(8,128)(2,1)S(1)} %gather_off.2.hs_ref, ...), custom_call_target="tpu_custom_call" | custom-call | flops 4831838208 | bytes 10485760 | tf_op jit(solution)/shard_map/edge_forward/pallas_call | solution.py:289
  28.4 2.2 %collective-permute-start.9 = (s16[656,256]{1,0:T(8,128)(2,1)S(1)}, s16[656,256]{1,0:T(8,128)(2,1)S(1)}, u32[]{:S(2)}, u32[]{:S(2)}) collective-permute-start(s16[656,256]{1,0:T(8,128)(2,1)S(1)} %get-tuple-element.84), channel_id=1, source_target_pairs={{0,28},{4,8},{8,4},{12,16},{16,12},{20,24},{24,20},{28,0},{1,29},{... | collective-permute-start | bytes 1007624 | tf_op jit(solution)/shard_map/ppermute | solution.py:815
  30.5 4.5 %near_sum.1 = (f32[256,256]{1,0:T(8,128)S(1)}, f32[256,256]{1,0:T(8,128)S(1)}, f32[512,256]{1,0:T(8,128)S(1)}) custom-call(s32[1,4096]{1,0:T(1,128)S(1)} %bitcast.21, bf16[4096,256]{1,0:T(8,128)(2,1)S(1)} %get-tuple-element.75.high_ref, bf16[4096,256]{1,0:T(8,128)(2,1)S(1)} %get-tuple-element.76.low_ref), custom_call_target="tpu_custom_call" | custom-call | flops 4294967296 | bytes 4194304 | tf_op jit(solution)/shard_map/near_sum/pallas_call | solution.py:374
  35.1 0.1 collective-permute-start.7
  35.1 0.5 collective-permute-start.8
  35.6 3.4 %edge_slope.1 = (bf16[4096,256]{1,0:T(8,128)(2,1)S(1)}, f32[4096,256]{1,0:T(8,128)S(1)}) custom-call(s32[32,128]{1,0:T(8,128)S(1)} %bitcast.25, bf16[4096,256]{1,0:T(8,128)(2,1)S(1)} %gather_off.2.hs_ref, bf16[4096,256]{1,0:T(8,128)(2,1)S(1)} %gather_off.3.hr_ref, bf16[4096,256]{1,0:T(8,128)(2,1)S(1)} %bitcast.18, bf16[1824,256]{1,0:T(8,128)(2,1)S(1)} %get-tuple-element.78.w_ref), custom_call_target="tpu_custom_call" | custom-call | flops 2147483648 | bytes 12582912 | tf_op jit(solution)/shard_map/edge_slope/pallas_call | solution.py:326
  39.0 0.0 collective-permute-done.8.more_ref
  39.0 0.2 collective-permute-done.9.off_ref
  39.2 1.2 %node_update.1 = (bf16[512,256]{1,0:T(8,128)(2,1)S(1)}, bf16[512,256]{1,0:T(8,128)(2,1)S(1)}, bf16[512,256]{1,0:T(8,128)(2,1)S(1)}, bf16[512,256]{1,0:T(8,128)(2...) custom-call(bf16[512,256]{1,0:T(8,128)(2,1)S(1)} %get-tuple-element.68.own_ref.h_ref, ...), custom_call_target="tpu_custom_call" | custom-call | flops 335544320 | bytes 2621440 | tf_op jit(solution)/shard_map/node_update/pallas_call | solution.py:427
  40.4 0.1 collective-permute-start.11
  40.5 1.8 %collective-permute-start.10 = (bf16[512,256]{1,0:T(8,128)(2,1)S(1)}, bf16[512,256]{1,0:T(8,128)(2,1)S(1)}, u32[]{:S(2)}, u32[]{:S(2)}) collective-permute-start(bf16[512,256]{1,0:T(8,128)(2,1)S(1)} %get-tuple-element.91.own_ref), channel_id=1, source_target_pairs={{0,28},{4,8},{8,4},{12,16},{16,12},{20,24},{24,20},{28,0},{1,29},{... | collective-permute-start | bytes 786440 | tf_op jit(solution)/shard_map/ppermute | solution.py:815
  42.3 1.3 %node_grads.1 = (f32[512,256]{1,0:T(8,128)}, f32[768,256]{1,0:T(8,128)S(1)}, f32[4,256]{1,0:T(4,128)S(1)}, f32[512,256]{1,0:T(8,128)S(1)}) custom-call(bf16[512,256]{1,0:T(8,128)(2,1)S(1)} %get-tuple-element.68.own_ref.h_ref, bf16[512,256]{1,0:T(8,128)(2,1)S(1)} %get-tuple-element.85.agg_ref, bf16[512,256]{1,0:T(8,128)(2,1)S(1)} %get-tuple-element.86.hidden_ref, ...), custom_call_target="tpu_custom_call" | custom-call | flops 268435456 | bytes 2359296 | tf_op jit(solution)/shard_map/node_grads/pallas_call | solution.py:466
  43.6 1.7 %edge_unit.1 = (f32[4096,256]{1,0:T(8,128)S(1)}, f32[4096,128]{1,0:T(8,128)S(1)}) custom-call(bf16[4096,256]{1,0:T(8,128)(2,1)S(1)} %get-tuple-element.94.hidden_ref, bf16[1824,256]{1,0:T(8,128)(2,1)S(1)} %get-tuple-element.78.w_ref), custom_call_target="tpu_custom_call" | custom-call | flops 536870912 | bytes 8388608 | tf_op jit(solution)/shard_map/edge_unit/pallas_call | solution.py:349
  45.3 0.0 collective-permute-done.11.pair_ref
  45.3 2.4 %gather_near.5.near_ref = bf16[4096,256]{1,0:T(8,128)(2,1)S(1)} custom-call(s32[32,128]{1,0:T(8,128)S(1)} %get-tuple-element.69.index_ref.recv_ref, bf16[512,256]{1,0:T(8,128)(2,1)S(1)} %get-tuple-element.91.own_ref, bf16[512,256]{1,0:T(8,128)(2,1)S(1)} %collective-permute-done.11.pair_ref), custom_call_target="tpu_custom_call" | custom-call | flops 2147483648 | bytes 2097152 | tf_op jit(solution)/shard_map/gather_near/pallas_call | solution.py:150
  47.7 2.1 %collective-permute-done.10.off_ref = bf16[512,256]{1,0:T(8,128)(2,1)S(1)} collective-permute-done((bf16[512,256]{1,0:T(8,128)(2,1)S(1)}, bf16[512,256]{1,0:T(8,128)(2,1)S(1)}, u32[]{:S(2)}, u32[]{:S(2)}) %collective-permute-start.10) | collective-permute-done | bytes 262176 | tf_op jit(solution)/shard_map/ppermute | solution.py:815
  49.8 7.5 %edge_backward.1 = (bf16[4096,256]{1,0:T(8,128)(2,1)S(1)}, f32[1824,128]{1,0:T(8,128)S(1)}, f32[1824,128]{1,0:T(8,128)S(1)}) custom-call(s32[32,128]{1,0:T(8,128)S(1)} %get-tuple-element.69.index_ref.recv_ref, s32[1,4096]{1,0:T(1,128)S(1)} %bitcast.26, bf16[512,256]{1,0:T(8,128)(2,1)S(1)} %collective-permute-done.10.off_ref, ...), custom_call_target="tpu_custom_call" | custom-call | flops 4294967296 | bytes 20971520 | tf_op jit(solution)/shard_map/edge_backward/pallas_call | solution.py:552
  57.3 0.2 collective-permute-start.12
  57.4 2.4 %collective-permute-done.12.other_ref = f32[1824,128]{1,0:T(8,128)S(1)} collective-permute-done((f32[1824,128]{1,0:T(8,128)S(1)}, f32[1824,128]{1,0:T(8,128)S(1)}, u32[]{:S(2)}, u32[]{:S(2)}) %collective-permute-start.12) | collective-permute-done | bytes 933920 | tf_op jit(solution)/shard_map/ppermute | solution.py:810
  59.8 0.1 parted.1
  59.9 2.4 %collective-permute-start.13 = (bf16[464,128]{1,0:T(8,128)(2,1)S(1)}, bf16[464,128]{1,0:T(8,128)(2,1)S(1)}, u32[]{:S(2)}, u32[]{:S(2)}) collective-permute-start(bf16[464,128]{1,0:T(8,128)(2,1)S(1)} %get-tuple-element.110), channel_id=1, source_target_pairs={{0,1},{1,0},{2,3},{3,2},{4,5},{5,4},{6,7},{7,6},{8,9},{9,8},{10,11... | collective-permute-start | bytes 356360 | tf_op jit(solution)/shard_map/ppermute | solution.py:810
  62.4 1.3 %collective-permute-start.14 = (bf16[464,128]{1,0:T(8,128)(2,1)S(1)}, bf16[464,128]{1,0:T(8,128)(2,1)S(1)}, u32[]{:S(2)}, u32[]{:S(2)}) collective-permute-start(bf16[464,128]{1,0:T(8,128)(2,1)S(1)} %get-tuple-element.111), channel_id=1, source_target_pairs={{0,2},{1,3},{2,0},{3,1},{4,6},{5,7},{6,4},{7,5},{8,10},{9,11},{10,... | collective-permute-start | bytes 356360 | tf_op jit(solution)/shard_map/ppermute | solution.py:810
  63.6 1.2 %collective-permute-start.15 = (bf16[464,128]{1,0:T(8,128)(2,1)S(1)}, bf16[464,128]{1,0:T(8,128)(2,1)S(1)}, u32[]{:S(2)}, u32[]{:S(2)}) collective-permute-start(bf16[464,128]{1,0:T(8,128)(2,1)S(1)} %get-tuple-element.112), channel_id=1, source_target_pairs={{0,3},{1,2},{2,1},{3,0},{4,7},{5,6},{6,5},{7,4},{8,11},{9,10},{10,... | collective-permute-start | bytes 356360 | tf_op jit(solution)/shard_map/ppermute | solution.py:810
  64.8 5.0 %sender_part.1.part_ref = f32[1536,256]{1,0:T(8,128)S(1)} custom-call(s32[1,4096]{1,0:T(1,128)S(1)} %bitcast.23, bf16[4096,256]{1,0:T(8,128)(2,1)S(1)} %get-tuple-element.104.d_pre_ref, bf16[1824,256]{1,0:T(8,128)(2,1)S(1)} %get-tuple-element.78.w_ref), custom_call_target="tpu_custom_call" | custom-call | flops 3221225472 | bytes 2097152 | tf_op jit(solution)/shard_map/sender_part/pallas_call | solution.py:590
  69.8 5.1 %receiver_part.1 = (f32[512,256]{1,0:T(8,128)S(1)}, bf16[512,256]{1,0:T(8,128)(2,1)S(1)}, bf16[512,256]{1,0:T(8,128)(2,1)S(1)}) custom-call(s32[1,4096]{1,0:T(1,128)S(1)} %bitcast.22, bf16[4096,256]{1,0:T(8,128)(2,1)S(1)} %get-tuple-element.104.d_pre_ref, bf16[1824,256]{1,0:T(8,128)(2,1)S(1)} %get-tuple-element.78.w_ref, ...), custom_call_target="tpu_custom_call" | custom-call | flops 3221225472 | bytes 2097152 | tf_op jit(solution)/shard_map/receiver_part/pallas_call | solution.py:626
  74.9 0.0 collective-permute-done.15.refs_2_
  74.9 0.1 gathered.1.mine_ref
  75.0 0.0 copy-start.2
  75.0 0.0 copy-start.3
  75.0 0.0 copy-start.4
  75.0 0.0 copy-start.5
  75.0 0.6 collective-permute-start.16
  75.6 1.9 %edge_grads.1 = bf16[4096,256]{1,0:T(8,128)(2,1)} custom-call(bf16[4096,256]{1,0:T(8,128)(2,1)S(1)} %get-tuple-element.104.d_pre_ref, bf16[1824,256]{1,0:T(8,128)(2,1)S(1)} %get-tuple-element.78.w_ref), custom_call_target="tpu_custom_call" | custom-call | flops 536870912 | bytes 4194304 | tf_op jit(solution)/shard_map/edge_grads/pallas_call | solution.py:649
  77.5 2.4 %collective-permute-done.16.other_ref = bf16[464,128]{1,0:T(8,128)(2,1)S(1)} collective-permute-done((bf16[464,128]{1,0:T(8,128)(2,1)S(1)}, bf16[464,128]{1,0:T(8,128)(2,1)S(1)}, u32[]{:S(2)}, u32[]{:S(2)}) %collective-permute-start.16) | collective-permute-done | bytes 118816 | tf_op jit(solution)/shard_map/ppermute | solution.py:810
  80.0 1.5 %collective-permute-start.17 = (bf16[464,128]{1,0:T(8,128)(2,1)S(1)}, bf16[464,128]{1,0:T(8,128)(2,1)S(1)}, u32[]{:S(2)}, u32[]{:S(2)}) collective-permute-start(bf16[464,128]{1,0:T(8,128)(2,1)S(1)} %add.6.mine_ref), channel_id=1, source_target_pairs={{0,16},{4,20},{8,24},{12,28},{16,0},{20,4},{24,8},{28,12},{1,17},{... | collective-permute-start | bytes 356360 | tf_op jit(solution)/shard_map/ppermute | solution.py:810
  81.4 3.4 %collective-permute-done.17.other_ref = bf16[464,128]{1,0:T(8,128)(2,1)S(1)} collective-permute-done((bf16[464,128]{1,0:T(8,128)(2,1)S(1)}, bf16[464,128]{1,0:T(8,128)(2,1)S(1)}, u32[]{:S(2)}, u32[]{:S(2)}) %collective-permute-start.17) | collective-permute-done | bytes 118816 | tf_op jit(solution)/shard_map/ppermute | solution.py:810
  84.9 0.2 finish.1.mine_ref
  85.1 0.5 collective-permute-start.21
  85.6 1.1 %collective-permute-start.22 = (bf16[512,256]{1,0:T(8,128)(2,1)S(1)}, bf16[512,256]{1,0:T(8,128)(2,1)S(1)}, u32[]{:S(2)}, u32[]{:S(2)}) collective-permute-start(bf16[512,256]{1,0:T(8,128)(2,1)S(1)} %get-tuple-element.118), channel_id=1, source_target_pairs={{0,28},{4,8},{8,4},{12,16},{16,12},{20,24},{24,20},{28,0},{1,29},{... | collective-permute-start | bytes 786440 | tf_op jit(solution)/shard_map/ppermute | solution.py:815
  86.7 1.7 %collective-permute-start.19 = (f32[32,128]{1,0:T(8,128)S(1)}, f32[32,128]{1,0:T(8,128)S(1)}, u32[]{:S(2)}, u32[]{:S(2)}) collective-permute-start(f32[32,128]{1,0:T(8,128)S(1)} %pad_maximum_fusion), channel_id=1, source_target_pairs={{0,1},{1,0},{2,3},{3,2},{4,5},{5,4},{6,7},{7,6},{8,9},{9,8},{10,11... | collective-permute-start | bytes 49160 | tf_op jit(solution)/shard_map/ppermute | solution.py:810
  88.5 2.1 %collective-permute-done.19 = f32[32,128]{1,0:T(8,128)S(1)} collective-permute-done((f32[32,128]{1,0:T(8,128)S(1)}, f32[32,128]{1,0:T(8,128)S(1)}, u32[]{:S(2)}, u32[]{:S(2)}) %collective-permute-start.19) | collective-permute-done | bytes 16416 | tf_op jit(solution)/shard_map/ppermute | solution.py:810
  90.5 2.6 %collective-permute-start.20 = (f32[32,128]{1,0:T(8,128)S(1)}, f32[32,128]{1,0:T(8,128)S(1)}, u32[]{:S(2)}, u32[]{:S(2)}) collective-permute-start(f32[32,128]{1,0:T(8,128)S(1)} %fusion.stats_ref), channel_id=1, source_target_pairs={{0,2},{1,3},{2,0},{3,1},{4,6},{5,7},{6,4},{7,5},{8,10},{9,11},{10,... | collective-permute-start | bytes 49160 | tf_op jit(solution)/shard_map/ppermute | solution.py:810
  93.8 1.1 %collective-permute-done.22.off_ref = bf16[512,256]{1,0:T(8,128)(2,1)S(1)} collective-permute-done((bf16[512,256]{1,0:T(8,128)(2,1)S(1)}, bf16[512,256]{1,0:T(8,128)(2,1)S(1)}, u32[]{:S(2)}, u32[]{:S(2)}) %collective-permute-start.22) | collective-permute-done | bytes 262176 | tf_op jit(solution)/shard_map/ppermute | solution.py:815
  94.9 0.3 collective-permute-done.20.more_ref
  95.2 2.3 %adam.1 = (f32[456,256]{1,0:T(8,128)}, f32[456,256]{1,0:T(8,128)}, f32[456,256]{1,0:T(8,128)}, f32[456,256]{1,0:T(8,128)}, f32[1,1]{1,0:T(1,128)}, /*index=5*/f32[8,256]{1,0:T(8,128)}, f32[512,256]{1,0:T(8,128)}) custom-call(f32[8,128]{1,0:T(8,128)S(1)} %broadcast_in_dim.15.step_ref, f32[32,128]{1,0:T(8,128)S(1)} %fusion.stats_ref, ...), custom_call_target="tpu_custom_call" | custom-call | flops 2334720 | bytes 3735552 | tf_op jit(solution)/shard_map/adam/pallas_call | solution.py:791
  (27 shorter events, 0.1 us)
Async XLA Ops:
  0.6 8.9 %collective-permute-start.1 = (bf16[512,256]{1,0:T(8,128)(2,1)}, bf16[512,256]{1,0:T(8,128)(2,1)S(1)}, u32[]{:S(2)}, u32[]{:S(2)}) collective-permute-start(bf16[512,256]{1,0:T(8,128)(2,1)} %bitcast.30), channel_id=1, source_target_pairs={{0,4},{4,0},{8,12},{12,8},{16,20},{20,16},{24,28},{28,24},{1,5},{5... | collective-permute-start | bytes 786440 | tf_op jit(solution)/shard_map/ppermute | solution.py:810
  2.3 12.1 %collective-permute-start.2 = (bf16[456,128]{1,0:T(8,128)(2,1)S(1)}, bf16[456,128]{1,0:T(8,128)(2,1)S(1)}, u32[]{:S(2)}, u32[]{:S(2)}) collective-permute-start(bf16[456,128]{1,0:T(8,128)(2,1)S(1)} %get-tuple-element.71.refs_0_), channel_id=1, source_target_pairs={{0,1},{1,0},{2,3},{3,2},{4,5},{5,4},{6,7},{7,6},{8,9},{9,8},{10,11... | collective-permute-start | bytes 350216 | tf_op jit(solution)/shard_map/ppermute | solution.py:810
  5.0 12.0 %collective-permute-start.3 = (bf16[456,128]{1,0:T(8,128)(2,1)S(1)}, bf16[456,128]{1,0:T(8,128)(2,1)S(1)}, u32[]{:S(2)}, u32[]{:S(2)}) collective-permute-start(bf16[456,128]{1,0:T(8,128)(2,1)S(1)} %get-tuple-element.71.refs_0_), channel_id=1, source_target_pairs={{0,2},{1,3},{2,0},{3,1},{4,6},{5,7},{6,4},{7,5},{8,10},{9,11},{10,... | collective-permute-start | bytes 350216 | tf_op jit(solution)/shard_map/ppermute | solution.py:810
  7.6 9.4 %collective-permute-start.4 = (bf16[456,128]{1,0:T(8,128)(2,1)S(1)}, bf16[456,128]{1,0:T(8,128)(2,1)S(1)}, u32[]{:S(2)}, u32[]{:S(2)}) collective-permute-start(bf16[456,128]{1,0:T(8,128)(2,1)S(1)} %get-tuple-element.71.refs_0_), channel_id=1, source_target_pairs={{0,3},{1,2},{2,1},{3,0},{4,7},{5,6},{6,5},{7,4},{8,11},{9,10},{10,... | collective-permute-start | bytes 350216 | tf_op jit(solution)/shard_map/ppermute | solution.py:810
  7.6 10.0 %collective-permute-start = (bf16[512,256]{1,0:T(8,128)(2,1)}, bf16[512,256]{1,0:T(8,128)(2,1)S(1)}, u32[]{:S(2)}, u32[]{:S(2)}) collective-permute-start(bf16[512,256]{1,0:T(8,128)(2,1)} %bitcast.32), channel_id=1, source_target_pairs={{0,28},{4,8},{8,4},{12,16},{16,12},{20,24},{24,20},{28,0},{1,29},{... | collective-permute-start | bytes 786440 | tf_op jit(solution)/shard_map/ppermute | solution.py:815
  17.0 3.2 %collective-permute-start.6 = (bf16[1368,128]{1,0:T(8,128)(2,1)S(1)}, bf16[1368,128]{1,0:T(8,128)(2,1)S(1)}, u32[]{:S(2)}, u32[]{:S(2)}) collective-permute-start(bf16[1368,128]{1,0:T(8,128)(2,1)S(1)} %constant_dynamic-update-slice_fusion.refs_1_), channel_id=1, source_target_pairs={{0,4},{4,0},{8,12},{12,8},{16,20},{20,16},{24,28},{28,24},{1,5},{5... | collective-permute-start | bytes 1050632 | tf_op jit(solution)/shard_map/ppermute | solution.py:810
  17.1 3.1 %collective-permute-start.5 = (bf16[456,128]{1,0:T(8,128)(2,1)S(1)}, bf16[456,128]{1,0:T(8,128)(2,1)S(1)}, u32[]{:S(2)}, u32[]{:S(2)}) collective-permute-start(bf16[456,128]{1,0:T(8,128)(2,1)S(1)} %get-tuple-element.71.refs_0_), channel_id=1, source_target_pairs={{0,4},{4,0},{8,12},{12,8},{16,20},{20,16},{24,28},{28,24},{1,5},{5... | collective-permute-start | bytes 350216 | tf_op jit(solution)/shard_map/ppermute | solution.py:810
  18.9 1.6 %copy-start.1 = (bf16[1,4096,256]{2,1,0:T(8,128)(2,1)S(1)}, bf16[1,4096,256]{2,1,0:T(8,128)(2,1)}, u32[]{:S(2)}) copy-start(bf16[1,4096,256]{2,1,0:T(8,128)(2,1)} %param.13) | copy-start | bytes 6291460
  18.9 1.6 %copy-start.6 = (s32[4096]{0:T(1024)S(1)}, s32[4096]{0:T(1024)}, u32[]{:S(2)}) copy-start(s32[4096]{0:T(1024)} %param.16) | copy-start | bytes 49156
  28.4 10.8 %collective-permute-start.9 = (s16[656,256]{1,0:T(8,128)(2,1)S(1)}, s16[656,256]{1,0:T(8,128)(2,1)S(1)}, u32[]{:S(2)}, u32[]{:S(2)}) collective-permute-start(s16[656,256]{1,0:T(8,128)(2,1)S(1)} %get-tuple-element.84), channel_id=1, source_target_pairs={{0,28},{4,8},{8,4},{12,16},{16,12},{20,24},{24,20},{28,0},{1,29},{... | collective-permute-start | bytes 1007624 | tf_op jit(solution)/shard_map/ppermute | solution.py:815
  35.1 4.0 %collective-permute-start.7 = (f32[256,256]{1,0:T(8,128)S(1)}, f32[256,256]{1,0:T(8,128)S(1)}, u32[]{:S(2)}, u32[]{:S(2)}) collective-permute-start(f32[256,256]{1,0:T(8,128)S(1)} %get-tuple-element.82), channel_id=1, source_target_pairs={{0,4},{4,0},{8,12},{12,8},{16,20},{20,16},{24,28},{28,24},{1,5},{5... | collective-permute-start | bytes 786440 | tf_op jit(solution)/shard_map/ppermute | solution.py:810
  35.1 3.9 %collective-permute-start.8 = (f32[256,256]{1,0:T(8,128)S(1)}, f32[256,256]{1,0:T(8,128)S(1)}, u32[]{:S(2)}, u32[]{:S(2)}) collective-permute-start(f32[256,256]{1,0:T(8,128)S(1)} %get-tuple-element.83), channel_id=1, source_target_pairs={{0,4},{4,0},{8,12},{12,8},{16,20},{20,16},{24,28},{28,24},{1,5},{5... | collective-permute-start | bytes 786440 | tf_op jit(solution)/shard_map/ppermute | solution.py:810
  35.6 3.6 %copy-start = (f32[1,512,256]{2,1,0:T(8,128)S(1)}, f32[1,512,256]{2,1,0:T(8,128)}, u32[]{:S(2)}) copy-start(f32[1,512,256]{2,1,0:T(8,128)} %param.23) | copy-start | bytes 1572868
  35.6 3.6 %copy-start.7 = (s32[512]{0:T(512)S(1)}, s32[512]{0:T(512)}, u32[]{:S(2)}) copy-start(s32[512]{0:T(512)} %param.17) | copy-start | bytes 6148
  40.4 4.8 %collective-permute-start.11 = (bf16[512,256]{1,0:T(8,128)(2,1)S(1)}, bf16[512,256]{1,0:T(8,128)(2,1)S(1)}, u32[]{:S(2)}, u32[]{:S(2)}) collective-permute-start(bf16[512,256]{1,0:T(8,128)(2,1)S(1)} %get-tuple-element.91.own_ref), channel_id=1, source_target_pairs={{0,4},{4,0},{8,12},{12,8},{16,20},{20,16},{24,28},{28,24},{1,5},{5... | collective-permute-start | bytes 786440 | tf_op jit(solution)/shard_map/ppermute | solution.py:810
  40.5 9.3 %collective-permute-start.10 = (bf16[512,256]{1,0:T(8,128)(2,1)S(1)}, bf16[512,256]{1,0:T(8,128)(2,1)S(1)}, u32[]{:S(2)}, u32[]{:S(2)}) collective-permute-start(bf16[512,256]{1,0:T(8,128)(2,1)S(1)} %get-tuple-element.91.own_ref), channel_id=1, source_target_pairs={{0,28},{4,8},{8,4},{12,16},{16,12},{20,24},{24,20},{28,0},{1,29},{... | collective-permute-start | bytes 786440 | tf_op jit(solution)/shard_map/ppermute | solution.py:815
  57.3 2.6 %collective-permute-start.12 = (f32[1824,128]{1,0:T(8,128)S(1)}, f32[1824,128]{1,0:T(8,128)S(1)}, u32[]{:S(2)}, u32[]{:S(2)}) collective-permute-start(f32[1824,128]{1,0:T(8,128)S(1)} %get-tuple-element.101), channel_id=1, source_target_pairs={{0,4},{4,0},{8,12},{12,8},{16,20},{20,16},{24,28},{28,24},{1,5},{5... | collective-permute-start | bytes 2801672 | tf_op jit(solution)/shard_map/ppermute | solution.py:810
  59.9 15.0 %collective-permute-start.13 = (bf16[464,128]{1,0:T(8,128)(2,1)S(1)}, bf16[464,128]{1,0:T(8,128)(2,1)S(1)}, u32[]{:S(2)}, u32[]{:S(2)}) collective-permute-start(bf16[464,128]{1,0:T(8,128)(2,1)S(1)} %get-tuple-element.110), channel_id=1, source_target_pairs={{0,1},{1,0},{2,3},{3,2},{4,5},{5,4},{6,7},{7,6},{8,9},{9,8},{10,11... | collective-permute-start | bytes 356360 | tf_op jit(solution)/shard_map/ppermute | solution.py:810
  62.4 12.5 %collective-permute-start.14 = (bf16[464,128]{1,0:T(8,128)(2,1)S(1)}, bf16[464,128]{1,0:T(8,128)(2,1)S(1)}, u32[]{:S(2)}, u32[]{:S(2)}) collective-permute-start(bf16[464,128]{1,0:T(8,128)(2,1)S(1)} %get-tuple-element.111), channel_id=1, source_target_pairs={{0,2},{1,3},{2,0},{3,1},{4,6},{5,7},{6,4},{7,5},{8,10},{9,11},{10,... | collective-permute-start | bytes 356360 | tf_op jit(solution)/shard_map/ppermute | solution.py:810
  63.6 11.3 %collective-permute-start.15 = (bf16[464,128]{1,0:T(8,128)(2,1)S(1)}, bf16[464,128]{1,0:T(8,128)(2,1)S(1)}, u32[]{:S(2)}, u32[]{:S(2)}) collective-permute-start(bf16[464,128]{1,0:T(8,128)(2,1)S(1)} %get-tuple-element.112), channel_id=1, source_target_pairs={{0,3},{1,2},{2,1},{3,0},{4,7},{5,6},{6,5},{7,4},{8,11},{9,10},{10,... | collective-permute-start | bytes 356360 | tf_op jit(solution)/shard_map/ppermute | solution.py:810
  75.0 20.2 %copy-start.2 = (f32[456,256]{1,0:T(8,128)S(1)}, f32[456,256]{1,0:T(8,128)}, u32[]{:S(2)}) copy-start(f32[456,256]{1,0:T(8,128)} %params_ref.1) | copy-start | bytes 1400836
  75.0 20.2 %copy-start.3 = (f32[456,256]{1,0:T(8,128)S(1)}, f32[456,256]{1,0:T(8,128)}, u32[]{:S(2)}) copy-start(f32[456,256]{1,0:T(8,128)} %first_ref.1) | copy-start | bytes 1400836
  75.0 20.2 %copy-start.4 = (f32[456,256]{1,0:T(8,128)S(1)}, f32[456,256]{1,0:T(8,128)}, u32[]{:S(2)}) copy-start(f32[456,256]{1,0:T(8,128)} %second_ref.1) | copy-start | bytes 1400836
  75.0 20.1 %copy-start.5 = (f32[456,256]{1,0:T(8,128)S(1)}, f32[456,256]{1,0:T(8,128)}, u32[]{:S(2)}) copy-start(f32[456,256]{1,0:T(8,128)} %averaged_ref.1) | copy-start | bytes 1400836
  75.0 4.9 %collective-permute-start.16 = (bf16[464,128]{1,0:T(8,128)(2,1)S(1)}, bf16[464,128]{1,0:T(8,128)(2,1)S(1)}, u32[]{:S(2)}, u32[]{:S(2)}) collective-permute-start(bf16[464,128]{1,0:T(8,128)(2,1)S(1)} %gathered.1.mine_ref), channel_id=1, source_target_pairs={{0,8},{4,12},{8,0},{12,4},{16,24},{20,28},{24,16},{28,20},{1,9},{5... | collective-permute-start | bytes 356360 | tf_op jit(solution)/shard_map/ppermute | solution.py:810
  80.0 4.9 %collective-permute-start.17 = (bf16[464,128]{1,0:T(8,128)(2,1)S(1)}, bf16[464,128]{1,0:T(8,128)(2,1)S(1)}, u32[]{:S(2)}, u32[]{:S(2)}) collective-permute-start(bf16[464,128]{1,0:T(8,128)(2,1)S(1)} %add.6.mine_ref), channel_id=1, source_target_pairs={{0,16},{4,20},{8,24},{12,28},{16,0},{20,4},{24,8},{28,12},{1,17},{... | collective-permute-start | bytes 356360 | tf_op jit(solution)/shard_map/ppermute | solution.py:810
  85.1 1.6 %collective-permute-start.18 = (f32[472,128]{1,0:T(8,128)S(1)}, f32[472,128]{1,0:T(8,128)S(1)}, u32[]{:S(2)}, u32[]{:S(2)}) collective-permute-start(f32[472,128]{1,0:T(8,128)S(1)} %finish.1.mine_ref), channel_id=1, source_target_pairs={{0,4},{4,0},{8,12},{12,8},{16,20},{20,16},{24,28},{28,24},{1,5},{5... | collective-permute-start | bytes 725000 | tf_op jit(solution)/shard_map/ppermute | solution.py:810
  85.1 8.8 %collective-permute-start.21 = (bf16[512,256]{1,0:T(8,128)(2,1)S(1)}, bf16[512,256]{1,0:T(8,128)(2,1)S(1)}, u32[]{:S(2)}, u32[]{:S(2)}) collective-permute-start(bf16[512,256]{1,0:T(8,128)(2,1)S(1)} %get-tuple-element.117), channel_id=1, source_target_pairs={{0,4},{4,0},{8,12},{12,8},{16,20},{20,16},{24,28},{28,24},{1,5},{5... | collective-permute-start | bytes 786440 | tf_op jit(solution)/shard_map/ppermute | solution.py:810
  85.6 9.3 %collective-permute-start.22 = (bf16[512,256]{1,0:T(8,128)(2,1)S(1)}, bf16[512,256]{1,0:T(8,128)(2,1)S(1)}, u32[]{:S(2)}, u32[]{:S(2)}) collective-permute-start(bf16[512,256]{1,0:T(8,128)(2,1)S(1)} %get-tuple-element.118), channel_id=1, source_target_pairs={{0,28},{4,8},{8,4},{12,16},{16,12},{20,24},{24,20},{28,0},{1,29},{... | collective-permute-start | bytes 786440 | tf_op jit(solution)/shard_map/ppermute | solution.py:815
  86.7 3.8 %collective-permute-start.19 = (f32[32,128]{1,0:T(8,128)S(1)}, f32[32,128]{1,0:T(8,128)S(1)}, u32[]{:S(2)}, u32[]{:S(2)}) collective-permute-start(f32[32,128]{1,0:T(8,128)S(1)} %pad_maximum_fusion), channel_id=1, source_target_pairs={{0,1},{1,0},{2,3},{3,2},{4,5},{5,4},{6,7},{7,6},{8,9},{9,8},{10,11... | collective-permute-start | bytes 49160 | tf_op jit(solution)/shard_map/ppermute | solution.py:810
  90.5 4.6 %collective-permute-start.20 = (f32[32,128]{1,0:T(8,128)S(1)}, f32[32,128]{1,0:T(8,128)S(1)}, u32[]{:S(2)}, u32[]{:S(2)}) collective-permute-start(f32[32,128]{1,0:T(8,128)S(1)} %fusion.stats_ref), channel_id=1, source_target_pairs={{0,2},{1,3},{2,0},{3,1},{4,6},{5,7},{6,4},{7,5},{8,10},{9,11},{10,... | collective-permute-start | bytes 49160 | tf_op jit(solution)/shard_map/ppermute | solution.py:810

commit v6 on v5

--- a/solution.py
+++ b/solution.py
@@ -21,6 +21,7 @@
 STEPS = 18
 LOG_TWO = 0.6931471805599453
 TILE = 2048
+PART = 512
 B16 = jnp.bfloat16
 F32 = jnp.float32
 I32 = jnp.int32
@@ -244,23 +245,26 @@
     return codes * jnp.concatenate([jnp.concatenate(scale, axis=0)] * (width // LANES), axis=1)
 
 
+def ways(count):
+    return sorted(range(1, count), key=lambda k: (k < count // 2, k))
+
+
 def edge_forward_kernel(
     region_ref, recv_row_ref, hs_ref, hr_ref, x_ref, *refs,
 ):
     pieces, refs = refs[:-5], refs[-5:]
     w_ref, high_ref, low_ref, halo_ref, wide_ref = refs
-    step = pl.program_id(0)
-    rows = x_ref.shape[0]
-    width = x_ref.shape[1]
+    rows, width = x_ref.shape
     nodes = (halo_ref.shape[0] - 16) // 5 * 4
-    steps = pl.num_programs(0)
-
-    @pl.when(step == 0)
+
+    @pl.when(pl.program_id(0) == 0)
     def _():
         odd, f = odd_core(), lax.axis_index("feat")
         share = pieces[0].shape[0]
-        for k in range(w_ref.shape[0] // share):
-            rows = slice((k - 1) * share, k * share)
+        shares = w_ref.shape[0] // share
+        for k in range(shares):
+            at = ways(shares).index(k) if k else 0
+            rows = slice(at * share, (at + 1) * share)
             mine, other = (pieces[i][...] if k == 0 else pieces[i + 1][rows, :] for i in (0, 2))
             mine, other = mine.astype(F32), other.astype(F32)
             base = pl.multiple_of(jnp.bitwise_xor(f, k) * share, 8)
@@ -269,26 +273,30 @@
         w_ref[...] = wide_ref[...].astype(B16)
 
     vec = vectors_of(w_ref, width)
-    pre = before_silu(region_ref, step, hs_ref, hr_ref, x_ref, w_ref)
-    hidden = (pre / (1.0 + jnp.exp(-pre))).astype(B16)
-    unit, _ = normalized(hidden, w_ref, vec)
-    high, low = split(unit * vec[2:3, :] + vec[3:4, :])
-    base = pl.multiple_of(step * rows, rows)
-    high_ref[pl.ds(base, rows), :] = high
-    low_ref[pl.ds(base, rows), :] = low
-
-    @pl.when(step == steps - 1)
-    def _():
-        onehot = chosen_rows(recv_row_ref[...], 2 * nodes, nodes)
-        halo_ref[...] = encoded(dot(onehot, high_ref[...]) + dot(onehot, low_ref[...]))
+    total = None
+    for i in range(rows // PART + 1):
+        if i < rows // PART:
+            here = slice(i * PART, (i + 1) * PART)
+            pre = before_silu(region_ref, i, hs_ref.at[here, :], hr_ref.at[here, :], x_ref.at[here, :], w_ref)
+            hidden = (pre / (1.0 + jnp.exp(-pre))).astype(B16)
+            unit, _ = normalized(hidden, w_ref, vec)
+            high, low = split(unit * vec[2:3, :] + vec[3:4, :])
+            high_ref[here, :] = high
+            low_ref[here, :] = low
+        if i > 0:
+            last = slice((i - 1) * PART, i * PART)
+            onehot = chosen_rows(recv_row_ref[:, last], 2 * nodes, nodes)
+            more = dot(onehot, high_ref[last, :]) + dot(onehot, low_ref[last, :])
+            total = more if total is None else total + more
+    halo_ref[...] = encoded(total)
 
 
 def edge_forward(regions, recv, hs, hr, edges, pieces, total, nodes):
     count, width = edges.shape
-    tile = tiled(TILE, width)
+    tile = tiled(count, width)
     return pl.pallas_call(
         edge_forward_kernel,
-        grid=(count // TILE,),
+        grid=(1,),
         in_specs=[
             whole((count // LANES, LANES)), whole((1, count)), tile, tile, tile,
             *[whole(piece.shape) for piece in pieces],
@@ -836,12 +844,12 @@
     pair, off = neighbours(latents)
 
     mine, send, recv, latents = prologue(params, senders, receivers, latents)
-    fetched = [mine] + [flipped(mine, "feat", k) for k in range(1, feats)]
+    far = [flipped(mine, "feat", k) for k in ways(feats)]
 
     near_send = gather_near(send, latents, pair)
     near_recv = gather_near(recv, latents, pair)
-    others = jnp.concatenate(lax.optimization_barrier((near_send, near_recv, *fetched[1:]))[2:])
-    pieces = [fetched[0], others, flipped(fetched[0], "edge", 1), flipped(others, "edge", 1)]
+    others = jnp.concatenate(lax.optimization_barrier((near_send, near_recv, *far))[2:])
+    pieces = [mine, others, flipped(mine, "edge", 1), flipped(others, "edge", 1)]
     hs = gather_off(send, off, near_send)
     hr = gather_off(recv, off, near_recv)
     weights, high, low, to_off = edge_forward(regions, recv, hs, hr, edges, pieces, total, nodes)
@@ -866,7 +874,7 @@
 
     low_rows = vector_row % share
     part, *sent = parted(kept, flipped(sent, "edge", 1), share, low_rows)
-    came = [flipped(wire, "feat", k + 1) for k, wire in enumerate(sent)]
+    came = [flipped(sent[k - 1], "feat", k) for k in ways(feats)]
     d_pre, part = lax.optimization_barrier((d_pre, part))
     send_part = sender_part(send, d_pre, weights, nodes)
     part_own, part_pair, part_off = receiver_part(recv, d_pre, weights, send_part, back)

time: 97.8 us -> 96.9 us (level)
  starting transfers between devices: 26 us -> 24.6 us
  waiting for transfers between devices: 16.5 us -> 17.5 us
    ppermute x4, starting transfers between devices: 7.06 us -> 5.99 us  [across(): lax.ppermute(value, axis, [(i, (i + 1 if i % 2 else i - 1) % count) for i...]
  transfers between devices with their start and end apart: 23 -> 23, of which waited for: 9 -> 12; matrix products, arithmetic and copies ran while one was open for 0% -> 0% of each run, Pallas kernels for 35% -> 35%
where the time goes in v6:
time: 96.9 us; the launch traced here: 96.7 us
  Pallas kernels  52.5 us (54%)
  starting transfers between devices  24.6 us (25%)
  waiting for transfers between devices  17.5 us (18%)
  between operations  1.78 us (2%)
    ppermute x19, starting transfers between devices, flipped(): lax.ppermute(value, axis, [(i, i ^ bit) for i in range(lax.axis_size(axis...  18.6 us
    ppermute x19, waiting for transfers between devices, flipped(): lax.ppermute(value, axis, [(i, i ^ bit) for i in range(lax.axis_size(axis...  13.6 us
    pallas_call x1, Pallas kernels, edge_backward(): pl.pallas_call(edge_backward_kernel, grid=(count // TILE,), in_specs=[who...  7.49 us
    pallas_call x1, Pallas kernels, edge_forward(): pl.pallas_call(edge_forward_kernel, grid=(1,), in_specs=[whole((count //...  7.26 us
    pallas_call x3, Pallas kernels, gather_near(): pl.pallas_call(gather_near_kernel, grid=(1,), in_specs=[whole((edges // L...  7.23 us
    ppermute x4, starting transfers between devices, across(): lax.ppermute(value, axis, [(i, (i + 1 if i % 2 else i - 1) % count) for i...  5.99 us
    pallas_call x1, Pallas kernels, receiver_part(): pl.pallas_call(receiver_part_kernel, grid=(3,), in_specs=[whole((1, count...  5.1 us
    pallas_call x1, Pallas kernels, sender_part(): pl.pallas_call(sender_part_kernel, grid=(3,), in_specs=[whole((1, count))...  4.96 us
  transfers between devices with their start and end apart: 23, of which 12 were waited for; matrix products, arithmetic and copies ran while one was open for 0% of the time, Pallas kernels for 35%

profile of v6, /device:TPU:0, one launch (start us, length us, event | category | flops | bytes accessed | tf_op | source)
XLA Modules:
  0.0 96.7 jit_solution(12075837080857497683)
XLA Ops:
  0.6 0.5 collective-permute-start.1
  1.2 1.2 %prologue.1 = (bf16[456,128]{1,0:T(8,128)(2,1)S(1)}, s32[32,128]{1,0:T(8,128)S(1)}, s32[32,128]{1,0:T(8,128)S(1)}, bf16[512,256]{1,0:T(8,128)(2,1)S(1)}) custom-call(f32[456,256]{1,0:T(8,128)} %params_ref.1, s32[32,128]{1,0:T(8,128)} %bitcast.33, s32[32,128]{1,0:T(8,128)} %bitcast.34, bf16[512,256]{1,0:T(8,128)(2,1)} %bitcast.31), custom_call_target="tpu_custom_call" | custom-call | tf_op jit(solution)/shard_map/prologue/pallas_call | solution.py:122
  2.3 3.7 %collective-permute-start.2 = (bf16[456,128]{1,0:T(8,128)(2,1)S(1)}, bf16[456,128]{1,0:T(8,128)(2,1)S(1)}, u32[]{:S(2)}, u32[]{:S(2)}) collective-permute-start(bf16[456,128]{1,0:T(8,128)(2,1)S(1)} %get-tuple-element.71.refs_0_), channel_id=1, source_target_pairs={{0,2},{1,3},{2,0},{3,1},{4,6},{5,7},{6,4},{7,5},{8,10},{9,11},{10,... | collective-permute-start | bytes 350216 | tf_op jit(solution)/shard_map/ppermute | solution.py:818
  6.0 1.3 %collective-permute-start.3 = (bf16[456,128]{1,0:T(8,128)(2,1)S(1)}, bf16[456,128]{1,0:T(8,128)(2,1)S(1)}, u32[]{:S(2)}, u32[]{:S(2)}) collective-permute-start(bf16[456,128]{1,0:T(8,128)(2,1)S(1)} %get-tuple-element.71.refs_0_), channel_id=1, source_target_pairs={{0,3},{1,2},{2,1},{3,0},{4,7},{5,6},{6,5},{7,4},{8,11},{9,10},{10,... | collective-permute-start | bytes 350216 | tf_op jit(solution)/shard_map/ppermute | solution.py:818
  7.3 0.2 collective-permute-start.4
  7.6 2.0 %collective-permute-start = (bf16[512,256]{1,0:T(8,128)(2,1)}, bf16[512,256]{1,0:T(8,128)(2,1)S(1)}, u32[]{:S(2)}, u32[]{:S(2)}) collective-permute-start(bf16[512,256]{1,0:T(8,128)(2,1)} %bitcast.32), channel_id=1, source_target_pairs={{0,28},{4,8},{8,4},{12,16},{16,12},{20,24},{24,20},{28,0},{1,29},{... | collective-permute-start | bytes 786440 | tf_op jit(solution)/shard_map/ppermute | solution.py:823
  9.6 2.4 %gather_near.4.near_ref = bf16[4096,256]{1,0:T(8,128)(2,1)S(1)} custom-call(s32[32,128]{1,0:T(8,128)S(1)} %get-tuple-element.69.index_ref.recv_ref, bf16[512,256]{1,0:T(8,128)(2,1)S(1)} %get-tuple-element.68.own_ref.h_ref, bf16[512,256]{1,0:T(8,128)(2,1)S(1)} %collective-permute-done.1.pair_ref), custom_call_target="tpu_custom_call" | custom-call | flops 2147483648 | bytes 2097152 | tf_op jit(solution)/shard_map/gather_near/pallas_call | solution.py:151
  12.0 2.4 %gather_near.3.near_ref = bf16[4096,256]{1,0:T(8,128)(2,1)S(1)} custom-call(s32[32,128]{1,0:T(8,128)S(1)} %get-tuple-element.70.index_ref, bf16[512,256]{1,0:T(8,128)(2,1)S(1)} %get-tuple-element.68.own_ref.h_ref, bf16[512,256]{1,0:T(8,128)(2,1)S(1)} %collective-permute-done.1.pair_ref), custom_call_target="tpu_custom_call" | custom-call | flops 2147483648 | bytes 2097152 | tf_op jit(solution)/shard_map/gather_near/pallas_call | solution.py:151
  14.4 0.7 collective-permute-done.2
  15.1 0.0 collective-permute-done.3
  15.1 1.1 %collective-permute-done.4 = bf16[456,128]{1,0:T(8,128)(2,1)S(1)} collective-permute-done((bf16[456,128]{1,0:T(8,128)(2,1)S(1)}, bf16[456,128]{1,0:T(8,128)(2,1)S(1)}, u32[]{:S(2)}, u32[]{:S(2)}) %collective-permute-start.4) | collective-permute-done | bytes 116768 | tf_op jit(solution)/shard_map/ppermute | solution.py:818
  16.3 0.1 collective-permute-start.6
  16.4 0.5 collective-permute-start.5
  16.9 0.2 collective-permute-done.off_ref
  17.1 1.3 %gather_off.3.hr_ref = bf16[4096,256]{1,0:T(8,128)(2,1)S(1)} custom-call(s32[32,128]{1,0:T(8,128)S(1)} %get-tuple-element.69.index_ref.recv_ref, bf16[512,256]{1,0:T(8,128)(2,1)S(1)} %collective-permute-done.off_ref, bf16[4096,256]{1,0:T(8,128)(2,1)S(1)} %gather_near.4.near_ref), custom_call_target="tpu_custom_call" | custom-call | flops 1073741824 | bytes 4194304 | tf_op jit(solution)/shard_map/gather_off/pallas_call | solution.py:176
  18.4 0.0 copy-start.1
  18.4 0.0 copy-start.6
  18.5 1.3 %gather_off.2.hs_ref = bf16[4096,256]{1,0:T(8,128)(2,1)S(1)} custom-call(s32[32,128]{1,0:T(8,128)S(1)} %get-tuple-element.70.index_ref, bf16[512,256]{1,0:T(8,128)(2,1)S(1)} %collective-permute-done.off_ref, bf16[4096,256]{1,0:T(8,128)(2,1)S(1)} %gather_near.3.near_ref), custom_call_target="tpu_custom_call" | custom-call | flops 1073741824 | bytes 4194304 | tf_op jit(solution)/shard_map/gather_off/pallas_call | solution.py:176
  19.8 0.2 copy-done.1
  20.0 7.3 %edge_forward.1 = (bf16[1824,256]{1,0:T(8,128)(2,1)S(1)}, bf16[4096,256]{1,0:T(8,128)(2,1)S(1)}, bf16[4096,256]{1,0:T(8,128)(2,1)S(1)}, s16[656,256]{1,0:T(8,128)(2,1)S(1)}) custom-call(s32[32,128]{1,0:T(8,128)S(1)} %bitcast.24, s32[1,4096]{1,0:T(1,128)S(1)} %bitcast.20, bf16[4096,256]{1,0:T(8,128)(2,1)S(1)} %gather_off.2.hs_ref, ...), custom_call_target="tpu_custom_call" | custom-call | flops 4831838208 | bytes 10485760 | tf_op jit(solution)/shard_map/edge_forward/pallas_call | solution.py:297
  27.3 2.0 %collective-permute-start.9 = (s16[656,256]{1,0:T(8,128)(2,1)S(1)}, s16[656,256]{1,0:T(8,128)(2,1)S(1)}, u32[]{:S(2)}, u32[]{:S(2)}) collective-permute-start(s16[656,256]{1,0:T(8,128)(2,1)S(1)} %get-tuple-element.84), channel_id=1, source_target_pairs={{0,28},{4,8},{8,4},{12,16},{16,12},{20,24},{24,20},{28,0},{1,29},{... | collective-permute-start | bytes 1007624 | tf_op jit(solution)/shard_map/ppermute | solution.py:823
  29.3 4.5 %near_sum.1 = (f32[256,256]{1,0:T(8,128)S(1)}, f32[256,256]{1,0:T(8,128)S(1)}, f32[512,256]{1,0:T(8,128)S(1)}) custom-call(s32[1,4096]{1,0:T(1,128)S(1)} %bitcast.21, bf16[4096,256]{1,0:T(8,128)(2,1)S(1)} %get-tuple-element.75.high_ref, bf16[4096,256]{1,0:T(8,128)(2,1)S(1)} %get-tuple-element.76.low_ref), custom_call_target="tpu_custom_call" | custom-call | flops 4294967296 | bytes 4194304 | tf_op jit(solution)/shard_map/near_sum/pallas_call | solution.py:382
  33.8 0.1 collective-permute-start.7
  33.9 0.5 collective-permute-start.8
  34.4 3.4 %edge_slope.1 = (bf16[4096,256]{1,0:T(8,128)(2,1)S(1)}, f32[4096,256]{1,0:T(8,128)S(1)}) custom-call(s32[32,128]{1,0:T(8,128)S(1)} %bitcast.25, bf16[4096,256]{1,0:T(8,128)(2,1)S(1)} %gather_off.2.hs_ref, bf16[4096,256]{1,0:T(8,128)(2,1)S(1)} %gather_off.3.hr_ref, bf16[4096,256]{1,0:T(8,128)(2,1)S(1)} %bitcast.18, bf16[1824,256]{1,0:T(8,128)(2,1)S(1)} %get-tuple-element.78.w_ref), custom_call_target="tpu_custom_call" | custom-call | flops 2147483648 | bytes 12582912 | tf_op jit(solution)/shard_map/edge_slope/pallas_call | solution.py:334
  37.7 0.0 collective-permute-done.8.more_ref
  37.8 0.5 collective-permute-done.9.off_ref
  38.3 1.2 %node_update.1 = (bf16[512,256]{1,0:T(8,128)(2,1)S(1)}, bf16[512,256]{1,0:T(8,128)(2,1)S(1)}, bf16[512,256]{1,0:T(8,128)(2,1)S(1)}, bf16[512,256]{1,0:T(8,128)(2...) custom-call(bf16[512,256]{1,0:T(8,128)(2,1)S(1)} %get-tuple-element.68.own_ref.h_ref, ...), custom_call_target="tpu_custom_call" | custom-call | flops 335544320 | bytes 2621440 | tf_op jit(solution)/shard_map/node_update/pallas_call | solution.py:435
  39.5 0.1 collective-permute-start.11
  39.6 1.3 %collective-permute-start.10 = (bf16[512,256]{1,0:T(8,128)(2,1)S(1)}, bf16[512,256]{1,0:T(8,128)(2,1)S(1)}, u32[]{:S(2)}, u32[]{:S(2)}) collective-permute-start(bf16[512,256]{1,0:T(8,128)(2,1)S(1)} %get-tuple-element.91.own_ref), channel_id=1, source_target_pairs={{0,28},{4,8},{8,4},{12,16},{16,12},{20,24},{24,20},{28,0},{1,29},{... | collective-permute-start | bytes 786440 | tf_op jit(solution)/shard_map/ppermute | solution.py:823
  40.9 1.3 %node_grads.1 = (f32[512,256]{1,0:T(8,128)}, f32[768,256]{1,0:T(8,128)S(1)}, f32[4,256]{1,0:T(4,128)S(1)}, f32[512,256]{1,0:T(8,128)S(1)}) custom-call(bf16[512,256]{1,0:T(8,128)(2,1)S(1)} %get-tuple-element.68.own_ref.h_ref, bf16[512,256]{1,0:T(8,128)(2,1)S(1)} %get-tuple-element.85.agg_ref, bf16[512,256]{1,0:T(8,128)(2,1)S(1)} %get-tuple-element.86.hidden_ref, ...), custom_call_target="tpu_custom_call" | custom-call | flops 268435456 | bytes 2359296 | tf_op jit(solution)/shard_map/node_grads/pallas_call | solution.py:474
  42.2 1.7 %edge_unit.1 = (f32[4096,256]{1,0:T(8,128)S(1)}, f32[4096,128]{1,0:T(8,128)S(1)}) custom-call(bf16[4096,256]{1,0:T(8,128)(2,1)S(1)} %get-tuple-element.94.hidden_ref, bf16[1824,256]{1,0:T(8,128)(2,1)S(1)} %get-tuple-element.78.w_ref), custom_call_target="tpu_custom_call" | custom-call | flops 536870912 | bytes 8388608 | tf_op jit(solution)/shard_map/edge_unit/pallas_call | solution.py:357
  43.9 0.0 collective-permute-done.11.pair_ref
  43.9 2.4 %gather_near.5.near_ref = bf16[4096,256]{1,0:T(8,128)(2,1)S(1)} custom-call(s32[32,128]{1,0:T(8,128)S(1)} %get-tuple-element.69.index_ref.recv_ref, bf16[512,256]{1,0:T(8,128)(2,1)S(1)} %get-tuple-element.91.own_ref, bf16[512,256]{1,0:T(8,128)(2,1)S(1)} %collective-permute-done.11.pair_ref), custom_call_target="tpu_custom_call" | custom-call | flops 2147483648 | bytes 2097152 | tf_op jit(solution)/shard_map/gather_near/pallas_call | solution.py:151
  46.4 2.7 %collective-permute-done.10.off_ref = bf16[512,256]{1,0:T(8,128)(2,1)S(1)} collective-permute-done((bf16[512,256]{1,0:T(8,128)(2,1)S(1)}, bf16[512,256]{1,0:T(8,128)(2,1)S(1)}, u32[]{:S(2)}, u32[]{:S(2)}) %collective-permute-start.10) | collective-permute-done | bytes 262176 | tf_op jit(solution)/shard_map/ppermute | solution.py:823
  49.0 7.5 %edge_backward.1 = (bf16[4096,256]{1,0:T(8,128)(2,1)S(1)}, f32[1824,128]{1,0:T(8,128)S(1)}, f32[1824,128]{1,0:T(8,128)S(1)}) custom-call(s32[32,128]{1,0:T(8,128)S(1)} %get-tuple-element.69.index_ref.recv_ref, s32[1,4096]{1,0:T(1,128)S(1)} %bitcast.26, bf16[512,256]{1,0:T(8,128)(2,1)S(1)} %collective-permute-done.10.off_ref, ...), custom_call_target="tpu_custom_call" | custom-call | flops 4294967296 | bytes 20971520 | tf_op jit(solution)/shard_map/edge_backward/pallas_call | solution.py:560
  56.5 0.1 collective-permute-start.12
  56.6 2.5 %collective-permute-done.12.other_ref = f32[1824,128]{1,0:T(8,128)S(1)} collective-permute-done((f32[1824,128]{1,0:T(8,128)S(1)}, f32[1824,128]{1,0:T(8,128)S(1)}, u32[]{:S(2)}, u32[]{:S(2)}) %collective-permute-start.12) | collective-permute-done | bytes 933920 | tf_op jit(solution)/shard_map/ppermute | solution.py:818
  59.1 0.1 parted.1
  59.2 3.3 %collective-permute-start.13 = (bf16[464,128]{1,0:T(8,128)(2,1)S(1)}, bf16[464,128]{1,0:T(8,128)(2,1)S(1)}, u32[]{:S(2)}, u32[]{:S(2)}) collective-permute-start(bf16[464,128]{1,0:T(8,128)(2,1)S(1)} %get-tuple-element.110), channel_id=1, source_target_pairs={{0,2},{1,3},{2,0},{3,1},{4,6},{5,7},{6,4},{7,5},{8,10},{9,11},{10,... | collective-permute-start | bytes 356360 | tf_op jit(solution)/shard_map/ppermute | solution.py:818
  62.5 1.0 %collective-permute-start.14 = (bf16[464,128]{1,0:T(8,128)(2,1)S(1)}, bf16[464,128]{1,0:T(8,128)(2,1)S(1)}, u32[]{:S(2)}, u32[]{:S(2)}) collective-permute-start(bf16[464,128]{1,0:T(8,128)(2,1)S(1)} %get-tuple-element.111), channel_id=1, source_target_pairs={{0,3},{1,2},{2,1},{3,0},{4,7},{5,6},{6,5},{7,4},{8,11},{9,10},{10,... | collective-permute-start | bytes 356360 | tf_op jit(solution)/shard_map/ppermute | solution.py:818
  63.5 0.0 collective-permute-start.15
  63.5 5.0 %sender_part.1.part_ref = f32[1536,256]{1,0:T(8,128)S(1)} custom-call(s32[1,4096]{1,0:T(1,128)S(1)} %bitcast.23, bf16[4096,256]{1,0:T(8,128)(2,1)S(1)} %get-tuple-element.104.d_pre_ref, bf16[1824,256]{1,0:T(8,128)(2,1)S(1)} %get-tuple-element.78.w_ref), custom_call_target="tpu_custom_call" | custom-call | flops 3221225472 | bytes 2097152 | tf_op jit(solution)/shard_map/sender_part/pallas_call | solution.py:598
  68.5 5.1 %receiver_part.1 = (f32[512,256]{1,0:T(8,128)S(1)}, bf16[512,256]{1,0:T(8,128)(2,1)S(1)}, bf16[512,256]{1,0:T(8,128)(2,1)S(1)}) custom-call(s32[1,4096]{1,0:T(1,128)S(1)} %bitcast.22, bf16[4096,256]{1,0:T(8,128)(2,1)S(1)} %get-tuple-element.104.d_pre_ref, bf16[1824,256]{1,0:T(8,128)(2,1)S(1)} %get-tuple-element.78.w_ref, ...), custom_call_target="tpu_custom_call" | custom-call | flops 3221225472 | bytes 2097152 | tf_op jit(solution)/shard_map/receiver_part/pallas_call | solution.py:634
  73.6 0.1 gathered.1.mine_ref
  73.7 0.0 copy-start.2
  73.7 0.0 copy-start.3
  73.7 0.0 copy-start.4
  73.7 0.0 copy-start.5
  73.8 0.2 collective-permute-start.16
  73.9 1.9 %edge_grads.1 = bf16[4096,256]{1,0:T(8,128)(2,1)} custom-call(bf16[4096,256]{1,0:T(8,128)(2,1)S(1)} %get-tuple-element.104.d_pre_ref, bf16[1824,256]{1,0:T(8,128)(2,1)S(1)} %get-tuple-element.78.w_ref), custom_call_target="tpu_custom_call" | custom-call | flops 536870912 | bytes 4194304 | tf_op jit(solution)/shard_map/edge_grads/pallas_call | solution.py:657
  75.8 2.8 %collective-permute-done.16.other_ref = bf16[464,128]{1,0:T(8,128)(2,1)S(1)} collective-permute-done((bf16[464,128]{1,0:T(8,128)(2,1)S(1)}, bf16[464,128]{1,0:T(8,128)(2,1)S(1)}, u32[]{:S(2)}, u32[]{:S(2)}) %collective-permute-start.16) | collective-permute-done | bytes 118816 | tf_op jit(solution)/shard_map/ppermute | solution.py:818
  78.7 1.1 %collective-permute-start.17 = (bf16[464,128]{1,0:T(8,128)(2,1)S(1)}, bf16[464,128]{1,0:T(8,128)(2,1)S(1)}, u32[]{:S(2)}, u32[]{:S(2)}) collective-permute-start(bf16[464,128]{1,0:T(8,128)(2,1)S(1)} %add.6.mine_ref), channel_id=1, source_target_pairs={{0,16},{4,20},{8,24},{12,28},{16,0},{20,4},{24,8},{28,12},{1,17},{... | collective-permute-start | bytes 356360 | tf_op jit(solution)/shard_map/ppermute | solution.py:818
  79.8 3.8 %collective-permute-done.17.other_ref = bf16[464,128]{1,0:T(8,128)(2,1)S(1)} collective-permute-done((bf16[464,128]{1,0:T(8,128)(2,1)S(1)}, bf16[464,128]{1,0:T(8,128)(2,1)S(1)}, u32[]{:S(2)}, u32[]{:S(2)}) %collective-permute-start.17) | collective-permute-done | bytes 118816 | tf_op jit(solution)/shard_map/ppermute | solution.py:818
  83.6 0.2 finish.1.mine_ref
  83.8 0.5 collective-permute-start.21
  84.3 0.7 collective-permute-start.22
  85.0 0.3 collective-permute-done.18.other_ref
  85.3 2.0 %collective-permute-start.19 = (f32[32,128]{1,0:T(8,128)S(1)}, f32[32,128]{1,0:T(8,128)S(1)}, u32[]{:S(2)}, u32[]{:S(2)}) collective-permute-start(f32[32,128]{1,0:T(8,128)S(1)} %pad_maximum_fusion), channel_id=1, source_target_pairs={{0,1},{1,0},{2,3},{3,2},{4,5},{5,4},{6,7},{7,6},{8,9},{9,8},{10,11... | collective-permute-start | bytes 49160 | tf_op jit(solution)/shard_map/ppermute | solution.py:818
  87.3 1.7 %collective-permute-done.19 = f32[32,128]{1,0:T(8,128)S(1)} collective-permute-done((f32[32,128]{1,0:T(8,128)S(1)}, f32[32,128]{1,0:T(8,128)S(1)}, u32[]{:S(2)}, u32[]{:S(2)}) %collective-permute-start.19) | collective-permute-done | bytes 16416 | tf_op jit(solution)/shard_map/ppermute | solution.py:818
  89.0 3.4 %collective-permute-start.20 = (f32[32,128]{1,0:T(8,128)S(1)}, f32[32,128]{1,0:T(8,128)S(1)}, u32[]{:S(2)}, u32[]{:S(2)}) collective-permute-start(f32[32,128]{1,0:T(8,128)S(1)} %fusion.stats_ref), channel_id=1, source_target_pairs={{0,2},{1,3},{2,0},{3,1},{4,6},{5,7},{6,4},{7,5},{8,10},{9,11},{10,... | collective-permute-start | bytes 49160 | tf_op jit(solution)/shard_map/ppermute | solution.py:818
  93.1 0.4 collective-permute-done.22.off_ref
  93.6 0.6 collective-permute-done.20.more_ref
  94.2 2.3 %adam.1 = (f32[456,256]{1,0:T(8,128)}, f32[456,256]{1,0:T(8,128)}, f32[456,256]{1,0:T(8,128)}, f32[456,256]{1,0:T(8,128)}, f32[1,1]{1,0:T(1,128)}, /*index=5*/f32[8,256]{1,0:T(8,128)}, f32[512,256]{1,0:T(8,128)}) custom-call(f32[8,128]{1,0:T(8,128)S(1)} %broadcast_in_dim.15.step_ref, f32[32,128]{1,0:T(8,128)S(1)} %fusion.stats_ref, ...), custom_call_target="tpu_custom_call" | custom-call | flops 2334720 | bytes 3735552 | tf_op jit(solution)/shard_map/adam/pallas_call | solution.py:799
  (27 shorter events, 0.1 us)
Async XLA Ops:
  0.6 8.9 %collective-permute-start.1 = (bf16[512,256]{1,0:T(8,128)(2,1)}, bf16[512,256]{1,0:T(8,128)(2,1)S(1)}, u32[]{:S(2)}, u32[]{:S(2)}) collective-permute-start(bf16[512,256]{1,0:T(8,128)(2,1)} %bitcast.30), channel_id=1, source_target_pairs={{0,4},{4,0},{8,12},{12,8},{16,20},{20,16},{24,28},{28,24},{1,5},{5... | collective-permute-start | bytes 786440 | tf_op jit(solution)/shard_map/ppermute | solution.py:818
  2.3 12.8 %collective-permute-start.2 = (bf16[456,128]{1,0:T(8,128)(2,1)S(1)}, bf16[456,128]{1,0:T(8,128)(2,1)S(1)}, u32[]{:S(2)}, u32[]{:S(2)}) collective-permute-start(bf16[456,128]{1,0:T(8,128)(2,1)S(1)} %get-tuple-element.71.refs_0_), channel_id=1, source_target_pairs={{0,2},{1,3},{2,0},{3,1},{4,6},{5,7},{6,4},{7,5},{8,10},{9,11},{10,... | collective-permute-start | bytes 350216 | tf_op jit(solution)/shard_map/ppermute | solution.py:818
  6.0 9.1 %collective-permute-start.3 = (bf16[456,128]{1,0:T(8,128)(2,1)S(1)}, bf16[456,128]{1,0:T(8,128)(2,1)S(1)}, u32[]{:S(2)}, u32[]{:S(2)}) collective-permute-start(bf16[456,128]{1,0:T(8,128)(2,1)S(1)} %get-tuple-element.71.refs_0_), channel_id=1, source_target_pairs={{0,3},{1,2},{2,1},{3,0},{4,7},{5,6},{6,5},{7,4},{8,11},{9,10},{10,... | collective-permute-start | bytes 350216 | tf_op jit(solution)/shard_map/ppermute | solution.py:818
  7.3 8.9 %collective-permute-start.4 = (bf16[456,128]{1,0:T(8,128)(2,1)S(1)}, bf16[456,128]{1,0:T(8,128)(2,1)S(1)}, u32[]{:S(2)}, u32[]{:S(2)}) collective-permute-start(bf16[456,128]{1,0:T(8,128)(2,1)S(1)} %get-tuple-element.71.refs_0_), channel_id=1, source_target_pairs={{0,1},{1,0},{2,3},{3,2},{4,5},{5,4},{6,7},{7,6},{8,9},{9,8},{10,11... | collective-permute-start | bytes 350216 | tf_op jit(solution)/shard_map/ppermute | solution.py:818
  7.6 9.5 %collective-permute-start = (bf16[512,256]{1,0:T(8,128)(2,1)}, bf16[512,256]{1,0:T(8,128)(2,1)S(1)}, u32[]{:S(2)}, u32[]{:S(2)}) collective-permute-start(bf16[512,256]{1,0:T(8,128)(2,1)} %bitcast.32), channel_id=1, source_target_pairs={{0,28},{4,8},{8,4},{12,16},{16,12},{20,24},{24,20},{28,0},{1,29},{... | collective-permute-start | bytes 786440 | tf_op jit(solution)/shard_map/ppermute | solution.py:823
  16.3 3.5 %collective-permute-start.6 = (bf16[1368,128]{1,0:T(8,128)(2,1)S(1)}, bf16[1368,128]{1,0:T(8,128)(2,1)S(1)}, u32[]{:S(2)}, u32[]{:S(2)}) collective-permute-start(bf16[1368,128]{1,0:T(8,128)(2,1)S(1)} %constant_dynamic-update-slice_fusion.refs_1_), channel_id=1, source_target_pairs={{0,4},{4,0},{8,12},{12,8},{16,20},{20,16},{24,28},{28,24},{1,5},{5... | collective-permute-start | bytes 1050632 | tf_op jit(solution)/shard_map/ppermute | solution.py:818
  16.4 3.4 %collective-permute-start.5 = (bf16[456,128]{1,0:T(8,128)(2,1)S(1)}, bf16[456,128]{1,0:T(8,128)(2,1)S(1)}, u32[]{:S(2)}, u32[]{:S(2)}) collective-permute-start(bf16[456,128]{1,0:T(8,128)(2,1)S(1)} %get-tuple-element.71.refs_0_), channel_id=1, source_target_pairs={{0,4},{4,0},{8,12},{12,8},{16,20},{20,16},{24,28},{28,24},{1,5},{5... | collective-permute-start | bytes 350216 | tf_op jit(solution)/shard_map/ppermute | solution.py:818
  18.4 1.6 %copy-start.1 = (bf16[1,4096,256]{2,1,0:T(8,128)(2,1)S(1)}, bf16[1,4096,256]{2,1,0:T(8,128)(2,1)}, u32[]{:S(2)}) copy-start(bf16[1,4096,256]{2,1,0:T(8,128)(2,1)} %param.13) | copy-start | bytes 6291460
  18.4 1.6 %copy-start.6 = (s32[4096]{0:T(1024)S(1)}, s32[4096]{0:T(1024)}, u32[]{:S(2)}) copy-start(s32[4096]{0:T(1024)} %param.16) | copy-start | bytes 49156
  27.3 11.0 %collective-permute-start.9 = (s16[656,256]{1,0:T(8,128)(2,1)S(1)}, s16[656,256]{1,0:T(8,128)(2,1)S(1)}, u32[]{:S(2)}, u32[]{:S(2)}) collective-permute-start(s16[656,256]{1,0:T(8,128)(2,1)S(1)} %get-tuple-element.84), channel_id=1, source_target_pairs={{0,28},{4,8},{8,4},{12,16},{16,12},{20,24},{24,20},{28,0},{1,29},{... | collective-permute-start | bytes 1007624 | tf_op jit(solution)/shard_map/ppermute | solution.py:823
  33.8 4.0 %collective-permute-start.7 = (f32[256,256]{1,0:T(8,128)S(1)}, f32[256,256]{1,0:T(8,128)S(1)}, u32[]{:S(2)}, u32[]{:S(2)}) collective-permute-start(f32[256,256]{1,0:T(8,128)S(1)} %get-tuple-element.82), channel_id=1, source_target_pairs={{0,4},{4,0},{8,12},{12,8},{16,20},{20,16},{24,28},{28,24},{1,5},{5... | collective-permute-start | bytes 786440 | tf_op jit(solution)/shard_map/ppermute | solution.py:818
  33.9 3.9 %collective-permute-start.8 = (f32[256,256]{1,0:T(8,128)S(1)}, f32[256,256]{1,0:T(8,128)S(1)}, u32[]{:S(2)}, u32[]{:S(2)}) collective-permute-start(f32[256,256]{1,0:T(8,128)S(1)} %get-tuple-element.83), channel_id=1, source_target_pairs={{0,4},{4,0},{8,12},{12,8},{16,20},{20,16},{24,28},{28,24},{1,5},{5... | collective-permute-start | bytes 786440 | tf_op jit(solution)/shard_map/ppermute | solution.py:818
  34.4 3.9 %copy-start = (f32[1,512,256]{2,1,0:T(8,128)S(1)}, f32[1,512,256]{2,1,0:T(8,128)}, u32[]{:S(2)}) copy-start(f32[1,512,256]{2,1,0:T(8,128)} %param.23) | copy-start | bytes 1572868
  34.4 3.9 %copy-start.7 = (s32[512]{0:T(512)S(1)}, s32[512]{0:T(512)}, u32[]{:S(2)}) copy-start(s32[512]{0:T(512)} %param.17) | copy-start | bytes 6148
  39.5 4.4 %collective-permute-start.11 = (bf16[512,256]{1,0:T(8,128)(2,1)S(1)}, bf16[512,256]{1,0:T(8,128)(2,1)S(1)}, u32[]{:S(2)}, u32[]{:S(2)}) collective-permute-start(bf16[512,256]{1,0:T(8,128)(2,1)S(1)} %get-tuple-element.91.own_ref), channel_id=1, source_target_pairs={{0,4},{4,0},{8,12},{12,8},{16,20},{20,16},{24,28},{28,24},{1,5},{5... | collective-permute-start | bytes 786440 | tf_op jit(solution)/shard_map/ppermute | solution.py:818
  39.6 9.4 %collective-permute-start.10 = (bf16[512,256]{1,0:T(8,128)(2,1)S(1)}, bf16[512,256]{1,0:T(8,128)(2,1)S(1)}, u32[]{:S(2)}, u32[]{:S(2)}) collective-permute-start(bf16[512,256]{1,0:T(8,128)(2,1)S(1)} %get-tuple-element.91.own_ref), channel_id=1, source_target_pairs={{0,28},{4,8},{8,4},{12,16},{16,12},{20,24},{24,20},{28,0},{1,29},{... | collective-permute-start | bytes 786440 | tf_op jit(solution)/shard_map/ppermute | solution.py:823
  56.5 2.6 %collective-permute-start.12 = (f32[1824,128]{1,0:T(8,128)S(1)}, f32[1824,128]{1,0:T(8,128)S(1)}, u32[]{:S(2)}, u32[]{:S(2)}) collective-permute-start(f32[1824,128]{1,0:T(8,128)S(1)} %get-tuple-element.101), channel_id=1, source_target_pairs={{0,4},{4,0},{8,12},{12,8},{16,20},{20,16},{24,28},{28,24},{1,5},{5... | collective-permute-start | bytes 2801672 | tf_op jit(solution)/shard_map/ppermute | solution.py:818
  59.2 14.4 %collective-permute-start.13 = (bf16[464,128]{1,0:T(8,128)(2,1)S(1)}, bf16[464,128]{1,0:T(8,128)(2,1)S(1)}, u32[]{:S(2)}, u32[]{:S(2)}) collective-permute-start(bf16[464,128]{1,0:T(8,128)(2,1)S(1)} %get-tuple-element.110), channel_id=1, source_target_pairs={{0,2},{1,3},{2,0},{3,1},{4,6},{5,7},{6,4},{7,5},{8,10},{9,11},{10,... | collective-permute-start | bytes 356360 | tf_op jit(solution)/shard_map/ppermute | solution.py:818
  62.5 11.1 %collective-permute-start.14 = (bf16[464,128]{1,0:T(8,128)(2,1)S(1)}, bf16[464,128]{1,0:T(8,128)(2,1)S(1)}, u32[]{:S(2)}, u32[]{:S(2)}) collective-permute-start(bf16[464,128]{1,0:T(8,128)(2,1)S(1)} %get-tuple-element.111), channel_id=1, source_target_pairs={{0,3},{1,2},{2,1},{3,0},{4,7},{5,6},{6,5},{7,4},{8,11},{9,10},{10,... | collective-permute-start | bytes 356360 | tf_op jit(solution)/shard_map/ppermute | solution.py:818
  63.5 10.1 %collective-permute-start.15 = (bf16[464,128]{1,0:T(8,128)(2,1)S(1)}, bf16[464,128]{1,0:T(8,128)(2,1)S(1)}, u32[]{:S(2)}, u32[]{:S(2)}) collective-permute-start(bf16[464,128]{1,0:T(8,128)(2,1)S(1)} %get-tuple-element.112), channel_id=1, source_target_pairs={{0,1},{1,0},{2,3},{3,2},{4,5},{5,4},{6,7},{7,6},{8,9},{9,8},{10,11... | collective-permute-start | bytes 356360 | tf_op jit(solution)/shard_map/ppermute | solution.py:818
  73.7 20.5 %copy-start.2 = (f32[456,256]{1,0:T(8,128)S(1)}, f32[456,256]{1,0:T(8,128)}, u32[]{:S(2)}) copy-start(f32[456,256]{1,0:T(8,128)} %params_ref.1) | copy-start | bytes 1400836
  73.7 20.5 %copy-start.3 = (f32[456,256]{1,0:T(8,128)S(1)}, f32[456,256]{1,0:T(8,128)}, u32[]{:S(2)}) copy-start(f32[456,256]{1,0:T(8,128)} %first_ref.1) | copy-start | bytes 1400836
  73.7 20.5 %copy-start.4 = (f32[456,256]{1,0:T(8,128)S(1)}, f32[456,256]{1,0:T(8,128)}, u32[]{:S(2)}) copy-start(f32[456,256]{1,0:T(8,128)} %second_ref.1) | copy-start | bytes 1400836
  73.7 20.5 %copy-start.5 = (f32[456,256]{1,0:T(8,128)S(1)}, f32[456,256]{1,0:T(8,128)}, u32[]{:S(2)}) copy-start(f32[456,256]{1,0:T(8,128)} %averaged_ref.1) | copy-start | bytes 1400836
  73.8 4.9 %collective-permute-start.16 = (bf16[464,128]{1,0:T(8,128)(2,1)S(1)}, bf16[464,128]{1,0:T(8,128)(2,1)S(1)}, u32[]{:S(2)}, u32[]{:S(2)}) collective-permute-start(bf16[464,128]{1,0:T(8,128)(2,1)S(1)} %gathered.1.mine_ref), channel_id=1, source_target_pairs={{0,8},{4,12},{8,0},{12,4},{16,24},{20,28},{24,16},{28,20},{1,9},{5... | collective-permute-start | bytes 356360 | tf_op jit(solution)/shard_map/ppermute | solution.py:818
  78.7 4.9 %collective-permute-start.17 = (bf16[464,128]{1,0:T(8,128)(2,1)S(1)}, bf16[464,128]{1,0:T(8,128)(2,1)S(1)}, u32[]{:S(2)}, u32[]{:S(2)}) collective-permute-start(bf16[464,128]{1,0:T(8,128)(2,1)S(1)} %add.6.mine_ref), channel_id=1, source_target_pairs={{0,16},{4,20},{8,24},{12,28},{16,0},{20,4},{24,8},{28,12},{1,17},{... | collective-permute-start | bytes 356360 | tf_op jit(solution)/shard_map/ppermute | solution.py:818
  83.8 1.5 %collective-permute-start.18 = (f32[472,128]{1,0:T(8,128)S(1)}, f32[472,128]{1,0:T(8,128)S(1)}, u32[]{:S(2)}, u32[]{:S(2)}) collective-permute-start(f32[472,128]{1,0:T(8,128)S(1)} %finish.1.mine_ref), channel_id=1, source_target_pairs={{0,4},{4,0},{8,12},{12,8},{16,20},{20,16},{24,28},{28,24},{1,5},{5... | collective-permute-start | bytes 725000 | tf_op jit(solution)/shard_map/ppermute | solution.py:818
  83.8 9.4 %collective-permute-start.21 = (bf16[512,256]{1,0:T(8,128)(2,1)S(1)}, bf16[512,256]{1,0:T(8,128)(2,1)S(1)}, u32[]{:S(2)}, u32[]{:S(2)}) collective-permute-start(bf16[512,256]{1,0:T(8,128)(2,1)S(1)} %get-tuple-element.117), channel_id=1, source_target_pairs={{0,4},{4,0},{8,12},{12,8},{16,20},{20,16},{24,28},{28,24},{1,5},{5... | collective-permute-start | bytes 786440 | tf_op jit(solution)/shard_map/ppermute | solution.py:818
  84.3 9.3 %collective-permute-start.22 = (bf16[512,256]{1,0:T(8,128)(2,1)S(1)}, bf16[512,256]{1,0:T(8,128)(2,1)S(1)}, u32[]{:S(2)}, u32[]{:S(2)}) collective-permute-start(bf16[512,256]{1,0:T(8,128)(2,1)S(1)} %get-tuple-element.118), channel_id=1, source_target_pairs={{0,28},{4,8},{8,4},{12,16},{16,12},{20,24},{24,20},{28,0},{1,29},{... | collective-permute-start | bytes 786440 | tf_op jit(solution)/shard_map/ppermute | solution.py:823
  85.3 3.7 %collective-permute-start.19 = (f32[32,128]{1,0:T(8,128)S(1)}, f32[32,128]{1,0:T(8,128)S(1)}, u32[]{:S(2)}, u32[]{:S(2)}) collective-permute-start(f32[32,128]{1,0:T(8,128)S(1)} %pad_maximum_fusion), channel_id=1, source_target_pairs={{0,1},{1,0},{2,3},{3,2},{4,5},{5,4},{6,7},{7,6},{8,9},{9,8},{10,11... | collective-permute-start | bytes 49160 | tf_op jit(solution)/shard_map/ppermute | solution.py:818
  89.0 5.2 %collective-permute-start.20 = (f32[32,128]{1,0:T(8,128)S(1)}, f32[32,128]{1,0:T(8,128)S(1)}, u32[]{:S(2)}, u32[]{:S(2)}) collective-permute-start(f32[32,128]{1,0:T(8,128)S(1)} %fusion.stats_ref), channel_id=1, source_target_pairs={{0,2},{1,3},{2,0},{3,1},{4,6},{5,7},{6,4},{7,5},{8,10},{9,11},{10,... | collective-permute-start | bytes 49160 | tf_op jit(solution)/shard_map/ppermute | solution.py:818

commit v7 on v6

--- a/solution.py
+++ b/solution.py
@@ -529,10 +529,14 @@
 
         table_rows = node_grad_ref.shape[0] + 4 * width
         d_inner, d_pre = d_inner_ref[...], d_pre_ref[...]
-        second_sum = dot(jnp.ones((16, d_inner.shape[0]), B16), d_inner)[0:1, :]
-        table_grad = dot(chosen_rows(region_row_ref[...], 0, regions), d_pre)
-        put(3 * width, dot_rows(hidden_ref[...], d_inner))
-        put(0, dot_rows(hs_ref[...], d_pre))
+        left = jnp.concatenate([hidden_ref[...].T, jnp.ones((16, d_inner.shape[0]), B16)], axis=0)
+        both = dot(left, d_inner)
+        second_sum = both[width : width + 1, :]
+        put(3 * width, both[0:width, :])
+        left = jnp.concatenate([hs_ref[...].T, chosen_rows(region_row_ref[...], 0, -(-regions // 16) * 16)], axis=0)
+        both = dot(left, d_pre)
+        table_grad = both[width : width + regions, :]
+        put(0, both[0:width, :])
         put(width, dot_rows(hr_ref[...], d_pre))
         put(2 * width, dot_rows(x_ref[...], d_pre))
         put(4 * width, node_grad_ref[...])
@@ -609,14 +613,10 @@
     )(index.reshape(1, -1), d_pre, weights)
 
 
-def receiver_part_kernel(index_row_ref, d_pre_ref, w_ref, part_ref, back_ref, own_ref, pair_ref, off_ref):
-    nodes, width = back_ref.shape
-    slot = pl.program_id(0)
+def receiver_part_kernel(index_row_ref, d_pre_ref, w_ref, part_ref, pair_ref, off_ref):
+    nodes, width = pair_ref.shape
+    slot = pl.program_id(0) + 1
     part = node_part_of(index_row_ref, d_pre_ref, w_ref[width : 2 * width, :], slot, nodes) + part_ref[...]
-
-    @pl.when(slot == 0)
-    def _():
-        own_ref[...] = part + back_ref[...]
 
     @pl.when(slot == 1)
     def _():
@@ -627,22 +627,44 @@
         off_ref[...] = part.astype(B16)
 
 
-def receiver_part(index, d_pre, weights, part, back):
+def receiver_part(index, d_pre, weights, part, nodes):
     count, width = d_pre.shape
-    nodes = back.shape[0]
-    half = jax.ShapeDtypeStruct(back.shape, B16)
+    half = jax.ShapeDtypeStruct((nodes, width), B16)
     return pl.pallas_call(
         receiver_part_kernel,
-        grid=(3,),
+        grid=(2,),
         in_specs=[
-            whole((1, count)), whole((count, width)), whole(weights.shape), tiled(nodes, width), whole(back.shape),
+            whole((1, count)), whole((count, width)), whole(weights.shape),
+            pl.BlockSpec((nodes, width), lambda i: (i + 1, 0)),
         ],
-        out_specs=[whole(back.shape)] * 3,
-        out_shape=[jax.ShapeDtypeStruct(back.shape, F32), half, half],
+        out_specs=[whole((nodes, width))] * 2,
+        out_shape=[half, half],
         compiler_params=PARAMS,
         name="receiver_part",
         cost_estimate=pl.CostEstimate(
-            flops=6 * count * width * nodes, transcendentals=0, bytes_accessed=count * width * 2
+            flops=4 * count * width * nodes, transcendentals=0, bytes_accessed=count * width * 2
+        ),
+    )(index.reshape(1, -1), d_pre, weights, part)
+
+
+def own_part_kernel(index_row_ref, d_pre_ref, w_ref, part_ref, back_ref, own_ref):
+    nodes, width = own_ref.shape
+    part = node_part_of(index_row_ref, d_pre_ref, w_ref[width : 2 * width, :], 0, nodes)
+    own_ref[...] = part + (part_ref[...] + back_ref[...])
+
+
+def own_part(index, d_pre, weights, part, back):
+    count, width = d_pre.shape
+    return pl.pallas_call(
+        own_part_kernel,
+        grid=(1,),
+        in_specs=[whole((1, count)), whole((count, width)), whole(weights.shape), whole(back.shape), whole(back.shape)],
+        out_specs=whole(back.shape),
+        out_shape=jax.ShapeDtypeStruct(back.shape, F32),
+        compiler_params=PARAMS,
+        name="own_part",
+        cost_estimate=pl.CostEstimate(
+            flops=2 * count * width * back.shape[0], transcendentals=0, bytes_accessed=count * width * 2
         ),
     )(index.reshape(1, -1), d_pre, weights, part, back)
 
@@ -873,19 +895,21 @@
     )
 
     low_rows = vector_row % share
-    part, *sent = parted(kept, flipped(sent, "edge", 1), share, low_rows)
+    grad_edges = edge_grads(d_pre, weights)
+    other, grad_edges = lax.optimization_barrier((flipped(sent, "edge", 1), grad_edges))
+    part, *sent = parted(kept, other, share, low_rows)
     came = [flipped(sent[k - 1], "feat", k) for k in ways(feats)]
     d_pre, part = lax.optimization_barrier((d_pre, part))
     send_part = sender_part(send, d_pre, weights, nodes)
-    part_own, part_pair, part_off = receiver_part(recv, d_pre, weights, send_part, back)
-    part, part_own, part_pair, part_off = lax.optimization_barrier((part, part_own, part_pair, part_off))
+    part_pair, part_off = receiver_part(recv, d_pre, weights, send_part, nodes)
+    part, part_pair, part_off = lax.optimization_barrier((part, part_pair, part_off))
     wire = gathered(part, came, low_rows)
     bit = 2
     while 2 * bit < blocks:
         wire = add(wire, flipped(wire, "edge", bit), low_rows)
         bit *= 2
-    grad_edges = edge_grads(d_pre, weights)
-    wire, part_pair, part_off, grad_edges = lax.optimization_barrier((wire, part_pair, part_off, grad_edges))
+    part_own = own_part(recv, d_pre, weights, send_part, back)
+    wire, part_pair, part_off, part_own = lax.optimization_barrier((wire, part_pair, part_off, part_own))
     mine = finish(wire, flipped(wire, "edge", bit), share, low_rows, vector_row // share)
     grads_off = across(part_off, "edge")
     grads_pair = flipped(part_pair, "edge", 1)

time: 96.9 us -> 95.1 us (0.981)
  waiting for transfers between devices: 17.5 us -> 15.4 us
    ppermute x19, waiting for transfers between devices: 13.6 us -> 11 us  [flipped(): lax.ppermute(value, axis, [(i, i ^ bit) for i in range(lax.axis_size(axis...]
    pallas_call x1 -> x2, Pallas kernels: 5.1 us -> 5.03 us  [the longest x1 3.38 us: receiver_part(): pl.pallas_call(receiver_part_kernel, grid=(2,), in_specs=[whole((1, count...]
  transfers between devices with their start and end apart: 23 -> 23, of which waited for: 12 -> 12; matrix products, arithmetic and copies ran while one was open for 0% -> 0% of each run, Pallas kernels for 35% -> 36%
where the time goes in v7:
time: 95.1 us; the launch traced here: 94.9 us
  Pallas kernels  52 us (55%)
  starting transfers between devices  25.4 us (27%)
  waiting for transfers between devices  15.4 us (16%)
  between operations  1.75 us (2%)
    ppermute x19, starting transfers between devices, flipped(): lax.ppermute(value, axis, [(i, i ^ bit) for i in range(lax.axis_size(axis...  18.9 us
    ppermute x19, waiting for transfers between devices, flipped(): lax.ppermute(value, axis, [(i, i ^ bit) for i in range(lax.axis_size(axis...  11 us
    pallas_call x1, Pallas kernels, edge_forward(): pl.pallas_call(edge_forward_kernel, grid=(1,), in_specs=[whole((count //...  7.28 us
    pallas_call x3, Pallas kernels, gather_near(): pl.pallas_call(gather_near_kernel, grid=(1,), in_specs=[whole((edges // L...  7.23 us
    pallas_call x1, Pallas kernels, edge_backward(): pl.pallas_call(edge_backward_kernel, grid=(count // TILE,), in_specs=[who...  7.1 us
    ppermute x4, starting transfers between devices, across(): lax.ppermute(value, axis, [(i, (i + 1 if i % 2 else i - 1) % count) for i...  6.52 us
    pallas_call x1, Pallas kernels, sender_part(): pl.pallas_call(sender_part_kernel, grid=(3,), in_specs=[whole((1, count))...  4.96 us
    pallas_call x1, Pallas kernels, near_sum(): pl.pallas_call(near_sum_kernel, out_shape=[half, half, jax.ShapeDtypeStru...  4.51 us
  transfers between devices with their start and end apart: 23, of which 12 were waited for; matrix products, arithmetic and copies ran while one was open for 0% of the time, Pallas kernels for 36%

profile of v7, /device:TPU:0, one launch (start us, length us, event | category | flops | bytes accessed | tf_op | source)
XLA Modules:
  0.0 94.9 jit_solution(1050075518778573805)
XLA Ops:
  0.6 0.5 collective-permute-start.1
  1.2 1.2 %prologue.1 = (bf16[456,128]{1,0:T(8,128)(2,1)S(1)}, s32[32,128]{1,0:T(8,128)S(1)}, s32[32,128]{1,0:T(8,128)S(1)}, bf16[512,256]{1,0:T(8,128)(2,1)S(1)}) custom-call(f32[456,256]{1,0:T(8,128)} %params_ref.1, s32[32,128]{1,0:T(8,128)} %bitcast.34, s32[32,128]{1,0:T(8,128)} %bitcast.35, bf16[512,256]{1,0:T(8,128)(2,1)} %bitcast.32), custom_call_target="tpu_custom_call" | custom-call | tf_op jit(solution)/shard_map/prologue/pallas_call | solution.py:122
  2.3 3.7 %collective-permute-start.2 = (bf16[456,128]{1,0:T(8,128)(2,1)S(1)}, bf16[456,128]{1,0:T(8,128)(2,1)S(1)}, u32[]{:S(2)}, u32[]{:S(2)}) collective-permute-start(bf16[456,128]{1,0:T(8,128)(2,1)S(1)} %get-tuple-element.71.refs_0_), channel_id=1, source_target_pairs={{0,2},{1,3},{2,0},{3,1},{4,6},{5,7},{6,4},{7,5},{8,10},{9,11},{10,... | collective-permute-start | bytes 350216 | tf_op jit(solution)/shard_map/ppermute | solution.py:840
  6.0 1.3 %collective-permute-start.3 = (bf16[456,128]{1,0:T(8,128)(2,1)S(1)}, bf16[456,128]{1,0:T(8,128)(2,1)S(1)}, u32[]{:S(2)}, u32[]{:S(2)}) collective-permute-start(bf16[456,128]{1,0:T(8,128)(2,1)S(1)} %get-tuple-element.71.refs_0_), channel_id=1, source_target_pairs={{0,3},{1,2},{2,1},{3,0},{4,7},{5,6},{6,5},{7,4},{8,11},{9,10},{10,... | collective-permute-start | bytes 350216 | tf_op jit(solution)/shard_map/ppermute | solution.py:840
  7.3 0.2 collective-permute-start.4
  7.6 2.0 %collective-permute-start = (bf16[512,256]{1,0:T(8,128)(2,1)}, bf16[512,256]{1,0:T(8,128)(2,1)S(1)}, u32[]{:S(2)}, u32[]{:S(2)}) collective-permute-start(bf16[512,256]{1,0:T(8,128)(2,1)} %bitcast.33), channel_id=1, source_target_pairs={{0,28},{4,8},{8,4},{12,16},{16,12},{20,24},{24,20},{28,0},{1,29},{... | collective-permute-start | bytes 786440 | tf_op jit(solution)/shard_map/ppermute | solution.py:845
  9.6 2.4 %gather_near.4.near_ref = bf16[4096,256]{1,0:T(8,128)(2,1)S(1)} custom-call(s32[32,128]{1,0:T(8,128)S(1)} %get-tuple-element.69.index_ref.recv_ref, bf16[512,256]{1,0:T(8,128)(2,1)S(1)} %get-tuple-element.68.own_ref.h_ref, bf16[512,256]{1,0:T(8,128)(2,1)S(1)} %collective-permute-done.1.pair_ref), custom_call_target="tpu_custom_call" | custom-call | flops 2147483648 | bytes 2097152 | tf_op jit(solution)/shard_map/gather_near/pallas_call | solution.py:151
  12.0 2.4 %gather_near.3.near_ref = bf16[4096,256]{1,0:T(8,128)(2,1)S(1)} custom-call(s32[32,128]{1,0:T(8,128)S(1)} %get-tuple-element.70.index_ref, bf16[512,256]{1,0:T(8,128)(2,1)S(1)} %get-tuple-element.68.own_ref.h_ref, bf16[512,256]{1,0:T(8,128)(2,1)S(1)} %collective-permute-done.1.pair_ref), custom_call_target="tpu_custom_call" | custom-call | flops 2147483648 | bytes 2097152 | tf_op jit(solution)/shard_map/gather_near/pallas_call | solution.py:151
  14.4 0.7 collective-permute-done.2
  15.1 0.0 collective-permute-done.3
  15.1 1.1 %collective-permute-done.4 = bf16[456,128]{1,0:T(8,128)(2,1)S(1)} collective-permute-done((bf16[456,128]{1,0:T(8,128)(2,1)S(1)}, bf16[456,128]{1,0:T(8,128)(2,1)S(1)}, u32[]{:S(2)}, u32[]{:S(2)}) %collective-permute-start.4) | collective-permute-done | bytes 116768 | tf_op jit(solution)/shard_map/ppermute | solution.py:840
  16.3 0.1 collective-permute-start.6
  16.4 0.5 collective-permute-start.5
  16.9 0.2 collective-permute-done.off_ref
  17.1 1.3 %gather_off.3.hr_ref = bf16[4096,256]{1,0:T(8,128)(2,1)S(1)} custom-call(s32[32,128]{1,0:T(8,128)S(1)} %get-tuple-element.69.index_ref.recv_ref, bf16[512,256]{1,0:T(8,128)(2,1)S(1)} %collective-permute-done.off_ref, bf16[4096,256]{1,0:T(8,128)(2,1)S(1)} %gather_near.4.near_ref), custom_call_target="tpu_custom_call" | custom-call | flops 1073741824 | bytes 4194304 | tf_op jit(solution)/shard_map/gather_off/pallas_call | solution.py:176
  18.4 0.0 copy-start.1
  18.4 0.0 copy-start.6
  18.5 1.3 %gather_off.2.hs_ref = bf16[4096,256]{1,0:T(8,128)(2,1)S(1)} custom-call(s32[32,128]{1,0:T(8,128)S(1)} %get-tuple-element.70.index_ref, bf16[512,256]{1,0:T(8,128)(2,1)S(1)} %collective-permute-done.off_ref, bf16[4096,256]{1,0:T(8,128)(2,1)S(1)} %gather_near.3.near_ref), custom_call_target="tpu_custom_call" | custom-call | flops 1073741824 | bytes 4194304 | tf_op jit(solution)/shard_map/gather_off/pallas_call | solution.py:176
  19.8 0.2 copy-done.1
  20.0 7.3 %edge_forward.1 = (bf16[1824,256]{1,0:T(8,128)(2,1)S(1)}, bf16[4096,256]{1,0:T(8,128)(2,1)S(1)}, bf16[4096,256]{1,0:T(8,128)(2,1)S(1)}, s16[656,256]{1,0:T(8,128)(2,1)S(1)}) custom-call(s32[32,128]{1,0:T(8,128)S(1)} %bitcast.25, s32[1,4096]{1,0:T(1,128)S(1)} %bitcast.20, bf16[4096,256]{1,0:T(8,128)(2,1)S(1)} %gather_off.2.hs_ref, ...), custom_call_target="tpu_custom_call" | custom-call | flops 4831838208 | bytes 10485760 | tf_op jit(solution)/shard_map/edge_forward/pallas_call | solution.py:297
  27.3 2.0 %collective-permute-start.9 = (s16[656,256]{1,0:T(8,128)(2,1)S(1)}, s16[656,256]{1,0:T(8,128)(2,1)S(1)}, u32[]{:S(2)}, u32[]{:S(2)}) collective-permute-start(s16[656,256]{1,0:T(8,128)(2,1)S(1)} %get-tuple-element.84), channel_id=1, source_target_pairs={{0,28},{4,8},{8,4},{12,16},{16,12},{20,24},{24,20},{28,0},{1,29},{... | collective-permute-start | bytes 1007624 | tf_op jit(solution)/shard_map/ppermute | solution.py:845
  29.3 4.5 %near_sum.1 = (f32[256,256]{1,0:T(8,128)S(1)}, f32[256,256]{1,0:T(8,128)S(1)}, f32[512,256]{1,0:T(8,128)S(1)}) custom-call(s32[1,4096]{1,0:T(1,128)S(1)} %bitcast.21, bf16[4096,256]{1,0:T(8,128)(2,1)S(1)} %get-tuple-element.75.high_ref, bf16[4096,256]{1,0:T(8,128)(2,1)S(1)} %get-tuple-element.76.low_ref), custom_call_target="tpu_custom_call" | custom-call | flops 4294967296 | bytes 4194304 | tf_op jit(solution)/shard_map/near_sum/pallas_call | solution.py:382
  33.8 0.1 collective-permute-start.7
  33.9 0.5 collective-permute-start.8
  34.4 3.4 %edge_slope.1 = (bf16[4096,256]{1,0:T(8,128)(2,1)S(1)}, f32[4096,256]{1,0:T(8,128)S(1)}) custom-call(s32[32,128]{1,0:T(8,128)S(1)} %bitcast.26, bf16[4096,256]{1,0:T(8,128)(2,1)S(1)} %gather_off.2.hs_ref, bf16[4096,256]{1,0:T(8,128)(2,1)S(1)} %gather_off.3.hr_ref, bf16[4096,256]{1,0:T(8,128)(2,1)S(1)} %bitcast.18, bf16[1824,256]{1,0:T(8,128)(2,1)S(1)} %get-tuple-element.78.w_ref), custom_call_target="tpu_custom_call" | custom-call | flops 2147483648 | bytes 12582912 | tf_op jit(solution)/shard_map/edge_slope/pallas_call | solution.py:334
  37.8 0.0 collective-permute-done.7.pair_ref
  37.8 0.5 collective-permute-done.9.off_ref
  38.3 1.2 %node_update.1 = (bf16[512,256]{1,0:T(8,128)(2,1)S(1)}, bf16[512,256]{1,0:T(8,128)(2,1)S(1)}, bf16[512,256]{1,0:T(8,128)(2,1)S(1)}, bf16[512,256]{1,0:T(8,128)(2...) custom-call(bf16[512,256]{1,0:T(8,128)(2,1)S(1)} %get-tuple-element.68.own_ref.h_ref, ...), custom_call_target="tpu_custom_call" | custom-call | flops 335544320 | bytes 2621440 | tf_op jit(solution)/shard_map/node_update/pallas_call | solution.py:435
  39.6 0.1 collective-permute-start.11
  39.6 1.3 %collective-permute-start.10 = (bf16[512,256]{1,0:T(8,128)(2,1)S(1)}, bf16[512,256]{1,0:T(8,128)(2,1)S(1)}, u32[]{:S(2)}, u32[]{:S(2)}) collective-permute-start(bf16[512,256]{1,0:T(8,128)(2,1)S(1)} %get-tuple-element.91.own_ref), channel_id=1, source_target_pairs={{0,28},{4,8},{8,4},{12,16},{16,12},{20,24},{24,20},{28,0},{1,29},{... | collective-permute-start | bytes 786440 | tf_op jit(solution)/shard_map/ppermute | solution.py:845
  40.9 1.3 %node_grads.1 = (f32[512,256]{1,0:T(8,128)}, f32[768,256]{1,0:T(8,128)S(1)}, f32[4,256]{1,0:T(4,128)S(1)}, f32[512,256]{1,0:T(8,128)S(1)}) custom-call(bf16[512,256]{1,0:T(8,128)(2,1)S(1)} %get-tuple-element.68.own_ref.h_ref, bf16[512,256]{1,0:T(8,128)(2,1)S(1)} %get-tuple-element.85.agg_ref, bf16[512,256]{1,0:T(8,128)(2,1)S(1)} %get-tuple-element.86.hidden_ref, ...), custom_call_target="tpu_custom_call" | custom-call | flops 268435456 | bytes 2359296 | tf_op jit(solution)/shard_map/node_grads/pallas_call | solution.py:474
  42.2 1.7 %edge_unit.1 = (f32[4096,256]{1,0:T(8,128)S(1)}, f32[4096,128]{1,0:T(8,128)S(1)}) custom-call(bf16[4096,256]{1,0:T(8,128)(2,1)S(1)} %get-tuple-element.94.hidden_ref, bf16[1824,256]{1,0:T(8,128)(2,1)S(1)} %get-tuple-element.78.w_ref), custom_call_target="tpu_custom_call" | custom-call | flops 536870912 | bytes 8388608 | tf_op jit(solution)/shard_map/edge_unit/pallas_call | solution.py:357
  43.9 2.4 %gather_near.5.near_ref = bf16[4096,256]{1,0:T(8,128)(2,1)S(1)} custom-call(s32[32,128]{1,0:T(8,128)S(1)} %get-tuple-element.69.index_ref.recv_ref, bf16[512,256]{1,0:T(8,128)(2,1)S(1)} %get-tuple-element.91.own_ref, bf16[512,256]{1,0:T(8,128)(2,1)S(1)} %collective-permute-done.11.pair_ref), custom_call_target="tpu_custom_call" | custom-call | flops 2147483648 | bytes 2097152 | tf_op jit(solution)/shard_map/gather_near/pallas_call | solution.py:151
  46.4 2.7 %collective-permute-done.10.off_ref = bf16[512,256]{1,0:T(8,128)(2,1)S(1)} collective-permute-done((bf16[512,256]{1,0:T(8,128)(2,1)S(1)}, bf16[512,256]{1,0:T(8,128)(2,1)S(1)}, u32[]{:S(2)}, u32[]{:S(2)}) %collective-permute-start.10) | collective-permute-done | bytes 262176 | tf_op jit(solution)/shard_map/ppermute | solution.py:845
  49.1 7.1 %edge_backward.1 = (bf16[4096,256]{1,0:T(8,128)(2,1)S(1)}, f32[1824,128]{1,0:T(8,128)S(1)}, f32[1824,128]{1,0:T(8,128)S(1)}) custom-call(s32[32,128]{1,0:T(8,128)S(1)} %get-tuple-element.69.index_ref.recv_ref, s32[1,4096]{1,0:T(1,128)S(1)} %bitcast.27, bf16[512,256]{1,0:T(8,128)(2,1)S(1)} %collective-permute-done.10.off_ref, ...), custom_call_target="tpu_custom_call" | custom-call | flops 4294967296 | bytes 20971520 | tf_op jit(solution)/shard_map/edge_backward/pallas_call | solution.py:564
  56.2 0.1 collective-permute-start.12
  56.2 1.9 %edge_grads.1 = bf16[4096,256]{1,0:T(8,128)(2,1)} custom-call(bf16[4096,256]{1,0:T(8,128)(2,1)S(1)} %get-tuple-element.105.d_pre_ref, bf16[1824,256]{1,0:T(8,128)(2,1)S(1)} %get-tuple-element.78.w_ref), custom_call_target="tpu_custom_call" | custom-call | flops 536870912 | bytes 4194304 | tf_op jit(solution)/shard_map/edge_grads/pallas_call | solution.py:679
  58.2 0.5 collective-permute-done.12.other_ref
  58.7 0.1 parted.1
  58.8 3.3 %collective-permute-start.13 = (bf16[464,128]{1,0:T(8,128)(2,1)S(1)}, bf16[464,128]{1,0:T(8,128)(2,1)S(1)}, u32[]{:S(2)}, u32[]{:S(2)}) collective-permute-start(bf16[464,128]{1,0:T(8,128)(2,1)S(1)} %get-tuple-element.109), channel_id=1, source_target_pairs={{0,2},{1,3},{2,0},{3,1},{4,6},{5,7},{6,4},{7,5},{8,10},{9,11},{10,... | collective-permute-start | bytes 356360 | tf_op jit(solution)/shard_map/ppermute | solution.py:840
  62.1 1.1 %collective-permute-start.14 = (bf16[464,128]{1,0:T(8,128)(2,1)S(1)}, bf16[464,128]{1,0:T(8,128)(2,1)S(1)}, u32[]{:S(2)}, u32[]{:S(2)}) collective-permute-start(bf16[464,128]{1,0:T(8,128)(2,1)S(1)} %get-tuple-element.110), channel_id=1, source_target_pairs={{0,3},{1,2},{2,1},{3,0},{4,7},{5,6},{6,5},{7,4},{8,11},{9,10},{10,... | collective-permute-start | bytes 356360 | tf_op jit(solution)/shard_map/ppermute | solution.py:840
  63.2 0.0 collective-permute-start.15
  63.2 5.0 %sender_part.1.part_ref = f32[1536,256]{1,0:T(8,128)S(1)} custom-call(s32[1,4096]{1,0:T(1,128)S(1)} %bitcast.24, bf16[4096,256]{1,0:T(8,128)(2,1)S(1)} %get-tuple-element.105.d_pre_ref, bf16[1824,256]{1,0:T(8,128)(2,1)S(1)} %get-tuple-element.78.w_ref), custom_call_target="tpu_custom_call" | custom-call | flops 3221225472 | bytes 2097152 | tf_op jit(solution)/shard_map/sender_part/pallas_call | solution.py:602
  68.1 3.4 %receiver_part.1 = (bf16[512,256]{1,0:T(8,128)(2,1)S(1)}, bf16[512,256]{1,0:T(8,128)(2,1)S(1)}) custom-call(s32[1,4096]{1,0:T(1,128)S(1)} %bitcast.22, bf16[4096,256]{1,0:T(8,128)(2,1)S(1)} %get-tuple-element.105.d_pre_ref, bf16[1824,256]{1,0:T(8,128)(2,1)S(1)} %get-tuple-element.78.w_ref, f32[1536,256]{1,0:T(8,128)S(1)} %sender_part.1.part_ref), custom_call_target="tpu_custom_call" | custom-call | flops 2147483648 | bytes 2097152 | tf_op jit(solution)/shard_map/receiver_part/pallas_call | solution.py:633
  71.5 0.0 collective-permute-done.13.refs_0_
  71.5 0.6 collective-permute-done.15.refs_2_
  72.1 0.1 gathered.1.mine_ref
  72.2 0.8 collective-permute-start.16
  73.0 1.7 %own_part.1.own_ref = f32[512,256]{1,0:T(8,128)S(1)} custom-call(s32[1,4096]{1,0:T(1,128)S(1)} %bitcast.23, bf16[4096,256]{1,0:T(8,128)(2,1)S(1)} %get-tuple-element.105.d_pre_ref, bf16[1824,256]{1,0:T(8,128)(2,1)S(1)} %get-tuple-element.78.w_ref, f32[1536,256]{1,0:T(8,128)S(1)} %sender_part.1.part_ref, f32[512,256]{1,0:T(8,128)S(1)} %get-tuple-element.114.back_ref), custom_call_target="tpu_custom_call" | custom-call | flops 1073741824 | bytes 2097152 | tf_op jit(solution)/shard_map/own_part/pallas_call | solution.py:658
  74.6 2.4 %collective-permute-done.16.other_ref = bf16[464,128]{1,0:T(8,128)(2,1)S(1)} collective-permute-done((bf16[464,128]{1,0:T(8,128)(2,1)S(1)}, bf16[464,128]{1,0:T(8,128)(2,1)S(1)}, u32[]{:S(2)}, u32[]{:S(2)}) %collective-permute-start.16) | collective-permute-done | bytes 118816 | tf_op jit(solution)/shard_map/ppermute | solution.py:840
  77.1 1.5 %collective-permute-start.17 = (bf16[464,128]{1,0:T(8,128)(2,1)S(1)}, bf16[464,128]{1,0:T(8,128)(2,1)S(1)}, u32[]{:S(2)}, u32[]{:S(2)}) collective-permute-start(bf16[464,128]{1,0:T(8,128)(2,1)S(1)} %add.6.mine_ref), channel_id=1, source_target_pairs={{0,16},{4,20},{8,24},{12,28},{16,0},{20,4},{24,8},{28,12},{1,17},{... | collective-permute-start | bytes 356360 | tf_op jit(solution)/shard_map/ppermute | solution.py:840
  78.6 3.4 %collective-permute-done.17.other_ref = bf16[464,128]{1,0:T(8,128)(2,1)S(1)} collective-permute-done((bf16[464,128]{1,0:T(8,128)(2,1)S(1)}, bf16[464,128]{1,0:T(8,128)(2,1)S(1)}, u32[]{:S(2)}, u32[]{:S(2)}) %collective-permute-start.17) | collective-permute-done | bytes 118816 | tf_op jit(solution)/shard_map/ppermute | solution.py:840
  82.0 0.2 finish.1.mine_ref
  82.2 0.0 collective-permute-start.18
  82.2 0.5 collective-permute-start.21
  82.7 1.3 %collective-permute-start.22 = (bf16[512,256]{1,0:T(8,128)(2,1)S(1)}, bf16[512,256]{1,0:T(8,128)(2,1)S(1)}, u32[]{:S(2)}, u32[]{:S(2)}) collective-permute-start(bf16[512,256]{1,0:T(8,128)(2,1)S(1)} %get-tuple-element.118), channel_id=1, source_target_pairs={{0,28},{4,8},{8,4},{12,16},{16,12},{20,24},{24,20},{28,0},{1,29},{... | collective-permute-start | bytes 786440 | tf_op jit(solution)/shard_map/ppermute | solution.py:845
  83.9 0.0 collective-permute-done.18.other_ref
  84.0 2.0 %collective-permute-start.19 = (f32[32,128]{1,0:T(8,128)S(1)}, f32[32,128]{1,0:T(8,128)S(1)}, u32[]{:S(2)}, u32[]{:S(2)}) collective-permute-start(f32[32,128]{1,0:T(8,128)S(1)} %pad_maximum_fusion), channel_id=1, source_target_pairs={{0,1},{1,0},{2,3},{3,2},{4,5},{5,4},{6,7},{7,6},{8,9},{9,8},{10,11... | collective-permute-start | bytes 49160 | tf_op jit(solution)/shard_map/ppermute | solution.py:840
  86.0 1.8 %collective-permute-done.19 = f32[32,128]{1,0:T(8,128)S(1)} collective-permute-done((f32[32,128]{1,0:T(8,128)S(1)}, f32[32,128]{1,0:T(8,128)S(1)}, u32[]{:S(2)}, u32[]{:S(2)}) %collective-permute-start.19) | collective-permute-done | bytes 16416 | tf_op jit(solution)/shard_map/ppermute | solution.py:840
  87.8 2.7 %collective-permute-start.20 = (f32[32,128]{1,0:T(8,128)S(1)}, f32[32,128]{1,0:T(8,128)S(1)}, u32[]{:S(2)}, u32[]{:S(2)}) collective-permute-start(f32[32,128]{1,0:T(8,128)S(1)} %fusion.stats_ref), channel_id=1, source_target_pairs={{0,2},{1,3},{2,0},{3,1},{4,6},{5,7},{6,4},{7,5},{8,10},{9,11},{10,... | collective-permute-start | bytes 49160 | tf_op jit(solution)/shard_map/ppermute | solution.py:840
  91.1 0.0 collective-permute-done.21.pair_ref
  91.1 0.9 collective-permute-done.22.off_ref
  92.0 0.4 collective-permute-done.20.more_ref
  92.4 2.3 %adam.1 = (f32[456,256]{1,0:T(8,128)}, f32[456,256]{1,0:T(8,128)}, f32[456,256]{1,0:T(8,128)}, f32[456,256]{1,0:T(8,128)}, f32[1,1]{1,0:T(1,128)}, /*index=5*/f32[8,256]{1,0:T(8,128)}, f32[512,256]{1,0:T(8,128)}) custom-call(f32[8,128]{1,0:T(8,128)S(1)} %broadcast_in_dim.15.step_ref, f32[32,128]{1,0:T(8,128)S(1)} %fusion.stats_ref, ...), custom_call_target="tpu_custom_call" | custom-call | flops 2334720 | bytes 3735552 | tf_op jit(solution)/shard_map/adam/pallas_call | solution.py:821
  (28 shorter events, 0.1 us)
Async XLA Ops:
  0.6 8.9 %collective-permute-start.1 = (bf16[512,256]{1,0:T(8,128)(2,1)}, bf16[512,256]{1,0:T(8,128)(2,1)S(1)}, u32[]{:S(2)}, u32[]{:S(2)}) collective-permute-start(bf16[512,256]{1,0:T(8,128)(2,1)} %bitcast.31), channel_id=1, source_target_pairs={{0,4},{4,0},{8,12},{12,8},{16,20},{20,16},{24,28},{28,24},{1,5},{5... | collective-permute-start | bytes 786440 | tf_op jit(solution)/shard_map/ppermute | solution.py:840
  2.3 12.8 %collective-permute-start.2 = (bf16[456,128]{1,0:T(8,128)(2,1)S(1)}, bf16[456,128]{1,0:T(8,128)(2,1)S(1)}, u32[]{:S(2)}, u32[]{:S(2)}) collective-permute-start(bf16[456,128]{1,0:T(8,128)(2,1)S(1)} %get-tuple-element.71.refs_0_), channel_id=1, source_target_pairs={{0,2},{1,3},{2,0},{3,1},{4,6},{5,7},{6,4},{7,5},{8,10},{9,11},{10,... | collective-permute-start | bytes 350216 | tf_op jit(solution)/shard_map/ppermute | solution.py:840
  6.0 9.1 %collective-permute-start.3 = (bf16[456,128]{1,0:T(8,128)(2,1)S(1)}, bf16[456,128]{1,0:T(8,128)(2,1)S(1)}, u32[]{:S(2)}, u32[]{:S(2)}) collective-permute-start(bf16[456,128]{1,0:T(8,128)(2,1)S(1)} %get-tuple-element.71.refs_0_), channel_id=1, source_target_pairs={{0,3},{1,2},{2,1},{3,0},{4,7},{5,6},{6,5},{7,4},{8,11},{9,10},{10,... | collective-permute-start | bytes 350216 | tf_op jit(solution)/shard_map/ppermute | solution.py:840
  7.3 8.9 %collective-permute-start.4 = (bf16[456,128]{1,0:T(8,128)(2,1)S(1)}, bf16[456,128]{1,0:T(8,128)(2,1)S(1)}, u32[]{:S(2)}, u32[]{:S(2)}) collective-permute-start(bf16[456,128]{1,0:T(8,128)(2,1)S(1)} %get-tuple-element.71.refs_0_), channel_id=1, source_target_pairs={{0,1},{1,0},{2,3},{3,2},{4,5},{5,4},{6,7},{7,6},{8,9},{9,8},{10,11... | collective-permute-start | bytes 350216 | tf_op jit(solution)/shard_map/ppermute | solution.py:840
  7.6 9.5 %collective-permute-start = (bf16[512,256]{1,0:T(8,128)(2,1)}, bf16[512,256]{1,0:T(8,128)(2,1)S(1)}, u32[]{:S(2)}, u32[]{:S(2)}) collective-permute-start(bf16[512,256]{1,0:T(8,128)(2,1)} %bitcast.33), channel_id=1, source_target_pairs={{0,28},{4,8},{8,4},{12,16},{16,12},{20,24},{24,20},{28,0},{1,29},{... | collective-permute-start | bytes 786440 | tf_op jit(solution)/shard_map/ppermute | solution.py:845
  16.3 3.5 %collective-permute-start.6 = (bf16[1368,128]{1,0:T(8,128)(2,1)S(1)}, bf16[1368,128]{1,0:T(8,128)(2,1)S(1)}, u32[]{:S(2)}, u32[]{:S(2)}) collective-permute-start(bf16[1368,128]{1,0:T(8,128)(2,1)S(1)} %constant_dynamic-update-slice_fusion.refs_1_), channel_id=1, source_target_pairs={{0,4},{4,0},{8,12},{12,8},{16,20},{20,16},{24,28},{28,24},{1,5},{5... | collective-permute-start | bytes 1050632 | tf_op jit(solution)/shard_map/ppermute | solution.py:840
  16.4 3.4 %collective-permute-start.5 = (bf16[456,128]{1,0:T(8,128)(2,1)S(1)}, bf16[456,128]{1,0:T(8,128)(2,1)S(1)}, u32[]{:S(2)}, u32[]{:S(2)}) collective-permute-start(bf16[456,128]{1,0:T(8,128)(2,1)S(1)} %get-tuple-element.71.refs_0_), channel_id=1, source_target_pairs={{0,4},{4,0},{8,12},{12,8},{16,20},{20,16},{24,28},{28,24},{1,5},{5... | collective-permute-start | bytes 350216 | tf_op jit(solution)/shard_map/ppermute | solution.py:840
  18.4 1.6 %copy-start.1 = (bf16[1,4096,256]{2,1,0:T(8,128)(2,1)S(1)}, bf16[1,4096,256]{2,1,0:T(8,128)(2,1)}, u32[]{:S(2)}) copy-start(bf16[1,4096,256]{2,1,0:T(8,128)(2,1)} %param.13) | copy-start | bytes 6291460
  18.4 1.6 %copy-start.6 = (s32[4096]{0:T(1024)S(1)}, s32[4096]{0:T(1024)}, u32[]{:S(2)}) copy-start(s32[4096]{0:T(1024)} %param.16) | copy-start | bytes 49156
  27.3 11.0 %collective-permute-start.9 = (s16[656,256]{1,0:T(8,128)(2,1)S(1)}, s16[656,256]{1,0:T(8,128)(2,1)S(1)}, u32[]{:S(2)}, u32[]{:S(2)}) collective-permute-start(s16[656,256]{1,0:T(8,128)(2,1)S(1)} %get-tuple-element.84), channel_id=1, source_target_pairs={{0,28},{4,8},{8,4},{12,16},{16,12},{20,24},{24,20},{28,0},{1,29},{... | collective-permute-start | bytes 1007624 | tf_op jit(solution)/shard_map/ppermute | solution.py:845
  33.8 4.0 %collective-permute-start.7 = (f32[256,256]{1,0:T(8,128)S(1)}, f32[256,256]{1,0:T(8,128)S(1)}, u32[]{:S(2)}, u32[]{:S(2)}) collective-permute-start(f32[256,256]{1,0:T(8,128)S(1)} %get-tuple-element.82), channel_id=1, source_target_pairs={{0,4},{4,0},{8,12},{12,8},{16,20},{20,16},{24,28},{28,24},{1,5},{5... | collective-permute-start | bytes 786440 | tf_op jit(solution)/shard_map/ppermute | solution.py:840
  33.9 3.9 %collective-permute-start.8 = (f32[256,256]{1,0:T(8,128)S(1)}, f32[256,256]{1,0:T(8,128)S(1)}, u32[]{:S(2)}, u32[]{:S(2)}) collective-permute-start(f32[256,256]{1,0:T(8,128)S(1)} %get-tuple-element.83), channel_id=1, source_target_pairs={{0,4},{4,0},{8,12},{12,8},{16,20},{20,16},{24,28},{28,24},{1,5},{5... | collective-permute-start | bytes 786440 | tf_op jit(solution)/shard_map/ppermute | solution.py:840
  34.4 3.9 %copy-start = (f32[1,512,256]{2,1,0:T(8,128)S(1)}, f32[1,512,256]{2,1,0:T(8,128)}, u32[]{:S(2)}) copy-start(f32[1,512,256]{2,1,0:T(8,128)} %param.23) | copy-start | bytes 1572868
  34.4 3.9 %copy-start.7 = (s32[512]{0:T(512)S(1)}, s32[512]{0:T(512)}, u32[]{:S(2)}) copy-start(s32[512]{0:T(512)} %param.17) | copy-start | bytes 6148
  39.6 4.4 %collective-permute-start.11 = (bf16[512,256]{1,0:T(8,128)(2,1)S(1)}, bf16[512,256]{1,0:T(8,128)(2,1)S(1)}, u32[]{:S(2)}, u32[]{:S(2)}) collective-permute-start(bf16[512,256]{1,0:T(8,128)(2,1)S(1)} %get-tuple-element.91.own_ref), channel_id=1, source_target_pairs={{0,4},{4,0},{8,12},{12,8},{16,20},{20,16},{24,28},{28,24},{1,5},{5... | collective-permute-start | bytes 786440 | tf_op jit(solution)/shard_map/ppermute | solution.py:840
  39.6 9.4 %collective-permute-start.10 = (bf16[512,256]{1,0:T(8,128)(2,1)S(1)}, bf16[512,256]{1,0:T(8,128)(2,1)S(1)}, u32[]{:S(2)}, u32[]{:S(2)}) collective-permute-start(bf16[512,256]{1,0:T(8,128)(2,1)S(1)} %get-tuple-element.91.own_ref), channel_id=1, source_target_pairs={{0,28},{4,8},{8,4},{12,16},{16,12},{20,24},{24,20},{28,0},{1,29},{... | collective-permute-start | bytes 786440 | tf_op jit(solution)/shard_map/ppermute | solution.py:845
  56.2 2.6 %collective-permute-start.12 = (f32[1824,128]{1,0:T(8,128)S(1)}, f32[1824,128]{1,0:T(8,128)S(1)}, u32[]{:S(2)}, u32[]{:S(2)}) collective-permute-start(f32[1824,128]{1,0:T(8,128)S(1)} %get-tuple-element.101), channel_id=1, source_target_pairs={{0,4},{4,0},{8,12},{12,8},{16,20},{20,16},{24,28},{28,24},{1,5},{5... | collective-permute-start | bytes 2801672 | tf_op jit(solution)/shard_map/ppermute | solution.py:840
  58.8 12.7 %collective-permute-start.13 = (bf16[464,128]{1,0:T(8,128)(2,1)S(1)}, bf16[464,128]{1,0:T(8,128)(2,1)S(1)}, u32[]{:S(2)}, u32[]{:S(2)}) collective-permute-start(bf16[464,128]{1,0:T(8,128)(2,1)S(1)} %get-tuple-element.109), channel_id=1, source_target_pairs={{0,2},{1,3},{2,0},{3,1},{4,6},{5,7},{6,4},{7,5},{8,10},{9,11},{10,... | collective-permute-start | bytes 356360 | tf_op jit(solution)/shard_map/ppermute | solution.py:840
  62.1 9.4 %collective-permute-start.14 = (bf16[464,128]{1,0:T(8,128)(2,1)S(1)}, bf16[464,128]{1,0:T(8,128)(2,1)S(1)}, u32[]{:S(2)}, u32[]{:S(2)}) collective-permute-start(bf16[464,128]{1,0:T(8,128)(2,1)S(1)} %get-tuple-element.110), channel_id=1, source_target_pairs={{0,3},{1,2},{2,1},{3,0},{4,7},{5,6},{6,5},{7,4},{8,11},{9,10},{10,... | collective-permute-start | bytes 356360 | tf_op jit(solution)/shard_map/ppermute | solution.py:840
  63.2 8.9 %collective-permute-start.15 = (bf16[464,128]{1,0:T(8,128)(2,1)S(1)}, bf16[464,128]{1,0:T(8,128)(2,1)S(1)}, u32[]{:S(2)}, u32[]{:S(2)}) collective-permute-start(bf16[464,128]{1,0:T(8,128)(2,1)S(1)} %get-tuple-element.111), channel_id=1, source_target_pairs={{0,1},{1,0},{2,3},{3,2},{4,5},{5,4},{6,7},{7,6},{8,9},{9,8},{10,11... | collective-permute-start | bytes 356360 | tf_op jit(solution)/shard_map/ppermute | solution.py:840
  72.2 4.9 %collective-permute-start.16 = (bf16[464,128]{1,0:T(8,128)(2,1)S(1)}, bf16[464,128]{1,0:T(8,128)(2,1)S(1)}, u32[]{:S(2)}, u32[]{:S(2)}) collective-permute-start(bf16[464,128]{1,0:T(8,128)(2,1)S(1)} %gathered.1.mine_ref), channel_id=1, source_target_pairs={{0,8},{4,12},{8,0},{12,4},{16,24},{20,28},{24,16},{28,20},{1,9},{5... | collective-permute-start | bytes 356360 | tf_op jit(solution)/shard_map/ppermute | solution.py:840
  73.0 19.4 %copy-start.2 = (f32[456,256]{1,0:T(8,128)S(1)}, f32[456,256]{1,0:T(8,128)}, u32[]{:S(2)}) copy-start(f32[456,256]{1,0:T(8,128)} %params_ref.1) | copy-start | bytes 1400836
  73.0 19.4 %copy-start.3 = (f32[456,256]{1,0:T(8,128)S(1)}, f32[456,256]{1,0:T(8,128)}, u32[]{:S(2)}) copy-start(f32[456,256]{1,0:T(8,128)} %first_ref.1) | copy-start | bytes 1400836
  73.0 19.4 %copy-start.4 = (f32[456,256]{1,0:T(8,128)S(1)}, f32[456,256]{1,0:T(8,128)}, u32[]{:S(2)}) copy-start(f32[456,256]{1,0:T(8,128)} %second_ref.1) | copy-start | bytes 1400836
  73.0 19.4 %copy-start.5 = (f32[456,256]{1,0:T(8,128)S(1)}, f32[456,256]{1,0:T(8,128)}, u32[]{:S(2)}) copy-start(f32[456,256]{1,0:T(8,128)} %averaged_ref.1) | copy-start | bytes 1400836
  77.1 4.9 %collective-permute-start.17 = (bf16[464,128]{1,0:T(8,128)(2,1)S(1)}, bf16[464,128]{1,0:T(8,128)(2,1)S(1)}, u32[]{:S(2)}, u32[]{:S(2)}) collective-permute-start(bf16[464,128]{1,0:T(8,128)(2,1)S(1)} %add.6.mine_ref), channel_id=1, source_target_pairs={{0,16},{4,20},{8,24},{12,28},{16,0},{20,4},{24,8},{28,12},{1,17},{... | collective-permute-start | bytes 356360 | tf_op jit(solution)/shard_map/ppermute | solution.py:840
  82.2 1.8 %collective-permute-start.18 = (f32[472,128]{1,0:T(8,128)S(1)}, f32[472,128]{1,0:T(8,128)S(1)}, u32[]{:S(2)}, u32[]{:S(2)}) collective-permute-start(f32[472,128]{1,0:T(8,128)S(1)} %finish.1.mine_ref), channel_id=1, source_target_pairs={{0,4},{4,0},{8,12},{12,8},{16,20},{20,16},{24,28},{28,24},{1,5},{5... | collective-permute-start | bytes 725000 | tf_op jit(solution)/shard_map/ppermute | solution.py:840
  82.2 8.9 %collective-permute-start.21 = (bf16[512,256]{1,0:T(8,128)(2,1)S(1)}, bf16[512,256]{1,0:T(8,128)(2,1)S(1)}, u32[]{:S(2)}, u32[]{:S(2)}) collective-permute-start(bf16[512,256]{1,0:T(8,128)(2,1)S(1)} %get-tuple-element.117), channel_id=1, source_target_pairs={{0,4},{4,0},{8,12},{12,8},{16,20},{20,16},{24,28},{28,24},{1,5},{5... | collective-permute-start | bytes 786440 | tf_op jit(solution)/shard_map/ppermute | solution.py:840
  82.7 9.3 %collective-permute-start.22 = (bf16[512,256]{1,0:T(8,128)(2,1)S(1)}, bf16[512,256]{1,0:T(8,128)(2,1)S(1)}, u32[]{:S(2)}, u32[]{:S(2)}) collective-permute-start(bf16[512,256]{1,0:T(8,128)(2,1)S(1)} %get-tuple-element.118), channel_id=1, source_target_pairs={{0,28},{4,8},{8,4},{12,16},{16,12},{20,24},{24,20},{28,0},{1,29},{... | collective-permute-start | bytes 786440 | tf_op jit(solution)/shard_map/ppermute | solution.py:845
  84.0 3.8 %collective-permute-start.19 = (f32[32,128]{1,0:T(8,128)S(1)}, f32[32,128]{1,0:T(8,128)S(1)}, u32[]{:S(2)}, u32[]{:S(2)}) collective-permute-start(f32[32,128]{1,0:T(8,128)S(1)} %pad_maximum_fusion), channel_id=1, source_target_pairs={{0,1},{1,0},{2,3},{3,2},{4,5},{5,4},{6,7},{7,6},{8,9},{9,8},{10,11... | collective-permute-start | bytes 49160 | tf_op jit(solution)/shard_map/ppermute | solution.py:840
  87.8 4.6 %collective-permute-start.20 = (f32[32,128]{1,0:T(8,128)S(1)}, f32[32,128]{1,0:T(8,128)S(1)}, u32[]{:S(2)}, u32[]{:S(2)}) collective-permute-start(f32[32,128]{1,0:T(8,128)S(1)} %fusion.stats_ref), channel_id=1, source_target_pairs={{0,2},{1,3},{2,0},{3,1},{4,6},{5,7},{6,4},{7,5},{8,10},{9,11},{10,... | collective-permute-start | bytes 49160 | tf_op jit(solution)/shard_map/ppermute | solution.py:840

commit v8 on v7

--- a/solution.py
+++ b/solution.py
@@ -185,6 +185,25 @@
             flops=2 * edges * nodes * width, transcendentals=0, bytes_accessed=edges * width * 4
         ),
     )(index.reshape(-1, LANES), off, near)
+
+
+def off_choice_kernel(index_ref, out_ref):
+    rows, nodes = out_ref.shape
+    out_ref[...] = chosen_columns(index_ref, pl.program_id(0), rows, 2 * nodes, 3 * nodes)
+
+
+def off_choice(index, nodes):
+    edges = index.size
+    return pl.pallas_call(
+        off_choice_kernel,
+        grid=(edges // TILE,),
+        in_specs=[whole((edges // LANES, LANES))],
+        out_specs=tiled(TILE, nodes),
+        out_shape=jax.ShapeDtypeStruct((edges, nodes), B16),
+        compiler_params=PARAMS,
+        name="off_choice",
+        cost_estimate=pl.CostEstimate(flops=edges * nodes, transcendentals=0, bytes_accessed=edges * nodes * 2),
+    )(index.reshape(-1, LANES))
 
 
 def before_silu(region_ref, tile, hs_ref, hr_ref, x_ref, w_ref):
@@ -483,7 +502,7 @@
 
 
 def edge_backward_kernel(
-    recv_ref, region_row_ref, off_ref, near_ref, hs_ref, hr_ref, x_ref, hidden_ref, slope_ref, unit_ref,
+    choice_ref, region_row_ref, off_ref, near_ref, hs_ref, hr_ref, x_ref, hidden_ref, slope_ref, unit_ref,
     inverse_ref, w_ref, node_grad_ref, node_sum_ref,
     d_pre_ref, kept_ref, sent_ref,
     d_inner_ref, vec_acc_ref,
@@ -492,7 +511,6 @@
     steps = pl.num_programs(0)
     rows = slope_ref.shape[0]
     width = x_ref.shape[1]
-    nodes = off_ref.shape[0]
     regions = w_ref.shape[0] - 7 * width - 8
     vec = vectors_of(w_ref, width)
 
@@ -500,11 +518,11 @@
     def _():
         vec_acc_ref[...] = jnp.zeros_like(vec_acc_ref)
 
-    d_message = dot(chosen_columns(recv_ref, step, rows, 2 * nodes, 3 * nodes), off_ref[...])
+    d_message = dot(choice_ref[...], off_ref[...])
     d_message = d_message + near_ref[...].astype(F32)
     unit = unit_ref[...]
     scaled = d_message * vec[2:3, :]
-    inverse = inverse_ref[:, 0:1]
+    inverse = jnp.concatenate([inverse_ref[...]] * (width // LANES), axis=1)
     d_inner = inverse * (
         scaled
         - jnp.mean(scaled, axis=-1, keepdims=True)
@@ -555,7 +573,7 @@
 
 
 def edge_backward(
-    recv, regions, off, near, hs, hr, edges, hidden, slope, unit, inverse, weights, node_grad, node_sum,
+    choice, regions, off, near, hs, hr, edges, hidden, slope, unit, inverse, weights, node_grad, node_sum,
 ):
     count, width = edges.shape
     tile, full = tiled(TILE, width), whole((count, width))
@@ -565,7 +583,7 @@
         edge_backward_kernel,
         grid=(count // TILE,),
         in_specs=[
-            whole((count // LANES, LANES)), whole((1, count)),
+            tiled(TILE, off.shape[0]), whole((1, count)),
             whole(off.shape), tile, full, full, full, full, tile, tile, tiled(TILE, LANES),
             whole(weights.shape), whole(node_grad.shape), whole(node_sum.shape),
         ],
@@ -582,7 +600,7 @@
             flops=2 * count * width * (6 * width + off.shape[0]), transcendentals=0, bytes_accessed=count * width * 20
         ),
     )(
-        recv.reshape(-1, LANES), regions.reshape(1, -1), off, near, hs, hr, edges, hidden, slope, unit, inverse,
+        choice, regions.reshape(1, -1), off, near, hs, hr, edges, hidden, slope, unit, inverse,
         weights, node_grad, node_sum,
     )
 
@@ -888,10 +906,12 @@
         latents, agg, node_hidden, d_inner, d_pre, node_unit, weights, forced, upstream
     )
     near = gather_near(recv, d_agg, back_pair)
-    unit, inverse = edge_unit(lax.optimization_barrier((hidden, d_agg))[0], weights)
+    hidden, index = lax.optimization_barrier((hidden, recv, d_agg))[:2]
+    unit, inverse = edge_unit(hidden, weights)
+    choice = off_choice(index, nodes)
 
     d_pre, kept, sent = edge_backward(
-        recv, regions, back_off, near, hs, hr, edges, hidden, slope, unit, inverse, weights, node_grad, node_sum,
+        choice, regions, back_off, near, hs, hr, edges, hidden, slope, unit, inverse, weights, node_grad, node_sum,
     )
 
     low_rows = vector_row % share

time: 95.1 us -> 94.2 us (level)
    pallas_call x1 -> x2, Pallas kernels: 7.1 us -> 7.08 us  [the longest x1 6.24 us: edge_backward(): pl.pallas_call(edge_backward_kernel, grid=(count // TILE,), in_specs=[til...]
  transfers between devices with their start and end apart: 23 -> 23, of which waited for: 12 -> 12; matrix products, arithmetic and copies ran while one was open for 0% -> 0% of each run, Pallas kernels for 36% -> 37%
where the time goes in v8:
time: 94.2 us; the launch traced here: 94 us
  Pallas kernels  52 us (55%)
  starting transfers between devices  25.3 us (27%)
  waiting for transfers between devices  14.6 us (15%)
  between operations  1.76 us (2%)
    ppermute x19, starting transfers between devices, flipped(): lax.ppermute(value, axis, [(i, i ^ bit) for i in range(lax.axis_size(axis...  18.8 us
    ppermute x19, waiting for transfers between devices, flipped(): lax.ppermute(value, axis, [(i, i ^ bit) for i in range(lax.axis_size(axis...  11.1 us
    pallas_call x1, Pallas kernels, edge_forward(): pl.pallas_call(edge_forward_kernel, grid=(1,), in_specs=[whole((count //...  7.26 us
    pallas_call x3, Pallas kernels, gather_near(): pl.pallas_call(gather_near_kernel, grid=(1,), in_specs=[whole((edges // L...  7.22 us
    ppermute x4, starting transfers between devices, across(): lax.ppermute(value, axis, [(i, (i + 1 if i % 2 else i - 1) % count) for i...  6.52 us
    pallas_call x1, Pallas kernels, edge_backward(): pl.pallas_call(edge_backward_kernel, grid=(count // TILE,), in_specs=[til...  6.24 us
    pallas_call x1, Pallas kernels, sender_part(): pl.pallas_call(sender_part_kernel, grid=(3,), in_specs=[whole((1, count))...  4.96 us
    pallas_call x1, Pallas kernels, near_sum(): pl.pallas_call(near_sum_kernel, out_shape=[half, half, jax.ShapeDtypeStru...  4.5 us
  transfers between devices with their start and end apart: 23, of which 12 were waited for; matrix products, arithmetic and copies ran while one was open for 0% of the time, Pallas kernels for 37%

profile of v8, /device:TPU:0, one launch (start us, length us, event | category | flops | bytes accessed | tf_op | source)
XLA Modules:
  0.0 94.0 jit_solution(4755822570043119852)
XLA Ops:
  0.6 0.5 collective-permute-start.1
  1.2 1.2 %prologue.1 = (bf16[456,128]{1,0:T(8,128)(2,1)S(1)}, s32[32,128]{1,0:T(8,128)S(1)}, s32[32,128]{1,0:T(8,128)S(1)}, bf16[512,256]{1,0:T(8,128)(2,1)S(1)}) custom-call(f32[456,256]{1,0:T(8,128)} %params_ref.1, s32[32,128]{1,0:T(8,128)} %bitcast.36, s32[32,128]{1,0:T(8,128)} %bitcast.37, bf16[512,256]{1,0:T(8,128)(2,1)} %bitcast.34), custom_call_target="tpu_custom_call" | custom-call | tf_op jit(solution)/shard_map/prologue/pallas_call | solution.py:122
  2.3 3.7 %collective-permute-start.2 = (bf16[456,128]{1,0:T(8,128)(2,1)S(1)}, bf16[456,128]{1,0:T(8,128)(2,1)S(1)}, u32[]{:S(2)}, u32[]{:S(2)}) collective-permute-start(bf16[456,128]{1,0:T(8,128)(2,1)S(1)} %get-tuple-element.72.refs_0_), channel_id=1, source_target_pairs={{0,2},{1,3},{2,0},{3,1},{4,6},{5,7},{6,4},{7,5},{8,10},{9,11},{10,... | collective-permute-start | bytes 350216 | tf_op jit(solution)/shard_map/ppermute | solution.py:858
  6.0 1.3 %collective-permute-start.3 = (bf16[456,128]{1,0:T(8,128)(2,1)S(1)}, bf16[456,128]{1,0:T(8,128)(2,1)S(1)}, u32[]{:S(2)}, u32[]{:S(2)}) collective-permute-start(bf16[456,128]{1,0:T(8,128)(2,1)S(1)} %get-tuple-element.72.refs_0_), channel_id=1, source_target_pairs={{0,3},{1,2},{2,1},{3,0},{4,7},{5,6},{6,5},{7,4},{8,11},{9,10},{10,... | collective-permute-start | bytes 350216 | tf_op jit(solution)/shard_map/ppermute | solution.py:858
  7.3 0.2 collective-permute-start.4
  7.6 2.0 %collective-permute-start = (bf16[512,256]{1,0:T(8,128)(2,1)}, bf16[512,256]{1,0:T(8,128)(2,1)S(1)}, u32[]{:S(2)}, u32[]{:S(2)}) collective-permute-start(bf16[512,256]{1,0:T(8,128)(2,1)} %bitcast.35), channel_id=1, source_target_pairs={{0,28},{4,8},{8,4},{12,16},{16,12},{20,24},{24,20},{28,0},{1,29},{... | collective-permute-start | bytes 786440 | tf_op jit(solution)/shard_map/ppermute | solution.py:863
  9.6 0.0 collective-permute-done.1.pair_ref
  9.6 2.4 %gather_near.4.near_ref = bf16[4096,256]{1,0:T(8,128)(2,1)S(1)} custom-call(s32[32,128]{1,0:T(8,128)S(1)} %get-tuple-element.70.index_ref, bf16[512,256]{1,0:T(8,128)(2,1)S(1)} %get-tuple-element.69.own_ref.h_ref, bf16[512,256]{1,0:T(8,128)(2,1)S(1)} %collective-permute-done.1.pair_ref), custom_call_target="tpu_custom_call" | custom-call | flops 2147483648 | bytes 2097152 | tf_op jit(solution)/shard_map/gather_near/pallas_call | solution.py:151
  12.0 2.4 %gather_near.3.near_ref = bf16[4096,256]{1,0:T(8,128)(2,1)S(1)} custom-call(s32[32,128]{1,0:T(8,128)S(1)} %get-tuple-element.71.index_ref, bf16[512,256]{1,0:T(8,128)(2,1)S(1)} %get-tuple-element.69.own_ref.h_ref, bf16[512,256]{1,0:T(8,128)(2,1)S(1)} %collective-permute-done.1.pair_ref), custom_call_target="tpu_custom_call" | custom-call | flops 2147483648 | bytes 2097152 | tf_op jit(solution)/shard_map/gather_near/pallas_call | solution.py:151
  14.4 0.7 collective-permute-done.2
  15.1 0.0 collective-permute-done.3
  15.1 1.1 %collective-permute-done.4 = bf16[456,128]{1,0:T(8,128)(2,1)S(1)} collective-permute-done((bf16[456,128]{1,0:T(8,128)(2,1)S(1)}, bf16[456,128]{1,0:T(8,128)(2,1)S(1)}, u32[]{:S(2)}, u32[]{:S(2)}) %collective-permute-start.4) | collective-permute-done | bytes 116768 | tf_op jit(solution)/shard_map/ppermute | solution.py:858
  16.3 0.1 collective-permute-start.6
  16.4 0.5 collective-permute-start.5
  16.9 0.2 collective-permute-done.off_ref
  17.1 1.3 %gather_off.3.hr_ref = bf16[4096,256]{1,0:T(8,128)(2,1)S(1)} custom-call(s32[32,128]{1,0:T(8,128)S(1)} %get-tuple-element.70.index_ref, bf16[512,256]{1,0:T(8,128)(2,1)S(1)} %collective-permute-done.off_ref, bf16[4096,256]{1,0:T(8,128)(2,1)S(1)} %gather_near.4.near_ref), custom_call_target="tpu_custom_call" | custom-call | flops 1073741824 | bytes 4194304 | tf_op jit(solution)/shard_map/gather_off/pallas_call | solution.py:176
  18.4 0.0 copy-start
  18.4 0.0 copy-start.6
  18.5 1.3 %gather_off.2.hs_ref = bf16[4096,256]{1,0:T(8,128)(2,1)S(1)} custom-call(s32[32,128]{1,0:T(8,128)S(1)} %get-tuple-element.71.index_ref, bf16[512,256]{1,0:T(8,128)(2,1)S(1)} %collective-permute-done.off_ref, bf16[4096,256]{1,0:T(8,128)(2,1)S(1)} %gather_near.3.near_ref), custom_call_target="tpu_custom_call" | custom-call | flops 1073741824 | bytes 4194304 | tf_op jit(solution)/shard_map/gather_off/pallas_call | solution.py:176
  19.8 0.0 collective-permute-done.6.refs_3_
  19.8 0.2 copy-done
  20.0 7.3 %edge_forward.1 = (bf16[1824,256]{1,0:T(8,128)(2,1)S(1)}, bf16[4096,256]{1,0:T(8,128)(2,1)S(1)}, bf16[4096,256]{1,0:T(8,128)(2,1)S(1)}, s16[656,256]{1,0:T(8,128)(2,1)S(1)}) custom-call(s32[32,128]{1,0:T(8,128)S(1)} %bitcast.27, s32[1,4096]{1,0:T(1,128)S(1)} %bitcast.22, bf16[4096,256]{1,0:T(8,128)(2,1)S(1)} %gather_off.2.hs_ref, ...), custom_call_target="tpu_custom_call" | custom-call | flops 4831838208 | bytes 10485760 | tf_op jit(solution)/shard_map/edge_forward/pallas_call | solution.py:316
  27.3 2.0 %collective-permute-start.9 = (s16[656,256]{1,0:T(8,128)(2,1)S(1)}, s16[656,256]{1,0:T(8,128)(2,1)S(1)}, u32[]{:S(2)}, u32[]{:S(2)}) collective-permute-start(s16[656,256]{1,0:T(8,128)(2,1)S(1)} %get-tuple-element.85), channel_id=1, source_target_pairs={{0,28},{4,8},{8,4},{12,16},{16,12},{20,24},{24,20},{28,0},{1,29},{... | collective-permute-start | bytes 1007624 | tf_op jit(solution)/shard_map/ppermute | solution.py:863
  29.3 4.5 %near_sum.1 = (f32[256,256]{1,0:T(8,128)S(1)}, f32[256,256]{1,0:T(8,128)S(1)}, f32[512,256]{1,0:T(8,128)S(1)}) custom-call(s32[1,4096]{1,0:T(1,128)S(1)} %bitcast.23, bf16[4096,256]{1,0:T(8,128)(2,1)S(1)} %get-tuple-element.76.high_ref, bf16[4096,256]{1,0:T(8,128)(2,1)S(1)} %get-tuple-element.77.low_ref), custom_call_target="tpu_custom_call" | custom-call | flops 4294967296 | bytes 4194304 | tf_op jit(solution)/shard_map/near_sum/pallas_call | solution.py:401
  33.8 0.1 collective-permute-start.7
  33.9 0.5 collective-permute-start.8
  34.4 3.4 %edge_slope.1 = (bf16[4096,256]{1,0:T(8,128)(2,1)S(1)}, f32[4096,256]{1,0:T(8,128)S(1)}) custom-call(s32[32,128]{1,0:T(8,128)S(1)} %bitcast.28, bf16[4096,256]{1,0:T(8,128)(2,1)S(1)} %gather_off.2.hs_ref, bf16[4096,256]{1,0:T(8,128)(2,1)S(1)} %gather_off.3.hr_ref, bf16[4096,256]{1,0:T(8,128)(2,1)S(1)} %bitcast.18, bf16[1824,256]{1,0:T(8,128)(2,1)S(1)} %get-tuple-element.79.w_ref), custom_call_target="tpu_custom_call" | custom-call | flops 2147483648 | bytes 12582912 | tf_op jit(solution)/shard_map/edge_slope/pallas_call | solution.py:353
  37.7 0.0 collective-permute-done.8.more_ref
  37.8 0.5 collective-permute-done.9.off_ref
  38.3 1.2 %node_update.1 = (bf16[512,256]{1,0:T(8,128)(2,1)S(1)}, bf16[512,256]{1,0:T(8,128)(2,1)S(1)}, bf16[512,256]{1,0:T(8,128)(2,1)S(1)}, bf16[512,256]{1,0:T(8,128)(2...) custom-call(bf16[512,256]{1,0:T(8,128)(2,1)S(1)} %get-tuple-element.69.own_ref.h_ref, ...), custom_call_target="tpu_custom_call" | custom-call | flops 335544320 | bytes 2621440 | tf_op jit(solution)/shard_map/node_update/pallas_call | solution.py:454
  39.5 0.1 collective-permute-start.11
  39.6 1.3 %collective-permute-start.10 = (bf16[512,256]{1,0:T(8,128)(2,1)S(1)}, bf16[512,256]{1,0:T(8,128)(2,1)S(1)}, u32[]{:S(2)}, u32[]{:S(2)}) collective-permute-start(bf16[512,256]{1,0:T(8,128)(2,1)S(1)} %get-tuple-element.93.own_ref), channel_id=1, source_target_pairs={{0,28},{4,8},{8,4},{12,16},{16,12},{20,24},{24,20},{28,0},{1,29},{... | collective-permute-start | bytes 786440 | tf_op jit(solution)/shard_map/ppermute | solution.py:863
  40.9 1.3 %node_grads.1 = (f32[512,256]{1,0:T(8,128)}, f32[768,256]{1,0:T(8,128)S(1)}, f32[4,256]{1,0:T(4,128)S(1)}, f32[512,256]{1,0:T(8,128)S(1)}) custom-call(bf16[512,256]{1,0:T(8,128)(2,1)S(1)} %get-tuple-element.69.own_ref.h_ref, bf16[512,256]{1,0:T(8,128)(2,1)S(1)} %get-tuple-element.86.agg_ref, bf16[512,256]{1,0:T(8,128)(2,1)S(1)} %get-tuple-element.87.hidden_ref, ...), custom_call_target="tpu_custom_call" | custom-call | flops 268435456 | bytes 2359296 | tf_op jit(solution)/shard_map/node_grads/pallas_call | solution.py:493
  42.2 0.8 off_choice.1.choice_ref
  43.1 1.7 %edge_unit.1 = (f32[4096,256]{1,0:T(8,128)S(1)}, f32[4096,128]{1,0:T(8,128)S(1)}) custom-call(bf16[4096,256]{1,0:T(8,128)(2,1)S(1)} %get-tuple-element.95.hidden_ref, bf16[1824,256]{1,0:T(8,128)(2,1)S(1)} %get-tuple-element.79.w_ref), custom_call_target="tpu_custom_call" | custom-call | flops 536870912 | bytes 8388608 | tf_op jit(solution)/shard_map/edge_unit/pallas_call | solution.py:376
  44.8 2.4 %gather_near.5.near_ref = bf16[4096,256]{1,0:T(8,128)(2,1)S(1)} custom-call(s32[32,128]{1,0:T(8,128)S(1)} %get-tuple-element.70.index_ref, bf16[512,256]{1,0:T(8,128)(2,1)S(1)} %get-tuple-element.93.own_ref, bf16[512,256]{1,0:T(8,128)(2,1)S(1)} %collective-permute-done.11.pair_ref), custom_call_target="tpu_custom_call" | custom-call | flops 2147483648 | bytes 2097152 | tf_op jit(solution)/shard_map/gather_near/pallas_call | solution.py:151
  47.2 1.8 %collective-permute-done.10.off_ref = bf16[512,256]{1,0:T(8,128)(2,1)S(1)} collective-permute-done((bf16[512,256]{1,0:T(8,128)(2,1)S(1)}, bf16[512,256]{1,0:T(8,128)(2,1)S(1)}, u32[]{:S(2)}, u32[]{:S(2)}) %collective-permute-start.10) | collective-permute-done | bytes 262176 | tf_op jit(solution)/shard_map/ppermute | solution.py:863
  49.0 6.2 %edge_backward.1 = (bf16[4096,256]{1,0:T(8,128)(2,1)S(1)}, f32[1824,128]{1,0:T(8,128)S(1)}, f32[1824,128]{1,0:T(8,128)S(1)}) custom-call(bf16[4096,512]{1,0:T(8,128)(2,1)S(1)} %off_choice.1.choice_ref, s32[1,4096]{1,0:T(1,128)S(1)} %bitcast.29, bf16[512,256]{1,0:T(8,128)(2,1)S(1)} %collective-permute-done.10.off_ref, ...), custom_call_target="tpu_custom_call" | custom-call | flops 4294967296 | bytes 20971520 | tf_op jit(solution)/shard_map/edge_backward/pallas_call | solution.py:582
  55.3 0.1 collective-permute-start.12
  55.4 1.9 %edge_grads.1 = bf16[4096,256]{1,0:T(8,128)(2,1)} custom-call(bf16[4096,256]{1,0:T(8,128)(2,1)S(1)} %get-tuple-element.107.d_pre_ref, bf16[1824,256]{1,0:T(8,128)(2,1)S(1)} %get-tuple-element.79.w_ref), custom_call_target="tpu_custom_call" | custom-call | flops 536870912 | bytes 4194304 | tf_op jit(solution)/shard_map/edge_grads/pallas_call | solution.py:697
  57.3 0.6 collective-permute-done.12.other_ref
  57.8 0.1 parted.1
  57.9 3.3 %collective-permute-start.13 = (bf16[464,128]{1,0:T(8,128)(2,1)S(1)}, bf16[464,128]{1,0:T(8,128)(2,1)S(1)}, u32[]{:S(2)}, u32[]{:S(2)}) collective-permute-start(bf16[464,128]{1,0:T(8,128)(2,1)S(1)} %get-tuple-element.111), channel_id=1, source_target_pairs={{0,2},{1,3},{2,0},{3,1},{4,6},{5,7},{6,4},{7,5},{8,10},{9,11},{10,... | collective-permute-start | bytes 356360 | tf_op jit(solution)/shard_map/ppermute | solution.py:858
  61.2 1.0 %collective-permute-start.14 = (bf16[464,128]{1,0:T(8,128)(2,1)S(1)}, bf16[464,128]{1,0:T(8,128)(2,1)S(1)}, u32[]{:S(2)}, u32[]{:S(2)}) collective-permute-start(bf16[464,128]{1,0:T(8,128)(2,1)S(1)} %get-tuple-element.112), channel_id=1, source_target_pairs={{0,3},{1,2},{2,1},{3,0},{4,7},{5,6},{6,5},{7,4},{8,11},{9,10},{10,... | collective-permute-start | bytes 356360 | tf_op jit(solution)/shard_map/ppermute | solution.py:858
  62.3 5.0 %sender_part.1.part_ref = f32[1536,256]{1,0:T(8,128)S(1)} custom-call(s32[1,4096]{1,0:T(1,128)S(1)} %bitcast.26, bf16[4096,256]{1,0:T(8,128)(2,1)S(1)} %get-tuple-element.107.d_pre_ref, bf16[1824,256]{1,0:T(8,128)(2,1)S(1)} %get-tuple-element.79.w_ref), custom_call_target="tpu_custom_call" | custom-call | flops 3221225472 | bytes 2097152 | tf_op jit(solution)/shard_map/sender_part/pallas_call | solution.py:620
  67.2 3.4 %receiver_part.1 = (bf16[512,256]{1,0:T(8,128)(2,1)S(1)}, bf16[512,256]{1,0:T(8,128)(2,1)S(1)}) custom-call(s32[1,4096]{1,0:T(1,128)S(1)} %bitcast.24, bf16[4096,256]{1,0:T(8,128)(2,1)S(1)} %get-tuple-element.107.d_pre_ref, bf16[1824,256]{1,0:T(8,128)(2,1)S(1)} %get-tuple-element.79.w_ref, f32[1536,256]{1,0:T(8,128)S(1)} %sender_part.1.part_ref), custom_call_target="tpu_custom_call" | custom-call | flops 2147483648 | bytes 2097152 | tf_op jit(solution)/shard_map/receiver_part/pallas_call | solution.py:651
  70.6 0.0 collective-permute-done.13.refs_0_
  70.7 0.6 collective-permute-done.15.refs_2_
  71.2 0.1 gathered.1.mine_ref
  71.3 0.8 collective-permute-start.16
  72.1 1.7 %own_part.1.own_ref = f32[512,256]{1,0:T(8,128)S(1)} custom-call(s32[1,4096]{1,0:T(1,128)S(1)} %bitcast.25, bf16[4096,256]{1,0:T(8,128)(2,1)S(1)} %get-tuple-element.107.d_pre_ref, bf16[1824,256]{1,0:T(8,128)(2,1)S(1)} %get-tuple-element.79.w_ref, f32[1536,256]{1,0:T(8,128)S(1)} %sender_part.1.part_ref, f32[512,256]{1,0:T(8,128)S(1)} %get-tuple-element.116.back_ref), custom_call_target="tpu_custom_call" | custom-call | flops 1073741824 | bytes 2097152 | tf_op jit(solution)/shard_map/own_part/pallas_call | solution.py:676
  73.8 2.4 %collective-permute-done.16.other_ref = bf16[464,128]{1,0:T(8,128)(2,1)S(1)} collective-permute-done((bf16[464,128]{1,0:T(8,128)(2,1)S(1)}, bf16[464,128]{1,0:T(8,128)(2,1)S(1)}, u32[]{:S(2)}, u32[]{:S(2)}) %collective-permute-start.16) | collective-permute-done | bytes 118816 | tf_op jit(solution)/shard_map/ppermute | solution.py:858
  76.2 1.5 %collective-permute-start.17 = (bf16[464,128]{1,0:T(8,128)(2,1)S(1)}, bf16[464,128]{1,0:T(8,128)(2,1)S(1)}, u32[]{:S(2)}, u32[]{:S(2)}) collective-permute-start(bf16[464,128]{1,0:T(8,128)(2,1)S(1)} %add.6.mine_ref), channel_id=1, source_target_pairs={{0,16},{4,20},{8,24},{12,28},{16,0},{20,4},{24,8},{28,12},{1,17},{... | collective-permute-start | bytes 356360 | tf_op jit(solution)/shard_map/ppermute | solution.py:858
  77.7 3.5 %collective-permute-done.17.other_ref = bf16[464,128]{1,0:T(8,128)(2,1)S(1)} collective-permute-done((bf16[464,128]{1,0:T(8,128)(2,1)S(1)}, bf16[464,128]{1,0:T(8,128)(2,1)S(1)}, u32[]{:S(2)}, u32[]{:S(2)}) %collective-permute-start.17) | collective-permute-done | bytes 118816 | tf_op jit(solution)/shard_map/ppermute | solution.py:858
  81.1 0.2 finish.1.mine_ref
  81.3 0.0 collective-permute-start.18
  81.3 0.5 collective-permute-start.21
  81.8 1.3 %collective-permute-start.22 = (bf16[512,256]{1,0:T(8,128)(2,1)S(1)}, bf16[512,256]{1,0:T(8,128)(2,1)S(1)}, u32[]{:S(2)}, u32[]{:S(2)}) collective-permute-start(bf16[512,256]{1,0:T(8,128)(2,1)S(1)} %get-tuple-element.120), channel_id=1, source_target_pairs={{0,28},{4,8},{8,4},{12,16},{16,12},{20,24},{24,20},{28,0},{1,29},{... | collective-permute-start | bytes 786440 | tf_op jit(solution)/shard_map/ppermute | solution.py:863
  83.1 2.0 %collective-permute-start.19 = (f32[32,128]{1,0:T(8,128)S(1)}, f32[32,128]{1,0:T(8,128)S(1)}, u32[]{:S(2)}, u32[]{:S(2)}) collective-permute-start(f32[32,128]{1,0:T(8,128)S(1)} %pad_maximum_fusion), channel_id=1, source_target_pairs={{0,1},{1,0},{2,3},{3,2},{4,5},{5,4},{6,7},{7,6},{8,9},{9,8},{10,11... | collective-permute-start | bytes 49160 | tf_op jit(solution)/shard_map/ppermute | solution.py:858
  85.1 1.8 %collective-permute-done.19 = f32[32,128]{1,0:T(8,128)S(1)} collective-permute-done((f32[32,128]{1,0:T(8,128)S(1)}, f32[32,128]{1,0:T(8,128)S(1)}, u32[]{:S(2)}, u32[]{:S(2)}) %collective-permute-start.19) | collective-permute-done | bytes 16416 | tf_op jit(solution)/shard_map/ppermute | solution.py:858
  86.9 2.7 %collective-permute-start.20 = (f32[32,128]{1,0:T(8,128)S(1)}, f32[32,128]{1,0:T(8,128)S(1)}, u32[]{:S(2)}, u32[]{:S(2)}) collective-permute-start(f32[32,128]{1,0:T(8,128)S(1)} %fusion.stats_ref), channel_id=1, source_target_pairs={{0,2},{1,3},{2,0},{3,1},{4,6},{5,7},{6,4},{7,5},{8,10},{9,11},{10,... | collective-permute-start | bytes 49160 | tf_op jit(solution)/shard_map/ppermute | solution.py:858
  90.2 0.9 collective-permute-done.22.off_ref
  91.1 0.4 collective-permute-done.20.more_ref
  91.5 2.3 %adam.1 = (f32[456,256]{1,0:T(8,128)}, f32[456,256]{1,0:T(8,128)}, f32[456,256]{1,0:T(8,128)}, f32[456,256]{1,0:T(8,128)}, f32[1,1]{1,0:T(1,128)}, /*index=5*/f32[8,256]{1,0:T(8,128)}, f32[512,256]{1,0:T(8,128)}) custom-call(f32[8,128]{1,0:T(8,128)S(1)} %broadcast_in_dim.15.step_ref, f32[32,128]{1,0:T(8,128)S(1)} %fusion.stats_ref, ...), custom_call_target="tpu_custom_call" | custom-call | flops 2334720 | bytes 3735552 | tf_op jit(solution)/shard_map/adam/pallas_call | solution.py:839
  (29 shorter events, 0.1 us)
Async XLA Ops:
  0.6 8.9 %collective-permute-start.1 = (bf16[512,256]{1,0:T(8,128)(2,1)}, bf16[512,256]{1,0:T(8,128)(2,1)S(1)}, u32[]{:S(2)}, u32[]{:S(2)}) collective-permute-start(bf16[512,256]{1,0:T(8,128)(2,1)} %bitcast.33), channel_id=1, source_target_pairs={{0,4},{4,0},{8,12},{12,8},{16,20},{20,16},{24,28},{28,24},{1,5},{5... | collective-permute-start | bytes 786440 | tf_op jit(solution)/shard_map/ppermute | solution.py:858
  2.3 12.8 %collective-permute-start.2 = (bf16[456,128]{1,0:T(8,128)(2,1)S(1)}, bf16[456,128]{1,0:T(8,128)(2,1)S(1)}, u32[]{:S(2)}, u32[]{:S(2)}) collective-permute-start(bf16[456,128]{1,0:T(8,128)(2,1)S(1)} %get-tuple-element.72.refs_0_), channel_id=1, source_target_pairs={{0,2},{1,3},{2,0},{3,1},{4,6},{5,7},{6,4},{7,5},{8,10},{9,11},{10,... | collective-permute-start | bytes 350216 | tf_op jit(solution)/shard_map/ppermute | solution.py:858
  6.0 9.1 %collective-permute-start.3 = (bf16[456,128]{1,0:T(8,128)(2,1)S(1)}, bf16[456,128]{1,0:T(8,128)(2,1)S(1)}, u32[]{:S(2)}, u32[]{:S(2)}) collective-permute-start(bf16[456,128]{1,0:T(8,128)(2,1)S(1)} %get-tuple-element.72.refs_0_), channel_id=1, source_target_pairs={{0,3},{1,2},{2,1},{3,0},{4,7},{5,6},{6,5},{7,4},{8,11},{9,10},{10,... | collective-permute-start | bytes 350216 | tf_op jit(solution)/shard_map/ppermute | solution.py:858
  7.3 8.9 %collective-permute-start.4 = (bf16[456,128]{1,0:T(8,128)(2,1)S(1)}, bf16[456,128]{1,0:T(8,128)(2,1)S(1)}, u32[]{:S(2)}, u32[]{:S(2)}) collective-permute-start(bf16[456,128]{1,0:T(8,128)(2,1)S(1)} %get-tuple-element.72.refs_0_), channel_id=1, source_target_pairs={{0,1},{1,0},{2,3},{3,2},{4,5},{5,4},{6,7},{7,6},{8,9},{9,8},{10,11... | collective-permute-start | bytes 350216 | tf_op jit(solution)/shard_map/ppermute | solution.py:858
  7.6 9.5 %collective-permute-start = (bf16[512,256]{1,0:T(8,128)(2,1)}, bf16[512,256]{1,0:T(8,128)(2,1)S(1)}, u32[]{:S(2)}, u32[]{:S(2)}) collective-permute-start(bf16[512,256]{1,0:T(8,128)(2,1)} %bitcast.35), channel_id=1, source_target_pairs={{0,28},{4,8},{8,4},{12,16},{16,12},{20,24},{24,20},{28,0},{1,29},{... | collective-permute-start | bytes 786440 | tf_op jit(solution)/shard_map/ppermute | solution.py:863
  16.3 3.5 %collective-permute-start.6 = (bf16[1368,128]{1,0:T(8,128)(2,1)S(1)}, bf16[1368,128]{1,0:T(8,128)(2,1)S(1)}, u32[]{:S(2)}, u32[]{:S(2)}) collective-permute-start(bf16[1368,128]{1,0:T(8,128)(2,1)S(1)} %constant_dynamic-update-slice_fusion.refs_1_), channel_id=1, source_target_pairs={{0,4},{4,0},{8,12},{12,8},{16,20},{20,16},{24,28},{28,24},{1,5},{5... | collective-permute-start | bytes 1050632 | tf_op jit(solution)/shard_map/ppermute | solution.py:858
  16.4 3.4 %collective-permute-start.5 = (bf16[456,128]{1,0:T(8,128)(2,1)S(1)}, bf16[456,128]{1,0:T(8,128)(2,1)S(1)}, u32[]{:S(2)}, u32[]{:S(2)}) collective-permute-start(bf16[456,128]{1,0:T(8,128)(2,1)S(1)} %get-tuple-element.72.refs_0_), channel_id=1, source_target_pairs={{0,4},{4,0},{8,12},{12,8},{16,20},{20,16},{24,28},{28,24},{1,5},{5... | collective-permute-start | bytes 350216 | tf_op jit(solution)/shard_map/ppermute | solution.py:858
  18.4 1.6 %copy-start = (bf16[1,4096,256]{2,1,0:T(8,128)(2,1)S(1)}, bf16[1,4096,256]{2,1,0:T(8,128)(2,1)}, u32[]{:S(2)}) copy-start(bf16[1,4096,256]{2,1,0:T(8,128)(2,1)} %param.13) | copy-start | bytes 6291460
  18.4 1.6 %copy-start.6 = (s32[4096]{0:T(1024)S(1)}, s32[4096]{0:T(1024)}, u32[]{:S(2)}) copy-start(s32[4096]{0:T(1024)} %param.16) | copy-start | bytes 49156
  27.3 11.0 %collective-permute-start.9 = (s16[656,256]{1,0:T(8,128)(2,1)S(1)}, s16[656,256]{1,0:T(8,128)(2,1)S(1)}, u32[]{:S(2)}, u32[]{:S(2)}) collective-permute-start(s16[656,256]{1,0:T(8,128)(2,1)S(1)} %get-tuple-element.85), channel_id=1, source_target_pairs={{0,28},{4,8},{8,4},{12,16},{16,12},{20,24},{24,20},{28,0},{1,29},{... | collective-permute-start | bytes 1007624 | tf_op jit(solution)/shard_map/ppermute | solution.py:863
  33.8 4.0 %collective-permute-start.7 = (f32[256,256]{1,0:T(8,128)S(1)}, f32[256,256]{1,0:T(8,128)S(1)}, u32[]{:S(2)}, u32[]{:S(2)}) collective-permute-start(f32[256,256]{1,0:T(8,128)S(1)} %get-tuple-element.83), channel_id=1, source_target_pairs={{0,4},{4,0},{8,12},{12,8},{16,20},{20,16},{24,28},{28,24},{1,5},{5... | collective-permute-start | bytes 786440 | tf_op jit(solution)/shard_map/ppermute | solution.py:858
  33.9 3.9 %collective-permute-start.8 = (f32[256,256]{1,0:T(8,128)S(1)}, f32[256,256]{1,0:T(8,128)S(1)}, u32[]{:S(2)}, u32[]{:S(2)}) collective-permute-start(f32[256,256]{1,0:T(8,128)S(1)} %get-tuple-element.84), channel_id=1, source_target_pairs={{0,4},{4,0},{8,12},{12,8},{16,20},{20,16},{24,28},{28,24},{1,5},{5... | collective-permute-start | bytes 786440 | tf_op jit(solution)/shard_map/ppermute | solution.py:858
  34.4 3.9 %copy-start.1 = (f32[1,512,256]{2,1,0:T(8,128)S(1)}, f32[1,512,256]{2,1,0:T(8,128)}, u32[]{:S(2)}) copy-start(f32[1,512,256]{2,1,0:T(8,128)} %param.23) | copy-start | bytes 1572868
  34.4 3.9 %copy-start.7 = (s32[512]{0:T(512)S(1)}, s32[512]{0:T(512)}, u32[]{:S(2)}) copy-start(s32[512]{0:T(512)} %param.17) | copy-start | bytes 6148
  39.5 5.2 %collective-permute-start.11 = (bf16[512,256]{1,0:T(8,128)(2,1)S(1)}, bf16[512,256]{1,0:T(8,128)(2,1)S(1)}, u32[]{:S(2)}, u32[]{:S(2)}) collective-permute-start(bf16[512,256]{1,0:T(8,128)(2,1)S(1)} %get-tuple-element.93.own_ref), channel_id=1, source_target_pairs={{0,4},{4,0},{8,12},{12,8},{16,20},{20,16},{24,28},{28,24},{1,5},{5... | collective-permute-start | bytes 786440 | tf_op jit(solution)/shard_map/ppermute | solution.py:858
  39.6 9.4 %collective-permute-start.10 = (bf16[512,256]{1,0:T(8,128)(2,1)S(1)}, bf16[512,256]{1,0:T(8,128)(2,1)S(1)}, u32[]{:S(2)}, u32[]{:S(2)}) collective-permute-start(bf16[512,256]{1,0:T(8,128)(2,1)S(1)} %get-tuple-element.93.own_ref), channel_id=1, source_target_pairs={{0,28},{4,8},{8,4},{12,16},{16,12},{20,24},{24,20},{28,0},{1,29},{... | collective-permute-start | bytes 786440 | tf_op jit(solution)/shard_map/ppermute | solution.py:863
  55.3 2.6 %collective-permute-start.12 = (f32[1824,128]{1,0:T(8,128)S(1)}, f32[1824,128]{1,0:T(8,128)S(1)}, u32[]{:S(2)}, u32[]{:S(2)}) collective-permute-start(f32[1824,128]{1,0:T(8,128)S(1)} %get-tuple-element.103), channel_id=1, source_target_pairs={{0,4},{4,0},{8,12},{12,8},{16,20},{20,16},{24,28},{28,24},{1,5},{5... | collective-permute-start | bytes 2801672 | tf_op jit(solution)/shard_map/ppermute | solution.py:858
  57.9 12.7 %collective-permute-start.13 = (bf16[464,128]{1,0:T(8,128)(2,1)S(1)}, bf16[464,128]{1,0:T(8,128)(2,1)S(1)}, u32[]{:S(2)}, u32[]{:S(2)}) collective-permute-start(bf16[464,128]{1,0:T(8,128)(2,1)S(1)} %get-tuple-element.111), channel_id=1, source_target_pairs={{0,2},{1,3},{2,0},{3,1},{4,6},{5,7},{6,4},{7,5},{8,10},{9,11},{10,... | collective-permute-start | bytes 356360 | tf_op jit(solution)/shard_map/ppermute | solution.py:858
  61.2 9.4 %collective-permute-start.14 = (bf16[464,128]{1,0:T(8,128)(2,1)S(1)}, bf16[464,128]{1,0:T(8,128)(2,1)S(1)}, u32[]{:S(2)}, u32[]{:S(2)}) collective-permute-start(bf16[464,128]{1,0:T(8,128)(2,1)S(1)} %get-tuple-element.112), channel_id=1, source_target_pairs={{0,3},{1,2},{2,1},{3,0},{4,7},{5,6},{6,5},{7,4},{8,11},{9,10},{10,... | collective-permute-start | bytes 356360 | tf_op jit(solution)/shard_map/ppermute | solution.py:858
  62.3 9.0 %collective-permute-start.15 = (bf16[464,128]{1,0:T(8,128)(2,1)S(1)}, bf16[464,128]{1,0:T(8,128)(2,1)S(1)}, u32[]{:S(2)}, u32[]{:S(2)}) collective-permute-start(bf16[464,128]{1,0:T(8,128)(2,1)S(1)} %get-tuple-element.113), channel_id=1, source_target_pairs={{0,1},{1,0},{2,3},{3,2},{4,5},{5,4},{6,7},{7,6},{8,9},{9,8},{10,11... | collective-permute-start | bytes 356360 | tf_op jit(solution)/shard_map/ppermute | solution.py:858
  71.3 4.9 %collective-permute-start.16 = (bf16[464,128]{1,0:T(8,128)(2,1)S(1)}, bf16[464,128]{1,0:T(8,128)(2,1)S(1)}, u32[]{:S(2)}, u32[]{:S(2)}) collective-permute-start(bf16[464,128]{1,0:T(8,128)(2,1)S(1)} %gathered.1.mine_ref), channel_id=1, source_target_pairs={{0,8},{4,12},{8,0},{12,4},{16,24},{20,28},{24,16},{28,20},{1,9},{5... | collective-permute-start | bytes 356360 | tf_op jit(solution)/shard_map/ppermute | solution.py:858
  72.1 19.4 %copy-start.2 = (f32[456,256]{1,0:T(8,128)S(1)}, f32[456,256]{1,0:T(8,128)}, u32[]{:S(2)}) copy-start(f32[456,256]{1,0:T(8,128)} %params_ref.1) | copy-start | bytes 1400836
  72.1 19.4 %copy-start.3 = (f32[456,256]{1,0:T(8,128)S(1)}, f32[456,256]{1,0:T(8,128)}, u32[]{:S(2)}) copy-start(f32[456,256]{1,0:T(8,128)} %first_ref.1) | copy-start | bytes 1400836
  72.1 19.4 %copy-start.4 = (f32[456,256]{1,0:T(8,128)S(1)}, f32[456,256]{1,0:T(8,128)}, u32[]{:S(2)}) copy-start(f32[456,256]{1,0:T(8,128)} %second_ref.1) | copy-start | bytes 1400836
  72.1 19.4 %copy-start.5 = (f32[456,256]{1,0:T(8,128)S(1)}, f32[456,256]{1,0:T(8,128)}, u32[]{:S(2)}) copy-start(f32[456,256]{1,0:T(8,128)} %averaged_ref.1) | copy-start | bytes 1400836
  76.2 4.9 %collective-permute-start.17 = (bf16[464,128]{1,0:T(8,128)(2,1)S(1)}, bf16[464,128]{1,0:T(8,128)(2,1)S(1)}, u32[]{:S(2)}, u32[]{:S(2)}) collective-permute-start(bf16[464,128]{1,0:T(8,128)(2,1)S(1)} %add.6.mine_ref), channel_id=1, source_target_pairs={{0,16},{4,20},{8,24},{12,28},{16,0},{20,4},{24,8},{28,12},{1,17},{... | collective-permute-start | bytes 356360 | tf_op jit(solution)/shard_map/ppermute | solution.py:858
  81.3 1.8 %collective-permute-start.18 = (f32[472,128]{1,0:T(8,128)S(1)}, f32[472,128]{1,0:T(8,128)S(1)}, u32[]{:S(2)}, u32[]{:S(2)}) collective-permute-start(f32[472,128]{1,0:T(8,128)S(1)} %finish.1.mine_ref), channel_id=1, source_target_pairs={{0,4},{4,0},{8,12},{12,8},{16,20},{20,16},{24,28},{28,24},{1,5},{5... | collective-permute-start | bytes 725000 | tf_op jit(solution)/shard_map/ppermute | solution.py:858
  81.3 8.9 %collective-permute-start.21 = (bf16[512,256]{1,0:T(8,128)(2,1)S(1)}, bf16[512,256]{1,0:T(8,128)(2,1)S(1)}, u32[]{:S(2)}, u32[]{:S(2)}) collective-permute-start(bf16[512,256]{1,0:T(8,128)(2,1)S(1)} %get-tuple-element.119), channel_id=1, source_target_pairs={{0,4},{4,0},{8,12},{12,8},{16,20},{20,16},{24,28},{28,24},{1,5},{5... | collective-permute-start | bytes 786440 | tf_op jit(solution)/shard_map/ppermute | solution.py:858
  81.8 9.3 %collective-permute-start.22 = (bf16[512,256]{1,0:T(8,128)(2,1)S(1)}, bf16[512,256]{1,0:T(8,128)(2,1)S(1)}, u32[]{:S(2)}, u32[]{:S(2)}) collective-permute-start(bf16[512,256]{1,0:T(8,128)(2,1)S(1)} %get-tuple-element.120), channel_id=1, source_target_pairs={{0,28},{4,8},{8,4},{12,16},{16,12},{20,24},{24,20},{28,0},{1,29},{... | collective-permute-start | bytes 786440 | tf_op jit(solution)/shard_map/ppermute | solution.py:863
  83.1 3.8 %collective-permute-start.19 = (f32[32,128]{1,0:T(8,128)S(1)}, f32[32,128]{1,0:T(8,128)S(1)}, u32[]{:S(2)}, u32[]{:S(2)}) collective-permute-start(f32[32,128]{1,0:T(8,128)S(1)} %pad_maximum_fusion), channel_id=1, source_target_pairs={{0,1},{1,0},{2,3},{3,2},{4,5},{5,4},{6,7},{7,6},{8,9},{9,8},{10,11... | collective-permute-start | bytes 49160 | tf_op jit(solution)/shard_map/ppermute | solution.py:858
  86.9 4.6 %collective-permute-start.20 = (f32[32,128]{1,0:T(8,128)S(1)}, f32[32,128]{1,0:T(8,128)S(1)}, u32[]{:S(2)}, u32[]{:S(2)}) collective-permute-start(f32[32,128]{1,0:T(8,128)S(1)} %fusion.stats_ref), channel_id=1, source_target_pairs={{0,2},{1,3},{2,0},{3,1},{4,6},{5,7},{6,4},{7,5},{8,10},{9,11},{10,... | collective-permute-start | bytes 49160 | tf_op jit(solution)/shard_map/ppermute | solution.py:858

commit v9 on v8

--- a/solution.py
+++ b/solution.py
@@ -795,16 +795,16 @@
     latents_ref[...] = own_ref[...] + pair_ref[...].astype(F32) + off_ref[...].astype(F32)
     copies = [pltpu.make_async_copy(latents_ref, latents_hbm, sem.at[0])]
     copies[0].start()
-    stats = stats_ref[...] + more_ref[...]
-    norm = jnp.sqrt(stats[8:9, 0:1] + stats[24:25, 0:1])
+    stats, more = stats_ref[...], more_ref[...]
+    norm = jnp.sqrt(stats[8:9, 0:1] + more[8:9, 0:1])
     norm_ref[...] = norm
     factor = jnp.minimum(1.0, MAX_NORM / (norm + 1e-06))
     count = step_ref[0:1, 0:1]
     first_scale = 1.0 - jnp.exp(count * jnp.log(jnp.full((1, 1), BETA_ONE, F32)))
     second_scale = 1.0 - jnp.exp(count * jnp.log(jnp.full((1, 1), BETA_TWO, F32)))
     decay = jnp.minimum(AVERAGE_DECAY, (1.0 + count) / (10.0 + count))
-    vector_ref[:, 0:LANES] = jnp.where(odd, stats[16:24, :], stats[0:8, :]) * factor
-    vector_ref[:, LANES : 2 * LANES] = jnp.where(odd, stats[0:8, :], stats[16:24, :]) * factor
+    vector_ref[:, 0:LANES] = jnp.where(odd, more[0:8, :], stats[0:8, :]) * factor
+    vector_ref[:, LANES : 2 * LANES] = jnp.where(odd, stats[0:8, :], more[0:8, :]) * factor
     chunk = share // 3 if share % 24 == 0 else share
     for i in range(share // chunk):
         rows = slice(i * chunk, (i + 1) * chunk)
@@ -934,13 +934,13 @@
     grads_off = across(part_off, "edge")
     grads_pair = flipped(part_pair, "edge", 1)
 
-    other = flipped(mine, "edge", 1)
-    stats = jnp.concatenate([mine[share:], other[share:]], axis=0)
-    bit = 1
-    while 2 * bit < feats:
-        stats = stats + flipped(stats, "feat", bit)
-        bit *= 2
-    more = flipped(stats, "feat", bit)
+    other = flipped(mine[:share], "edge", 1)
+    held = {0: mine[share:], **{k: flipped(mine[share:], "feat", k) for k in ways(feats)}}
+    held = [held[k] for k in range(feats)]
+    while len(held) > 1:
+        held = [held[i] + held[i + 1] for i in range(0, len(held), 2)]
+    stats = held[0]
+    more = flipped(stats, "edge", 1)
     new_first, new_second, new_params, new_average, grad_norm, vector_grads, grad_latents = adam(
         step, stats, more, mine, other, params, first_moment, second_moment, averaged,
         part_own, grads_pair, grads_off,

time: 94.2 us -> 93.6 us (level)
    ppermute x19 -> x21, waiting for transfers between devices: 11.1 us -> 12.1 us  [flipped(): lax.ppermute(value, axis, [(i, i ^ bit) for i in range(lax.axis_size(axis...]
    ppermute x19 -> x21, starting transfers between devices: 18.8 us -> 18.3 us  [flipped(): lax.ppermute(value, axis, [(i, i ^ bit) for i in range(lax.axis_size(axis...]
  transfers between devices with their start and end apart: 23 -> 25, of which waited for: 12 -> 12; matrix products, arithmetic and copies ran while one was open for 0% -> 0% of each run, Pallas kernels for 37% -> 37%
where the time goes in v9:
time: 93.6 us; the launch traced here: 93.4 us
  Pallas kernels  52 us (56%)
  starting transfers between devices  24.5 us (26%)
  waiting for transfers between devices  14.8 us (16%)
  between operations  1.8 us (2%)
    ppermute x21, starting transfers between devices, flipped(): lax.ppermute(value, axis, [(i, i ^ bit) for i in range(lax.axis_size(axis...  18.3 us
    ppermute x21, waiting for transfers between devices, flipped(): lax.ppermute(value, axis, [(i, i ^ bit) for i in range(lax.axis_size(axis...  12.1 us
    pallas_call x1, Pallas kernels, edge_forward(): pl.pallas_call(edge_forward_kernel, grid=(1,), in_specs=[whole((count //...  7.26 us
    pallas_call x3, Pallas kernels, gather_near(): pl.pallas_call(gather_near_kernel, grid=(1,), in_specs=[whole((edges // L...  7.22 us
    pallas_call x1, Pallas kernels, edge_backward(): pl.pallas_call(edge_backward_kernel, grid=(count // TILE,), in_specs=[til...  6.24 us
    ppermute x4, starting transfers between devices, across(): lax.ppermute(value, axis, [(i, (i + 1 if i % 2 else i - 1) % count) for i...  6.19 us
    pallas_call x1, Pallas kernels, sender_part(): pl.pallas_call(sender_part_kernel, grid=(3,), in_specs=[whole((1, count))...  4.96 us
    pallas_call x1, Pallas kernels, near_sum(): pl.pallas_call(near_sum_kernel, out_shape=[half, half, jax.ShapeDtypeStru...  4.5 us
  transfers between devices with their start and end apart: 25, of which 12 were waited for; matrix products, arithmetic and copies ran while one was open for 0% of the time, Pallas kernels for 37%

profile of v9, /device:TPU:0, one launch (start us, length us, event | category | flops | bytes accessed | tf_op | source)
XLA Modules:
  0.0 93.4 jit_solution(11767467409684150657)
XLA Ops:
  0.6 0.5 collective-permute-start.1
  1.2 1.2 %prologue.1 = (bf16[456,128]{1,0:T(8,128)(2,1)S(1)}, s32[32,128]{1,0:T(8,128)S(1)}, s32[32,128]{1,0:T(8,128)S(1)}, bf16[512,256]{1,0:T(8,128)(2,1)S(1)}) custom-call(f32[456,256]{1,0:T(8,128)} %params_ref.1, s32[32,128]{1,0:T(8,128)} %bitcast.36, s32[32,128]{1,0:T(8,128)} %bitcast.37, bf16[512,256]{1,0:T(8,128)(2,1)} %bitcast.34), custom_call_target="tpu_custom_call" | custom-call | tf_op jit(solution)/shard_map/prologue/pallas_call | solution.py:122
  2.3 3.7 %collective-permute-start.2 = (bf16[456,128]{1,0:T(8,128)(2,1)S(1)}, bf16[456,128]{1,0:T(8,128)(2,1)S(1)}, u32[]{:S(2)}, u32[]{:S(2)}) collective-permute-start(bf16[456,128]{1,0:T(8,128)(2,1)S(1)} %get-tuple-element.72.refs_0_), channel_id=1, source_target_pairs={{0,2},{1,3},{2,0},{3,1},{4,6},{5,7},{6,4},{7,5},{8,10},{9,11},{10,... | collective-permute-start | bytes 350216 | tf_op jit(solution)/shard_map/ppermute | solution.py:858
  6.0 1.3 %collective-permute-start.3 = (bf16[456,128]{1,0:T(8,128)(2,1)S(1)}, bf16[456,128]{1,0:T(8,128)(2,1)S(1)}, u32[]{:S(2)}, u32[]{:S(2)}) collective-permute-start(bf16[456,128]{1,0:T(8,128)(2,1)S(1)} %get-tuple-element.72.refs_0_), channel_id=1, source_target_pairs={{0,3},{1,2},{2,1},{3,0},{4,7},{5,6},{6,5},{7,4},{8,11},{9,10},{10,... | collective-permute-start | bytes 350216 | tf_op jit(solution)/shard_map/ppermute | solution.py:858
  7.3 0.2 collective-permute-start.4
  7.6 2.0 %collective-permute-start = (bf16[512,256]{1,0:T(8,128)(2,1)}, bf16[512,256]{1,0:T(8,128)(2,1)S(1)}, u32[]{:S(2)}, u32[]{:S(2)}) collective-permute-start(bf16[512,256]{1,0:T(8,128)(2,1)} %bitcast.35), channel_id=1, source_target_pairs={{0,28},{4,8},{8,4},{12,16},{16,12},{20,24},{24,20},{28,0},{1,29},{... | collective-permute-start | bytes 786440 | tf_op jit(solution)/shard_map/ppermute | solution.py:863
  9.6 2.4 %gather_near.4.near_ref = bf16[4096,256]{1,0:T(8,128)(2,1)S(1)} custom-call(s32[32,128]{1,0:T(8,128)S(1)} %get-tuple-element.70.index_ref, bf16[512,256]{1,0:T(8,128)(2,1)S(1)} %get-tuple-element.69.own_ref.h_ref, bf16[512,256]{1,0:T(8,128)(2,1)S(1)} %collective-permute-done.1.pair_ref), custom_call_target="tpu_custom_call" | custom-call | flops 2147483648 | bytes 2097152 | tf_op jit(solution)/shard_map/gather_near/pallas_call | solution.py:151
  12.0 2.4 %gather_near.3.near_ref = bf16[4096,256]{1,0:T(8,128)(2,1)S(1)} custom-call(s32[32,128]{1,0:T(8,128)S(1)} %get-tuple-element.71.index_ref, bf16[512,256]{1,0:T(8,128)(2,1)S(1)} %get-tuple-element.69.own_ref.h_ref, bf16[512,256]{1,0:T(8,128)(2,1)S(1)} %collective-permute-done.1.pair_ref), custom_call_target="tpu_custom_call" | custom-call | flops 2147483648 | bytes 2097152 | tf_op jit(solution)/shard_map/gather_near/pallas_call | solution.py:151
  14.4 0.7 collective-permute-done.2
  15.1 0.0 collective-permute-done.3
  15.1 1.1 %collective-permute-done.4 = bf16[456,128]{1,0:T(8,128)(2,1)S(1)} collective-permute-done((bf16[456,128]{1,0:T(8,128)(2,1)S(1)}, bf16[456,128]{1,0:T(8,128)(2,1)S(1)}, u32[]{:S(2)}, u32[]{:S(2)}) %collective-permute-start.4) | collective-permute-done | bytes 116768 | tf_op jit(solution)/shard_map/ppermute | solution.py:858
  16.3 0.1 collective-permute-start.6
  16.4 0.5 collective-permute-start.5
  16.9 0.2 collective-permute-done.off_ref
  17.1 1.3 %gather_off.3.hr_ref = bf16[4096,256]{1,0:T(8,128)(2,1)S(1)} custom-call(s32[32,128]{1,0:T(8,128)S(1)} %get-tuple-element.70.index_ref, bf16[512,256]{1,0:T(8,128)(2,1)S(1)} %collective-permute-done.off_ref, bf16[4096,256]{1,0:T(8,128)(2,1)S(1)} %gather_near.4.near_ref), custom_call_target="tpu_custom_call" | custom-call | flops 1073741824 | bytes 4194304 | tf_op jit(solution)/shard_map/gather_off/pallas_call | solution.py:176
  18.4 0.0 copy-start
  18.4 0.0 copy-start.6
  18.5 1.3 %gather_off.2.hs_ref = bf16[4096,256]{1,0:T(8,128)(2,1)S(1)} custom-call(s32[32,128]{1,0:T(8,128)S(1)} %get-tuple-element.71.index_ref, bf16[512,256]{1,0:T(8,128)(2,1)S(1)} %collective-permute-done.off_ref, bf16[4096,256]{1,0:T(8,128)(2,1)S(1)} %gather_near.3.near_ref), custom_call_target="tpu_custom_call" | custom-call | flops 1073741824 | bytes 4194304 | tf_op jit(solution)/shard_map/gather_off/pallas_call | solution.py:176
  19.8 0.0 collective-permute-done.6.refs_3_
  19.8 0.2 copy-done
  20.0 7.3 %edge_forward.1 = (bf16[1824,256]{1,0:T(8,128)(2,1)S(1)}, bf16[4096,256]{1,0:T(8,128)(2,1)S(1)}, bf16[4096,256]{1,0:T(8,128)(2,1)S(1)}, s16[656,256]{1,0:T(8,128)(2,1)S(1)}) custom-call(s32[32,128]{1,0:T(8,128)S(1)} %bitcast.27, s32[1,4096]{1,0:T(1,128)S(1)} %bitcast.22, bf16[4096,256]{1,0:T(8,128)(2,1)S(1)} %gather_off.2.hs_ref, ...), custom_call_target="tpu_custom_call" | custom-call | flops 4831838208 | bytes 10485760 | tf_op jit(solution)/shard_map/edge_forward/pallas_call | solution.py:316
  27.3 2.0 %collective-permute-start.9 = (s16[656,256]{1,0:T(8,128)(2,1)S(1)}, s16[656,256]{1,0:T(8,128)(2,1)S(1)}, u32[]{:S(2)}, u32[]{:S(2)}) collective-permute-start(s16[656,256]{1,0:T(8,128)(2,1)S(1)} %get-tuple-element.85), channel_id=1, source_target_pairs={{0,28},{4,8},{8,4},{12,16},{16,12},{20,24},{24,20},{28,0},{1,29},{... | collective-permute-start | bytes 1007624 | tf_op jit(solution)/shard_map/ppermute | solution.py:863
  29.3 4.5 %near_sum.1 = (f32[256,256]{1,0:T(8,128)S(1)}, f32[256,256]{1,0:T(8,128)S(1)}, f32[512,256]{1,0:T(8,128)S(1)}) custom-call(s32[1,4096]{1,0:T(1,128)S(1)} %bitcast.23, bf16[4096,256]{1,0:T(8,128)(2,1)S(1)} %get-tuple-element.76.high_ref, bf16[4096,256]{1,0:T(8,128)(2,1)S(1)} %get-tuple-element.77.low_ref), custom_call_target="tpu_custom_call" | custom-call | flops 4294967296 | bytes 4194304 | tf_op jit(solution)/shard_map/near_sum/pallas_call | solution.py:401
  33.8 0.1 collective-permute-start.7
  33.9 0.5 collective-permute-start.8
  34.4 3.4 %edge_slope.1 = (bf16[4096,256]{1,0:T(8,128)(2,1)S(1)}, f32[4096,256]{1,0:T(8,128)S(1)}) custom-call(s32[32,128]{1,0:T(8,128)S(1)} %bitcast.28, bf16[4096,256]{1,0:T(8,128)(2,1)S(1)} %gather_off.2.hs_ref, bf16[4096,256]{1,0:T(8,128)(2,1)S(1)} %gather_off.3.hr_ref, bf16[4096,256]{1,0:T(8,128)(2,1)S(1)} %bitcast.18, bf16[1824,256]{1,0:T(8,128)(2,1)S(1)} %get-tuple-element.79.w_ref), custom_call_target="tpu_custom_call" | custom-call | flops 2147483648 | bytes 12582912 | tf_op jit(solution)/shard_map/edge_slope/pallas_call | solution.py:353
  37.7 0.0 collective-permute-done.8.more_ref
  37.8 0.5 collective-permute-done.9.off_ref
  38.3 1.2 %node_update.1 = (bf16[512,256]{1,0:T(8,128)(2,1)S(1)}, bf16[512,256]{1,0:T(8,128)(2,1)S(1)}, bf16[512,256]{1,0:T(8,128)(2,1)S(1)}, bf16[512,256]{1,0:T(8,128)(2...) custom-call(bf16[512,256]{1,0:T(8,128)(2,1)S(1)} %get-tuple-element.69.own_ref.h_ref, ...), custom_call_target="tpu_custom_call" | custom-call | flops 335544320 | bytes 2621440 | tf_op jit(solution)/shard_map/node_update/pallas_call | solution.py:454
  39.5 0.1 collective-permute-start.11
  39.6 1.3 %collective-permute-start.10 = (bf16[512,256]{1,0:T(8,128)(2,1)S(1)}, bf16[512,256]{1,0:T(8,128)(2,1)S(1)}, u32[]{:S(2)}, u32[]{:S(2)}) collective-permute-start(bf16[512,256]{1,0:T(8,128)(2,1)S(1)} %get-tuple-element.93.own_ref), channel_id=1, source_target_pairs={{0,28},{4,8},{8,4},{12,16},{16,12},{20,24},{24,20},{28,0},{1,29},{... | collective-permute-start | bytes 786440 | tf_op jit(solution)/shard_map/ppermute | solution.py:863
  40.9 1.3 %node_grads.1 = (f32[512,256]{1,0:T(8,128)}, f32[768,256]{1,0:T(8,128)S(1)}, f32[4,256]{1,0:T(4,128)S(1)}, f32[512,256]{1,0:T(8,128)S(1)}) custom-call(bf16[512,256]{1,0:T(8,128)(2,1)S(1)} %get-tuple-element.69.own_ref.h_ref, bf16[512,256]{1,0:T(8,128)(2,1)S(1)} %get-tuple-element.86.agg_ref, bf16[512,256]{1,0:T(8,128)(2,1)S(1)} %get-tuple-element.87.hidden_ref, ...), custom_call_target="tpu_custom_call" | custom-call | flops 268435456 | bytes 2359296 | tf_op jit(solution)/shard_map/node_grads/pallas_call | solution.py:493
  42.2 0.8 off_choice.1.choice_ref
  43.1 1.7 %edge_unit.1 = (f32[4096,256]{1,0:T(8,128)S(1)}, f32[4096,128]{1,0:T(8,128)S(1)}) custom-call(bf16[4096,256]{1,0:T(8,128)(2,1)S(1)} %get-tuple-element.95.hidden_ref, bf16[1824,256]{1,0:T(8,128)(2,1)S(1)} %get-tuple-element.79.w_ref), custom_call_target="tpu_custom_call" | custom-call | flops 536870912 | bytes 8388608 | tf_op jit(solution)/shard_map/edge_unit/pallas_call | solution.py:376
  44.8 2.4 %gather_near.5.near_ref = bf16[4096,256]{1,0:T(8,128)(2,1)S(1)} custom-call(s32[32,128]{1,0:T(8,128)S(1)} %get-tuple-element.70.index_ref, bf16[512,256]{1,0:T(8,128)(2,1)S(1)} %get-tuple-element.93.own_ref, bf16[512,256]{1,0:T(8,128)(2,1)S(1)} %collective-permute-done.11.pair_ref), custom_call_target="tpu_custom_call" | custom-call | flops 2147483648 | bytes 2097152 | tf_op jit(solution)/shard_map/gather_near/pallas_call | solution.py:151
  47.2 1.8 %collective-permute-done.10.off_ref = bf16[512,256]{1,0:T(8,128)(2,1)S(1)} collective-permute-done((bf16[512,256]{1,0:T(8,128)(2,1)S(1)}, bf16[512,256]{1,0:T(8,128)(2,1)S(1)}, u32[]{:S(2)}, u32[]{:S(2)}) %collective-permute-start.10) | collective-permute-done | bytes 262176 | tf_op jit(solution)/shard_map/ppermute | solution.py:863
  49.0 6.2 %edge_backward.1 = (bf16[4096,256]{1,0:T(8,128)(2,1)S(1)}, f32[1824,128]{1,0:T(8,128)S(1)}, f32[1824,128]{1,0:T(8,128)S(1)}) custom-call(bf16[4096,512]{1,0:T(8,128)(2,1)S(1)} %off_choice.1.choice_ref, s32[1,4096]{1,0:T(1,128)S(1)} %bitcast.29, bf16[512,256]{1,0:T(8,128)(2,1)S(1)} %collective-permute-done.10.off_ref, ...), custom_call_target="tpu_custom_call" | custom-call | flops 4294967296 | bytes 20971520 | tf_op jit(solution)/shard_map/edge_backward/pallas_call | solution.py:582
  55.3 0.1 collective-permute-start.12
  55.4 1.9 %edge_grads.1 = bf16[4096,256]{1,0:T(8,128)(2,1)} custom-call(bf16[4096,256]{1,0:T(8,128)(2,1)S(1)} %get-tuple-element.107.d_pre_ref, bf16[1824,256]{1,0:T(8,128)(2,1)S(1)} %get-tuple-element.79.w_ref), custom_call_target="tpu_custom_call" | custom-call | flops 536870912 | bytes 4194304 | tf_op jit(solution)/shard_map/edge_grads/pallas_call | solution.py:697
  57.3 0.6 collective-permute-done.12.other_ref
  57.8 0.1 parted.1
  57.9 3.3 %collective-permute-start.13 = (bf16[464,128]{1,0:T(8,128)(2,1)S(1)}, bf16[464,128]{1,0:T(8,128)(2,1)S(1)}, u32[]{:S(2)}, u32[]{:S(2)}) collective-permute-start(bf16[464,128]{1,0:T(8,128)(2,1)S(1)} %get-tuple-element.111), channel_id=1, source_target_pairs={{0,2},{1,3},{2,0},{3,1},{4,6},{5,7},{6,4},{7,5},{8,10},{9,11},{10,... | collective-permute-start | bytes 356360 | tf_op jit(solution)/shard_map/ppermute | solution.py:858
  61.2 1.0 %collective-permute-start.14 = (bf16[464,128]{1,0:T(8,128)(2,1)S(1)}, bf16[464,128]{1,0:T(8,128)(2,1)S(1)}, u32[]{:S(2)}, u32[]{:S(2)}) collective-permute-start(bf16[464,128]{1,0:T(8,128)(2,1)S(1)} %get-tuple-element.112), channel_id=1, source_target_pairs={{0,3},{1,2},{2,1},{3,0},{4,7},{5,6},{6,5},{7,4},{8,11},{9,10},{10,... | collective-permute-start | bytes 356360 | tf_op jit(solution)/shard_map/ppermute | solution.py:858
  62.3 5.0 %sender_part.1.part_ref = f32[1536,256]{1,0:T(8,128)S(1)} custom-call(s32[1,4096]{1,0:T(1,128)S(1)} %bitcast.26, bf16[4096,256]{1,0:T(8,128)(2,1)S(1)} %get-tuple-element.107.d_pre_ref, bf16[1824,256]{1,0:T(8,128)(2,1)S(1)} %get-tuple-element.79.w_ref), custom_call_target="tpu_custom_call" | custom-call | flops 3221225472 | bytes 2097152 | tf_op jit(solution)/shard_map/sender_part/pallas_call | solution.py:620
  67.2 3.4 %receiver_part.1 = (bf16[512,256]{1,0:T(8,128)(2,1)S(1)}, bf16[512,256]{1,0:T(8,128)(2,1)S(1)}) custom-call(s32[1,4096]{1,0:T(1,128)S(1)} %bitcast.24, bf16[4096,256]{1,0:T(8,128)(2,1)S(1)} %get-tuple-element.107.d_pre_ref, bf16[1824,256]{1,0:T(8,128)(2,1)S(1)} %get-tuple-element.79.w_ref, f32[1536,256]{1,0:T(8,128)S(1)} %sender_part.1.part_ref), custom_call_target="tpu_custom_call" | custom-call | flops 2147483648 | bytes 2097152 | tf_op jit(solution)/shard_map/receiver_part/pallas_call | solution.py:651
  70.6 0.0 collective-permute-done.13.refs_0_
  70.6 0.0 collective-permute-done.14.refs_1_
  70.7 0.6 collective-permute-done.15.refs_2_
  71.2 0.1 gathered.1.mine_ref
  71.3 0.8 collective-permute-start.16
  72.1 1.7 %own_part.1.own_ref = f32[512,256]{1,0:T(8,128)S(1)} custom-call(s32[1,4096]{1,0:T(1,128)S(1)} %bitcast.25, bf16[4096,256]{1,0:T(8,128)(2,1)S(1)} %get-tuple-element.107.d_pre_ref, bf16[1824,256]{1,0:T(8,128)(2,1)S(1)} %get-tuple-element.79.w_ref, f32[1536,256]{1,0:T(8,128)S(1)} %sender_part.1.part_ref, f32[512,256]{1,0:T(8,128)S(1)} %get-tuple-element.116.back_ref), custom_call_target="tpu_custom_call" | custom-call | flops 1073741824 | bytes 2097152 | tf_op jit(solution)/shard_map/own_part/pallas_call | solution.py:676
  73.8 2.4 %collective-permute-done.16.other_ref = bf16[464,128]{1,0:T(8,128)(2,1)S(1)} collective-permute-done((bf16[464,128]{1,0:T(8,128)(2,1)S(1)}, bf16[464,128]{1,0:T(8,128)(2,1)S(1)}, u32[]{:S(2)}, u32[]{:S(2)}) %collective-permute-start.16) | collective-permute-done | bytes 118816 | tf_op jit(solution)/shard_map/ppermute | solution.py:858
  76.2 1.5 %collective-permute-start.17 = (bf16[464,128]{1,0:T(8,128)(2,1)S(1)}, bf16[464,128]{1,0:T(8,128)(2,1)S(1)}, u32[]{:S(2)}, u32[]{:S(2)}) collective-permute-start(bf16[464,128]{1,0:T(8,128)(2,1)S(1)} %add.16.mine_ref), channel_id=1, source_target_pairs={{0,16},{4,20},{8,24},{12,28},{16,0},{20,4},{24,8},{28,12},{1,17},{... | collective-permute-start | bytes 356360 | tf_op jit(solution)/shard_map/ppermute | solution.py:858
  77.7 0.9 collective-permute-start.24
  78.6 2.5 %collective-permute-done.17.other_ref = bf16[464,128]{1,0:T(8,128)(2,1)S(1)} collective-permute-done((bf16[464,128]{1,0:T(8,128)(2,1)S(1)}, bf16[464,128]{1,0:T(8,128)(2,1)S(1)}, u32[]{:S(2)}, u32[]{:S(2)}) %collective-permute-start.17) | collective-permute-done | bytes 118816 | tf_op jit(solution)/shard_map/ppermute | solution.py:858
  81.1 0.2 finish.1.mine_ref
  81.3 2.1 %collective-permute-start.18 = (f32[16,128]{1,0:T(8,128)S(1)}, f32[16,128]{1,0:T(8,128)S(1)}, u32[]{:S(2)}, u32[]{:S(2)}) collective-permute-start(f32[16,128]{1,0:T(8,128)S(1)} %slice.11), channel_id=1, source_target_pairs={{0,1},{1,0},{2,3},{3,2},{4,5},{5,4},{6,7},{7,6},{8,9},{9,8},{10,11... | collective-permute-start | bytes 24584 | tf_op jit(solution)/shard_map/ppermute | solution.py:858
  83.5 0.7 collective-permute-start.19
  84.2 1.7 %collective-permute-start.20 = (f32[16,128]{1,0:T(8,128)S(1)}, f32[16,128]{1,0:T(8,128)S(1)}, u32[]{:S(2)}, u32[]{:S(2)}) collective-permute-start(f32[16,128]{1,0:T(8,128)S(1)} %slice.11), channel_id=1, source_target_pairs={{0,3},{1,2},{2,1},{3,0},{4,7},{5,6},{6,5},{7,4},{8,11},{9,10},{10,... | collective-permute-start | bytes 24584 | tf_op jit(solution)/shard_map/ppermute | solution.py:858
  85.9 0.1 collective-permute-start.22
  86.0 2.0 %collective-permute-done.19 = f32[16,128]{1,0:T(8,128)S(1)} collective-permute-done((f32[16,128]{1,0:T(8,128)S(1)}, f32[16,128]{1,0:T(8,128)S(1)}, u32[]{:S(2)}, u32[]{:S(2)}) %collective-permute-start.19) | collective-permute-done | bytes 8224 | tf_op jit(solution)/shard_map/ppermute | solution.py:858
  88.0 1.6 %collective-permute-done.20 = f32[16,128]{1,0:T(8,128)S(1)} collective-permute-done((f32[16,128]{1,0:T(8,128)S(1)}, f32[16,128]{1,0:T(8,128)S(1)}, u32[]{:S(2)}, u32[]{:S(2)}) %collective-permute-start.20) | collective-permute-done | bytes 8224 | tf_op jit(solution)/shard_map/ppermute | solution.py:858
  90.3 0.5 collective-permute-done.21.more_ref
  90.9 2.3 %adam.1 = (f32[456,256]{1,0:T(8,128)}, f32[456,256]{1,0:T(8,128)}, f32[456,256]{1,0:T(8,128)}, f32[456,256]{1,0:T(8,128)}, f32[1,1]{1,0:T(1,128)}, /*index=5*/f32[8,256]{1,0:T(8,128)}, f32[512,256]{1,0:T(8,128)}) custom-call(f32[8,128]{1,0:T(8,128)S(1)} %broadcast_in_dim.15.step_ref, f32[16,128]{1,0:T(8,128)S(1)} %add_add_fusion.stats_ref, ...), custom_call_target="tpu_custom_call" | custom-call | flops 2334720 | bytes 3735552 | tf_op jit(solution)/shard_map/adam/pallas_call | solution.py:839
  (32 shorter events, 0.2 us)
Async XLA Ops:
  0.6 8.9 %collective-permute-start.1 = (bf16[512,256]{1,0:T(8,128)(2,1)}, bf16[512,256]{1,0:T(8,128)(2,1)S(1)}, u32[]{:S(2)}, u32[]{:S(2)}) collective-permute-start(bf16[512,256]{1,0:T(8,128)(2,1)} %bitcast.33), channel_id=1, source_target_pairs={{0,4},{4,0},{8,12},{12,8},{16,20},{20,16},{24,28},{28,24},{1,5},{5... | collective-permute-start | bytes 786440 | tf_op jit(solution)/shard_map/ppermute | solution.py:858
  2.3 12.8 %collective-permute-start.2 = (bf16[456,128]{1,0:T(8,128)(2,1)S(1)}, bf16[456,128]{1,0:T(8,128)(2,1)S(1)}, u32[]{:S(2)}, u32[]{:S(2)}) collective-permute-start(bf16[456,128]{1,0:T(8,128)(2,1)S(1)} %get-tuple-element.72.refs_0_), channel_id=1, source_target_pairs={{0,2},{1,3},{2,0},{3,1},{4,6},{5,7},{6,4},{7,5},{8,10},{9,11},{10,... | collective-permute-start | bytes 350216 | tf_op jit(solution)/shard_map/ppermute | solution.py:858
  6.0 9.1 %collective-permute-start.3 = (bf16[456,128]{1,0:T(8,128)(2,1)S(1)}, bf16[456,128]{1,0:T(8,128)(2,1)S(1)}, u32[]{:S(2)}, u32[]{:S(2)}) collective-permute-start(bf16[456,128]{1,0:T(8,128)(2,1)S(1)} %get-tuple-element.72.refs_0_), channel_id=1, source_target_pairs={{0,3},{1,2},{2,1},{3,0},{4,7},{5,6},{6,5},{7,4},{8,11},{9,10},{10,... | collective-permute-start | bytes 350216 | tf_op jit(solution)/shard_map/ppermute | solution.py:858
  7.3 8.9 %collective-permute-start.4 = (bf16[456,128]{1,0:T(8,128)(2,1)S(1)}, bf16[456,128]{1,0:T(8,128)(2,1)S(1)}, u32[]{:S(2)}, u32[]{:S(2)}) collective-permute-start(bf16[456,128]{1,0:T(8,128)(2,1)S(1)} %get-tuple-element.72.refs_0_), channel_id=1, source_target_pairs={{0,1},{1,0},{2,3},{3,2},{4,5},{5,4},{6,7},{7,6},{8,9},{9,8},{10,11... | collective-permute-start | bytes 350216 | tf_op jit(solution)/shard_map/ppermute | solution.py:858
  7.6 9.5 %collective-permute-start = (bf16[512,256]{1,0:T(8,128)(2,1)}, bf16[512,256]{1,0:T(8,128)(2,1)S(1)}, u32[]{:S(2)}, u32[]{:S(2)}) collective-permute-start(bf16[512,256]{1,0:T(8,128)(2,1)} %bitcast.35), channel_id=1, source_target_pairs={{0,28},{4,8},{8,4},{12,16},{16,12},{20,24},{24,20},{28,0},{1,29},{... | collective-permute-start | bytes 786440 | tf_op jit(solution)/shard_map/ppermute | solution.py:863
  16.3 3.5 %collective-permute-start.6 = (bf16[1368,128]{1,0:T(8,128)(2,1)S(1)}, bf16[1368,128]{1,0:T(8,128)(2,1)S(1)}, u32[]{:S(2)}, u32[]{:S(2)}) collective-permute-start(bf16[1368,128]{1,0:T(8,128)(2,1)S(1)} %constant_dynamic-update-slice_fusion.refs_1_), channel_id=1, source_target_pairs={{0,4},{4,0},{8,12},{12,8},{16,20},{20,16},{24,28},{28,24},{1,5},{5... | collective-permute-start | bytes 1050632 | tf_op jit(solution)/shard_map/ppermute | solution.py:858
  16.4 3.4 %collective-permute-start.5 = (bf16[456,128]{1,0:T(8,128)(2,1)S(1)}, bf16[456,128]{1,0:T(8,128)(2,1)S(1)}, u32[]{:S(2)}, u32[]{:S(2)}) collective-permute-start(bf16[456,128]{1,0:T(8,128)(2,1)S(1)} %get-tuple-element.72.refs_0_), channel_id=1, source_target_pairs={{0,4},{4,0},{8,12},{12,8},{16,20},{20,16},{24,28},{28,24},{1,5},{5... | collective-permute-start | bytes 350216 | tf_op jit(solution)/shard_map/ppermute | solution.py:858
  18.4 1.6 %copy-start = (bf16[1,4096,256]{2,1,0:T(8,128)(2,1)S(1)}, bf16[1,4096,256]{2,1,0:T(8,128)(2,1)}, u32[]{:S(2)}) copy-start(bf16[1,4096,256]{2,1,0:T(8,128)(2,1)} %param.13) | copy-start | bytes 6291460
  18.4 1.6 %copy-start.6 = (s32[4096]{0:T(1024)S(1)}, s32[4096]{0:T(1024)}, u32[]{:S(2)}) copy-start(s32[4096]{0:T(1024)} %param.16) | copy-start | bytes 49156
  27.3 11.0 %collective-permute-start.9 = (s16[656,256]{1,0:T(8,128)(2,1)S(1)}, s16[656,256]{1,0:T(8,128)(2,1)S(1)}, u32[]{:S(2)}, u32[]{:S(2)}) collective-permute-start(s16[656,256]{1,0:T(8,128)(2,1)S(1)} %get-tuple-element.85), channel_id=1, source_target_pairs={{0,28},{4,8},{8,4},{12,16},{16,12},{20,24},{24,20},{28,0},{1,29},{... | collective-permute-start | bytes 1007624 | tf_op jit(solution)/shard_map/ppermute | solution.py:863
  33.8 4.0 %collective-permute-start.7 = (f32[256,256]{1,0:T(8,128)S(1)}, f32[256,256]{1,0:T(8,128)S(1)}, u32[]{:S(2)}, u32[]{:S(2)}) collective-permute-start(f32[256,256]{1,0:T(8,128)S(1)} %get-tuple-element.83), channel_id=1, source_target_pairs={{0,4},{4,0},{8,12},{12,8},{16,20},{20,16},{24,28},{28,24},{1,5},{5... | collective-permute-start | bytes 786440 | tf_op jit(solution)/shard_map/ppermute | solution.py:858
  33.9 3.9 %collective-permute-start.8 = (f32[256,256]{1,0:T(8,128)S(1)}, f32[256,256]{1,0:T(8,128)S(1)}, u32[]{:S(2)}, u32[]{:S(2)}) collective-permute-start(f32[256,256]{1,0:T(8,128)S(1)} %get-tuple-element.84), channel_id=1, source_target_pairs={{0,4},{4,0},{8,12},{12,8},{16,20},{20,16},{24,28},{28,24},{1,5},{5... | collective-permute-start | bytes 786440 | tf_op jit(solution)/shard_map/ppermute | solution.py:858
  34.4 3.9 %copy-start.1 = (f32[1,512,256]{2,1,0:T(8,128)S(1)}, f32[1,512,256]{2,1,0:T(8,128)}, u32[]{:S(2)}) copy-start(f32[1,512,256]{2,1,0:T(8,128)} %param.23) | copy-start | bytes 1572868
  34.4 3.9 %copy-start.7 = (s32[512]{0:T(512)S(1)}, s32[512]{0:T(512)}, u32[]{:S(2)}) copy-start(s32[512]{0:T(512)} %param.17) | copy-start | bytes 6148
  39.5 5.2 %collective-permute-start.11 = (bf16[512,256]{1,0:T(8,128)(2,1)S(1)}, bf16[512,256]{1,0:T(8,128)(2,1)S(1)}, u32[]{:S(2)}, u32[]{:S(2)}) collective-permute-start(bf16[512,256]{1,0:T(8,128)(2,1)S(1)} %get-tuple-element.93.own_ref), channel_id=1, source_target_pairs={{0,4},{4,0},{8,12},{12,8},{16,20},{20,16},{24,28},{28,24},{1,5},{5... | collective-permute-start | bytes 786440 | tf_op jit(solution)/shard_map/ppermute | solution.py:858
  39.6 9.4 %collective-permute-start.10 = (bf16[512,256]{1,0:T(8,128)(2,1)S(1)}, bf16[512,256]{1,0:T(8,128)(2,1)S(1)}, u32[]{:S(2)}, u32[]{:S(2)}) collective-permute-start(bf16[512,256]{1,0:T(8,128)(2,1)S(1)} %get-tuple-element.93.own_ref), channel_id=1, source_target_pairs={{0,28},{4,8},{8,4},{12,16},{16,12},{20,24},{24,20},{28,0},{1,29},{... | collective-permute-start | bytes 786440 | tf_op jit(solution)/shard_map/ppermute | solution.py:863
  55.3 2.6 %collective-permute-start.12 = (f32[1824,128]{1,0:T(8,128)S(1)}, f32[1824,128]{1,0:T(8,128)S(1)}, u32[]{:S(2)}, u32[]{:S(2)}) collective-permute-start(f32[1824,128]{1,0:T(8,128)S(1)} %get-tuple-element.103), channel_id=1, source_target_pairs={{0,4},{4,0},{8,12},{12,8},{16,20},{20,16},{24,28},{28,24},{1,5},{5... | collective-permute-start | bytes 2801672 | tf_op jit(solution)/shard_map/ppermute | solution.py:858
  57.9 12.7 %collective-permute-start.13 = (bf16[464,128]{1,0:T(8,128)(2,1)S(1)}, bf16[464,128]{1,0:T(8,128)(2,1)S(1)}, u32[]{:S(2)}, u32[]{:S(2)}) collective-permute-start(bf16[464,128]{1,0:T(8,128)(2,1)S(1)} %get-tuple-element.111), channel_id=1, source_target_pairs={{0,2},{1,3},{2,0},{3,1},{4,6},{5,7},{6,4},{7,5},{8,10},{9,11},{10,... | collective-permute-start | bytes 356360 | tf_op jit(solution)/shard_map/ppermute | solution.py:858
  61.2 9.4 %collective-permute-start.14 = (bf16[464,128]{1,0:T(8,128)(2,1)S(1)}, bf16[464,128]{1,0:T(8,128)(2,1)S(1)}, u32[]{:S(2)}, u32[]{:S(2)}) collective-permute-start(bf16[464,128]{1,0:T(8,128)(2,1)S(1)} %get-tuple-element.112), channel_id=1, source_target_pairs={{0,3},{1,2},{2,1},{3,0},{4,7},{5,6},{6,5},{7,4},{8,11},{9,10},{10,... | collective-permute-start | bytes 356360 | tf_op jit(solution)/shard_map/ppermute | solution.py:858
  62.3 9.0 %collective-permute-start.15 = (bf16[464,128]{1,0:T(8,128)(2,1)S(1)}, bf16[464,128]{1,0:T(8,128)(2,1)S(1)}, u32[]{:S(2)}, u32[]{:S(2)}) collective-permute-start(bf16[464,128]{1,0:T(8,128)(2,1)S(1)} %get-tuple-element.113), channel_id=1, source_target_pairs={{0,1},{1,0},{2,3},{3,2},{4,5},{5,4},{6,7},{7,6},{8,9},{9,8},{10,11... | collective-permute-start | bytes 356360 | tf_op jit(solution)/shard_map/ppermute | solution.py:858
  71.3 4.9 %collective-permute-start.16 = (bf16[464,128]{1,0:T(8,128)(2,1)S(1)}, bf16[464,128]{1,0:T(8,128)(2,1)S(1)}, u32[]{:S(2)}, u32[]{:S(2)}) collective-permute-start(bf16[464,128]{1,0:T(8,128)(2,1)S(1)} %gathered.1.mine_ref), channel_id=1, source_target_pairs={{0,8},{4,12},{8,0},{12,4},{16,24},{20,28},{24,16},{28,20},{1,9},{5... | collective-permute-start | bytes 356360 | tf_op jit(solution)/shard_map/ppermute | solution.py:858
  72.1 18.8 %copy-start.2 = (f32[456,256]{1,0:T(8,128)S(1)}, f32[456,256]{1,0:T(8,128)}, u32[]{:S(2)}) copy-start(f32[456,256]{1,0:T(8,128)} %params_ref.1) | copy-start | bytes 1400836
  72.1 18.8 %copy-start.3 = (f32[456,256]{1,0:T(8,128)S(1)}, f32[456,256]{1,0:T(8,128)}, u32[]{:S(2)}) copy-start(f32[456,256]{1,0:T(8,128)} %first_ref.1) | copy-start | bytes 1400836
  72.1 18.8 %copy-start.4 = (f32[456,256]{1,0:T(8,128)S(1)}, f32[456,256]{1,0:T(8,128)}, u32[]{:S(2)}) copy-start(f32[456,256]{1,0:T(8,128)} %second_ref.1) | copy-start | bytes 1400836
  72.1 18.8 %copy-start.5 = (f32[456,256]{1,0:T(8,128)S(1)}, f32[456,256]{1,0:T(8,128)}, u32[]{:S(2)}) copy-start(f32[456,256]{1,0:T(8,128)} %averaged_ref.1) | copy-start | bytes 1400836
  76.2 4.9 %collective-permute-start.17 = (bf16[464,128]{1,0:T(8,128)(2,1)S(1)}, bf16[464,128]{1,0:T(8,128)(2,1)S(1)}, u32[]{:S(2)}, u32[]{:S(2)}) collective-permute-start(bf16[464,128]{1,0:T(8,128)(2,1)S(1)} %add.16.mine_ref), channel_id=1, source_target_pairs={{0,16},{4,20},{8,24},{12,28},{16,0},{20,4},{24,8},{28,12},{1,17},{... | collective-permute-start | bytes 356360 | tf_op jit(solution)/shard_map/ppermute | solution.py:858
  77.7 13.2 %collective-permute-start.23 = (bf16[512,256]{1,0:T(8,128)(2,1)S(1)}, bf16[512,256]{1,0:T(8,128)(2,1)S(1)}, u32[]{:S(2)}, u32[]{:S(2)}) collective-permute-start(bf16[512,256]{1,0:T(8,128)(2,1)S(1)} %get-tuple-element.119), channel_id=1, source_target_pairs={{0,4},{4,0},{8,12},{12,8},{16,20},{20,16},{24,28},{28,24},{1,5},{5... | collective-permute-start | bytes 786440 | tf_op jit(solution)/shard_map/ppermute | solution.py:858
  77.7 13.2 %collective-permute-start.24 = (bf16[512,256]{1,0:T(8,128)(2,1)S(1)}, bf16[512,256]{1,0:T(8,128)(2,1)S(1)}, u32[]{:S(2)}, u32[]{:S(2)}) collective-permute-start(bf16[512,256]{1,0:T(8,128)(2,1)S(1)} %get-tuple-element.120), channel_id=1, source_target_pairs={{0,28},{4,8},{8,4},{12,16},{16,12},{20,24},{24,20},{28,0},{1,29},{... | collective-permute-start | bytes 786440 | tf_op jit(solution)/shard_map/ppermute | solution.py:863
  81.3 4.6 %collective-permute-start.18 = (f32[16,128]{1,0:T(8,128)S(1)}, f32[16,128]{1,0:T(8,128)S(1)}, u32[]{:S(2)}, u32[]{:S(2)}) collective-permute-start(f32[16,128]{1,0:T(8,128)S(1)} %slice.11), channel_id=1, source_target_pairs={{0,1},{1,0},{2,3},{3,2},{4,5},{5,4},{6,7},{7,6},{8,9},{9,8},{10,11... | collective-permute-start | bytes 24584 | tf_op jit(solution)/shard_map/ppermute | solution.py:858
  83.5 4.5 %collective-permute-start.19 = (f32[16,128]{1,0:T(8,128)S(1)}, f32[16,128]{1,0:T(8,128)S(1)}, u32[]{:S(2)}, u32[]{:S(2)}) collective-permute-start(f32[16,128]{1,0:T(8,128)S(1)} %slice.11), channel_id=1, source_target_pairs={{0,2},{1,3},{2,0},{3,1},{4,6},{5,7},{6,4},{7,5},{8,10},{9,11},{10,... | collective-permute-start | bytes 24584 | tf_op jit(solution)/shard_map/ppermute | solution.py:858
  84.2 5.4 %collective-permute-start.20 = (f32[16,128]{1,0:T(8,128)S(1)}, f32[16,128]{1,0:T(8,128)S(1)}, u32[]{:S(2)}, u32[]{:S(2)}) collective-permute-start(f32[16,128]{1,0:T(8,128)S(1)} %slice.11), channel_id=1, source_target_pairs={{0,3},{1,2},{2,1},{3,0},{4,7},{5,6},{6,5},{7,4},{8,11},{9,10},{10,... | collective-permute-start | bytes 24584 | tf_op jit(solution)/shard_map/ppermute | solution.py:858
  85.9 4.9 %collective-permute-start.22 = (f32[456,128]{1,0:T(8,128)S(1)}, f32[456,128]{1,0:T(8,128)S(1)}, u32[]{:S(2)}, u32[]{:S(2)}) collective-permute-start(f32[456,128]{1,0:T(8,128)S(1)} %slice.12), channel_id=1, source_target_pairs={{0,4},{4,0},{8,12},{12,8},{16,20},{20,16},{24,28},{28,24},{1,5},{5... | collective-permute-start | bytes 700424 | tf_op jit(solution)/shard_map/ppermute | solution.py:858
  89.7 1.2 %collective-permute-start.21 = (f32[16,128]{1,0:T(8,128)S(1)}, f32[16,128]{1,0:T(8,128)S(1)}, u32[]{:S(2)}, u32[]{:S(2)}) collective-permute-start(f32[16,128]{1,0:T(8,128)S(1)} %add_add_fusion.stats_ref), channel_id=1, source_target_pairs={{0,4},{4,0},{8,12},{12,8},{16,20},{20,16},{24,28},{28,24},{1,5},{5... | collective-permute-start | bytes 24584 | tf_op jit(solution)/shard_map/ppermute | solution.py:858

commit v10 on v9

--- a/solution.py
+++ b/solution.py
@@ -187,6 +187,25 @@
     )(index.reshape(-1, LANES), off, near)
 
 
+def off_rows_kernel(index_row_ref, out_ref):
+    nodes = out_ref.shape[0]
+    out_ref[...] = chosen_rows(index_row_ref[...], 2 * nodes, nodes)
+
+
+def off_rows(index, nodes):
+    edges = index.size
+    return pl.pallas_call(
+        off_rows_kernel,
+        grid=(edges // TILE,),
+        in_specs=[pl.BlockSpec((1, TILE), lambda i: (0, i))],
+        out_specs=pl.BlockSpec((nodes, TILE), lambda i: (0, i)),
+        out_shape=jax.ShapeDtypeStruct((nodes, edges), B16),
+        compiler_params=PARAMS,
+        name="off_rows",
+        cost_estimate=pl.CostEstimate(flops=edges * nodes, transcendentals=0, bytes_accessed=edges * nodes * 2),
+    )(index.reshape(1, -1))
+
+
 def off_choice_kernel(index_ref, out_ref):
     rows, nodes = out_ref.shape
     out_ref[...] = chosen_columns(index_ref, pl.program_id(0), rows, 2 * nodes, 3 * nodes)
@@ -269,7 +288,7 @@
 
 
 def edge_forward_kernel(
-    region_ref, recv_row_ref, hs_ref, hr_ref, x_ref, *refs,
+    region_ref, choice_ref, hs_ref, hr_ref, x_ref, *refs,
 ):
     pieces, refs = refs[:-5], refs[-5:]
     w_ref, high_ref, low_ref, halo_ref, wide_ref = refs
@@ -304,20 +323,20 @@
             low_ref[here, :] = low
         if i > 0:
             last = slice((i - 1) * PART, i * PART)
-            onehot = chosen_rows(recv_row_ref[:, last], 2 * nodes, nodes)
+            onehot = choice_ref[:, last]
             more = dot(onehot, high_ref[last, :]) + dot(onehot, low_ref[last, :])
             total = more if total is None else total + more
     halo_ref[...] = encoded(total)
 
 
-def edge_forward(regions, recv, hs, hr, edges, pieces, total, nodes):
+def edge_forward(regions, choice, hs, hr, edges, pieces, total, nodes):
     count, width = edges.shape
     tile = tiled(count, width)
     return pl.pallas_call(
         edge_forward_kernel,
         grid=(1,),
         in_specs=[
-            whole((count // LANES, LANES)), whole((1, count)), tile, tile, tile,
+            whole((count // LANES, LANES)), whole(choice.shape), tile, tile, tile,
             *[whole(piece.shape) for piece in pieces],
         ],
         out_specs=[
@@ -337,7 +356,7 @@
             flops=2 * count * width * (5 * width + 2 * nodes), transcendentals=2 * count * width,
             bytes_accessed=count * width * 10,
         ),
-    )(regions.reshape(-1, LANES), recv.reshape(1, -1), hs, hr, edges, *pieces)
+    )(regions.reshape(-1, LANES), choice, hs, hr, edges, *pieces)
 
 
 def edge_slope_kernel(region_ref, hs_ref, hr_ref, x_ref, w_ref, hidden_ref, slope_ref):
@@ -888,11 +907,12 @@
 
     near_send = gather_near(send, latents, pair)
     near_recv = gather_near(recv, latents, pair)
-    others = jnp.concatenate(lax.optimization_barrier((near_send, near_recv, *far))[2:])
+    off_sums = off_rows(recv, nodes)
+    others = jnp.concatenate(lax.optimization_barrier((near_send, near_recv, off_sums, *far))[3:])
     pieces = [mine, others, flipped(mine, "edge", 1), flipped(others, "edge", 1)]
     hs = gather_off(send, off, near_send)
     hr = gather_off(recv, off, near_recv)
-    weights, high, low, to_off = edge_forward(regions, recv, hs, hr, edges, pieces, total, nodes)
+    weights, high, low, to_off = edge_forward(regions, off_sums, hs, hr, edges, pieces, total, nodes)
     from_off = across(to_off, "edge")
     to_pair, more, own = near_sum(recv, high, low, nodes)
     from_pair, more = flipped(to_pair, "edge", 1), flipped(more, "edge", 1)

time: 93.6 us -> 93.5 us (level)
  waiting for transfers between devices: 14.8 us -> 13.6 us
    ppermute x21, waiting for transfers between devices: 12.1 us -> 11 us  [flipped(): lax.ppermute(value, axis, [(i, i ^ bit) for i in range(lax.axis_size(axis...]
    pallas_call x0 -> x1, Pallas kernels: none -> 1 us  [off_rows(): pl.pallas_call(off_rows_kernel, grid=(edges // TILE,), in_specs=[pl.Block...]
  transfers between devices with their start and end apart: 25 -> 25, of which waited for: 12 -> 11; matrix products, arithmetic and copies ran while one was open for 0% -> 0% of each run, Pallas kernels for 37% -> 38%
where the time goes in v10:
time: 93.5 us; the launch traced here: 93.3 us
  Pallas kernels  52.9 us (57%)
  starting transfers between devices  24.6 us (26%)
  waiting for transfers between devices  13.6 us (15%)
  between operations  1.83 us (2%)
    ppermute x21, starting transfers between devices, flipped(): lax.ppermute(value, axis, [(i, i ^ bit) for i in range(lax.axis_size(axis...  18.4 us
    ppermute x21, waiting for transfers between devices, flipped(): lax.ppermute(value, axis, [(i, i ^ bit) for i in range(lax.axis_size(axis...  11 us
    pallas_call x3, Pallas kernels, gather_near(): pl.pallas_call(gather_near_kernel, grid=(1,), in_specs=[whole((edges // L...  7.23 us
    pallas_call x1, Pallas kernels, edge_forward(): pl.pallas_call(edge_forward_kernel, grid=(1,), in_specs=[whole((count //...  7.19 us
    pallas_call x1, Pallas kernels, edge_backward(): pl.pallas_call(edge_backward_kernel, grid=(count // TILE,), in_specs=[til...  6.25 us
    ppermute x4, starting transfers between devices, across(): lax.ppermute(value, axis, [(i, (i + 1 if i % 2 else i - 1) % count) for i...  6.18 us
    pallas_call x1, Pallas kernels, sender_part(): pl.pallas_call(sender_part_kernel, grid=(3,), in_specs=[whole((1, count))...  4.96 us
    pallas_call x1, Pallas kernels, near_sum(): pl.pallas_call(near_sum_kernel, out_shape=[half, half, jax.ShapeDtypeStru...  4.5 us
  transfers between devices with their start and end apart: 25, of which 11 were waited for; matrix products, arithmetic and copies ran while one was open for 0% of the time, Pallas kernels for 38%

profile of v10, /device:TPU:0, one launch (start us, length us, event | category | flops | bytes accessed | tf_op | source)
XLA Modules:
  0.0 93.3 jit_solution(1344010704920648147)
XLA Ops:
  0.6 0.5 collective-permute-start.1
  1.2 1.2 %prologue.1 = (bf16[456,128]{1,0:T(8,128)(2,1)S(1)}, s32[32,128]{1,0:T(8,128)S(1)}, s32[32,128]{1,0:T(8,128)S(1)}, bf16[512,256]{1,0:T(8,128)(2,1)S(1)}) custom-call(f32[456,256]{1,0:T(8,128)} %params_ref.1, s32[32,128]{1,0:T(8,128)} %bitcast.36, s32[32,128]{1,0:T(8,128)} %bitcast.37, bf16[512,256]{1,0:T(8,128)(2,1)} %bitcast.34), custom_call_target="tpu_custom_call" | custom-call | tf_op jit(solution)/shard_map/prologue/pallas_call | solution.py:122
  2.3 3.7 %collective-permute-start.2 = (bf16[456,128]{1,0:T(8,128)(2,1)S(1)}, bf16[456,128]{1,0:T(8,128)(2,1)S(1)}, u32[]{:S(2)}, u32[]{:S(2)}) collective-permute-start(bf16[456,128]{1,0:T(8,128)(2,1)S(1)} %get-tuple-element.72.refs_0_), channel_id=1, source_target_pairs={{0,2},{1,3},{2,0},{3,1},{4,6},{5,7},{6,4},{7,5},{8,10},{9,11},{10,... | collective-permute-start | bytes 350216 | tf_op jit(solution)/shard_map/ppermute | solution.py:877
  6.0 1.3 %collective-permute-start.3 = (bf16[456,128]{1,0:T(8,128)(2,1)S(1)}, bf16[456,128]{1,0:T(8,128)(2,1)S(1)}, u32[]{:S(2)}, u32[]{:S(2)}) collective-permute-start(bf16[456,128]{1,0:T(8,128)(2,1)S(1)} %get-tuple-element.72.refs_0_), channel_id=1, source_target_pairs={{0,3},{1,2},{2,1},{3,0},{4,7},{5,6},{6,5},{7,4},{8,11},{9,10},{10,... | collective-permute-start | bytes 350216 | tf_op jit(solution)/shard_map/ppermute | solution.py:877
  7.3 0.2 collective-permute-start.4
  7.6 2.0 %collective-permute-start = (bf16[512,256]{1,0:T(8,128)(2,1)}, bf16[512,256]{1,0:T(8,128)(2,1)S(1)}, u32[]{:S(2)}, u32[]{:S(2)}) collective-permute-start(bf16[512,256]{1,0:T(8,128)(2,1)} %bitcast.35), channel_id=1, source_target_pairs={{0,28},{4,8},{8,4},{12,16},{16,12},{20,24},{24,20},{28,0},{1,29},{... | collective-permute-start | bytes 786440 | tf_op jit(solution)/shard_map/ppermute | solution.py:882
  9.6 1.0 %off_rows.1.choice_ref = bf16[512,4096]{1,0:T(8,128)(2,1)S(1)} custom-call(s32[1,4096]{1,0:T(1,128)S(1)} %bitcast.22), custom_call_target="tpu_custom_call" | custom-call | flops 2097152 | bytes 4194304 | tf_op jit(solution)/shard_map/off_rows/pallas_call | solution.py:197
  10.6 2.4 %gather_near.4.near_ref = bf16[4096,256]{1,0:T(8,128)(2,1)S(1)} custom-call(s32[32,128]{1,0:T(8,128)S(1)} %get-tuple-element.70.index_ref, bf16[512,256]{1,0:T(8,128)(2,1)S(1)} %get-tuple-element.69.own_ref.h_ref, bf16[512,256]{1,0:T(8,128)(2,1)S(1)} %collective-permute-done.1.pair_ref), custom_call_target="tpu_custom_call" | custom-call | flops 2147483648 | bytes 2097152 | tf_op jit(solution)/shard_map/gather_near/pallas_call | solution.py:151
  13.0 2.4 %gather_near.3.near_ref = bf16[4096,256]{1,0:T(8,128)(2,1)S(1)} custom-call(s32[32,128]{1,0:T(8,128)S(1)} %get-tuple-element.71.index_ref, bf16[512,256]{1,0:T(8,128)(2,1)S(1)} %get-tuple-element.69.own_ref.h_ref, bf16[512,256]{1,0:T(8,128)(2,1)S(1)} %collective-permute-done.1.pair_ref), custom_call_target="tpu_custom_call" | custom-call | flops 2147483648 | bytes 2097152 | tf_op jit(solution)/shard_map/gather_near/pallas_call | solution.py:151
  15.4 0.8 collective-permute-done.4
  16.3 0.1 collective-permute-start.6
  16.4 0.5 collective-permute-start.5
  16.9 0.2 collective-permute-done.off_ref
  17.1 1.3 %gather_off.3.hr_ref = bf16[4096,256]{1,0:T(8,128)(2,1)S(1)} custom-call(s32[32,128]{1,0:T(8,128)S(1)} %get-tuple-element.70.index_ref, bf16[512,256]{1,0:T(8,128)(2,1)S(1)} %collective-permute-done.off_ref, bf16[4096,256]{1,0:T(8,128)(2,1)S(1)} %gather_near.4.near_ref), custom_call_target="tpu_custom_call" | custom-call | flops 1073741824 | bytes 4194304 | tf_op jit(solution)/shard_map/gather_off/pallas_call | solution.py:176
  18.4 0.0 copy-start
  18.4 0.0 copy-start.6
  18.5 1.3 %gather_off.2.hs_ref = bf16[4096,256]{1,0:T(8,128)(2,1)S(1)} custom-call(s32[32,128]{1,0:T(8,128)S(1)} %get-tuple-element.71.index_ref, bf16[512,256]{1,0:T(8,128)(2,1)S(1)} %collective-permute-done.off_ref, bf16[4096,256]{1,0:T(8,128)(2,1)S(1)} %gather_near.3.near_ref), custom_call_target="tpu_custom_call" | custom-call | flops 1073741824 | bytes 4194304 | tf_op jit(solution)/shard_map/gather_off/pallas_call | solution.py:176
  19.8 0.0 collective-permute-done.5.refs_2_
  19.8 0.0 collective-permute-done.6.refs_3_
  19.8 0.2 copy-done
  20.0 7.2 %edge_forward.1 = (bf16[1824,256]{1,0:T(8,128)(2,1)S(1)}, bf16[4096,256]{1,0:T(8,128)(2,1)S(1)}, bf16[4096,256]{1,0:T(8,128)(2,1)S(1)}, s16[656,256]{1,0:T(8,128)(2,1)S(1)}) custom-call(s32[32,128]{1,0:T(8,128)S(1)} %bitcast.27, bf16[512,4096]{1,0:T(8,128)(2,1)S(1)} %off_rows.1.choice_ref, bf16[4096,256]{1,0:T(8,128)(2,1)S(1)} %gather_off.2.hs_ref, ...), custom_call_target="tpu_custom_call" | custom-call | flops 4831838208 | bytes 10485760 | tf_op jit(solution)/shard_map/edge_forward/pallas_call | solution.py:335
  27.2 2.0 %collective-permute-start.9 = (s16[656,256]{1,0:T(8,128)(2,1)S(1)}, s16[656,256]{1,0:T(8,128)(2,1)S(1)}, u32[]{:S(2)}, u32[]{:S(2)}) collective-permute-start(s16[656,256]{1,0:T(8,128)(2,1)S(1)} %get-tuple-element.85), channel_id=1, source_target_pairs={{0,28},{4,8},{8,4},{12,16},{16,12},{20,24},{24,20},{28,0},{1,29},{... | collective-permute-start | bytes 1007624 | tf_op jit(solution)/shard_map/ppermute | solution.py:882
  29.2 4.5 %near_sum.1 = (f32[256,256]{1,0:T(8,128)S(1)}, f32[256,256]{1,0:T(8,128)S(1)}, f32[512,256]{1,0:T(8,128)S(1)}) custom-call(s32[1,4096]{1,0:T(1,128)S(1)} %bitcast.23, bf16[4096,256]{1,0:T(8,128)(2,1)S(1)} %get-tuple-element.76.high_ref, bf16[4096,256]{1,0:T(8,128)(2,1)S(1)} %get-tuple-element.77.low_ref), custom_call_target="tpu_custom_call" | custom-call | flops 4294967296 | bytes 4194304 | tf_op jit(solution)/shard_map/near_sum/pallas_call | solution.py:420
  33.7 0.1 collective-permute-start.7
  33.8 0.5 collective-permute-start.8
  34.3 3.4 %edge_slope.1 = (bf16[4096,256]{1,0:T(8,128)(2,1)S(1)}, f32[4096,256]{1,0:T(8,128)S(1)}) custom-call(s32[32,128]{1,0:T(8,128)S(1)} %bitcast.28, bf16[4096,256]{1,0:T(8,128)(2,1)S(1)} %gather_off.2.hs_ref, bf16[4096,256]{1,0:T(8,128)(2,1)S(1)} %gather_off.3.hr_ref, bf16[4096,256]{1,0:T(8,128)(2,1)S(1)} %bitcast.18, bf16[1824,256]{1,0:T(8,128)(2,1)S(1)} %get-tuple-element.79.w_ref), custom_call_target="tpu_custom_call" | custom-call | flops 2147483648 | bytes 12582912 | tf_op jit(solution)/shard_map/edge_slope/pallas_call | solution.py:372
  37.7 0.0 collective-permute-done.8.more_ref
  37.7 0.5 collective-permute-done.9.off_ref
  38.2 1.2 %node_update.1 = (bf16[512,256]{1,0:T(8,128)(2,1)S(1)}, bf16[512,256]{1,0:T(8,128)(2,1)S(1)}, bf16[512,256]{1,0:T(8,128)(2,1)S(1)}, bf16[512,256]{1,0:T(8,128)(2...) custom-call(bf16[512,256]{1,0:T(8,128)(2,1)S(1)} %get-tuple-element.69.own_ref.h_ref, ...), custom_call_target="tpu_custom_call" | custom-call | flops 335544320 | bytes 2621440 | tf_op jit(solution)/shard_map/node_update/pallas_call | solution.py:473
  39.5 0.1 collective-permute-start.11
  39.6 1.3 %collective-permute-start.10 = (bf16[512,256]{1,0:T(8,128)(2,1)S(1)}, bf16[512,256]{1,0:T(8,128)(2,1)S(1)}, u32[]{:S(2)}, u32[]{:S(2)}) collective-permute-start(bf16[512,256]{1,0:T(8,128)(2,1)S(1)} %get-tuple-element.93.own_ref), channel_id=1, source_target_pairs={{0,28},{4,8},{8,4},{12,16},{16,12},{20,24},{24,20},{28,0},{1,29},{... | collective-permute-start | bytes 786440 | tf_op jit(solution)/shard_map/ppermute | solution.py:882
  40.8 1.3 %node_grads.1 = (f32[512,256]{1,0:T(8,128)}, f32[768,256]{1,0:T(8,128)S(1)}, f32[4,256]{1,0:T(4,128)S(1)}, f32[512,256]{1,0:T(8,128)S(1)}) custom-call(bf16[512,256]{1,0:T(8,128)(2,1)S(1)} %get-tuple-element.69.own_ref.h_ref, bf16[512,256]{1,0:T(8,128)(2,1)S(1)} %get-tuple-element.86.agg_ref, bf16[512,256]{1,0:T(8,128)(2,1)S(1)} %get-tuple-element.87.hidden_ref, ...), custom_call_target="tpu_custom_call" | custom-call | flops 268435456 | bytes 2359296 | tf_op jit(solution)/shard_map/node_grads/pallas_call | solution.py:512
  42.1 0.8 off_choice.1.choice_ref
  43.0 1.7 %edge_unit.1 = (f32[4096,256]{1,0:T(8,128)S(1)}, f32[4096,128]{1,0:T(8,128)S(1)}) custom-call(bf16[4096,256]{1,0:T(8,128)(2,1)S(1)} %get-tuple-element.95.hidden_ref, bf16[1824,256]{1,0:T(8,128)(2,1)S(1)} %get-tuple-element.79.w_ref), custom_call_target="tpu_custom_call" | custom-call | flops 536870912 | bytes 8388608 | tf_op jit(solution)/shard_map/edge_unit/pallas_call | solution.py:395
  44.7 0.0 collective-permute-done.11.pair_ref
  44.7 2.4 %gather_near.5.near_ref = bf16[4096,256]{1,0:T(8,128)(2,1)S(1)} custom-call(s32[32,128]{1,0:T(8,128)S(1)} %get-tuple-element.70.index_ref, bf16[512,256]{1,0:T(8,128)(2,1)S(1)} %get-tuple-element.93.own_ref, bf16[512,256]{1,0:T(8,128)(2,1)S(1)} %collective-permute-done.11.pair_ref), custom_call_target="tpu_custom_call" | custom-call | flops 2147483648 | bytes 2097152 | tf_op jit(solution)/shard_map/gather_near/pallas_call | solution.py:151
  47.1 1.8 %collective-permute-done.10.off_ref = bf16[512,256]{1,0:T(8,128)(2,1)S(1)} collective-permute-done((bf16[512,256]{1,0:T(8,128)(2,1)S(1)}, bf16[512,256]{1,0:T(8,128)(2,1)S(1)}, u32[]{:S(2)}, u32[]{:S(2)}) %collective-permute-start.10) | collective-permute-done | bytes 262176 | tf_op jit(solution)/shard_map/ppermute | solution.py:882
  49.0 6.2 %edge_backward.1 = (bf16[4096,256]{1,0:T(8,128)(2,1)S(1)}, f32[1824,128]{1,0:T(8,128)S(1)}, f32[1824,128]{1,0:T(8,128)S(1)}) custom-call(bf16[4096,512]{1,0:T(8,128)(2,1)S(1)} %off_choice.1.choice_ref, s32[1,4096]{1,0:T(1,128)S(1)} %bitcast.29, bf16[512,256]{1,0:T(8,128)(2,1)S(1)} %collective-permute-done.10.off_ref, ...), custom_call_target="tpu_custom_call" | custom-call | flops 4294967296 | bytes 20971520 | tf_op jit(solution)/shard_map/edge_backward/pallas_call | solution.py:601
  55.2 0.1 collective-permute-start.12
  55.3 1.9 %edge_grads.1 = bf16[4096,256]{1,0:T(8,128)(2,1)} custom-call(bf16[4096,256]{1,0:T(8,128)(2,1)S(1)} %get-tuple-element.107.d_pre_ref, bf16[1824,256]{1,0:T(8,128)(2,1)S(1)} %get-tuple-element.79.w_ref), custom_call_target="tpu_custom_call" | custom-call | flops 536870912 | bytes 4194304 | tf_op jit(solution)/shard_map/edge_grads/pallas_call | solution.py:716
  57.2 0.6 collective-permute-done.12.other_ref
  57.8 0.1 parted.1
  57.9 3.3 %collective-permute-start.13 = (bf16[464,128]{1,0:T(8,128)(2,1)S(1)}, bf16[464,128]{1,0:T(8,128)(2,1)S(1)}, u32[]{:S(2)}, u32[]{:S(2)}) collective-permute-start(bf16[464,128]{1,0:T(8,128)(2,1)S(1)} %get-tuple-element.111), channel_id=1, source_target_pairs={{0,2},{1,3},{2,0},{3,1},{4,6},{5,7},{6,4},{7,5},{8,10},{9,11},{10,... | collective-permute-start | bytes 356360 | tf_op jit(solution)/shard_map/ppermute | solution.py:877
  61.1 1.1 %collective-permute-start.14 = (bf16[464,128]{1,0:T(8,128)(2,1)S(1)}, bf16[464,128]{1,0:T(8,128)(2,1)S(1)}, u32[]{:S(2)}, u32[]{:S(2)}) collective-permute-start(bf16[464,128]{1,0:T(8,128)(2,1)S(1)} %get-tuple-element.112), channel_id=1, source_target_pairs={{0,3},{1,2},{2,1},{3,0},{4,7},{5,6},{6,5},{7,4},{8,11},{9,10},{10,... | collective-permute-start | bytes 356360 | tf_op jit(solution)/shard_map/ppermute | solution.py:877
  62.2 5.0 %sender_part.1.part_ref = f32[1536,256]{1,0:T(8,128)S(1)} custom-call(s32[1,4096]{1,0:T(1,128)S(1)} %bitcast.26, bf16[4096,256]{1,0:T(8,128)(2,1)S(1)} %get-tuple-element.107.d_pre_ref, bf16[1824,256]{1,0:T(8,128)(2,1)S(1)} %get-tuple-element.79.w_ref), custom_call_target="tpu_custom_call" | custom-call | flops 3221225472 | bytes 2097152 | tf_op jit(solution)/shard_map/sender_part/pallas_call | solution.py:639
  67.2 3.4 %receiver_part.1 = (bf16[512,256]{1,0:T(8,128)(2,1)S(1)}, bf16[512,256]{1,0:T(8,128)(2,1)S(1)}) custom-call(s32[1,4096]{1,0:T(1,128)S(1)} %bitcast.24, bf16[4096,256]{1,0:T(8,128)(2,1)S(1)} %get-tuple-element.107.d_pre_ref, bf16[1824,256]{1,0:T(8,128)(2,1)S(1)} %get-tuple-element.79.w_ref, f32[1536,256]{1,0:T(8,128)S(1)} %sender_part.1.part_ref), custom_call_target="tpu_custom_call" | custom-call | flops 2147483648 | bytes 2097152 | tf_op jit(solution)/shard_map/receiver_part/pallas_call | solution.py:670
  70.6 0.0 collective-permute-done.13.refs_0_
  70.6 0.5 collective-permute-done.15.refs_2_
  71.1 0.1 gathered.1.mine_ref
  71.2 0.8 collective-permute-start.16
  72.0 1.6 %own_part.1.own_ref = f32[512,256]{1,0:T(8,128)S(1)} custom-call(s32[1,4096]{1,0:T(1,128)S(1)} %bitcast.25, bf16[4096,256]{1,0:T(8,128)(2,1)S(1)} %get-tuple-element.107.d_pre_ref, bf16[1824,256]{1,0:T(8,128)(2,1)S(1)} %get-tuple-element.79.w_ref, f32[1536,256]{1,0:T(8,128)S(1)} %sender_part.1.part_ref, f32[512,256]{1,0:T(8,128)S(1)} %get-tuple-element.116.back_ref), custom_call_target="tpu_custom_call" | custom-call | flops 1073741824 | bytes 2097152 | tf_op jit(solution)/shard_map/own_part/pallas_call | solution.py:695
  73.7 2.4 %collective-permute-done.16.other_ref = bf16[464,128]{1,0:T(8,128)(2,1)S(1)} collective-permute-done((bf16[464,128]{1,0:T(8,128)(2,1)S(1)}, bf16[464,128]{1,0:T(8,128)(2,1)S(1)}, u32[]{:S(2)}, u32[]{:S(2)}) %collective-permute-start.16) | collective-permute-done | bytes 118816 | tf_op jit(solution)/shard_map/ppermute | solution.py:877
  76.1 1.5 %collective-permute-start.17 = (bf16[464,128]{1,0:T(8,128)(2,1)S(1)}, bf16[464,128]{1,0:T(8,128)(2,1)S(1)}, u32[]{:S(2)}, u32[]{:S(2)}) collective-permute-start(bf16[464,128]{1,0:T(8,128)(2,1)S(1)} %add.16.mine_ref), channel_id=1, source_target_pairs={{0,16},{4,20},{8,24},{12,28},{16,0},{20,4},{24,8},{28,12},{1,17},{... | collective-permute-start | bytes 356360 | tf_op jit(solution)/shard_map/ppermute | solution.py:877
  77.6 0.9 collective-permute-start.24
  78.5 2.5 %collective-permute-done.17.other_ref = bf16[464,128]{1,0:T(8,128)(2,1)S(1)} collective-permute-done((bf16[464,128]{1,0:T(8,128)(2,1)S(1)}, bf16[464,128]{1,0:T(8,128)(2,1)S(1)}, u32[]{:S(2)}, u32[]{:S(2)}) %collective-permute-start.17) | collective-permute-done | bytes 118816 | tf_op jit(solution)/shard_map/ppermute | solution.py:877
  81.0 0.2 finish.1.mine_ref
  81.2 2.2 %collective-permute-start.18 = (f32[16,128]{1,0:T(8,128)S(1)}, f32[16,128]{1,0:T(8,128)S(1)}, u32[]{:S(2)}, u32[]{:S(2)}) collective-permute-start(f32[16,128]{1,0:T(8,128)S(1)} %slice.11), channel_id=1, source_target_pairs={{0,1},{1,0},{2,3},{3,2},{4,5},{5,4},{6,7},{7,6},{8,9},{9,8},{10,11... | collective-permute-start | bytes 24584 | tf_op jit(solution)/shard_map/ppermute | solution.py:877
  83.4 0.7 collective-permute-start.19
  84.1 1.7 %collective-permute-start.20 = (f32[16,128]{1,0:T(8,128)S(1)}, f32[16,128]{1,0:T(8,128)S(1)}, u32[]{:S(2)}, u32[]{:S(2)}) collective-permute-start(f32[16,128]{1,0:T(8,128)S(1)} %slice.11), channel_id=1, source_target_pairs={{0,3},{1,2},{2,1},{3,0},{4,7},{5,6},{6,5},{7,4},{8,11},{9,10},{10,... | collective-permute-start | bytes 24584 | tf_op jit(solution)/shard_map/ppermute | solution.py:877
  85.9 0.1 collective-permute-start.22
  86.0 2.0 %collective-permute-done.19 = f32[16,128]{1,0:T(8,128)S(1)} collective-permute-done((f32[16,128]{1,0:T(8,128)S(1)}, f32[16,128]{1,0:T(8,128)S(1)}, u32[]{:S(2)}, u32[]{:S(2)}) %collective-permute-start.19) | collective-permute-done | bytes 8224 | tf_op jit(solution)/shard_map/ppermute | solution.py:877
  88.0 1.6 %collective-permute-done.20 = f32[16,128]{1,0:T(8,128)S(1)} collective-permute-done((f32[16,128]{1,0:T(8,128)S(1)}, f32[16,128]{1,0:T(8,128)S(1)}, u32[]{:S(2)}, u32[]{:S(2)}) %collective-permute-start.20) | collective-permute-done | bytes 8224 | tf_op jit(solution)/shard_map/ppermute | solution.py:877
  90.2 0.5 collective-permute-done.21.more_ref
  90.8 2.3 %adam.1 = (f32[456,256]{1,0:T(8,128)}, f32[456,256]{1,0:T(8,128)}, f32[456,256]{1,0:T(8,128)}, f32[456,256]{1,0:T(8,128)}, f32[1,1]{1,0:T(1,128)}, /*index=5*/f32[8,256]{1,0:T(8,128)}, f32[512,256]{1,0:T(8,128)}) custom-call(f32[8,128]{1,0:T(8,128)S(1)} %broadcast_in_dim.15.step_ref, f32[16,128]{1,0:T(8,128)S(1)} %add_add_fusion.stats_ref, ...), custom_call_target="tpu_custom_call" | custom-call | flops 2334720 | bytes 3735552 | tf_op jit(solution)/shard_map/adam/pallas_call | solution.py:858
  (33 shorter events, 0.2 us)
Async XLA Ops:
  0.6 9.9 %collective-permute-start.1 = (bf16[512,256]{1,0:T(8,128)(2,1)}, bf16[512,256]{1,0:T(8,128)(2,1)S(1)}, u32[]{:S(2)}, u32[]{:S(2)}) collective-permute-start(bf16[512,256]{1,0:T(8,128)(2,1)} %bitcast.33), channel_id=1, source_target_pairs={{0,4},{4,0},{8,12},{12,8},{16,20},{20,16},{24,28},{28,24},{1,5},{5... | collective-permute-start | bytes 786440 | tf_op jit(solution)/shard_map/ppermute | solution.py:877
  2.3 13.1 %collective-permute-start.2 = (bf16[456,128]{1,0:T(8,128)(2,1)S(1)}, bf16[456,128]{1,0:T(8,128)(2,1)S(1)}, u32[]{:S(2)}, u32[]{:S(2)}) collective-permute-start(bf16[456,128]{1,0:T(8,128)(2,1)S(1)} %get-tuple-element.72.refs_0_), channel_id=1, source_target_pairs={{0,2},{1,3},{2,0},{3,1},{4,6},{5,7},{6,4},{7,5},{8,10},{9,11},{10,... | collective-permute-start | bytes 350216 | tf_op jit(solution)/shard_map/ppermute | solution.py:877
  6.0 9.4 %collective-permute-start.3 = (bf16[456,128]{1,0:T(8,128)(2,1)S(1)}, bf16[456,128]{1,0:T(8,128)(2,1)S(1)}, u32[]{:S(2)}, u32[]{:S(2)}) collective-permute-start(bf16[456,128]{1,0:T(8,128)(2,1)S(1)} %get-tuple-element.72.refs_0_), channel_id=1, source_target_pairs={{0,3},{1,2},{2,1},{3,0},{4,7},{5,6},{6,5},{7,4},{8,11},{9,10},{10,... | collective-permute-start | bytes 350216 | tf_op jit(solution)/shard_map/ppermute | solution.py:877
  7.3 8.9 %collective-permute-start.4 = (bf16[456,128]{1,0:T(8,128)(2,1)S(1)}, bf16[456,128]{1,0:T(8,128)(2,1)S(1)}, u32[]{:S(2)}, u32[]{:S(2)}) collective-permute-start(bf16[456,128]{1,0:T(8,128)(2,1)S(1)} %get-tuple-element.72.refs_0_), channel_id=1, source_target_pairs={{0,1},{1,0},{2,3},{3,2},{4,5},{5,4},{6,7},{7,6},{8,9},{9,8},{10,11... | collective-permute-start | bytes 350216 | tf_op jit(solution)/shard_map/ppermute | solution.py:877
  7.6 9.5 %collective-permute-start = (bf16[512,256]{1,0:T(8,128)(2,1)}, bf16[512,256]{1,0:T(8,128)(2,1)S(1)}, u32[]{:S(2)}, u32[]{:S(2)}) collective-permute-start(bf16[512,256]{1,0:T(8,128)(2,1)} %bitcast.35), channel_id=1, source_target_pairs={{0,28},{4,8},{8,4},{12,16},{16,12},{20,24},{24,20},{28,0},{1,29},{... | collective-permute-start | bytes 786440 | tf_op jit(solution)/shard_map/ppermute | solution.py:882
  16.3 3.5 %collective-permute-start.6 = (bf16[1368,128]{1,0:T(8,128)(2,1)S(1)}, bf16[1368,128]{1,0:T(8,128)(2,1)S(1)}, u32[]{:S(2)}, u32[]{:S(2)}) collective-permute-start(bf16[1368,128]{1,0:T(8,128)(2,1)S(1)} %constant_dynamic-update-slice_fusion.refs_1_), channel_id=1, source_target_pairs={{0,4},{4,0},{8,12},{12,8},{16,20},{20,16},{24,28},{28,24},{1,5},{5... | collective-permute-start | bytes 1050632 | tf_op jit(solution)/shard_map/ppermute | solution.py:877
  16.4 3.4 %collective-permute-start.5 = (bf16[456,128]{1,0:T(8,128)(2,1)S(1)}, bf16[456,128]{1,0:T(8,128)(2,1)S(1)}, u32[]{:S(2)}, u32[]{:S(2)}) collective-permute-start(bf16[456,128]{1,0:T(8,128)(2,1)S(1)} %get-tuple-element.72.refs_0_), channel_id=1, source_target_pairs={{0,4},{4,0},{8,12},{12,8},{16,20},{20,16},{24,28},{28,24},{1,5},{5... | collective-permute-start | bytes 350216 | tf_op jit(solution)/shard_map/ppermute | solution.py:877
  18.4 1.6 %copy-start = (bf16[1,4096,256]{2,1,0:T(8,128)(2,1)S(1)}, bf16[1,4096,256]{2,1,0:T(8,128)(2,1)}, u32[]{:S(2)}) copy-start(bf16[1,4096,256]{2,1,0:T(8,128)(2,1)} %param.13) | copy-start | bytes 6291460
  18.4 1.6 %copy-start.6 = (s32[4096]{0:T(1024)S(1)}, s32[4096]{0:T(1024)}, u32[]{:S(2)}) copy-start(s32[4096]{0:T(1024)} %param.16) | copy-start | bytes 49156
  27.2 11.0 %collective-permute-start.9 = (s16[656,256]{1,0:T(8,128)(2,1)S(1)}, s16[656,256]{1,0:T(8,128)(2,1)S(1)}, u32[]{:S(2)}, u32[]{:S(2)}) collective-permute-start(s16[656,256]{1,0:T(8,128)(2,1)S(1)} %get-tuple-element.85), channel_id=1, source_target_pairs={{0,28},{4,8},{8,4},{12,16},{16,12},{20,24},{24,20},{28,0},{1,29},{... | collective-permute-start | bytes 1007624 | tf_op jit(solution)/shard_map/ppermute | solution.py:882
  33.7 4.0 %collective-permute-start.7 = (f32[256,256]{1,0:T(8,128)S(1)}, f32[256,256]{1,0:T(8,128)S(1)}, u32[]{:S(2)}, u32[]{:S(2)}) collective-permute-start(f32[256,256]{1,0:T(8,128)S(1)} %get-tuple-element.83), channel_id=1, source_target_pairs={{0,4},{4,0},{8,12},{12,8},{16,20},{20,16},{24,28},{28,24},{1,5},{5... | collective-permute-start | bytes 786440 | tf_op jit(solution)/shard_map/ppermute | solution.py:877
  33.8 3.9 %collective-permute-start.8 = (f32[256,256]{1,0:T(8,128)S(1)}, f32[256,256]{1,0:T(8,128)S(1)}, u32[]{:S(2)}, u32[]{:S(2)}) collective-permute-start(f32[256,256]{1,0:T(8,128)S(1)} %get-tuple-element.84), channel_id=1, source_target_pairs={{0,4},{4,0},{8,12},{12,8},{16,20},{20,16},{24,28},{28,24},{1,5},{5... | collective-permute-start | bytes 786440 | tf_op jit(solution)/shard_map/ppermute | solution.py:877
  34.3 4.0 %copy-start.1 = (f32[1,512,256]{2,1,0:T(8,128)S(1)}, f32[1,512,256]{2,1,0:T(8,128)}, u32[]{:S(2)}) copy-start(f32[1,512,256]{2,1,0:T(8,128)} %param.23) | copy-start | bytes 1572868
  34.3 4.0 %copy-start.7 = (s32[512]{0:T(512)S(1)}, s32[512]{0:T(512)}, u32[]{:S(2)}) copy-start(s32[512]{0:T(512)} %param.17) | copy-start | bytes 6148
  39.5 5.2 %collective-permute-start.11 = (bf16[512,256]{1,0:T(8,128)(2,1)S(1)}, bf16[512,256]{1,0:T(8,128)(2,1)S(1)}, u32[]{:S(2)}, u32[]{:S(2)}) collective-permute-start(bf16[512,256]{1,0:T(8,128)(2,1)S(1)} %get-tuple-element.93.own_ref), channel_id=1, source_target_pairs={{0,4},{4,0},{8,12},{12,8},{16,20},{20,16},{24,28},{28,24},{1,5},{5... | collective-permute-start | bytes 786440 | tf_op jit(solution)/shard_map/ppermute | solution.py:877
  39.6 9.4 %collective-permute-start.10 = (bf16[512,256]{1,0:T(8,128)(2,1)S(1)}, bf16[512,256]{1,0:T(8,128)(2,1)S(1)}, u32[]{:S(2)}, u32[]{:S(2)}) collective-permute-start(bf16[512,256]{1,0:T(8,128)(2,1)S(1)} %get-tuple-element.93.own_ref), channel_id=1, source_target_pairs={{0,28},{4,8},{8,4},{12,16},{16,12},{20,24},{24,20},{28,0},{1,29},{... | collective-permute-start | bytes 786440 | tf_op jit(solution)/shard_map/ppermute | solution.py:882
  55.2 2.6 %collective-permute-start.12 = (f32[1824,128]{1,0:T(8,128)S(1)}, f32[1824,128]{1,0:T(8,128)S(1)}, u32[]{:S(2)}, u32[]{:S(2)}) collective-permute-start(f32[1824,128]{1,0:T(8,128)S(1)} %get-tuple-element.103), channel_id=1, source_target_pairs={{0,4},{4,0},{8,12},{12,8},{16,20},{20,16},{24,28},{28,24},{1,5},{5... | collective-permute-start | bytes 2801672 | tf_op jit(solution)/shard_map/ppermute | solution.py:877
  57.9 12.7 %collective-permute-start.13 = (bf16[464,128]{1,0:T(8,128)(2,1)S(1)}, bf16[464,128]{1,0:T(8,128)(2,1)S(1)}, u32[]{:S(2)}, u32[]{:S(2)}) collective-permute-start(bf16[464,128]{1,0:T(8,128)(2,1)S(1)} %get-tuple-element.111), channel_id=1, source_target_pairs={{0,2},{1,3},{2,0},{3,1},{4,6},{5,7},{6,4},{7,5},{8,10},{9,11},{10,... | collective-permute-start | bytes 356360 | tf_op jit(solution)/shard_map/ppermute | solution.py:877
  61.1 9.4 %collective-permute-start.14 = (bf16[464,128]{1,0:T(8,128)(2,1)S(1)}, bf16[464,128]{1,0:T(8,128)(2,1)S(1)}, u32[]{:S(2)}, u32[]{:S(2)}) collective-permute-start(bf16[464,128]{1,0:T(8,128)(2,1)S(1)} %get-tuple-element.112), channel_id=1, source_target_pairs={{0,3},{1,2},{2,1},{3,0},{4,7},{5,6},{6,5},{7,4},{8,11},{9,10},{10,... | collective-permute-start | bytes 356360 | tf_op jit(solution)/shard_map/ppermute | solution.py:877
  62.2 8.9 %collective-permute-start.15 = (bf16[464,128]{1,0:T(8,128)(2,1)S(1)}, bf16[464,128]{1,0:T(8,128)(2,1)S(1)}, u32[]{:S(2)}, u32[]{:S(2)}) collective-permute-start(bf16[464,128]{1,0:T(8,128)(2,1)S(1)} %get-tuple-element.113), channel_id=1, source_target_pairs={{0,1},{1,0},{2,3},{3,2},{4,5},{5,4},{6,7},{7,6},{8,9},{9,8},{10,11... | collective-permute-start | bytes 356360 | tf_op jit(solution)/shard_map/ppermute | solution.py:877
  71.2 4.9 %collective-permute-start.16 = (bf16[464,128]{1,0:T(8,128)(2,1)S(1)}, bf16[464,128]{1,0:T(8,128)(2,1)S(1)}, u32[]{:S(2)}, u32[]{:S(2)}) collective-permute-start(bf16[464,128]{1,0:T(8,128)(2,1)S(1)} %gathered.1.mine_ref), channel_id=1, source_target_pairs={{0,8},{4,12},{8,0},{12,4},{16,24},{20,28},{24,16},{28,20},{1,9},{5... | collective-permute-start | bytes 356360 | tf_op jit(solution)/shard_map/ppermute | solution.py:877
  72.0 18.8 %copy-start.2 = (f32[456,256]{1,0:T(8,128)S(1)}, f32[456,256]{1,0:T(8,128)}, u32[]{:S(2)}) copy-start(f32[456,256]{1,0:T(8,128)} %params_ref.1) | copy-start | bytes 1400836
  72.0 18.8 %copy-start.3 = (f32[456,256]{1,0:T(8,128)S(1)}, f32[456,256]{1,0:T(8,128)}, u32[]{:S(2)}) copy-start(f32[456,256]{1,0:T(8,128)} %first_ref.1) | copy-start | bytes 1400836
  72.0 18.8 %copy-start.4 = (f32[456,256]{1,0:T(8,128)S(1)}, f32[456,256]{1,0:T(8,128)}, u32[]{:S(2)}) copy-start(f32[456,256]{1,0:T(8,128)} %second_ref.1) | copy-start | bytes 1400836
  72.0 18.8 %copy-start.5 = (f32[456,256]{1,0:T(8,128)S(1)}, f32[456,256]{1,0:T(8,128)}, u32[]{:S(2)}) copy-start(f32[456,256]{1,0:T(8,128)} %averaged_ref.1) | copy-start | bytes 1400836
  76.1 4.9 %collective-permute-start.17 = (bf16[464,128]{1,0:T(8,128)(2,1)S(1)}, bf16[464,128]{1,0:T(8,128)(2,1)S(1)}, u32[]{:S(2)}, u32[]{:S(2)}) collective-permute-start(bf16[464,128]{1,0:T(8,128)(2,1)S(1)} %add.16.mine_ref), channel_id=1, source_target_pairs={{0,16},{4,20},{8,24},{12,28},{16,0},{20,4},{24,8},{28,12},{1,17},{... | collective-permute-start | bytes 356360 | tf_op jit(solution)/shard_map/ppermute | solution.py:877
  77.6 13.2 %collective-permute-start.23 = (bf16[512,256]{1,0:T(8,128)(2,1)S(1)}, bf16[512,256]{1,0:T(8,128)(2,1)S(1)}, u32[]{:S(2)}, u32[]{:S(2)}) collective-permute-start(bf16[512,256]{1,0:T(8,128)(2,1)S(1)} %get-tuple-element.119), channel_id=1, source_target_pairs={{0,4},{4,0},{8,12},{12,8},{16,20},{20,16},{24,28},{28,24},{1,5},{5... | collective-permute-start | bytes 786440 | tf_op jit(solution)/shard_map/ppermute | solution.py:877
  77.6 13.2 %collective-permute-start.24 = (bf16[512,256]{1,0:T(8,128)(2,1)S(1)}, bf16[512,256]{1,0:T(8,128)(2,1)S(1)}, u32[]{:S(2)}, u32[]{:S(2)}) collective-permute-start(bf16[512,256]{1,0:T(8,128)(2,1)S(1)} %get-tuple-element.120), channel_id=1, source_target_pairs={{0,28},{4,8},{8,4},{12,16},{16,12},{20,24},{24,20},{28,0},{1,29},{... | collective-permute-start | bytes 786440 | tf_op jit(solution)/shard_map/ppermute | solution.py:882
  81.2 4.7 %collective-permute-start.18 = (f32[16,128]{1,0:T(8,128)S(1)}, f32[16,128]{1,0:T(8,128)S(1)}, u32[]{:S(2)}, u32[]{:S(2)}) collective-permute-start(f32[16,128]{1,0:T(8,128)S(1)} %slice.11), channel_id=1, source_target_pairs={{0,1},{1,0},{2,3},{3,2},{4,5},{5,4},{6,7},{7,6},{8,9},{9,8},{10,11... | collective-permute-start | bytes 24584 | tf_op jit(solution)/shard_map/ppermute | solution.py:877
  83.4 4.5 %collective-permute-start.19 = (f32[16,128]{1,0:T(8,128)S(1)}, f32[16,128]{1,0:T(8,128)S(1)}, u32[]{:S(2)}, u32[]{:S(2)}) collective-permute-start(f32[16,128]{1,0:T(8,128)S(1)} %slice.11), channel_id=1, source_target_pairs={{0,2},{1,3},{2,0},{3,1},{4,6},{5,7},{6,4},{7,5},{8,10},{9,11},{10,... | collective-permute-start | bytes 24584 | tf_op jit(solution)/shard_map/ppermute | solution.py:877
  84.1 5.4 %collective-permute-start.20 = (f32[16,128]{1,0:T(8,128)S(1)}, f32[16,128]{1,0:T(8,128)S(1)}, u32[]{:S(2)}, u32[]{:S(2)}) collective-permute-start(f32[16,128]{1,0:T(8,128)S(1)} %slice.11), channel_id=1, source_target_pairs={{0,3},{1,2},{2,1},{3,0},{4,7},{5,6},{6,5},{7,4},{8,11},{9,10},{10,... | collective-permute-start | bytes 24584 | tf_op jit(solution)/shard_map/ppermute | solution.py:877
  85.9 4.9 %collective-permute-start.22 = (f32[456,128]{1,0:T(8,128)S(1)}, f32[456,128]{1,0:T(8,128)S(1)}, u32[]{:S(2)}, u32[]{:S(2)}) collective-permute-start(f32[456,128]{1,0:T(8,128)S(1)} %slice.12), channel_id=1, source_target_pairs={{0,4},{4,0},{8,12},{12,8},{16,20},{20,16},{24,28},{28,24},{1,5},{5... | collective-permute-start | bytes 700424 | tf_op jit(solution)/shard_map/ppermute | solution.py:877
  89.6 1.2 %collective-permute-start.21 = (f32[16,128]{1,0:T(8,128)S(1)}, f32[16,128]{1,0:T(8,128)S(1)}, u32[]{:S(2)}, u32[]{:S(2)}) collective-permute-start(f32[16,128]{1,0:T(8,128)S(1)} %add_add_fusion.stats_ref), channel_id=1, source_target_pairs={{0,4},{4,0},{8,12},{12,8},{16,20},{20,16},{24,28},{28,24},{1,5},{5... | collective-permute-start | bytes 24584 | tf_op jit(solution)/shard_map/ppermute | solution.py:877
